TPU v7x, 32 devices: a whole 2x2x4 slice. The times are simulated.
32 devices in a mesh: dp: 8 (over z, y), mp: 4 (over x, core).
Axes of the slice: x: 2, y: 2, z: 4, core: 2. Of those that a mesh axis runs over, the one named last changes fastest.
Arguments:
- hidden: bfloat16 [24, 1024, 1024], P('dp', 'mp'), may hold values from -6 to 6
- cotangent: bfloat16 [24, 1024, 1024], P('dp', 'mp'), may hold values from -6 to 6
- adapter_ids: int32 [24], P('dp'), may hold values from 0 to 7
- attn_gain: bfloat16 [1024], replicated, may hold values from 0.25 to 1.75
- mlp_gain: bfloat16 [1024], replicated, may hold values from 0.25 to 1.75
- joined_weight: bfloat16 [1024, 3, 1024], P('dp', None, 'mp'), may hold values from -0.1875 to 0.1875
- merge_weight_matrix: bfloat16 [1024, 1024], P('dp', 'mp'), may hold values from -0.75 to 0.75
- expand_weight: bfloat16 [1024, 2, 2624], P('dp', None, 'mp'), may hold values from -0.1875 to 0.1875
- shrink_weight_matrix: bfloat16 [1024, 2624], P('dp', 'mp'), may hold values from -0.15625 to 0.15625
- joined_lower: bfloat16 [8, 1024, 16], replicated, may hold values from -0.1875 to 0.1875
- joined_up_matrices: bfloat16 [8, 16, 3, 1024], P(None, None, None, 'mp'), may hold values from -0.375 to 0.375
- merge_lower: bfloat16 [8, 1024, 16], P(None, 'mp'), may hold values from -0.75 to 0.75
- merge_up_matrices: bfloat16 [8, 16, 1024], replicated, may hold values from -0.375 to 0.375
- expand_lower: bfloat16 [8, 1024, 16], replicated, may hold values from -0.1875 to 0.1875
- expand_up_matrices: bfloat16 [8, 16, 2, 2624], P(None, None, None, 'mp'), may hold values from -0.375 to 0.375
- shrink_lower: bfloat16 [8, 2624, 16], P(None, 'mp'), may hold values from -0.15625 to 0.15625
- shrink_up_matrices: bfloat16 [8, 16, 1024], replicated, may hold values from -0.375 to 0.375
Outputs:
- output: bfloat16 [24, 1024, 1024], P('dp', 'mp')
- hidden_grad: bfloat16 [24, 1024, 1024], P('dp', 'mp')
- joined_lower_grad: float32 [8, 1024, 16], replicated
- joined_upper_grad: float32 [8, 16, 3, 1024], P(None, None, None, 'mp')
- merge_lower_grad: float32 [8, 1024, 16], P(None, 'mp')
- merge_upper_grad: float32 [8, 16, 1024], replicated
- expand_lower_grad: float32 [8, 1024, 16], replicated
- expand_upper_grad: float32 [8, 16, 2, 2624], P(None, None, None, 'mp')
- shrink_lower_grad: float32 [8, 2624, 16], P(None, 'mp')
- shrink_upper_grad: float32 [8, 16, 1024], replicated
All inputs are finite; a program needn't handle non-finite values.
Results may differ from a plain program's by a relative error of at most 0.024.
Values may be sent and summed in bfloat16 or wider, within the bound.
No kernel may reach another device: no remote copies, remote signals or barrier semaphores. Data moves between devices by JAX's collectives and lax.ppermute only.
A program may use at most 320 MiB of HBM per device.

v0:
```python
import jax
import jax.numpy as jnp
from jax import lax
from jax.sharding import PartitionSpec as P

HEAD_DIM = 64
ADAPTERS = 8


MATMUL_PRECISION = lax.Precision.HIGHEST
ADAPTER_SCALE = 2.0
NORM_EPS = 1e-05
ROPE_BASE = 160000.0


def norm_rows(values, norm_gain):
    centred = values - jnp.mean(values, axis=-1, keepdims=True)
    spread = jnp.mean(centred * centred, axis=-1, keepdims=True)
    return centred * lax.rsqrt(spread + NORM_EPS) * norm_gain


def rotary_tables(length, head_width):
    half_width = head_width // 2
    inverse = ROPE_BASE ** (-(jnp.arange(half_width, dtype=jnp.float32) * 2.0 / head_width))
    angles = jnp.arange(length, dtype=jnp.float32)[:, None] * inverse[None, :]
    angles = jnp.concatenate([angles, angles], axis=1)
    return (jnp.cos(angles), jnp.sin(angles))


def rotate(values, cosine_table, sine_table):
    half_width = values.shape[-1] // 2
    turned = jnp.concatenate([-values[..., half_width:], values[..., :half_width]], axis=-1)
    return values * cosine_table[:, None, :] + turned * sine_table[:, None, :]


def gated_units(expanded_hidden):
    return jax.nn.gelu(expanded_hidden[:, 0], approximate=False) * expanded_hidden[:, 1]


def pick_table(lookup, which_set):
    matches = jnp.arange(lookup.shape[0], dtype=jnp.int32) == which_set
    shaped = matches.reshape((lookup.shape[0],) + (1,) * (lookup.ndim - 1))
    return jnp.sum(jnp.where(shaped, lookup.astype(jnp.float32), 0.0), axis=0)


def pick_all(tables, which_set):
    picked = [pick_table(lookup, which_set) for lookup in tables]
    return tuple(
        (
            picked[position].astype(jnp.bfloat16) if position % 2 == 0 else picked[position]
            for position in range(8)
        )
    )


def spread_table(gradient, which_set, set_count):
    matches = (jnp.arange(set_count, dtype=jnp.int32) == which_set).astype(jnp.float32)
    return matches.reshape((set_count,) + (1,) * gradient.ndim) * gradient[None]


def share_rows(values):
    return lax.all_gather(values, "mp", axis=0, tiled=True)


def total_rows(values):
    return lax.psum_scatter(
        values.astype(jnp.bfloat16), "mp", scatter_dimension=0, tiled=True
    ).astype(jnp.float32)


def share_grads(values):
    return lax.all_gather(values, "mp", axis=0, tiled=True)


def total_grads(values):
    return lax.psum_scatter(
        values.astype(jnp.bfloat16), "mp", scatter_dimension=0, tiled=True
    ).astype(jnp.float32)


def forward_micro(own_rows, norm_gains, weights, picked, rope_tables):
    attn_gain, mlp_gain = norm_gains
    joined_weight, merge_weight_matrix, expand_weight, shrink_weight_matrix = weights
    (
        joined_lower,
        joined_up_matrices,
        merge_lower,
        merge_up_matrices,
        expand_lower,
        expand_up_matrices,
        shrink_lower,
        shrink_up_matrices,
    ) = picked
    cosine_table, sine_table = rope_tables
    start_rows = own_rows.astype(jnp.float32)
    normed = norm_rows(start_rows, attn_gain).astype(jnp.bfloat16)
    whole = share_rows(normed)
    length = whole.shape[0]
    width_here = joined_weight.shape[2]
    heads_here = width_here // HEAD_DIM
    joined_down_proj = jnp.dot(whole, joined_lower, preferred_element_type=jnp.float32)
    joined_projection = jnp.einsum(
        "ld,dce->lce", whole, joined_weight, preferred_element_type=jnp.float32
    )
    joined_projection = joined_projection + ADAPTER_SCALE * jnp.einsum(
        "vj,jfk->vfk", joined_down_proj, joined_up_matrices, precision=MATMUL_PRECISION
    )
    query_rows = rotate(
        joined_projection[:, 0].reshape(length, heads_here, HEAD_DIM), cosine_table, sine_table
    ).astype(jnp.bfloat16)
    key_rows = rotate(
        joined_projection[:, 1].reshape(length, heads_here, HEAD_DIM), cosine_table, sine_table
    ).astype(jnp.bfloat16)
    value_rows = joined_projection[:, 2].reshape(length, heads_here, HEAD_DIM).astype(jnp.bfloat16)
    score_scale = HEAD_DIM ** (-0.5)
    scores = (
        jnp.einsum("qhe,khe->hqk", query_rows, key_rows, preferred_element_type=jnp.float32)
        * score_scale
    )
    row_top = jnp.max(scores, axis=-1, keepdims=True)
    raised = jnp.exp(scores - row_top)
    row_total = jnp.sum(raised, axis=-1, keepdims=True)
    attn_probs = (raised / row_total).astype(jnp.bfloat16)
    log_total = row_top + jnp.log(row_total)
    context_rows = jnp.einsum(
        "hqk,khe->qhe", attn_probs, value_rows, preferred_element_type=jnp.float32
    )
    context_rows = context_rows.reshape(length, width_here).astype(jnp.bfloat16)
    merge_down_proj = jnp.dot(context_rows, merge_lower, preferred_element_type=jnp.float32)
    merged_output = jnp.einsum(
        "le,oe->lo", context_rows, merge_weight_matrix, preferred_element_type=jnp.float32
    )
    merged_output = merged_output + ADAPTER_SCALE * jnp.dot(
        merge_down_proj, merge_up_matrices, precision=MATMUL_PRECISION
    )
    middle = start_rows + total_rows(merged_output)
    normed_mlp = norm_rows(middle, mlp_gain).astype(jnp.bfloat16)
    whole_mlp = share_rows(normed_mlp)
    expand_down_proj = jnp.dot(whole_mlp, expand_lower, preferred_element_type=jnp.float32)
    expanded_hidden = jnp.einsum(
        "ld,dcf->lcf", whole_mlp, expand_weight, preferred_element_type=jnp.float32
    )
    expanded_hidden = expanded_hidden + ADAPTER_SCALE * jnp.einsum(
        "xv,vmj->xmj", expand_down_proj, expand_up_matrices, precision=MATMUL_PRECISION
    )
    activated_hidden = gated_units(expanded_hidden).astype(jnp.bfloat16)
    shrink_down_proj = jnp.dot(activated_hidden, shrink_lower, preferred_element_type=jnp.float32)
    shrunk_output = jnp.einsum(
        "lf,of->lo", activated_hidden, shrink_weight_matrix, preferred_element_type=jnp.float32
    )
    shrunk_output = shrunk_output + ADAPTER_SCALE * jnp.dot(
        shrink_down_proj, shrink_up_matrices, precision=MATMUL_PRECISION
    )
    output_rows = (middle + total_rows(shrunk_output)).astype(jnp.bfloat16)
    stored = (
        start_rows,
        whole,
        joined_down_proj,
        query_rows,
        key_rows,
        value_rows,
        log_total,
        context_rows,
        merge_down_proj,
        middle,
        whole_mlp,
        expand_down_proj,
        expanded_hidden,
        activated_hidden,
        shrink_down_proj,
    )
    return (output_rows, stored)


def backward_micro(own_grad, stored, norm_gains, weights, picked, rope_tables):
    attn_gain, mlp_gain = norm_gains
    joined_weight, merge_weight_matrix, expand_weight, shrink_weight_matrix = weights
    (
        joined_lower,
        joined_up_matrices,
        merge_lower,
        merge_up_matrices,
        expand_lower,
        expand_up_matrices,
        shrink_lower,
        shrink_up_matrices,
    ) = picked
    cosine_table, sine_table = rope_tables
    (
        start_rows,
        whole,
        joined_down_proj,
        query_rows,
        key_rows,
        value_rows,
        log_total,
        context_rows,
        merge_down_proj,
        middle,
        whole_mlp,
        expand_down_proj,
        expanded_hidden,
        activated_hidden,
        shrink_down_proj,
    ) = stored
    length = whole.shape[0]
    width_here = joined_weight.shape[2]
    heads_here = width_here // HEAD_DIM
    out_grad = own_grad.astype(jnp.float32)
    grad_whole = share_grads(own_grad)
    wide_gradient = grad_whole.astype(jnp.float32)
    shrink_down_grad = ADAPTER_SCALE * jnp.dot(
        wide_gradient, shrink_up_matrices.T, precision=MATMUL_PRECISION
    )
    shrink_up_gradient = ADAPTER_SCALE * jnp.dot(
        shrink_down_proj.T, wide_gradient, precision=MATMUL_PRECISION
    )
    grad_activated = jnp.dot(grad_whole, shrink_weight_matrix, preferred_element_type=jnp.float32)
    grad_activated = grad_activated + jnp.dot(
        shrink_down_grad, shrink_lower.astype(jnp.float32).T, precision=MATMUL_PRECISION
    )
    grad_shrink_lower = jnp.dot(
        activated_hidden.astype(jnp.float32).T, shrink_down_grad, precision=MATMUL_PRECISION
    )
    unused_units, pull_gate = jax.vjp(gated_units, expanded_hidden)
    grad_expanded = pull_gate(grad_activated)[0].astype(jnp.bfloat16)
    expand_wide = grad_expanded.astype(jnp.float32)
    expand_down_grad = ADAPTER_SCALE * jnp.einsum(
        "lcf,rcf->lr", expand_wide, expand_up_matrices, precision=MATMUL_PRECISION
    )
    expand_up_gradient = ADAPTER_SCALE * jnp.einsum(
        "lr,lcf->rcf", expand_down_proj, expand_wide, precision=MATMUL_PRECISION
    )
    grad_normed_mlp = jnp.einsum(
        "lcf,dcf->ld", grad_expanded, expand_weight, preferred_element_type=jnp.float32
    )
    grad_normed_mlp = grad_normed_mlp + jnp.dot(
        expand_down_grad, expand_lower.astype(jnp.float32).T, precision=MATMUL_PRECISION
    )
    grad_expand_lower = jnp.dot(
        whole_mlp.astype(jnp.float32).T, expand_down_grad, precision=MATMUL_PRECISION
    )
    unused_mid, pull_mlp = jax.vjp(lambda inputs: norm_rows(inputs, mlp_gain), middle)
    grad_middle = out_grad + pull_mlp(total_grads(grad_normed_mlp))[0]
    middle_low = grad_middle.astype(jnp.bfloat16)
    attn_grad = share_grads(middle_low)
    attention_wide = attn_grad.astype(jnp.float32)
    merge_down_grad = ADAPTER_SCALE * jnp.dot(
        attention_wide, merge_up_matrices.T, precision=MATMUL_PRECISION
    )
    merge_up_gradient = ADAPTER_SCALE * jnp.dot(
        merge_down_proj.T, attention_wide, precision=MATMUL_PRECISION
    )
    grad_context = jnp.einsum(
        "lo,oe->le", attn_grad, merge_weight_matrix, preferred_element_type=jnp.float32
    )
    grad_context = (
        grad_context
        + jnp.dot(merge_down_grad, merge_lower.astype(jnp.float32).T, precision=MATMUL_PRECISION)
    ).astype(jnp.bfloat16)
    grad_merge_lower = jnp.dot(
        context_rows.astype(jnp.float32).T, merge_down_grad, precision=MATMUL_PRECISION
    )
    grad_heads = grad_context.reshape(length, heads_here, HEAD_DIM)
    score_scale = HEAD_DIM ** (-0.5)
    scores = (
        jnp.einsum("qhe,khe->hqk", query_rows, key_rows, preferred_element_type=jnp.float32)
        * score_scale
    )
    probs_wide = jnp.exp(scores - log_total)
    attn_probs = probs_wide.astype(jnp.bfloat16)
    grad_values = jnp.einsum(
        "hqk,qhe->khe", attn_probs, grad_heads, preferred_element_type=jnp.float32
    )
    grad_probs = jnp.einsum(
        "qhe,khe->hqk", grad_heads, value_rows, preferred_element_type=jnp.float32
    )
    grad_scores = probs_wide * (
        grad_probs - jnp.sum(probs_wide * grad_probs, axis=-1, keepdims=True)
    )
    grad_scores = grad_scores.astype(jnp.bfloat16)
    grad_query = (
        jnp.einsum("hqk,khe->qhe", grad_scores, key_rows, preferred_element_type=jnp.float32)
        * score_scale
    )
    grad_keys = (
        jnp.einsum("hqk,qhe->khe", grad_scores, query_rows, preferred_element_type=jnp.float32)
        * score_scale
    )
    unused_rot, pull_rope = jax.vjp(
        lambda inputs: rotate(inputs, cosine_table, sine_table), grad_query
    )
    grad_joined = jnp.stack(
        [
            pull_rope(grad_query)[0].reshape(length, width_here),
            pull_rope(grad_keys)[0].reshape(length, width_here),
            grad_values.reshape(length, width_here),
        ],
        axis=1,
    ).astype(jnp.bfloat16)
    joined_wide = grad_joined.astype(jnp.float32)
    joined_down_grad = ADAPTER_SCALE * jnp.einsum(
        "lce,rce->lr", joined_wide, joined_up_matrices, precision=MATMUL_PRECISION
    )
    joined_up_gradient = ADAPTER_SCALE * jnp.einsum(
        "lr,lce->rce", joined_down_proj, joined_wide, precision=MATMUL_PRECISION
    )
    grad_normed = jnp.einsum(
        "lce,dce->ld", grad_joined, joined_weight, preferred_element_type=jnp.float32
    )
    grad_normed = grad_normed + jnp.dot(
        joined_down_grad, joined_lower.astype(jnp.float32).T, precision=MATMUL_PRECISION
    )
    grad_joined_lower = jnp.dot(
        whole.astype(jnp.float32).T, joined_down_grad, precision=MATMUL_PRECISION
    )
    unused_first, pull_first = jax.vjp(lambda inputs: norm_rows(inputs, attn_gain), start_rows)
    grad_hidden = (grad_middle + pull_first(total_grads(grad_normed))[0]).astype(jnp.bfloat16)
    grads = (
        grad_joined_lower,
        joined_up_gradient,
        grad_merge_lower,
        merge_up_gradient,
        grad_expand_lower,
        expand_up_gradient,
        grad_shrink_lower,
        shrink_up_gradient,
    )
    return (grad_hidden, grads)


def local(
    hidden,
    cotangent,
    adapter_ids,
    attn_gain,
    mlp_gain,
    joined_weight,
    merge_weight_matrix,
    expand_weight,
    shrink_weight_matrix,
    joined_lower,
    joined_up_matrices,
    merge_lower,
    merge_up_matrices,
    expand_lower,
    expand_up_matrices,
    shrink_lower,
    shrink_up_matrices,
):
    micro_count = hidden.shape[0]
    own_count = hidden.shape[1]
    seq_length = own_count * lax.axis_size("mp")
    rope_tables = rotary_tables(seq_length, HEAD_DIM)
    norm_gains = (attn_gain.astype(jnp.float32), mlp_gain.astype(jnp.float32))
    tables = (
        joined_lower,
        joined_up_matrices,
        merge_lower,
        merge_up_matrices,
        expand_lower,
        expand_up_matrices,
        shrink_lower,
        shrink_up_matrices,
    )
    outputs = []
    stored_all = []
    for micro_step in range(micro_count):
        weights = (
            lax.all_gather(joined_weight, "dp", axis=0, tiled=True),
            lax.all_gather(merge_weight_matrix, "dp", axis=0, tiled=True),
            lax.all_gather(expand_weight, "dp", axis=0, tiled=True),
            lax.all_gather(shrink_weight_matrix, "dp", axis=0, tiled=True),
        )
        picked = pick_all(tables, adapter_ids[micro_step])
        result, stored = forward_micro(hidden[micro_step], norm_gains, weights, picked, rope_tables)
        outputs.append(result)
        stored_all.append(stored)
    totals = None
    grads_out = []
    for micro_step in range(micro_count):
        which_set = adapter_ids[micro_step]
        weights = (
            lax.all_gather(joined_weight, "dp", axis=0, tiled=True),
            lax.all_gather(merge_weight_matrix, "dp", axis=0, tiled=True),
            lax.all_gather(expand_weight, "dp", axis=0, tiled=True),
            lax.all_gather(shrink_weight_matrix, "dp", axis=0, tiled=True),
        )
        picked = pick_all(tables, which_set)
        grad_hidden, grads = backward_micro(
            cotangent[micro_step], stored_all[micro_step], norm_gains, weights, picked, rope_tables
        )
        grads_out.append(grad_hidden)
        spread = tuple((spread_table(gradient, which_set, ADAPTERS) for gradient in grads))
        if totals is None:
            totals = spread
        else:
            totals = tuple((running + added for running, added in zip(totals, spread)))
    summed_all = lax.psum((totals[0], totals[3], totals[4], totals[7]), ("dp", "mp"))
    summed_dp = lax.psum((totals[1], totals[2], totals[5], totals[6]), "dp")
    return (
        jnp.stack(outputs),
        jnp.stack(grads_out),
        summed_all[0],
        summed_dp[0],
        summed_dp[1],
        summed_all[1],
        summed_all[2],
        summed_dp[2],
        summed_dp[3],
        summed_all[3],
    )


def solution(mesh):
    in_specs = (
        P("dp", "mp", None),
        P("dp", "mp", None),
        P("dp"),
        P(),
        P(),
        P("dp", None, "mp"),
        P("dp", "mp"),
        P("dp", None, "mp"),
        P("dp", "mp"),
        P(),
        P(None, None, None, "mp"),
        P(None, "mp", None),
        P(),
        P(),
        P(None, None, None, "mp"),
        P(None, "mp", None),
        P(),
    )
    out_specs = (
        P("dp", "mp", None),
        P("dp", "mp", None),
        P(),
        P(None, None, None, "mp"),
        P(None, "mp", None),
        P(),
        P(),
        P(None, None, None, "mp"),
        P(None, "mp", None),
        P(),
    )
    return jax.shard_map(local, mesh=mesh, in_specs=in_specs, out_specs=out_specs, check_vma=False)
```

profile of v0, /device:TPU:0, one launch (start us, length us, event | category | flops | bytes accessed | tf_op | source)
XLA Modules:
  0.0 1304.6 jit_solution(48727404700520118)
XLA Ops:
  22.2 33.4 %all_gather.34 = bf16[1024,256]{1,0:T(8,128)(2,1)S(1)} all-gather(bf16[128,256]{1,0:T(8,128)(2,1)S(1)} %copy-done.215), channel_id=1, replica_groups=mesh['dp'=8,'mp'=4] {'dp'}, dimensions={0}, use_global_device_ids=true | all-gather | bytes 589824 | tf_op jit(solution)/shard_map/all_gather | solution.py:371
  58.0 29.6 %all-gather.21.cloned.1.call-done = bf16[1024,3,256]{0,2,1:T(8,128)(2,1)} async-done(((bf16[128,3,256]{0,2,1:T(8,128)(2,1)}), bf16[1024,3,256]{0,2,1:T(8,128)(2,1)}) %all-gather.21.cloned.1.call-update) | async-done | bytes 1572880 | tf_op jit(solution)/shard_map/all_gather | solution.py:370
  95.4 8.2 multiply_reduce_fusion.5
  103.6 8.5 fusion
  112.2 8.1 fusion.143
  121.3 5.0 add_convert_fusion.8
  126.4 29.7 %reduce-scatter.13.cloned.1.call-done = bf16[256,1024]{1,0:T(8,128)(2,1)} async-done(((bf16[1024,1024]{1,0:T(8,128)(2,1)}), bf16[256,1024]{1,0:T(8,128)(2,1)}) %reduce-scatter.13.cloned.1.call-update) | async-done | bytes 524304 | tf_op jit(solution)/shard_map/reduce_scatter | solution.py:66
  160.7 22.1 %all-gather.33.cloned.1.call-done = bf16[1024,1024]{1,0:T(8,128)(2,1)} async-done(((bf16[256,1024]{1,0:T(8,128)(2,1)}), bf16[1024,1024]{1,0:T(8,128)(2,1)}) %all-gather.33.cloned.1.call-update) | async-done | bytes 2097168 | tf_op jit(solution)/shard_map/all_gather | solution.py:62
  185.0 3.9 fusion.101
  193.8 13.6 %all-gather.29.cloned.1.call-done = bf16[1024,1024]{1,0:T(8,128)(2,1)} async-done(((bf16[256,1024]{1,0:T(8,128)(2,1)}), bf16[1024,1024]{1,0:T(8,128)(2,1)}) %all-gather.29.cloned.1.call-update) | async-done | bytes 2097168 | tf_op jit(solution)/shard_map/all_gather | solution.py:62
  207.4 4.0 fusion.105
  219.6 8.3 multiply_reduce_fusion.4
  227.9 8.5 fusion.1
  236.5 7.6 fusion.142
  245.7 5.0 add_convert_fusion.6
  251.0 8.9 multiply_reduce_fusion.3
  259.9 8.6 fusion.2
  268.6 7.6 fusion.141
  277.2 5.0 add_convert_fusion.4
  287.2 29.1 %reduce-scatter.21.cloned.1.call-done = bf16[256,1024]{1,0:T(8,128)(2,1)} async-done(((bf16[1024,1024]{1,0:T(8,128)(2,1)}), bf16[256,1024]{1,0:T(8,128)(2,1)}) %reduce-scatter.21.cloned.1.call-update) | async-done | bytes 524304 | tf_op jit(solution)/shard_map/reduce_scatter | solution.py:66
  326.4 14.8 %all-gather.45.cloned.1.call-done = bf16[1,1024,1024]{2,1,0:T(8,128)(2,1)} async-done(((bf16[1,256,1024]{2,1,0:T(8,128)(2,1)}), bf16[1,1024,1024]{2,1,0:T(8,128)(2,1)}) %all-gather.45.cloned.1.call-update) | async-done | bytes 2097168 | tf_op jit(solution)/shard_map/all_gather | solution.py:72
  344.5 21.5 %all-gather.47.cloned.1.call-done = bf16[1,1024,1024]{2,1,0:T(8,128)(2,1)} async-done(((bf16[1,256,1024]{2,1,0:T(8,128)(2,1)}), bf16[1,1024,1024]{2,1,0:T(8,128)(2,1)}) %all-gather.47.cloned.1.call-update) | async-done | bytes 2097168 | tf_op jit(solution)/shard_map/all_gather | solution.py:72
  366.0 4.0 fusion.162
  370.0 20.7 %all-gather.43.cloned.1.call-done = bf16[1,1024,1024]{2,1,0:T(8,128)(2,1)} async-done(((bf16[1,256,1024]{2,1,0:T(8,128)(2,1)}), bf16[1,1024,1024]{2,1,0:T(8,128)(2,1)}) %all-gather.43.cloned.1.call-update) | async-done | bytes 2097168 | tf_op jit(solution)/shard_map/all_gather | solution.py:72
  390.7 4.0 fusion.150
  394.7 40.9 %all-gather.27.cloned.1.call-done = bf16[1024,656]{0,1:T(8,128)(2,1)} async-done(((bf16[128,656]{0,1:T(8,128)(2,1)}), bf16[1024,656]{0,1:T(8,128)(2,1)}) %all-gather.27.cloned.1.call-update) | async-done | bytes 1343504 | tf_op jit(solution)/shard_map/all_gather | solution.py:373
  451.3 7.6 all-gather.23.cloned.1.call-done
  461.1 57.7 %all-gather.25.cloned.1.call-done = bf16[1024,2,656]{0,2,1:T(8,128)(2,1)} async-done(((bf16[128,2,656]{0,2,1:T(8,128)(2,1)}), bf16[1024,2,656]{0,2,1:T(8,128)(2,1)}) %all-gather.25.cloned.1.call-update) | async-done | bytes 2686992 | tf_op jit(solution)/shard_map/all_gather | solution.py:372
  518.8 5.4 fusion.107
  524.2 4.5 multiply_add_fusion.2
  528.7 6.0 multiply_bitcast_fusion.2
  547.5 5.7 fusion.103
  553.9 4.5 multiply_add_fusion.1
  558.5 6.3 multiply_bitcast_fusion.1
  577.5 5.6 fusion.99
  583.7 4.5 multiply_add_fusion
  588.3 6.0 multiply_bitcast_fusion
  608.6 4.0 fusion.311
  612.7 5.5 add_convert_fusion.7
  623.7 5.0 add_convert_fusion.5
  634.1 5.0 add_convert_fusion.3
  639.3 28.3 %reduce-scatter.33.cloned.1.call-done = bf16[256,1024]{1,0:T(8,128)(2,1)} async-done(((bf16[1024,1024]{1,0:T(8,128)(2,1)}), bf16[256,1024]{1,0:T(8,128)(2,1)}) %reduce-scatter.33.cloned.1.call-update) | async-done | bytes 524304 | tf_op jit(solution)/shard_map/reduce_scatter | solution.py:76
  670.1 31.4 %reduce-scatter.15.cloned.1.call-done = bf16[256,1024]{1,0:T(8,128)(2,1)} async-done(((bf16[1024,1024]{1,0:T(8,128)(2,1)}), bf16[256,1024]{1,0:T(8,128)(2,1)}) %reduce-scatter.15.cloned.1.call-update) | async-done | bytes 524304 | tf_op jit(solution)/shard_map/reduce_scatter | solution.py:66
  701.6 34.0 %reduce-scatter.19.cloned.1.call-done = bf16[256,1024]{1,0:T(8,128)(2,1)} async-done(((bf16[1024,1024]{1,0:T(8,128)(2,1)}), bf16[256,1024]{1,0:T(8,128)(2,1)}) %reduce-scatter.19.cloned.1.call-update) | async-done | bytes 524304 | tf_op jit(solution)/shard_map/reduce_scatter | solution.py:66
  735.6 4.3 fusion.293
  739.9 29.7 %reduce-scatter.23.cloned.1.call-done = bf16[256,1024]{1,0:T(8,128)(2,1)} async-done(((bf16[1024,1024]{1,0:T(8,128)(2,1)}), bf16[256,1024]{1,0:T(8,128)(2,1)}) %reduce-scatter.23.cloned.1.call-update) | async-done | bytes 524304 | tf_op jit(solution)/shard_map/reduce_scatter | solution.py:66
  775.2 21.3 %all-gather.37.cloned.1.call-done = bf16[1024,1024]{1,0:T(8,128)(2,1)} async-done(((bf16[256,1024]{1,0:T(8,128)(2,1)}), bf16[1024,1024]{1,0:T(8,128)(2,1)}) %all-gather.37.cloned.1.call-update) | async-done | bytes 2097168 | tf_op jit(solution)/shard_map/all_gather | solution.py:72
  803.0 9.2 fusion.132
  812.2 13.0 multiply_reduce_fusion.2
  825.2 10.8 multiply_convert_fusion.2
  836.1 6.2 convolution_bitcast_fusion.4
  852.5 15.5 %multiply_reduce_fusion = (f32[4,1024]{1,0:T(4,128)S(1)}, f32[4,1024,1024]{1,2,0:T(8,128)}) fusion(f32[4,1024,1024]{1,2,0:T(8,128)} %get-tuple-element.169, f32[4,1024]{1,0:T(4,128)S(1)} %log_add_fusion, bf16[1024,4,64]{0,2,1:T(8,128)(2,1)S(1)} %bitcast.791, bf16[1024,4,64]{0,2,1:T(8,128)(2,1)S(1)} %bitcast.809), kind=kOutput, calls=%fused_computation.1 | convolution fusion | flops 553644032 | bytes 34635776 | tf_op jit(solution)/shard_map/qhe,khe->hqk/dot_general | solution.py:275
  868.6 10.9 multiply_convert_fusion
  879.5 7.2 convolution_bitcast_fusion
  895.8 15.5 %multiply_reduce_fusion.1 = (f32[4,1024]{1,0:T(4,128)S(1)}, f32[4,1024,1024]{1,2,0:T(8,128)}) fusion(f32[4,1024,1024]{1,2,0:T(8,128)} %get-tuple-element.167, f32[4,1024]{1,0:T(4,128)S(1)} %log_add_fusion.1, bf16[1024,4,64]{0,2,1:T(8,128)(2,1)S(1)} %bitcast.789, bf16[1024,4,64]{0,2,1:T(8,128)(2,1)S(1)} %bitcast.807), kind=kOutput, calls=%fused_computation.4 | convolution fusion | flops 553644032 | bytes 34635776 | tf_op jit(solution)/shard_map/qhe,khe->hqk/dot_general | solution.py:275
  912.0 11.1 multiply_convert_fusion.1
  923.1 6.2 convolution_bitcast_fusion.2
  949.6 8.4 fusion.138
  962.7 4.7 fusion.15
  967.7 4.1 convolution_multiply_fusion.2
  986.9 8.5 fusion.135
  1027.1 20.2 %reduce-scatter.31.cloned.1.call-done = bf16[256,1024]{1,0:T(8,128)(2,1)} async-done(((bf16[1024,1024]{1,0:T(8,128)(2,1)}), bf16[256,1024]{1,0:T(8,128)(2,1)}) %reduce-scatter.31.cloned.1.call-update) | async-done | bytes 524304 | tf_op jit(solution)/shard_map/reduce_scatter | solution.py:76
  1055.5 133.3 %all-reduce.23.cloned.1.call-done = (f32[8,1024,16]{1,2,0:T(8,128)}, f32[8,16,1024]{2,1,0:T(8,128)}, f32[8,1024,16]{1,2,0:T(8,128)}, f32[8,16,1024]{2,1,0:T(8,128)}) async-done(((f32[8,1024,16]{1,2,0:T(8,128)}, f32[8,16,1024]{2,1,0:T(8,128)}, f32[8,1024,16]{1,2,0:T(8,128)}, f32[8,16,1024]{2,1,0:T(8,128)}), (f32[8,1024,16]{1,2,0:T(8,128)}, f32[8,16,1024]{2,1,0:T(8,128)}, f32[8,1024,16]{1,2,0:T(8,128)}, ...) | async-done | bytes 2097168 | tf_op jit(solution)/shard_map/psum | solution.py:399
  1188.8 98.2 %all-reduce.25.cloned.1.call-done = (f32[8,16,3,256]{3,1,2,0:T(8,128)}, f32[8,256,16]{1,2,0:T(8,128)}, f32[8,16,2,656]{3,2,1,0:T(2,128)}, f32[8,656,16]{1,2,0:T(8,128)}) async-done(((f32[8,16,3,256]{3,1,2,0:T(8,128)}, f32[8,256,16]{1,2,0:T(8,128)}, f32[8,16,2,656]{3,2,1,0:T(2,128)}, f32[8,656,16]{1,2,0:T(8,128)}), (f32[8,16,3,256]{3,1,2,0:T(8,128)}, f32[8,256,16]{1,2,0:T(8,128)}, ...) | async-done | bytes 1531920 | tf_op jit(solution)/shard_map/psum | solution.py:400
  (866 shorter events, 259.7 us)
Async XLA Ops:
  7.2 48.4 %all-gather.19.cloned.1.call-start = ((), (), s32[]{:S(2)}) async-start(), calls=%async_computation.12 | async-start | bytes 2621440 | tf_op jit(solution)/shard_map/all_gather | solution.py:62
  11.7 146.9 %copy-start.189 = (f32[1024]{0:T(1024)}, f32[1024]{0:T(1024)S(1)}, u32[]{:S(2)}) copy-start(f32[1024]{0:T(1024)S(1)} %convert_element_type.468) | copy-start | bytes 12292
  13.9 73.7 %all-gather.21.cloned.1.call-start = ((), (), s32[]{:S(2)}) async-start(), calls=%async_computation.13 | async-start | bytes 1769472 | tf_op jit(solution)/shard_map/all_gather | solution.py:370
  14.8 141.2 %reduce-scatter.13.cloned.1.call-start = ((), (), s32[]{:S(2)}) async-start(), calls=%async_computation.14 | async-start | bytes 2621440 | tf_op jit(solution)/shard_map/reduce_scatter | solution.py:66
  16.3 41.7 %copy-start.244 = (pred[8]{0:T(512)(128)(4,1)}, pred[8]{0:T(512)(128)(4,1)S(1)}, u32[]{:S(2)}) copy-start(pred[8]{0:T(512)(128)(4,1)S(1)} %iota_compare_fusion.2) | copy-start | bytes 28
  17.6 40.4 %copy-start.236 = (pred[8]{0:T(512)(128)(4,1)}, pred[8]{0:T(512)(128)(4,1)S(1)}, u32[]{:S(2)}) copy-start(pred[8]{0:T(512)(128)(4,1)S(1)} %get-tuple-element.177) | copy-start | bytes 28
  17.6 40.4 %copy-start.238 = (pred[8]{0:T(512)(128)(4,1)}, pred[8]{0:T(512)(128)(4,1)S(1)}, u32[]{:S(2)}) copy-start(pred[8]{0:T(512)(128)(4,1)S(1)} %get-tuple-element.178) | copy-start | bytes 28
  17.7 102.6 %copy-start.213 = (bf16[256,16]{0,1:T(8,128)(2,1)}, bf16[256,16]{0,1:T(8,128)(2,1)S(1)}, u32[]{:S(2)}) copy-start(bf16[256,16]{0,1:T(8,128)(2,1)S(1)} %get-tuple-element.51) | copy-start | bytes 24580
  17.7 227.2 %copy-start.209 = (bf16[256,16]{0,1:T(8,128)(2,1)}, bf16[256,16]{0,1:T(8,128)(2,1)S(1)}, u32[]{:S(2)}) copy-start(bf16[256,16]{0,1:T(8,128)(2,1)S(1)} %get-tuple-element.52) | copy-start | bytes 24580
  17.7 258.5 %copy-start.211 = (bf16[256,16]{0,1:T(8,128)(2,1)}, bf16[256,16]{0,1:T(8,128)(2,1)S(1)}, u32[]{:S(2)}) copy-start(bf16[256,16]{0,1:T(8,128)(2,1)S(1)} %get-tuple-element.53) | copy-start | bytes 24580
  19.5 75.3 %copy-start.78 = (f32[1024,64]{0,1:T(8,128)}, f32[1024,64]{0,1:T(8,128)S(1)}, u32[]{:S(2)}) copy-start(f32[1024,64]{0,1:T(8,128)S(1)} %get-tuple-element.156) | copy-start | bytes 786436
  20.3 71.2 %copy-start.195 = (f32[16,3,256]{2,0,1:T(8,128)}, f32[16,3,256]{2,0,1:T(8,128)S(1)}, u32[]{:S(2)}) copy-start(f32[16,3,256]{2,0,1:T(8,128)S(1)} %get-tuple-element.48) | copy-start | bytes 147460
  20.3 168.7 %copy-start.193 = (f32[16,3,256]{2,0,1:T(8,128)}, f32[16,3,256]{2,0,1:T(8,128)S(1)}, u32[]{:S(2)}) copy-start(f32[16,3,256]{2,0,1:T(8,128)S(1)} %get-tuple-element.50) | copy-start | bytes 147460
  21.2 70.3 %copy-start.158 = (bf16[1024,16]{0,1:T(8,128)(2,1)}, bf16[1024,16]{0,1:T(8,128)(2,1)S(1)}, u32[]{:S(2)}) copy-start(bf16[1024,16]{0,1:T(8,128)(2,1)S(1)} %get-tuple-element.42) | copy-start | bytes 98308
  21.2 161.6 %copy-start.156 = (bf16[1024,16]{0,1:T(8,128)(2,1)}, bf16[1024,16]{0,1:T(8,128)(2,1)S(1)}, u32[]{:S(2)}) copy-start(bf16[1024,16]{0,1:T(8,128)(2,1)S(1)} %get-tuple-element.44) | copy-start | bytes 98308
  22.2 99.0 %copy-start.129 = (f32[16,1024]{1,0:T(8,128)}, f32[16,1024]{1,0:T(8,128)S(1)}, u32[]{:S(2)}) copy-start(f32[16,1024]{1,0:T(8,128)S(1)} %get-tuple-element.39) | copy-start | bytes 196612
  22.2 222.9 %copy-start.125 = (f32[16,1024]{1,0:T(8,128)}, f32[16,1024]{1,0:T(8,128)S(1)}, u32[]{:S(2)}) copy-start(f32[16,1024]{1,0:T(8,128)S(1)} %get-tuple-element.40) | copy-start | bytes 196612
  22.2 255.0 %copy-start.127 = (f32[16,1024]{1,0:T(8,128)}, f32[16,1024]{1,0:T(8,128)S(1)}, u32[]{:S(2)}) copy-start(f32[16,1024]{1,0:T(8,128)S(1)} %get-tuple-element.41) | copy-start | bytes 196612
  121.2 34.8 %copy-start = (bf16[3,256,1024]{2,1,0:T(8,128)(2,1)S(1)}, bf16[3,256,1024]{2,1,0:T(8,128)(2,1)}, u32[]{:S(2)}) copy-start(bf16[3,256,1024]{2,1,0:T(8,128)(2,1)} %param.17) | copy-start | bytes 4718596
  126.2 56.5 %all-gather.33.cloned.1.call-start = ((), (), s32[]{:S(2)}) async-start(), calls=%async_computation.23 | async-start | bytes 2621440 | tf_op jit(solution)/shard_map/all_gather | solution.py:62
  126.3 58.7 %copy-start.224 = (f32[256]{0:T(256)}, f32[256]{0:T(256)S(1)}, u32[]{:S(2)}) copy-start(f32[256]{0:T(256)S(1)} %get-tuple-element.180) | copy-start | bytes 3076
  126.3 58.7 %copy-start.226 = (f32[256]{0:T(256)}, f32[256]{0:T(256)S(1)}, u32[]{:S(2)}) copy-start(f32[256]{0:T(256)S(1)} %get-tuple-element.179) | copy-start | bytes 3076
  160.0 47.4 %all-gather.29.cloned.1.call-start = ((), (), s32[]{:S(2)}) async-start(), calls=%async_computation.19 | async-start | bytes 2621440 | tf_op jit(solution)/shard_map/all_gather | solution.py:62
  160.6 126.5 %reduce-scatter.17.cloned.1.call-start = ((), (), s32[]{:S(2)}) async-start(), calls=%async_computation.20 | async-start | bytes 2621440 | tf_op jit(solution)/shard_map/reduce_scatter | solution.py:66
  250.7 65.6 %reduce-scatter.21.cloned.1.call-start = ((), (), s32[]{:S(2)}) async-start(), calls=%async_computation.24 | async-start | bytes 2621440 | tf_op jit(solution)/shard_map/reduce_scatter | solution.py:66
  282.3 34.0 %copy-start.25 = (bf16[256,1024]{1,0:T(8,128)(2,1)S(1)}, bf16[256,1024]{1,0:T(8,128)(2,1)}, u32[]{:S(2)}) copy-start(bf16[256,1024]{1,0:T(8,128)(2,1)} %reduce-scatter.13.cloned.1.call-done) | copy-start | bytes 1572868
  282.3 58.8 %all-gather.45.cloned.1.call-start = ((), (), s32[]{:S(2)}) async-start(), calls=%async_computation.37 | async-start | bytes 2621440 | tf_op jit(solution)/shard_map/all_gather | solution.py:72
  285.0 81.0 %all-gather.47.cloned.1.call-start = ((), (), s32[]{:S(2)}) async-start(), calls=%async_computation.38 | async-start | bytes 2621440 | tf_op jit(solution)/shard_map/all_gather | solution.py:72
  285.7 105.0 %all-gather.43.cloned.1.call-start = ((), (), s32[]{:S(2)}) async-start(), calls=%async_computation.36 | async-start | bytes 2621440 | tf_op jit(solution)/shard_map/all_gather | solution.py:72
  286.3 149.3 %all-gather.27.cloned.1.call-start = ((), (), s32[]{:S(2)}) async-start(), calls=%async_computation.17 | async-start | bytes 1511424 | tf_op jit(solution)/shard_map/all_gather | solution.py:373
  287.0 171.8 %all-gather.23.cloned.1.call-start = ((), (), s32[]{:S(2)}) async-start(), calls=%async_computation.15 | async-start | bytes 2621440 | tf_op jit(solution)/shard_map/all_gather | solution.py:62
  287.1 34.6 %copy-start.207 = (f32[1024]{0:T(1024)}, f32[1024]{0:T(1024)S(1)}, u32[]{:S(2)}) copy-start(f32[1024]{0:T(1024)S(1)} %convert_element_type.485) | copy-start | bytes 12292
  287.1 34.5 %copy-start.232 = (f32[256]{0:T(256)}, f32[256]{0:T(256)S(1)}, u32[]{:S(2)}) copy-start(f32[256]{0:T(256)S(1)} %broadcast_multiply_fusion.12) | copy-start | bytes 3076
  321.7 197.1 %all-gather.25.cloned.1.call-start = ((), (), s32[]{:S(2)}) async-start(), calls=%async_computation.16 | async-start | bytes 3022848 | tf_op jit(solution)/shard_map/all_gather | solution.py:372
  322.5 225.0 %all-gather.31.cloned.1.call-start = ((), (), s32[]{:S(2)}) async-start(), calls=%async_computation.21 | async-start | bytes 2621440 | tf_op jit(solution)/shard_map/all_gather | solution.py:62
  323.7 115.4 %copy-start.185 = (bf16[656,16]{0,1:T(8,128)(2,1)}, bf16[656,16]{0,1:T(8,128)(2,1)S(1)}, u32[]{:S(2)}) copy-start(bf16[656,16]{0,1:T(8,128)(2,1)S(1)} %get-tuple-element.46) | copy-start | bytes 62980
  323.7 119.8 %copy-start.183 = (bf16[656,16]{0,1:T(8,128)(2,1)}, bf16[656,16]{0,1:T(8,128)(2,1)S(1)}, u32[]{:S(2)}) copy-start(bf16[656,16]{0,1:T(8,128)(2,1)S(1)} %get-tuple-element.47) | copy-start | bytes 62980
  326.3 251.1 %all-gather.35.cloned.1.call-start = ((), (), s32[]{:S(2)}) async-start(), calls=%async_computation.25 | async-start | bytes 2621440 | tf_op jit(solution)/shard_map/all_gather | solution.py:62
  344.5 94.6 %copy-start.113 = (f32[16,1024]{1,0:T(8,128)}, f32[16,1024]{1,0:T(8,128)S(1)}, u32[]{:S(2)}) copy-start(f32[16,1024]{1,0:T(8,128)S(1)} %fusion.156) | copy-start | bytes 196612
  451.0 188.2 %reduce-scatter.25.cloned.1.call-start = ((), (), s32[]{:S(2)}) async-start(), calls=%async_computation.27 | async-start | bytes 2621440 | tf_op jit(solution)/shard_map/reduce_scatter | solution.py:76
  461.1 63.1 %copy-start.99 = (f32[1024,16,1]{0,1,2:T(8,128)}, f32[1024,16,1]{0,1,2:T(8,128)S(1)}, u32[]{:S(2)}) copy-start(f32[1024,16,1]{0,1,2:T(8,128)S(1)} %convolution_bitcast_fusion.16) | copy-start | bytes 196612
  547.2 92.1 %reduce-scatter.29.cloned.1.call-start = ((), (), s32[]{:S(2)}) async-start(), calls=%async_computation.30 | async-start | bytes 2621440 | tf_op jit(solution)/shard_map/reduce_scatter | solution.py:76
  577.2 90.4 %reduce-scatter.33.cloned.1.call-start = ((), (), s32[]{:S(2)}) async-start(), calls=%async_computation.33 | async-start | bytes 2621440 | tf_op jit(solution)/shard_map/reduce_scatter | solution.py:76
  606.6 94.9 %reduce-scatter.15.cloned.1.call-start = ((), (), s32[]{:S(2)}) async-start(), calls=%async_computation.18 | async-start | bytes 2621440 | tf_op jit(solution)/shard_map/reduce_scatter | solution.py:66
  618.2 117.4 %reduce-scatter.19.cloned.1.call-start = ((), (), s32[]{:S(2)}) async-start(), calls=%async_computation.22 | async-start | bytes 2621440 | tf_op jit(solution)/shard_map/reduce_scatter | solution.py:66
  628.7 140.8 %reduce-scatter.23.cloned.1.call-start = ((), (), s32[]{:S(2)}) async-start(), calls=%async_computation.26 | async-start | bytes 2621440 | tf_op jit(solution)/shard_map/reduce_scatter | solution.py:66
  639.2 96.4 %copy-start.275 = (f32[256]{0:T(256)S(1)}, f32[256]{0:T(256)}, u32[]{:S(2)}) copy-start(f32[256]{0:T(256)} %copy-done.274) | copy-start | bytes 3076
  639.2 96.4 %copy-start.277 = (f32[256]{0:T(256)S(1)}, f32[256]{0:T(256)}, u32[]{:S(2)}) copy-start(f32[256]{0:T(256)} %copy-done.276) | copy-start | bytes 3076
  639.2 157.4 %all-gather.37.cloned.1.call-start = ((), (), s32[]{:S(2)}) async-start(), calls=%async_computation.28 | async-start | bytes 2621440 | tf_op jit(solution)/shard_map/all_gather | solution.py:72
  670.1 69.8 %copy-start.269 = (f32[256]{0:T(256)S(1)}, f32[256]{0:T(256)}, u32[]{:S(2)}) copy-start(f32[256]{0:T(256)} %copy-done.268) | copy-start | bytes 3076
  670.1 99.4 %copy-start.261 = (f32[256]{0:T(256)S(1)}, f32[256]{0:T(256)}, u32[]{:S(2)}) copy-start(f32[256]{0:T(256)} %copy-done.260) | copy-start | bytes 3076
  739.9 34.0 %copy-start.254 = (f32[256]{0:T(256)}, f32[256]{0:T(256)S(1)}, u32[]{:S(2)}) copy-start(f32[256]{0:T(256)S(1)} %negate_multiply_fusion.6) | copy-start | bytes 3076
  773.9 72.1 %all-gather.41.cloned.1.call-start = ((), (), s32[]{:S(2)}) async-start(), calls=%async_computation.34 | async-start | bytes 2621440 | tf_op jit(solution)/shard_map/all_gather | solution.py:72
  774.6 114.7 %all-gather.39.cloned.1.call-start = ((), (), s32[]{:S(2)}) async-start(), calls=%async_computation.31 | async-start | bytes 2621440 | tf_op jit(solution)/shard_map/all_gather | solution.py:72
  774.8 93.2 %copy-start.163 = (f32[4,1024]{1,0:T(4,128)}, f32[4,1024]{1,0:T(4,128)S(1)}, u32[]{:S(2)}) copy-start(f32[4,1024]{1,0:T(4,128)S(1)} %log_add_fusion) | copy-start | bytes 49156
  775.2 251.9 %reduce-scatter.27.cloned.1.call-start = ((), (), s32[]{:S(2)}) async-start(), calls=%async_computation.29 | async-start | bytes 2621440 | tf_op jit(solution)/shard_map/reduce_scatter | solution.py:76
  947.6 79.6 %reduce-scatter.35.cloned.1.call-start = ((), (), s32[]{:S(2)}) async-start(), calls=%async_computation.35 | async-start | bytes 2621440 | tf_op jit(solution)/shard_map/reduce_scatter | solution.py:76
  948.3 54.7 %copy-start.246 = (f32[8]{0:T(128)}, f32[8]{0:T(128)S(1)}, u32[]{:S(2)}) copy-start(f32[8]{0:T(128)S(1)} %fusion.289) | copy-start | bytes 100
  949.6 53.4 %copy-start.240 = (f32[8]{0:T(128)}, f32[8]{0:T(128)S(1)}, u32[]{:S(2)}) copy-start(f32[8]{0:T(128)S(1)} %get-tuple-element.181) | copy-start | bytes 100
  949.6 53.4 %copy-start.242 = (f32[8]{0:T(128)}, f32[8]{0:T(128)S(1)}, u32[]{:S(2)}) copy-start(f32[8]{0:T(128)S(1)} %get-tuple-element.182) | copy-start | bytes 100
  967.4 79.9 %reduce-scatter.31.cloned.1.call-start = ((), (), s32[]{:S(2)}) async-start(), calls=%async_computation.32 | async-start | bytes 2621440 | tf_op jit(solution)/shard_map/reduce_scatter | solution.py:76
  1002.7 186.1 %all-reduce.23.cloned.1.call-start = ((), (), s32[]{:S(2)}) async-start(), calls=%async_computation.39 | async-start | bytes 4194304 | tf_op jit(solution)/shard_map/psum | solution.py:399
  1023.1 263.9 %all-reduce.25.cloned.1.call-start = ((), (), s32[]{:S(2)}) async-start(), calls=%async_computation.40 | async-start | bytes 3407872 | tf_op jit(solution)/shard_map/psum | solution.py:400
  1188.8 105.5 %copy-start.142 = (f32[8,1024,16]{1,2,0:T(8,128)S(1)}, f32[8,1024,16]{1,2,0:T(8,128)}, u32[]{:S(2)}) copy-start(f32[8,1024,16]{1,2,0:T(8,128)} %get-tuple-element.189) | copy-start | bytes 1572868
  (267 other events, 1948.2 us)
Sparse Core Ops, SparseCore 0:
  14.1 25.2 all-gather.18
  42.0 45.5 all-gather.20
  126.4 29.5 reduce-scatter.12
  160.2 22.5 all-gather.32
  184.8 22.5 all-gather.28
  250.8 31.4 reduce-scatter.16
  284.8 31.4 reduce-scatter.20
  318.5 22.5 all-gather.44
  343.4 22.5 all-gather.46
  368.0 22.5 all-gather.42
  392.9 42.5 all-gather.26
  437.6 21.1 all-gather.22
  461.1 57.6 all-gather.24
  520.9 20.7 all-gather.30
  543.1 22.5 all-gather.34
  568.3 31.4 reduce-scatter.24
  602.1 31.4 reduce-scatter.28
  636.1 31.4 reduce-scatter.32
  670.1 31.4 reduce-scatter.14
  704.1 31.3 reduce-scatter.18
  738.1 31.4 reduce-scatter.22
  774.0 22.5 all-gather.36
  798.2 22.5 all-gather.40
  822.4 22.6 all-gather.38
  947.7 31.7 reduce-scatter.26
  981.9 31.3 reduce-scatter.34
  1015.8 31.4 reduce-scatter.30
  1054.2 134.5 all-reduce.22
  1194.4 92.5 all-reduce.24
where the time goes:
time: 1310 us; the launch traced here: 1300 us
  waiting for transfers between devices  688 us (53%)
  matrix products  378 us (29%)
  other arithmetic  146 us (11%)
  local copies, waits for them, and re-layouts  36.7 us (3%)
  blocking collectives  33.4 us (3%)
  between operations  18.7 us (1%)
    reduce_scatter x6, waiting for transfers between devices, total_rows(): lax.psum_scatter(values.astype(jnp.bfloat16), 'mp', scatter_dimension=0,...  154 us
    psum x1, waiting for transfers between devices, local(): lax.psum((totals[0], totals[3], totals[4], totals[7]), ('dp', 'mp'))  133 us
    psum x1, waiting for transfers between devices, local(): summed_dp = lax.psum((totals[1], totals[2], totals[5], totals[6]), 'dp')  98.2 us
    all_gather x6, waiting for transfers between devices, share_grads(): return lax.all_gather(values, 'mp', axis=0, tiled=True)  78.3 us
    all_gather x1, waiting for transfers between devices, local(): lax.all_gather(expand_weight, 'dp', axis=0, tiled=True)  57.7 us
    reduce_scatter x6, waiting for transfers between devices, total_grads(): lax.psum_scatter(values.astype(jnp.bfloat16), 'mp', scatter_dimension=0,...  48.6 us
    dot_general x3, matrix products, backward_micro(): jnp.einsum('qhe,khe->hqk', grad_heads, value_rows, preferred_element_type...  44.1 us
    all_gather x6, waiting for transfers between devices, share_rows(): return lax.all_gather(values, 'mp', axis=0, tiled=True)  43.4 us
  transfers between devices with their start and end apart: 29, of which 19 were waited for; matrix products, arithmetic and copies ran while one was open for 30% of the time, Pallas kernels for 0%

commit v1 on v0

v1 whole, which is shorter than its diff:
```python
import jax
import jax.numpy as jnp
from jax import lax
from jax.experimental import pallas as pl
from jax.experimental.pallas import tpu as pltpu
from jax.sharding import PartitionSpec as P

HEAD_DIM = 64
ADAPTERS = 8
ADAPTER_SCALE = 2.0
NORM_EPS = 1e-05
ROPE_BASE = 160000.0
LANES = 128
BF = jnp.bfloat16
F32 = jnp.float32


def nt(a, b):
    return lax.dot_general(a, b, (((1,), (1,)), ((), ())), preferred_element_type=F32)


def nn(a, b):
    return lax.dot_general(a, b, (((1,), (0,)), ((), ())), preferred_element_type=F32)


def tn(a, b):
    return lax.dot_general(a, b, (((0,), (0,)), ((), ())), preferred_element_type=F32)


def lanes_of(ref, first=0, count=None):
    count = ref.shape[2] if count is None else count
    return jnp.concatenate(
        [ref[part, 0, pl.ds(first, count), :] for part in range(ref.shape[0])], axis=1
    )


def full(shape):
    return pl.BlockSpec(shape, lambda *_: (0,) * len(shape))


def norm_parts(values):
    centred = values - jnp.mean(values, axis=-1, keepdims=True)
    spread = jnp.mean(centred * centred, axis=-1, keepdims=True)
    scale = lax.rsqrt(spread + NORM_EPS)
    return centred * scale, scale


def norm_back(grads, normed, scale, gain):
    weighted = grads * gain
    return scale * (
        weighted
        - jnp.mean(weighted, axis=-1, keepdims=True)
        - normed * jnp.mean(weighted * normed, axis=-1, keepdims=True)
    )


def turn(values, cosine, sine_up, sine_down):
    width = values.shape[1]
    half = HEAD_DIM // 2
    return (
        values * cosine
        + pltpu.roll(values, width - half, 1) * sine_up
        + pltpu.roll(values, half, 1) * sine_down
    )


def project_kernel(
    rows, weight, low, up, mask, cosine, sine_up, sine_down,
    query, pairs_a, pairs_b, down, *, split, wide
):
    @pl.when(pl.program_id(0) == 0)
    def _():
        down[...] = (nt(rows[...], low[...]) * (ADAPTER_SCALE * mask[...])).astype(BF)

    table = lanes_of(weight)
    out = nt(rows[...], table) + nn(down[...], up[0])
    cos, su, sd = cosine[...], sine_up[...], sine_down[...]
    turned = turn(out[:, :wide], cos, su, sd)
    query[...] = (turned * HEAD_DIM**-0.5).astype(BF)
    key = turn(out[:, wide : 2 * wide], cos, su, sd).astype(BF)
    value = out[:, 2 * wide :].astype(BF)
    pairs_a[0] = key[:split]
    pairs_a[1] = value[:split]
    pairs_b[0] = key[split:]
    pairs_b[1] = value[split:]


def project(rows, weight, low, up, mask, tables, split):
    count, model = rows.shape
    parts, blocks, tall, lane = weight.shape
    wide = tall // 3
    rank = low.shape[0]
    rest = count - split
    return pl.pallas_call(
        lambda *refs: project_kernel(*refs, split=split, wide=wide),
        grid=(blocks,),
        in_specs=[
            full((count, model)),
            pl.BlockSpec((parts, 1, tall, lane), lambda m: (0, m, 0, 0)),
            full((rank, model)),
            pl.BlockSpec((1, rank, tall), lambda m: (m, 0, 0)),
            full((count, rank)),
            full((count, wide)),
            full((count, wide)),
            full((count, wide)),
        ],
        out_specs=[
            pl.BlockSpec((count, wide), lambda m: (0, m)),
            pl.BlockSpec((2, split, wide), lambda m: (0, 0, m)),
            pl.BlockSpec((2, rest, wide), lambda m: (0, 0, m)),
            full((count, rank)),
        ],
        out_shape=[
            jax.ShapeDtypeStruct((count, blocks * wide), BF),
            jax.ShapeDtypeStruct((2, split, blocks * wide), BF),
            jax.ShapeDtypeStruct((2, rest, blocks * wide), BF),
            jax.ShapeDtypeStruct((count, rank), BF),
        ],
        name="project",
    )(rows, weight, low, up, mask, *tables)


def project_back_kernel(
    rows, grad_query, own_a, got_a, own_b, got_b, weight, low, up, mask, down,
    cosine, sine_up, sine_down, out, up_grad, low_grad, down_grad, *, split, wide, blocks
):
    step = pl.program_id(0)

    @pl.when(step == 0)
    def _():
        out[...] = jnp.zeros(out.shape, F32)
        down_grad[...] = jnp.zeros(down_grad.shape, F32)

    cos, su, sd = cosine[...], -sine_up[...], -sine_down[...]
    query = turn(grad_query[...] * HEAD_DIM**-0.5, cos, su, sd).astype(BF)
    key = jnp.concatenate(
        [own_a[0] + got_a[0].astype(F32), own_b[0] + got_b[0].astype(F32)], axis=0
    )
    key = turn(key, cos, su, sd).astype(BF)
    value = jnp.concatenate(
        [own_a[1] + got_a[1].astype(F32), own_b[1] + got_b[1].astype(F32)], axis=0
    ).astype(BF)
    grads = jnp.concatenate([query, key, value], axis=1)
    table = lanes_of(weight)
    out[...] += nn(grads, table)
    down_grad[...] += nt(grads, up[0])
    up_grad[0] = tn(down[...], grads)

    @pl.when(step == blocks - 1)
    def _():
        small = (down_grad[...] * (ADAPTER_SCALE * mask[...])).astype(BF)
        out[...] += nn(small, low[...])
        low_grad[...] = tn(small, rows[...])


def project_back(rows, grad_query, own_a, got_a, own_b, got_b, weight, low, up, mask, down, tables, split):
    count, model = rows.shape
    parts, blocks, tall, lane = weight.shape
    wide = tall // 3
    rank = low.shape[0]
    rest = count - split
    pair_a = pl.BlockSpec((2, split, wide), lambda m: (0, 0, m))
    pair_b = pl.BlockSpec((2, rest, wide), lambda m: (0, 0, m))
    return pl.pallas_call(
        lambda *refs: project_back_kernel(*refs, split=split, wide=wide, blocks=blocks),
        grid=(blocks,),
        in_specs=[
            full((count, model)),
            pl.BlockSpec((count, wide), lambda m: (0, m)),
            pair_a,
            pair_a,
            pair_b,
            pair_b,
            pl.BlockSpec((parts, 1, tall, lane), lambda m: (0, m, 0, 0)),
            full((rank, model)),
            pl.BlockSpec((1, rank, tall), lambda m: (m, 0, 0)),
            full((count, rank)),
            full((count, rank)),
            full((count, wide)),
            full((count, wide)),
            full((count, wide)),
        ],
        out_specs=[
            full((count, model)),
            pl.BlockSpec((1, rank, tall), lambda m: (m, 0, 0)),
            full((rank, model)),
        ],
        out_shape=[
            jax.ShapeDtypeStruct((count, model), F32),
            jax.ShapeDtypeStruct((blocks, rank, tall), F32),
            jax.ShapeDtypeStruct((rank, model), F32),
        ],
        scratch_shapes=[pltpu.VMEM((count, rank), F32)],
        name="project_back",
    )(rows, grad_query, own_a, got_a, own_b, got_b, weight, low, up, mask, down, *tables)


def one_head(values, head):
    lane = lax.broadcasted_iota(jnp.int32, values.shape, 1)
    return jnp.where((lane // HEAD_DIM) == head, values, jnp.zeros_like(values))


def attend_kernel(query, *refs):
    *pairs, context, log_total = refs
    rows = query[...]
    keys = jnp.concatenate([pair[0] for pair in pairs], axis=0)
    values = jnp.concatenate([pair[1] for pair in pairs], axis=0)
    turned = values.T
    outs = []
    for head in range(2):
        scores = nt(keys, one_head(rows, head))
        top = jnp.max(scores, axis=0, keepdims=True)
        raised = jnp.exp(scores - top)
        total = jnp.sum(raised, axis=0, keepdims=True)
        part = nn(turned[head * HEAD_DIM : (head + 1) * HEAD_DIM], raised.astype(BF))
        outs.append(part * (1.0 / total))
        log_total[0, head : head + 1] = top + jnp.log(total)
    context[...] = jnp.concatenate(outs, axis=0).T.astype(BF)


def attend(query, first, count, pairs):
    model = query.shape[1]
    blocks = model // LANES
    at = first // count
    return pl.pallas_call(
        attend_kernel,
        grid=(blocks,),
        in_specs=[pl.BlockSpec((count, LANES), lambda h: (at, h))]
        + [pl.BlockSpec((2, pair.shape[1], LANES), lambda h: (0, 0, h)) for pair in pairs],
        out_specs=[
            pl.BlockSpec((count, LANES), lambda h: (0, h)),
            pl.BlockSpec((1, 2, count), lambda h: (h, 0, 0)),
        ],
        out_shape=[
            jax.ShapeDtypeStruct((count, model), BF),
            jax.ShapeDtypeStruct((blocks, 2, count), F32),
        ],
        name="attend",
    )(query, *pairs)


def attend_back_kernel(query, grad, log_total, *refs, pieces):
    pairs = refs[:pieces]
    grad_query = refs[pieces]
    grad_pairs = refs[pieces + 1 :]
    rows = query[...]
    outer = grad[...]
    keys = jnp.concatenate([pair[0] for pair in pairs], axis=0)
    values = jnp.concatenate([pair[1] for pair in pairs], axis=0)
    turned = keys.T
    query_parts = []
    grad_keys = None
    grad_values = None
    for head in range(2):
        own = one_head(rows, head)
        own_grad = one_head(outer, head)
        scores = nt(keys, own)
        probs = jnp.exp(scores - log_total[0, head : head + 1])
        wide = nt(values, own_grad)
        mean = jnp.sum(probs * wide, axis=0, keepdims=True)
        back = (probs * (wide - mean)).astype(BF)
        query_parts.append(nn(turned[head * HEAD_DIM : (head + 1) * HEAD_DIM], back))
        more_keys = nn(back, own)
        more_values = nn(probs.astype(BF), own_grad)
        grad_keys = more_keys if grad_keys is None else grad_keys + more_keys
        grad_values = more_values if grad_values is None else grad_values + more_values
    grad_query[...] = jnp.concatenate(query_parts, axis=0).T
    start = 0
    for out in grad_pairs:
        size = out.shape[1]
        out[0] = grad_keys[start : start + size].astype(out.dtype)
        out[1] = grad_values[start : start + size].astype(out.dtype)
        start += size


def attend_back(query, grad, first, count, log_total, pairs, kinds):
    model = query.shape[1]
    blocks = model // LANES
    at = first // count
    row_spec = pl.BlockSpec((count, LANES), lambda h: (at, h))
    pair_specs = [pl.BlockSpec((2, pair.shape[1], LANES), lambda h: (0, 0, h)) for pair in pairs]
    return pl.pallas_call(
        lambda *refs: attend_back_kernel(*refs, pieces=len(pairs)),
        grid=(blocks,),
        in_specs=[row_spec, row_spec, pl.BlockSpec((1, 2, count), lambda h: (h, 0, 0))] + pair_specs,
        out_specs=[pl.BlockSpec((count, LANES), lambda h: (0, h))] + pair_specs,
        out_shape=[jax.ShapeDtypeStruct((count, model), F32)]
        + [jax.ShapeDtypeStruct(pair.shape, kind) for pair, kind in zip(pairs, kinds)],
        name="attend_back",
    )(query, grad, log_total, *pairs)


def block_rows(weight):
    return jnp.concatenate(
        [
            jnp.concatenate([weight[part, m] for part in range(weight.shape[0])], axis=1)
            for m in range(weight.shape[1])
        ],
        axis=0,
    )


def merge_kernel(context, start, weight, low, up, mask, gain, middle, normed, down):
    rows = context[...]
    small = (nt(rows, low[...]) * (ADAPTER_SCALE * mask[...])).astype(BF)
    down[...] = small
    total = start[...].astype(F32) + nn(rows, block_rows(weight)) + nn(small, up[...])
    middle[...] = total
    normed[...] = (norm_parts(total)[0] * gain[...]).astype(BF)


def merge(context, start, weight, low, up, mask, gain):
    count, model = context.shape
    tile = 256
    rank = low.shape[0]
    row = pl.BlockSpec((tile, model), lambda t: (t, 0))
    small = pl.BlockSpec((tile, rank), lambda t: (t, 0))
    return pl.pallas_call(
        merge_kernel,
        grid=(count // tile,),
        in_specs=[row, row, full(weight.shape), full(low.shape), full(up.shape), small, full((1, model))],
        out_specs=[row, row, small],
        out_shape=[
            jax.ShapeDtypeStruct((count, model), F32),
            jax.ShapeDtypeStruct((count, model), BF),
            jax.ShapeDtypeStruct((count, rank), BF),
        ],
        name="merge",
    )(context, start, weight, low, up, mask, gain)


def merge_back_kernel(
    grad_normed, middle, out_grad, context, down, weight, low, up, mask, gain,
    grad_middle, grad_context, low_grad, up_grad
):
    @pl.when(pl.program_id(0) == 0)
    def _():
        low_grad[...] = jnp.zeros(low_grad.shape, F32)
        up_grad[...] = jnp.zeros(up_grad.shape, F32)

    normed, scale = norm_parts(middle[...])
    total = out_grad[...].astype(F32) + norm_back(grad_normed[...], normed, scale, gain[...])
    grad_middle[...] = total
    rows = total.astype(BF)
    small = (nt(rows, up[...]) * (ADAPTER_SCALE * mask[...])).astype(BF)
    grad_context[...] = (nt(rows, block_rows(weight)) + nn(small, low[...])).astype(BF)
    low_grad[...] += tn(small, context[...])
    up_grad[...] += tn(down[...], rows)


def merge_back(grad_normed, middle, out_grad, context, down, weight, low, up, mask, gain):
    count, model = context.shape
    tile = 256
    rank = low.shape[0]
    row = pl.BlockSpec((tile, model), lambda t: (t, 0))
    small = pl.BlockSpec((tile, rank), lambda t: (t, 0))
    return pl.pallas_call(
        merge_back_kernel,
        grid=(count // tile,),
        in_specs=[row, row, row, row, small, full(weight.shape), full(low.shape), full(up.shape), small, full((1, model))],
        out_specs=[row, row, full((rank, model)), full((rank, model))],
        out_shape=[
            jax.ShapeDtypeStruct((count, model), F32),
            jax.ShapeDtypeStruct((count, model), BF),
            jax.ShapeDtypeStruct((rank, model), F32),
            jax.ShapeDtypeStruct((rank, model), F32),
        ],
        name="merge_back",
    )(grad_normed, middle, out_grad, context, down, weight, low, up, mask, gain)


def gated_kernel(
    rows, out_grad, expand, shrink, expand_up, shrink_low, expand_low, shrink_up, mask,
    total, grad_rows, expand_up_grad, shrink_low_grad, expand_low_grad, shrink_up_grad,
    down, down_grad, late, late_grad, *, width, blocks
):
    step = pl.program_id(0)
    scaled = ADAPTER_SCALE * mask[...]

    @pl.when(step == 0)
    def _():
        total[...] = jnp.zeros(total.shape, F32)
        grad_rows[...] = jnp.zeros(grad_rows.shape, F32)
        down[...] = (nt(rows[...], expand_low[...]) * scaled).astype(BF)
        down_grad[...] = (nt(out_grad[...], shrink_up[...]) * scaled).astype(BF)
        late[...] = jnp.zeros(late.shape, F32)
        late_grad[...] = jnp.zeros(late_grad.shape, F32)

    values = lanes_of(expand, 0, width)
    gates = lanes_of(expand, width, width)
    outs = lanes_of(shrink)
    up_values = expand_up[0, :, :width]
    up_gates = expand_up[0, :, expand_up.shape[2] // 2 : expand_up.shape[2] // 2 + width]
    low_outs = shrink_low[0, :, :width]
    first = nt(rows[...], values) + nn(down[...], up_values)
    second = nt(rows[...], gates) + nn(down[...], up_gates)
    chance = 0.5 + 0.5 * lax.erf(first * (0.5**0.5))
    curve = first * chance
    slope = chance + first * (jnp.exp(-0.5 * first * first) * 0.3989422804014327)
    active = (curve * second).astype(BF)
    grads = nt(out_grad[...], outs) + nn(down_grad[...], low_outs)
    first_grad = (grads * second * slope).astype(BF)
    second_grad = (grads * curve).astype(BF)
    total[...] += nn(active, outs)
    late[...] += nt(active, low_outs)
    grad_rows[...] += nn(first_grad, values) + nn(second_grad, gates)
    late_grad[...] += nt(first_grad, up_values) + nt(second_grad, up_gates)
    expand_up_grad[0, 0] = tn(down[...], first_grad)
    expand_up_grad[0, 1] = tn(down[...], second_grad)
    shrink_low_grad[0] = tn(down_grad[...], active)

    @pl.when(step == blocks - 1)
    def _():
        small = (late[...] * scaled).astype(BF)
        total[...] += nn(small, shrink_up[...])
        shrink_up_grad[...] = tn(small, out_grad[...])
        small_grad = (late_grad[...] * scaled).astype(BF)
        grad_rows[...] += nn(small_grad, expand_low[...])
        expand_low_grad[...] = tn(small_grad, rows[...])


def gated(rows, out_grad, weights, width, expand_up, shrink_low, expand_low, shrink_up, mask):
    count, model = rows.shape
    parts, blocks, _, lane = weights.shape
    rank = expand_low.shape[0]
    pad = shrink_low.shape[2]
    return pl.pallas_call(
        lambda *refs: gated_kernel(*refs, width=width, blocks=blocks),
        grid=(blocks,),
        in_specs=[
            full((count, model)),
            full((count, model)),
            pl.BlockSpec((parts, 1, 2 * width, lane), lambda m: (0, m, 0, 0)),
            pl.BlockSpec((parts, 1, width, lane), lambda m: (0, m, 2, 0)),
            pl.BlockSpec((1, rank, 2 * pad), lambda m: (m, 0, 0)),
            pl.BlockSpec((1, rank, pad), lambda m: (m, 0, 0)),
            full((rank, model)),
            full((rank, model)),
            full((count, rank)),
        ],
        out_specs=[
            full((count, model)),
            full((count, model)),
            pl.BlockSpec((1, 2, rank, width), lambda m: (m, 0, 0, 0)),
            pl.BlockSpec((1, rank, width), lambda m: (m, 0, 0)),
            full((rank, model)),
            full((rank, model)),
        ],
        out_shape=[
            jax.ShapeDtypeStruct((count, model), F32),
            jax.ShapeDtypeStruct((count, model), F32),
            jax.ShapeDtypeStruct((blocks, 2, rank, width), F32),
            jax.ShapeDtypeStruct((blocks, rank, width), F32),
            jax.ShapeDtypeStruct((rank, model), F32),
            jax.ShapeDtypeStruct((rank, model), F32),
        ],
        scratch_shapes=[
            pltpu.VMEM((count, rank), BF),
            pltpu.VMEM((count, rank), BF),
            pltpu.VMEM((count, rank), F32),
            pltpu.VMEM((count, rank), F32),
        ],
        name="gated",
    )(rows, out_grad, weights, weights, expand_up, shrink_low, expand_low, shrink_up, mask)


def pair_swap(values, bit):
    size = lax.axis_size("mp")
    return lax.ppermute(values, "mp", [(i, i ^ bit) for i in range(size)])


def gather_weight(rows):
    parts, blocks = lax.axis_size("dp"), lax.axis_size("mp")
    count, own = rows.shape
    whole = lax.all_gather(rows, ("dp", "mp"), axis=0, tiled=True).reshape(parts, blocks, count, own)
    if own == LANES:
        return whole
    tiles = parts * own // LANES
    whole = whole.transpose(1, 2, 0, 3).reshape(blocks, count, tiles, LANES)
    return whole.transpose(2, 0, 1, 3)


def local(
    hidden,
    cotangent,
    adapter_ids,
    attn_gain,
    mlp_gain,
    joined_weight,
    merge_weight_matrix,
    expand_weight,
    shrink_weight_matrix,
    joined_lower,
    joined_up_matrices,
    merge_lower,
    merge_up_matrices,
    expand_lower,
    expand_up_matrices,
    shrink_lower,
    shrink_up_matrices,
):
    parts, blocks = lax.axis_size("dp"), lax.axis_size("mp")
    place = lax.axis_index("mp")
    pair = place // 2
    core = place % 2
    own_rows, model = hidden.shape[1], hidden.shape[2]
    row_in = joined_weight.shape[0]
    wide = joined_weight.shape[2]
    width = expand_weight.shape[2]
    rank = joined_lower.shape[2]
    split = 2 * own_rows
    count = 3 * own_rows

    joined_whole = gather_weight(joined_weight.reshape(row_in, 3 * wide).T)
    rest = jnp.concatenate(
        [expand_weight.reshape(row_in, 2 * width).T, shrink_weight_matrix.T], axis=0
    )
    merge_whole = gather_weight(merge_weight_matrix.T)
    rest_whole = gather_weight(rest)

    keep = lax.dynamic_index_in_dim(hidden, pair, 0, keepdims=False)
    give = lax.dynamic_index_in_dim(hidden, 1 - pair, 0, keepdims=False)
    start = jnp.concatenate([keep, pair_swap(give, 2), hidden[2]], axis=0)
    keep_grad = lax.dynamic_index_in_dim(cotangent, pair, 0, keepdims=False)
    give_grad = lax.dynamic_index_in_dim(cotangent, 1 - pair, 0, keepdims=False)
    out_grad = jnp.concatenate([keep_grad, pair_swap(give_grad, 2), cotangent[2]], axis=0)

    sets = jnp.stack([adapter_ids[pair], adapter_ids[2]])

    def whole_low(table):
        picked = jnp.take(table, sets, axis=0)
        return picked.transpose(0, 2, 1).reshape(2 * rank, -1)

    def whole_up(table):
        return jnp.take(table, sets, axis=0).reshape(2 * rank, -1)

    joined_low = whole_low(joined_lower)
    expand_low = whole_low(expand_lower)
    merge_up = whole_up(merge_up_matrices)
    shrink_up = whole_up(shrink_up_matrices)
    pad = -(-width // LANES) * LANES
    side = [(0, 0), (0, 0), (0, pad - width)]
    mine = jnp.concatenate(
        [
            joined_up_matrices.reshape(ADAPTERS, rank, 3 * wide),
            merge_lower.transpose(0, 2, 1),
            jnp.pad(expand_up_matrices[:, :, 0], side),
            jnp.pad(expand_up_matrices[:, :, 1], side),
            jnp.pad(shrink_lower.transpose(0, 2, 1), side),
        ],
        axis=2,
    )
    mine = jnp.take(mine, adapter_ids, axis=0)
    across = pair_swap(mine, 2)
    beside = pair_swap(mine, 1)
    corner = pair_swap(across, 1)
    around = jnp.stack([mine, beside, across, corner])
    order = place ^ jnp.arange(blocks)
    split_sets = jnp.take(around, order, axis=0)
    split_sets = jnp.take(split_sets, jnp.stack([pair, 2]), axis=1).reshape(blocks, 2 * rank, -1)
    at = 3 * wide
    joined_up = split_sets[:, :, :at]
    merge_low = split_sets[:, :, at : at + wide].transpose(1, 0, 2).reshape(2 * rank, blocks * wide)
    expand_up = split_sets[:, :, at + wide : at + wide + 2 * pad]
    shrink_low = split_sets[:, :, at + wide + 2 * pad :]
    group = (jnp.arange(count) >= split).astype(jnp.int32)
    mask = (group[:, None] == (jnp.arange(2 * rank) // rank)[None, :]).astype(F32)

    steps = jnp.arange(own_rows)
    spots = jnp.concatenate(
        [
            place * own_rows + steps,
            (place ^ 2) * own_rows + steps,
            place * own_rows + steps,
        ]
    ).astype(F32)
    half = HEAD_DIM // 2
    inverse = ROPE_BASE ** (-(jnp.arange(half, dtype=F32) * 2.0 / HEAD_DIM))
    angles = spots[:, None] * inverse[None, :]
    cosine, sine, none = jnp.cos(angles), jnp.sin(angles), jnp.zeros_like(angles)
    heads = wide // HEAD_DIM
    tables = (
        jnp.tile(jnp.concatenate([cosine, cosine], axis=1), (1, heads)),
        jnp.tile(jnp.concatenate([-sine, none], axis=1), (1, heads)),
        jnp.tile(jnp.concatenate([none, sine], axis=1), (1, heads)),
    )

    attn_scale = attn_gain.astype(F32)[None, :]
    mlp_scale = mlp_gain.astype(F32)[None, :]
    first_normed, first_scale = norm_parts(start.astype(F32))
    normed = (first_normed * attn_scale).astype(BF)

    query, pairs_a, pairs_b, joined_down = project(
        normed, joined_whole, joined_low, joined_up, mask, tables, split
    )
    beside_a = pair_swap(pairs_a, 1)
    across_b = pair_swap(pairs_b, 2)
    beside_b = pair_swap(pairs_b, 1)
    corner_b = pair_swap(across_b, 1)
    sets_a = (pairs_a, beside_a)
    sets_b = (pairs_b, across_b, beside_b, corner_b)
    context_a, log_a = attend(query, 0, split, sets_a)
    context_b, log_b = attend(query, split, own_rows, sets_b)
    context = jnp.concatenate([context_a, context_b], axis=0)
    middle, normed_mlp, merge_down = merge(
        context, start, merge_whole, merge_low, merge_up, mask, mlp_scale
    )
    (
        shrunk,
        grad_normed_mlp,
        expand_up_grad,
        shrink_low_grad,
        expand_low_grad,
        shrink_up_grad,
    ) = gated(
        normed_mlp, out_grad, rest_whole, width,
        expand_up, shrink_low, expand_low, shrink_up, mask,
    )
    result = (middle + shrunk).astype(BF)
    back = pair_swap(result[own_rows:split], 2)

    grad_middle, grad_context, merge_low_grad, merge_up_grad = merge_back(
        grad_normed_mlp, middle, out_grad, context, merge_down,
        merge_whole, merge_low, merge_up, mask, mlp_scale,
    )
    grad_query_b, own_b, far_b, near_b, last_b = attend_back(
        query, grad_context, split, own_rows, log_b, sets_b, (F32, F32, BF, BF)
    )
    near_got = pair_swap(near_b, 1)
    last_got = pair_swap(last_b, 1)
    far_sum = (far_b + last_got.astype(F32)).astype(BF)
    own_b = own_b + near_got.astype(F32)
    got_b = pair_swap(far_sum, 2)
    grad_query_a, own_a, near_a = attend_back(
        query, grad_context, 0, split, log_a, sets_a, (F32, BF)
    )
    got_a = pair_swap(near_a, 1)
    grad_query = jnp.concatenate([grad_query_a, grad_query_b], axis=0)
    grad_normed, joined_up_grad, joined_low_grad = project_back(
        normed, grad_query, own_a, got_a, own_b, got_b,
        joined_whole, joined_low, joined_up, mask, joined_down, tables, split,
    )
    grad_start = grad_middle + norm_back(grad_normed, first_normed, first_scale, attn_scale)
    grad_start = grad_start.astype(BF)
    back_grad = pair_swap(grad_start[own_rows:split], 2)

    def settle(values, swapped):
        mine_first = jnp.stack([values[:own_rows], swapped])
        other_first = jnp.stack([swapped, values[:own_rows]])
        two = jnp.where(pair == 0, mine_first, other_first)
        return jnp.concatenate([two, values[None, split:]], axis=0)

    every_id = lax.all_gather(adapter_ids, "dp", axis=0)
    first_ids = jnp.repeat(every_id[:, :2], blocks // 2, axis=1)
    ids = jnp.stack([first_ids, jnp.broadcast_to(every_id[:, 2:], first_ids.shape)], axis=2)
    choose = (jnp.arange(ADAPTERS)[:, None] == ids.reshape(1, -1)).astype(BF)

    def by_block(grad):
        return grad.reshape(2 * rank, blocks, -1).transpose(1, 0, 2)

    def spread(pieces):
        sizes = [piece.shape[2] for piece in pieces]
        packed = jnp.concatenate([piece.astype(BF) for piece in pieces], axis=2)
        total = packed.shape[2]
        packed = packed.reshape(blocks, 2, parts, -1).transpose(2, 0, 1, 3)
        packed = packed.reshape(parts * blocks, 2, -1)
        landed = lax.all_to_all(packed, ("dp", "mp"), 0, 0, tiled=True)
        landed = landed.reshape(parts * blocks * 2, -1)
        summed = jnp.dot(choose, landed, preferred_element_type=F32)
        return summed.astype(BF), sizes, total

    def share(summed, sizes, total, common):
        whole = lax.all_gather(summed, "dp", axis=0)
        whole = whole.transpose(1, 0, 2).reshape(ADAPTERS, rank, total)
        cuts, start_at = [], 0
        for size, shared in zip(sizes, common):
            cuts.append(whole[:, :, start_at : start_at + size])
            start_at += size
        joint = [cut for cut, shared in zip(cuts, common) if shared]
        joint = lax.all_gather(jnp.stack(joint), "mp", axis=0)
        outs, at_joint = [], 0
        for cut, shared in zip(cuts, common):
            if shared:
                outs.append(joint[:, at_joint].transpose(1, 2, 0, 3).reshape(ADAPTERS, rank, -1).astype(F32))
                at_joint += 1
            else:
                outs.append(cut.astype(F32))
        return outs

    early = spread(
        [
            by_block(expand_low_grad),
            by_block(shrink_up_grad),
            expand_up_grad[:, 0],
            expand_up_grad[:, 1],
            shrink_low_grad,
            by_block(merge_up_grad),
            by_block(merge_low_grad),
        ]
    )
    out_early = share(*early, (True, True, False, False, False, True, False))
    late = spread([by_block(joined_low_grad), joined_up_grad])
    out_late = share(*late, (True, False))

    def tall(values):
        return values.transpose(0, 2, 1)

    return (
        settle(result, back),
        settle(grad_start, back_grad),
        tall(out_late[0]),
        out_late[1].reshape(ADAPTERS, rank, 3, wide),
        tall(out_early[6]),
        out_early[5],
        tall(out_early[0]),
        jnp.stack([out_early[2], out_early[3]], axis=2),
        tall(out_early[4]),
        out_early[1],
    )


def solution(mesh):
    in_specs = (
        P("dp", "mp", None),
        P("dp", "mp", None),
        P("dp"),
        P(),
        P(),
        P("dp", None, "mp"),
        P("dp", "mp"),
        P("dp", None, "mp"),
        P("dp", "mp"),
        P(),
        P(None, None, None, "mp"),
        P(None, "mp", None),
        P(),
        P(),
        P(None, None, None, "mp"),
        P(None, "mp", None),
        P(),
    )
    out_specs = (
        P("dp", "mp", None),
        P("dp", "mp", None),
        P(),
        P(None, None, None, "mp"),
        P(None, "mp", None),
        P(),
        P(),
        P(None, None, None, "mp"),
        P(None, "mp", None),
        P(),
    )
    return jax.shard_map(local, mesh=mesh, in_specs=in_specs, out_specs=out_specs, check_vma=False)
```

time: 1310 us -> 547 us (0.42)
  waiting for transfers between devices: 688 us -> 148 us
  matrix products: 378 us -> 0.34 us
  Pallas kernels: 0 us -> 176 us
  other arithmetic: 146 us -> 40.2 us
  blocking collectives: 33.4 us -> 95.2 us
  starting transfers between devices: 3.23 us -> 18.8 us
    dot_general x114 -> x2, matrix products: 378 us -> 0.34 us  [spread(): summed = jnp.dot(choose, landed, preferred_element_type=F32)]
    psum x2 -> x0, waiting for transfers between devices: 232 us -> none  [the longest x1 133 us: local(): lax.psum((totals[0], totals[3], totals[4], totals[7]), ('dp', 'mp'))]
    reduce_scatter x12 -> x0, waiting for transfers between devices: 202 us -> none  [the longest x6 154 us: total_rows(): lax.psum_scatter(values.astype(jnp.bfloat16), 'mp', scatter_dimension=0,...]
    pallas_call x0 -> x9, Pallas kernels: none -> 176 us  [the longest x1 49.4 us: gated(): pl.pallas_call(lambda *refs: gated_kernel(*refs, width=width, blocks=bloc...]
    all_gather x15 -> x3, waiting for transfers between devices: 250 us -> 97.7 us  [gather_weight(): lax.all_gather(rows, ('dp', 'mp'), axis=0, tiled=True)]
    reduce_sum x19 -> x3, other arithmetic: 54 us -> 3.81 us  [the longest x1 2.98 us: norm_back(): jnp.mean(weighted, axis=-1, keepdims=True)]
    ppermute x0 -> x15, waiting for transfers between devices: none -> 44.1 us  [pair_swap(): return lax.ppermute(values, 'mp', [(i, i ^ bit) for i in range(size)])]
    all_gather x1 -> x4, blocking collectives: 33.4 us -> 76.6 us  [the longest x2 63.2 us: share(): whole = lax.all_gather(summed, 'dp', axis=0)]
  transfers between devices with their start and end apart: 29 -> 20, of which waited for: 19 -> 6; matrix products, arithmetic and copies ran while one was open for 30% -> 13% of each run, Pallas kernels for 0% -> 15%
where the time goes in v1:
time: 547 us; the launch traced here: 541 us
  Pallas kernels  176 us (32%)
  waiting for transfers between devices  148 us (27%)
  blocking collectives  95.2 us (17%)
  local copies, waits for them, and re-layouts  47.8 us (9%)
  other arithmetic  40.2 us (7%)
  starting transfers between devices  18.8 us (3%)
  between operations  15.7 us (3%)
    all_gather x3, waiting for transfers between devices, gather_weight(): lax.all_gather(rows, ('dp', 'mp'), axis=0, tiled=True)  97.7 us
    all_gather x2, blocking collectives, share(): whole = lax.all_gather(summed, 'dp', axis=0)  63.2 us
    pallas_call x1, Pallas kernels, gated(): pl.pallas_call(lambda *refs: gated_kernel(*refs, width=width, blocks=bloc...  49.4 us
    pallas_call x2, Pallas kernels, attend_back(): pl.pallas_call(lambda *refs: attend_back_kernel(*refs, pieces=len(pairs))...  47.6 us
    ppermute x15, waiting for transfers between devices, pair_swap(): return lax.ppermute(values, 'mp', [(i, i ^ bit) for i in range(size)])  44.1 us
    pallas_call x2, Pallas kernels, attend(): pl.pallas_call(attend_kernel, grid=(blocks,), in_specs=[pl.BlockSpec((cou...  32.4 us
    unnamed x1, blocking collectives  18.6 us
    pallas_call x1, Pallas kernels, project_back(): pl.pallas_call(lambda *refs: project_back_kernel(*refs, split=split, wide...  16 us
  transfers between devices with their start and end apart: 20, of which 6 were waited for; matrix products, arithmetic and copies ran while one was open for 13% of the time, Pallas kernels for 15%

profile of v1, /device:TPU:0, one launch (start us, length us, event | category | flops | bytes accessed | tf_op | source)
XLA Modules:
  0.0 541.5 jit_solution(17824145874938473445)
XLA Ops:
  7.3 1.9 copy.106
  10.0 1.9 pad_maximum_fusion.6
  16.2 1.7 gather_fusion
  18.7 2.9 collective-permute-start.2
  21.7 0.9 dynamic-slice_bitcast_fusion.3
  23.4 1.4 compare_and_fusion
  26.6 1.1 copy.111.refs_5_.refs_11_
  27.8 1.2 copy.112.refs_6_.refs_12_
  29.0 1.2 copy.113.refs_7_.refs_13_
  31.1 0.9 compare_convert_fusion.refs_4_.mask.refs_8_.refs_9_
  32.5 9.5 %collective-permute-done = bf16[256,1024]{1,0:T(8,128)(2,1)S(1)} collective-permute-done((bf16[256,1024]{1,0:T(8,128)(2,1)}, bf16[256,1024]{1,0:T(8,128)(2,1)S(1)}, u32[]{:S(2)}, u32[]{:S(2)}) %collective-permute-start) | collective-permute-done | bytes 524320 | tf_op jit(solution)/shard_map/ppermute | solution.py:469
  42.9 1.7 fusion.5.refs_0_
  44.6 1.2 pad_maximum_fusion.5
  47.5 0.9 copy-done.9
  49.2 35.9 %all-gather.9.cloned.1.call-done = bf16[24576,128]{1,0:T(8,128)(2,1)} async-done(((bf16[768,128]{1,0:T(8,128)(2,1)}), bf16[24576,128]{1,0:T(8,128)(2,1)}) %all-gather.9.cloned.1.call-update) | async-done | bytes 6291472 | tf_op jit(solution)/shard_map/all_gather | solution.py:475
  85.1 12.7 %project.1 = (bf16[768,1024]{1,0:T(8,128)(2,1)}, bf16[2,512,1024]{2,1,0:T(8,128)(2,1)}, bf16[2,256,1024]{2,1,0:T(8,128)(2,1)}, bf16[768,32]{1,0:T(8,128)(2,1)}) custom-call(bf16[768,1024]{1,0:T(8,128)(2,1)} %fusion.5.refs_0_, bf16[8,4,768,128]{3,2,1,0:T(8,128)(2,1)} %bitcast.187, bf16[32,1024]{1,0:T(8,128)(2,1)} %bitcast.205, ...), custom_call_target="tpu_custom_call" | custom-call | tf_op jit(solution)/shard_map/project/pallas_call | solution.py:94
  97.8 1.5 collective-permute-start.5
  99.7 25.0 %collective-permute-done.5.refs_1_.refs_4_ = bf16[2,256,1024]{2,1,0:T(8,128)(2,1)S(1)} collective-permute-done((bf16[2,256,1024]{2,1,0:T(8,128)(2,1)}, bf16[2,256,1024]{2,1,0:T(8,128)(2,1)S(1)}, u32[]{:S(2)}, u32[]{:S(2)}) %collective-permute-start.5) | collective-permute-done | bytes 1048608 | tf_op jit(solution)/shard_map/ppermute | solution.py:469
  124.8 2.9 dynamic-slice_bitcast_fusion.1
  127.7 1.4 collective-permute-start.8
  129.7 1.5 gather_fusion.6
  131.2 1.5 gather_fusion.4
  133.5 9.6 %collective-permute-done.8 = bf16[256,1024]{1,0:T(8,128)(2,1)} collective-permute-done((bf16[256,1024]{1,0:T(8,128)(2,1)}, bf16[256,1024]{1,0:T(8,128)(2,1)}, u32[]{:S(2)}, u32[]{:S(2)}) %collective-permute-start.8) | collective-permute-done | bytes 524320 | tf_op jit(solution)/shard_map/ppermute | solution.py:469
  143.0 2.7 pad_maximum_fusion.2.refs_1_.out_grad
  147.1 4.1 copy.114
  151.2 1.3 copy-done.6
  152.5 18.0 %attend.2 = (bf16[512,1024]{1,0:T(8,128)(2,1)}, f32[8,2,512]{2,1,0:T(2,128)}) custom-call(bf16[768,1024]{1,0:T(8,128)(2,1)} %get-tuple-element.44.query.refs_0_, bf16[2,512,1024]{2,1,0:T(8,128)(2,1)} %get-tuple-element.45.refs_0_.refs_3_, bf16[2,512,1024]{2,1,0:T(8,128)(2,1)} %copy-done.6), custom_call_target="tpu_custom_call" | custom-call | tf_op jit(solution)/shard_map/attend/pallas_call | solution.py:225
  170.6 1.3 constant_dynamic-update-slice_fusion.2
  171.9 14.4 %attend.3 = (bf16[256,1024]{1,0:T(8,128)(2,1)}, f32[8,2,256]{2,1,0:T(2,128)}) custom-call(bf16[768,1024]{1,0:T(8,128)(2,1)} %get-tuple-element.44.query.refs_0_, bf16[2,256,1024]{2,1,0:T(8,128)(2,1)} %get-tuple-element.47.refs_0_.refs_3_, bf16[2,256,1024]{2,1,0:T(8,128)(2,1)} %copy-done.8, bf16[2,256,1024]{2,1,0:T(8,128)(2,1)} %collective-permute-done.6.refs_2_.refs_5_, ...), custom_call_target="tpu_custom_call" | custom-call | tf_op jit(solution)/shard_map/attend/pallas_call | solution.py:225
  186.2 1.1 constant_dynamic-update-slice_fusion.1.context
  187.3 1.2 copy-done.5
  188.5 7.2 %merge.1 = (f32[768,1024]{1,0:T(8,128)}, bf16[768,1024]{1,0:T(8,128)(2,1)}, bf16[768,32]{1,0:T(8,128)(2,1)}) custom-call(bf16[768,1024]{1,0:T(8,128)(2,1)} %copy-done.5, bf16[768,1024]{1,0:T(8,128)(2,1)} %copy-done.2, bf16[8,4,256,128]{3,2,1,0:T(8,128)(2,1)} %bitcast.189, bf16[32,1024]{1,0:T(8,128)(2,1)} %bitcast.203, bf16[32,1024]{1,0:T(8,128)(2,1)} %bitcast.207, ...), custom_call_target="tpu_custom_call" | custom-call | tf_op jit(solution)/shard_map/merge/pallas_call | solution.py:318
  195.7 61.8 %all-gather.13.cloned.1.call-done = bf16[62976,128]{1,0:T(8,128)(2,1)} async-done(((bf16[1968,128]{1,0:T(8,128)(2,1)}), bf16[62976,128]{1,0:T(8,128)(2,1)}) %all-gather.13.cloned.1.call-update) | async-done | bytes 16121872 | tf_op jit(solution)/shard_map/all_gather | solution.py:475
  257.5 49.4 %gated.1 = (f32[768,1024]{1,0:T(8,128)}, f32[768,1024]{1,0:T(8,128)}, f32[4,2,32,656]{3,2,1,0:T(8,128)}, f32[4,32,656]{2,1,0:T(8,128)}, f32[32,1024]{1,0:T(8,128)}, /*index=5*/f32[32,1024]{1,0:T(8,128)}) custom-call(bf16[768,1024]{1,0:T(8,128)(2,1)} %get-tuple-element.50.refs_0_, bf16[768,1024]{1,0:T(8,128)(2,1)} %pad_maximum_fusion.2.refs_1_.out_grad, ...), custom_call_target="tpu_custom_call" | custom-call | tf_op jit(solution)/shard_map/gated/pallas_call | solution.py:427
  306.9 3.5 add_convert_fusion
  310.4 10.3 %merge_back.1 = (f32[768,1024]{1,0:T(8,128)}, bf16[768,1024]{1,0:T(8,128)(2,1)}, f32[32,1024]{1,0:T(8,128)}, f32[32,1024]{1,0:T(8,128)}) custom-call(f32[768,1024]{1,0:T(8,128)} %get-tuple-element.52.grad_normed, f32[768,1024]{1,0:T(8,128)} %get-tuple-element.49.middle, bf16[768,1024]{1,0:T(8,128)(2,1)} %pad_maximum_fusion.2.refs_1_.out_grad, ...), custom_call_target="tpu_custom_call" | custom-call | tf_op jit(solution)/shard_map/merge_back/pallas_call | solution.py:357
  320.7 18.7 %attend_back.3 = (f32[256,1024]{1,0:T(8,128)}, f32[2,256,1024]{2,1,0:T(8,128)}, f32[2,256,1024]{2,1,0:T(8,128)}, bf16[2,256,1024]{2,1,0:T(8,128)(2,1)}, bf16[2,256,1024]{2,1,0:T(8,128)(2,1)}) custom-call(bf16[768,1024]{1,0:T(8,128)(2,1)} %get-tuple-element.44.query.refs_0_, bf16[768,1024]{1,0:T(8,128)(2,1)} %get-tuple-element.55.refs_1_, ...), custom_call_target="tpu_custom_call" | custom-call | tf_op jit(solution)/shard_map/attend_back/pallas_call | solution.py:282
  339.8 0.9 slice_bitcast_fusion.3
  340.7 1.5 collective-permute-start.9
  343.6 1.5 copy.130
  345.1 2.8 all-to-all-start.1
  349.7 18.6 %all-reduce.5 = s32[24]{0:T(128)S(1)} all-reduce(s32[24]{0:T(128)S(1)} %dynamic-update-slice), channel_id=2, replica_groups=mesh['dp'=8,'mp'=4] {'dp'}, use_global_device_ids=true, to_apply=%add.5 | all-reduce | flops 24 | bytes 192
  368.9 28.9 %attend_back.2 = (f32[512,1024]{1,0:T(8,128)}, f32[2,512,1024]{2,1,0:T(8,128)}, bf16[2,512,1024]{2,1,0:T(8,128)(2,1)}) custom-call(bf16[768,1024]{1,0:T(8,128)(2,1)} %get-tuple-element.44.query.refs_0_, bf16[768,1024]{1,0:T(8,128)(2,1)} %get-tuple-element.55.refs_1_, f32[8,2,512]{2,1,0:T(2,128)} %get-tuple-element.56.refs_2_, ...), custom_call_target="tpu_custom_call" | custom-call | tf_op jit(solution)/shard_map/attend_back/pallas_call | solution.py:282
  397.8 4.1 pad_maximum_fusion.refs_1_
  401.9 1.4 maximum_select_fusion
  403.3 1.3 pad_maximum_fusion.3
  405.5 2.8 add_convert_fusion.1
  408.2 1.5 collective-permute-start.13
  409.7 1.7 convert_add_fusion.refs_4_
  412.1 32.3 %all-gather.3 = bf16[64,5984]{1,0:T(8,128)(2,1)S(1)} all-gather(bf16[8,5984]{1,0:T(8,128)(2,1)S(1)} %convolution_convert_fusion), channel_id=5, replica_groups=mesh['dp'=8,'mp'=4] {'dp'}, dimensions={0}, use_global_device_ids=true | all-gather | bytes 861696 | tf_op jit(solution)/shard_map/all_gather | solution.py:673
  445.1 0.9 convert_bitcast_fusion.4
  446.1 1.5 copy.136
  448.3 7.7 %all-gather.4 = bf16[12,8,16,256]{3,2,1,0:T(8,128)(2,1)S(1)} all-gather(bf16[3,8,16,256]{3,2,1,0:T(8,128)(2,1)S(1)} %pad_maximum_fusion.9), channel_id=6, replica_groups=mesh['dp'=8,'mp'=4] {'mp'}, dimensions={0}, use_global_device_ids=true | all-gather | bytes 983040 | tf_op jit(solution)/shard_map/all_gather | solution.py:680
  458.8 16.0 %project_back.1 = (f32[768,1024]{1,0:T(8,128)}, f32[4,32,768]{2,1,0:T(8,128)}, f32[32,1024]{1,0:T(8,128)}) custom-call(bf16[768,1024]{1,0:T(8,128)(2,1)} %fusion.5.refs_0_, f32[768,1024]{1,0:T(8,128)} %pad_maximum_fusion.refs_1_, f32[2,512,1024]{2,1,0:T(8,128)} %get-tuple-element.60.refs_2_, bf16[2,512,1024]{2,1,0:T(8,128)(2,1)} %collective-permute-done.10.refs_3_, ...), custom_call_target="tpu_custom_call" | custom-call | tf_op jit(solution)/shard_map/project_back/pallas_call | solution.py:164
  474.8 0.9 convert_element_type.188
  475.8 3.0 multiply_reduce_fusion
  478.9 1.0 copy.122
  479.9 3.7 all-to-all-start
  483.6 3.4 fusion.10
  487.2 1.8 collective-permute-start.14
  489.0 5.2 all-to-all-done
  494.4 30.8 %all-gather.1 = bf16[64,2048]{1,0:T(8,128)(2,1)S(1)} all-gather(bf16[8,2048]{1,0:T(8,128)(2,1)S(1)} %convolution_convert_fusion.1), channel_id=3, replica_groups=mesh['dp'=8,'mp'=4] {'dp'}, dimensions={0}, use_global_device_ids=true | all-gather | bytes 294912 | tf_op jit(solution)/shard_map/all_gather | solution.py:673
  526.4 5.8 %all-gather.2 = bf16[32,16,256]{2,1,0:T(8,128)(2,1)S(1)} all-gather(bf16[8,16,256]{2,1,0:T(8,128)(2,1)S(1)} %slice.155), channel_id=4, replica_groups=mesh['dp'=8,'mp'=4] {'mp'}, dimensions={0}, use_global_device_ids=true | all-gather | bytes 327680 | tf_op jit(solution)/shard_map/all_gather | solution.py:680
  533.2 1.3 pad_maximum_fusion.4
  (190 shorter events, 28.4 us)
Async XLA Ops:
  7.2 17.7 %copy-start = (bf16[8,1024,16]{1,2,0:T(8,128)(2,1)S(1)}, bf16[8,1024,16]{1,2,0:T(8,128)(2,1)}, u32[]{:S(2)}) copy-start(bf16[8,1024,16]{1,2,0:T(8,128)(2,1)} %param.34) | copy-start | bytes 786436
  7.2 4.7 copy-start.19
  7.2 4.7 copy-start.28
  7.2 5.4 %copy-start.25 = (bf16[8,256,16]{1,2,0:T(8,128)(2,1)S(1)}, bf16[8,256,16]{1,2,0:T(8,128)(2,1)}, u32[]{:S(2)}) copy-start(bf16[8,256,16]{1,2,0:T(8,128)(2,1)} %param.32) | copy-start | bytes 196612
  7.2 6.0 %copy-start.14 = (bf16[8,16,2,656]{3,2,1,0:T(2,128)(2,1)S(1)}, bf16[8,16,2,656]{3,2,1,0:T(2,128)(2,1)}, u32[]{:S(2)}) copy-start(bf16[8,16,2,656]{3,2,1,0:T(2,128)(2,1)} %param.35) | copy-start | bytes 1007620
  7.2 77.8 %all-gather.9.cloned.1.call-start = ((), (), s32[]{:S(2)}) async-start(), calls=%async_computation.2 | async-start | bytes 6488064 | tf_op jit(solution)/shard_map/all_gather | solution.py:475
  9.2 138.0 %all-gather.11.cloned.1.call-start = ((), (), s32[]{:S(2)}) async-start(), calls=%async_computation.3 | async-start | bytes 2162688 | tf_op jit(solution)/shard_map/all_gather | solution.py:475
  9.9 247.6 %all-gather.13.cloned.1.call-start = ((), (), s32[]{:S(2)}) async-start(), calls=%async_computation.4 | async-start | bytes 16625664 | tf_op jit(solution)/shard_map/all_gather | solution.py:475
  11.9 3.5 copy-start.20
  14.0 7.7 %copy-start.13 = (bf16[3,256,1024]{2,1,0:T(8,128)(2,1)S(1)}, bf16[3,256,1024]{2,1,0:T(8,128)(2,1)}, u32[]{:S(2)}) copy-start(bf16[3,256,1024]{2,1,0:T(8,128)(2,1)} %param.21) | copy-start | bytes 4718596
  16.2 6.7 %copy-start.26 = (bf16[1024]{0:T(1024)(128)(2,1)S(1)}, bf16[1024]{0:T(1024)(128)(2,1)}, u32[]{:S(2)}) copy-start(bf16[1024]{0:T(1024)(128)(2,1)} %param.24) | copy-start | bytes 6148
  18.7 13.3 %collective-permute-start.2 = (bf16[3,16,3328]{2,1,0:T(8,128)(2,1)}, bf16[3,16,3328]{2,1,0:T(8,128)(2,1)}, u32[]{:S(2)}, u32[]{:S(2)}) collective-permute-start(bf16[3,16,3328]{2,1,0:T(8,128)(2,1)} %broadcast_select_fusion.1), channel_id=1, source_target_pairs={{0,2},{1,3},{2,0},{3,1},{4,6},{5,7},{6,4},{7,5},{8,10},{9,11},{10,... | collective-permute-start | bytes 958472 | tf_op jit(solution)/shard_map/ppermute | solution.py:469
  21.7 22.9 %collective-permute-start.1 = (bf16[3,16,3328]{2,1,0:T(8,128)(2,1)}, bf16[3,16,3328]{2,1,0:T(8,128)(2,1)}, u32[]{:S(2)}, u32[]{:S(2)}) collective-permute-start(bf16[3,16,3328]{2,1,0:T(8,128)(2,1)} %broadcast_select_fusion.1), channel_id=1, source_target_pairs={{0,1},{1,0},{2,3},{3,2},{4,5},{5,4},{6,7},{7,6},{8,9},{9,8},{10,11... | collective-permute-start | bytes 958472 | tf_op jit(solution)/shard_map/ppermute | solution.py:469
  21.7 3.7 copy-start.15
  22.6 19.5 %collective-permute-start = (bf16[256,1024]{1,0:T(8,128)(2,1)}, bf16[256,1024]{1,0:T(8,128)(2,1)S(1)}, u32[]{:S(2)}, u32[]{:S(2)}) collective-permute-start(bf16[256,1024]{1,0:T(8,128)(2,1)} %get-tuple-element.133), channel_id=1, source_target_pairs={{0,2},{1,3},{2,0},{3,1},{4,6},{5,7},{6,4},{7,5},{8,10},{9,11},{10,... | collective-permute-start | bytes 1572872 | tf_op jit(solution)/shard_map/ppermute | solution.py:469
  32.0 12.6 %collective-permute-start.3 = (bf16[3,16,3328]{2,1,0:T(8,128)(2,1)}, bf16[3,16,3328]{2,1,0:T(8,128)(2,1)S(1)}, u32[]{:S(2)}, u32[]{:S(2)}) collective-permute-start(bf16[3,16,3328]{2,1,0:T(8,128)(2,1)} %collective-permute-done.2), channel_id=1, source_target_pairs={{0,1},{1,0},{2,3},{3,2},{4,5},{5,4},{6,7},{7,6},{8,9},{9,8},{10,11... | collective-permute-start | bytes 958472 | tf_op jit(solution)/shard_map/ppermute | solution.py:469
  42.3 2.3 copy-start.2
  47.5 0.9 copy-start.9
  97.8 31.3 %copy-start.27 = (bf16[1024]{0:T(1024)(128)(2,1)S(1)}, bf16[1024]{0:T(1024)(128)(2,1)}, u32[]{:S(2)}) copy-start(bf16[1024]{0:T(1024)(128)(2,1)} %param.25) | copy-start | bytes 6148
  97.8 27.0 %collective-permute-start.5 = (bf16[2,256,1024]{2,1,0:T(8,128)(2,1)}, bf16[2,256,1024]{2,1,0:T(8,128)(2,1)S(1)}, u32[]{:S(2)}, u32[]{:S(2)}) collective-permute-start(bf16[2,256,1024]{2,1,0:T(8,128)(2,1)} %get-tuple-element.47.refs_0_.refs_3_), channel_id=1, source_target_pairs={{0,2},{1,3},{2,0},{3,1},{4,6},{5,7},{6,4},{7,5},{8,10},{9,11},{10,... | collective-permute-start | bytes 3145736 | tf_op jit(solution)/shard_map/ppermute | solution.py:469
  99.2 52.0 %collective-permute-start.4 = (bf16[2,512,1024]{2,1,0:T(8,128)(2,1)}, bf16[2,512,1024]{2,1,0:T(8,128)(2,1)S(1)}, u32[]{:S(2)}, u32[]{:S(2)}) collective-permute-start(bf16[2,512,1024]{2,1,0:T(8,128)(2,1)} %get-tuple-element.45.refs_0_.refs_3_), channel_id=1, source_target_pairs={{0,1},{1,0},{2,3},{3,2},{4,5},{5,4},{6,7},{7,6},{8,9},{9,8},{10,11... | collective-permute-start | bytes 6291464 | tf_op jit(solution)/shard_map/ppermute | solution.py:469
  99.2 72.6 %collective-permute-start.6 = (bf16[2,256,1024]{2,1,0:T(8,128)(2,1)}, bf16[2,256,1024]{2,1,0:T(8,128)(2,1)}, u32[]{:S(2)}, u32[]{:S(2)}) collective-permute-start(bf16[2,256,1024]{2,1,0:T(8,128)(2,1)} %get-tuple-element.47.refs_0_.refs_3_), channel_id=1, source_target_pairs={{0,1},{1,0},{2,3},{3,2},{4,5},{5,4},{6,7},{7,6},{8,9},{9,8},{10,11... | collective-permute-start | bytes 3145736 | tf_op jit(solution)/shard_map/ppermute | solution.py:469
  124.8 21.0 %copy-start.8 = (bf16[2,256,1024]{2,1,0:T(8,128)(2,1)}, bf16[2,256,1024]{2,1,0:T(8,128)(2,1)S(1)}, u32[]{:S(2)}) copy-start(bf16[2,256,1024]{2,1,0:T(8,128)(2,1)S(1)} %collective-permute-done.5.refs_1_.refs_4_) | copy-start | bytes 3145732
  124.8 47.1 %collective-permute-start.7 = (bf16[2,256,1024]{2,1,0:T(8,128)(2,1)S(1)}, bf16[2,256,1024]{2,1,0:T(8,128)(2,1)}, u32[]{:S(2)}, u32[]{:S(2)}) collective-permute-start(bf16[2,256,1024]{2,1,0:T(8,128)(2,1)S(1)} %collective-permute-done.5.refs_1_.refs_4_), channel_id=1, source_target_pairs={{0,1},{1,0},{2,3},{3,2},{4,5},{5,4},{6,7},{7,6},{8,9},{9,8},{10,11... | collective-permute-start | bytes 3145736 | tf_op jit(solution)/shard_map/ppermute | solution.py:469
  127.7 15.3 %collective-permute-start.8 = (bf16[256,1024]{1,0:T(8,128)(2,1)}, bf16[256,1024]{1,0:T(8,128)(2,1)}, u32[]{:S(2)}, u32[]{:S(2)}) collective-permute-start(bf16[256,1024]{1,0:T(8,128)(2,1)} %get-tuple-element.130), channel_id=1, source_target_pairs={{0,2},{1,3},{2,0},{3,1},{4,6},{5,7},{6,4},{7,5},{8,10},{9,11},{10,... | collective-permute-start | bytes 1572872 | tf_op jit(solution)/shard_map/ppermute | solution.py:469
  132.7 13.0 %copy-start.10 = (bf16[4,32,3328]{2,1,0:T(8,128)(2,1)S(1)}, bf16[4,32,3328]{2,1,0:T(8,128)(2,1)}, u32[]{:S(2)}) copy-start(bf16[4,32,3328]{2,1,0:T(8,128)(2,1)} %copy-done.9) | copy-start | bytes 2555908
  151.2 1.3 copy-start.6
  187.3 1.2 copy-start.5
  257.5 49.4 %copy-start.4 = (f32[768,1024]{1,0:T(8,128)S(1)}, f32[768,1024]{1,0:T(8,128)}, u32[]{:S(2)}) copy-start(f32[768,1024]{1,0:T(8,128)} %get-tuple-element.49.middle) | copy-start | bytes 9437188
  320.7 19.1 %copy-start.7 = (bf16[768,1024]{1,0:T(8,128)(2,1)S(1)}, bf16[768,1024]{1,0:T(8,128)(2,1)}, u32[]{:S(2)}) copy-start(bf16[768,1024]{1,0:T(8,128)(2,1)} %add_convert_fusion) | copy-start | bytes 4718596
  339.4 2.8 copy-start.18
  339.4 2.8 copy-start.24
  339.5 2.9 copy-start.23
  339.5 2.9 copy-start.22
  339.5 2.9 copy-start.21
  339.5 2.9 copy-start.16
  339.5 65.1 %collective-permute-start.12 = (bf16[2,256,1024]{2,1,0:T(8,128)(2,1)}, bf16[2,256,1024]{2,1,0:T(8,128)(2,1)}, u32[]{:S(2)}, u32[]{:S(2)}) collective-permute-start(bf16[2,256,1024]{2,1,0:T(8,128)(2,1)} %get-tuple-element.65), channel_id=1, source_target_pairs={{0,1},{1,0},{2,3},{3,2},{4,5},{5,4},{6,7},{7,6},{8,9},{9,8},{10,11... | collective-permute-start | bytes 3145736 | tf_op jit(solution)/shard_map/ppermute | solution.py:469
  340.7 61.2 %collective-permute-start.9 = (bf16[256,1024]{1,0:T(8,128)(2,1)}, bf16[256,1024]{1,0:T(8,128)(2,1)}, u32[]{:S(2)}, u32[]{:S(2)}) collective-permute-start(bf16[256,1024]{1,0:T(8,128)(2,1)} %get-tuple-element.127), channel_id=1, source_target_pairs={{0,2},{1,3},{2,0},{3,1},{4,6},{5,7},{6,4},{7,5},{8,10},{9,11},{10,... | collective-permute-start | bytes 1572872 | tf_op jit(solution)/shard_map/ppermute | solution.py:469
  343.0 5.2 copy-start.29
  345.1 66.3 %all-to-all-start.1 = ((bf16[32,2,5984]{2,1,0:T(2,128)(2,1)}), bf16[32,2,5984]{2,1,0:T(2,128)(2,1)S(1)}, u32[]{:S(2)}, u32[]{:S(2)}) async-start(bf16[32,2,5984]{2,1,0:T(2,128)(2,1)} %bitcast.64), calls=%async_computation.1 | async-start | bytes 1540096 | tf_op jit(solution)/shard_map/all_to_all | solution.py:667
  347.9 61.8 %collective-permute-start.11 = (bf16[2,256,1024]{2,1,0:T(8,128)(2,1)}, bf16[2,256,1024]{2,1,0:T(8,128)(2,1)S(1)}, u32[]{:S(2)}, u32[]{:S(2)}) collective-permute-start(bf16[2,256,1024]{2,1,0:T(8,128)(2,1)} %get-tuple-element.63), channel_id=1, source_target_pairs={{0,1},{1,0},{2,3},{3,2},{4,5},{5,4},{6,7},{7,6},{8,9},{9,8},{10,11... | collective-permute-start | bytes 3145736 | tf_op jit(solution)/shard_map/ppermute | solution.py:469
  397.8 60.9 %collective-permute-start.10 = (bf16[2,512,1024]{2,1,0:T(8,128)(2,1)}, bf16[2,512,1024]{2,1,0:T(8,128)(2,1)}, u32[]{:S(2)}, u32[]{:S(2)}) collective-permute-start(bf16[2,512,1024]{2,1,0:T(8,128)(2,1)} %get-tuple-element.61), channel_id=1, source_target_pairs={{0,1},{1,0},{2,3},{3,2},{4,5},{5,4},{6,7},{7,6},{8,9},{9,8},{10,11... | collective-permute-start | bytes 6291464 | tf_op jit(solution)/shard_map/ppermute | solution.py:469
  403.3 2.2 copy-start.12
  405.5 4.2 copy-start.11
  408.2 50.5 %collective-permute-start.13 = (bf16[2,256,1024]{2,1,0:T(8,128)(2,1)}, bf16[2,256,1024]{2,1,0:T(8,128)(2,1)}, u32[]{:S(2)}, u32[]{:S(2)}) collective-permute-start(bf16[2,256,1024]{2,1,0:T(8,128)(2,1)} %add_convert_fusion.1), channel_id=1, source_target_pairs={{0,2},{1,3},{2,0},{3,1},{4,6},{5,7},{6,4},{7,5},{8,10},{9,11},{10,... | collective-permute-start | bytes 3145736 | tf_op jit(solution)/shard_map/ppermute | solution.py:469
  458.8 17.0 %copy-start.3 = (bf16[768,1024]{1,0:T(8,128)(2,1)S(1)}, bf16[768,1024]{1,0:T(8,128)(2,1)}, u32[]{:S(2)}) copy-start(bf16[768,1024]{1,0:T(8,128)(2,1)} %copy-done.2) | copy-start | bytes 4718596
  475.8 3.0 copy-start.17
  479.9 14.3 %all-to-all-start = ((bf16[32,2,2048]{2,1,0:T(2,128)(2,1)}), bf16[32,2,2048]{2,1,0:T(2,128)(2,1)S(1)}, u32[]{:S(2)}, u32[]{:S(2)}) async-start(bf16[32,2,2048]{2,1,0:T(2,128)(2,1)} %bitcast.51), calls=%async_computation | async-start | bytes 524288 | tf_op jit(solution)/shard_map/all_to_all | solution.py:667
  487.2 45.9 %collective-permute-start.14 = (bf16[256,1024]{1,0:T(8,128)(2,1)S(1)}, bf16[256,1024]{1,0:T(8,128)(2,1)S(1)}, u32[]{:S(2)}, u32[]{:S(2)}) collective-permute-start(bf16[256,1024]{1,0:T(8,128)(2,1)S(1)} %get-tuple-element.124), channel_id=1, source_target_pairs={{0,2},{1,3},{2,0},{3,1},{4,6},{5,7},{6,4},{7,5},{8,10},{9,11},{10,... | collective-permute-start | bytes 1572872 | tf_op jit(solution)/shard_map/ppermute | solution.py:469
  533.0 1.5 copy-start.1
Sparse Core Ops, SparseCore 0:
  11.5 73.5 all-gather.8
  87.9 55.0 all-gather.10
  146.5 110.8 all-gather.12

commit v2 on v1

v2 whole, which is shorter than its diff:
```python
import jax
import jax.numpy as jnp
from jax import lax
from jax.experimental import pallas as pl
from jax.experimental.pallas import tpu as pltpu
from jax.sharding import PartitionSpec as P

HEAD_DIM = 64
ADAPTERS = 8
ADAPTER_SCALE = 2.0
NORM_EPS = 1e-05
ROPE_BASE = 160000.0
LANES = 128
BF = jnp.bfloat16
F32 = jnp.float32


def nt(a, b):
    return lax.dot_general(a, b, (((1,), (1,)), ((), ())), preferred_element_type=F32)


def nn(a, b):
    return lax.dot_general(a, b, (((1,), (0,)), ((), ())), preferred_element_type=F32)


def tn(a, b):
    return lax.dot_general(a, b, (((0,), (0,)), ((), ())), preferred_element_type=F32)


def lanes_of(ref, first=0, count=None, spot=None):
    count = ref.shape[2] if count is None else count
    places = [part if spot is None else spot[1 + part] for part in range(ref.shape[0])]
    return jnp.concatenate([ref[place, 0, pl.ds(first, count), :] for place in places], axis=1)


def full(shape):
    return pl.BlockSpec(shape, lambda *_: (0,) * len(shape))


def norm_parts(values):
    centred = values - jnp.mean(values, axis=-1, keepdims=True)
    spread = jnp.mean(centred * centred, axis=-1, keepdims=True)
    scale = lax.rsqrt(spread + NORM_EPS)
    return centred * scale, scale


def norm_back(grads, normed, scale, gain):
    weighted = grads * gain
    return scale * (
        weighted
        - jnp.mean(weighted, axis=-1, keepdims=True)
        - normed * jnp.mean(weighted * normed, axis=-1, keepdims=True)
    )


def turn(values, cosine, sine):
    width = values.shape[1]
    half = HEAD_DIM // 2
    many = width // LANES
    if many > 1:
        cosine = jnp.concatenate([cosine] * many, axis=1)
        sine = jnp.concatenate([sine] * many, axis=1)
    lane = lax.broadcasted_iota(jnp.int32, values.shape, 1)
    turned = jnp.where(
        lane % HEAD_DIM < half,
        -pltpu.roll(values, width - half, 1),
        pltpu.roll(values, half, 1),
    )
    return values * cosine + turned * sine


def project_kernel(
    place, own, beside, across, corner, weight, low, up, cosine, sine,
    query, key, value, down, *, wide
):
    table = lanes_of(weight, 0, 3 * wide, place)
    for step, piece in enumerate((own, beside, across, corner)):
        spot = place[0] ^ step
        rows = piece[0]
        small = (nt(rows, low[0]) * ADAPTER_SCALE).astype(BF)
        down[0, step] = small
        out = nt(rows, table) + nn(small, up[0])
        cos, sin = cosine[spot], sine[spot]
        turned = turn(out[:, :wide], cos, sin)
        query[0, spot] = (turned * HEAD_DIM**-0.5).astype(BF)
        key[0, spot] = turn(out[:, wide : 2 * wide], cos, sin).astype(BF)
        value[0, spot] = out[:, 2 * wide :].astype(BF)


def project(place, pieces, weight, low, up, tables):
    seqs, own, model = pieces[0].shape
    tall = up.shape[2]
    wide = tall // 3
    rank = low.shape[1]
    blocks = len(pieces)
    piece = pl.BlockSpec((1, own, model), lambda s, p: (s, 0, 0))
    result = pl.BlockSpec((1, blocks, own, wide), lambda s, p: (s, 0, 0, 0))
    table = pl.BlockSpec((blocks, own, LANES), lambda s, p: (0, 0, 0))
    return pl.pallas_call(
        lambda *refs: project_kernel(*refs, wide=wide),
        grid_spec=pltpu.PrefetchScalarGridSpec(
            num_scalar_prefetch=1,
            grid=(seqs,),
            in_specs=[piece] * blocks
            + [
                pl.BlockSpec(weight.shape, lambda s, p: (0, 0, 0, 0)),
                pl.BlockSpec((1, rank, model), lambda s, p: (s, 0, 0)),
                pl.BlockSpec((1, rank, tall), lambda s, p: (s, 0, 0)),
                table,
                table,
            ],
            out_specs=[result] * 3
            + [pl.BlockSpec((1, blocks, own, rank), lambda s, p: (s, 0, 0, 0))],
        ),
        out_shape=[jax.ShapeDtypeStruct((seqs, blocks, own, wide), BF)] * 3
        + [jax.ShapeDtypeStruct((seqs, blocks, own, rank), BF)],
        name="project",
    )(place, *pieces, weight, low, up, *tables)


def joined_grads_kernel(
    place, grad_query, grad_key, grad_value, own, beside, across, corner, up, down,
    small_grad, up_grad, low_grad
):
    up_total = jnp.zeros(up_grad.shape, F32)
    low_total = jnp.zeros(low_grad.shape, F32)
    for step, piece in enumerate((own, beside, across, corner)):
        spot = place[0] ^ step
        grads = jnp.concatenate([grad_query[spot], grad_key[spot], grad_value[spot]], axis=1)
        small = (nt(grads, up[0]) * ADAPTER_SCALE).astype(BF)
        small_grad[step] = small
        up_total += tn(down[0, step], grads)
        low_total += tn(small, piece[0])
    up_grad[...] = up_total
    low_grad[...] = low_total


def joined_grads(place, seq, grads, pieces, up, down):
    _, own, model = pieces[0].shape
    _, rank, tall = up.shape
    wide = tall // 3
    blocks = len(pieces)
    whole = lambda shape: pl.BlockSpec(shape, lambda i, p: (0,) * len(shape))
    of_seq = lambda shape: pl.BlockSpec((1,) + shape, lambda i, p: (seq,) + (0,) * len(shape))
    return pl.pallas_call(
        joined_grads_kernel,
        grid_spec=pltpu.PrefetchScalarGridSpec(
            num_scalar_prefetch=1,
            grid=(1,),
            in_specs=[whole((blocks, own, wide))] * 3
            + [of_seq((own, model))] * blocks
            + [of_seq((rank, tall)), of_seq((blocks, own, rank))],
            out_specs=[whole((blocks, own, rank)), whole((rank, tall)), whole((rank, model))],
        ),
        out_shape=[
            jax.ShapeDtypeStruct((blocks, own, rank), BF),
            jax.ShapeDtypeStruct((rank, tall), F32),
            jax.ShapeDtypeStruct((rank, model), F32),
        ],
        name="joined_grads",
    )(place, *grads, *pieces, up, down)


def project_back_kernel(place, grad_query, grad_key, grad_value, small_grad, weight, low, here, there):
    table = lanes_of(weight, 0, 3 * grad_query.shape[2], place)
    for step in range(grad_query.shape[0]):
        spot = place[0] ^ step
        grads = jnp.concatenate([grad_query[spot], grad_key[spot], grad_value[spot]], axis=1)
        out = nn(grads, table) + nn(small_grad[step], low[0])
        if step % 2:
            there[step // 2] = out.astype(BF)
        else:
            here[step // 2] = out


def project_back(place, seq, grads, small_grad, weight, low):
    blocks, own, wide = grads[0].shape
    _, rank, model = low.shape
    whole = lambda shape: pl.BlockSpec(shape, lambda i, p: (0,) * len(shape))
    return pl.pallas_call(
        project_back_kernel,
        grid_spec=pltpu.PrefetchScalarGridSpec(
            num_scalar_prefetch=1,
            grid=(1,),
            in_specs=[whole((blocks, own, wide))] * 3
            + [
                whole((blocks, own, rank)),
                whole(weight.shape),
                pl.BlockSpec((1, rank, model), lambda i, p: (seq, 0, 0)),
            ],
            out_specs=[whole((blocks // 2, own, model))] * 2,
        ),
        out_shape=[
            jax.ShapeDtypeStruct((blocks // 2, own, model), F32),
            jax.ShapeDtypeStruct((blocks // 2, own, model), BF),
        ],
        name="project_back",
    )(place, *grads, small_grad, weight, low)


def one_head(values, head):
    lane = lax.broadcasted_iota(jnp.int32, values.shape, 1)
    return jnp.where((lane // HEAD_DIM) == head, values, jnp.zeros_like(values))


def attend_kernel(place, query, key, value, *outs):
    *contexts, log_total = outs
    blocks, own = query.shape[1:3]
    keys = key[0].reshape(blocks * own, LANES)
    turned = value[0].reshape(blocks * own, LANES).T
    for step in range(0, blocks, 2):
        rows = jnp.concatenate([query[0, place[0] ^ (step + i)] for i in range(2)], axis=0)
        parts = []
        for head in range(2):
            scores = nt(keys, one_head(rows, head))
            top = jnp.max(scores, axis=0, keepdims=True)
            raised = jnp.exp(scores - top)
            total = jnp.sum(raised, axis=0, keepdims=True)
            part = nn(turned[head * HEAD_DIM : (head + 1) * HEAD_DIM], raised.astype(BF))
            parts.append(part * (1.0 / total))
            logs = top + jnp.log(total)
            for i in range(2):
                log_total[0, step + i, head : head + 1] = logs[:, i * own : (i + 1) * own]
        merged = jnp.concatenate(parts, axis=0).T.astype(BF)
        for i in range(2):
            contexts[step + i][...] = merged[i * own : (i + 1) * own]


def attend(place, query, key, value, seq):
    _, blocks, own, wide = query.shape
    pairs = wide // LANES
    whole = pl.BlockSpec((1, blocks, own, LANES), lambda h, p: (seq, 0, 0, h))
    *contexts, logs = pl.pallas_call(
        attend_kernel,
        grid_spec=pltpu.PrefetchScalarGridSpec(
            num_scalar_prefetch=1,
            grid=(pairs,),
            in_specs=[whole] * 3,
            out_specs=[pl.BlockSpec((own, LANES), lambda h, p: (0, h))] * blocks
            + [pl.BlockSpec((1, blocks, 2, own), lambda h, p: (h, 0, 0, 0))],
        ),
        out_shape=[jax.ShapeDtypeStruct((own, wide), BF)] * blocks
        + [jax.ShapeDtypeStruct((pairs, blocks, 2, own), F32)],
        name="attend",
    )(place, query, key, value)
    return contexts, logs


def attend_back_kernel(place, query, key, value, *refs):
    blocks, own = query.shape[1:3]
    pieces = refs[:blocks]
    log_total, cosine, sine, grad_query, grad_key, grad_value = refs[blocks:]
    keys = key[0].reshape(blocks * own, LANES)
    values = value[0].reshape(blocks * own, LANES)
    turned = keys.T
    grad_keys = jnp.zeros(keys.shape, F32)
    grad_values = jnp.zeros(keys.shape, F32)
    for step in range(0, blocks, 2):
        spots = [place[0] ^ (step + i) for i in range(2)]
        rows = jnp.concatenate([query[0, spot] for spot in spots], axis=0)
        outer = jnp.concatenate([pieces[step + i][...] for i in range(2)], axis=0)
        parts = []
        for head in range(2):
            mine = one_head(rows, head)
            mine_grad = one_head(outer, head)
            scores = nt(keys, mine)
            logs = jnp.concatenate([log_total[0, step + i, head : head + 1] for i in range(2)], axis=1)
            probs = jnp.exp(scores - logs)
            wide = nt(values, mine_grad)
            mean = jnp.sum(probs * wide, axis=0, keepdims=True)
            back = (probs * (wide - mean)).astype(BF)
            parts.append(nn(turned[head * HEAD_DIM : (head + 1) * HEAD_DIM], back))
            grad_keys += nn(back, mine)
            grad_values += nn(probs.astype(BF), mine_grad)
        queries = jnp.concatenate(parts, axis=0).T * HEAD_DIM**-0.5
        for i, spot in enumerate(spots):
            part = queries[i * own : (i + 1) * own]
            grad_query[spot] = turn(part, cosine[spot], -sine[spot]).astype(BF)
    for step in range(blocks):
        part = slice(step * own, (step + 1) * own)
        grad_key[step] = turn(grad_keys[part], cosine[step], -sine[step]).astype(BF)
        grad_value[step] = grad_values[part].astype(BF)


def attend_back(place, query, key, value, seq, pieces, log_total, tables):
    _, blocks, own, wide = query.shape
    pairs = wide // LANES
    whole = pl.BlockSpec((1, blocks, own, LANES), lambda h, p: (seq, 0, 0, h))
    column = pl.BlockSpec((blocks, own, LANES), lambda h, p: (0, 0, h))
    table = pl.BlockSpec((blocks, own, LANES), lambda h, p: (0, 0, 0))
    return pl.pallas_call(
        attend_back_kernel,
        grid_spec=pltpu.PrefetchScalarGridSpec(
            num_scalar_prefetch=1,
            grid=(pairs,),
            in_specs=[whole] * 3
            + [pl.BlockSpec((own, LANES), lambda h, p: (0, h))] * blocks
            + [pl.BlockSpec((1, blocks, 2, own), lambda h, p: (h, 0, 0, 0)), table, table],
            out_specs=[column] * 3,
        ),
        out_shape=[jax.ShapeDtypeStruct((blocks, own, wide), BF)] * 3,
        name="attend_back",
    )(place, query, key, value, *pieces, log_total, *tables)


def merge_kernel(spot, *refs, blocks, seqs):
    contexts = refs[: blocks * seqs]
    start, near, far, low, up, gain, middle, normed, down = refs[blocks * seqs :]
    tables = [lanes_of((far if i // 2 else near).at[:, pl.ds(i % 2, 1)], spot=spot) for i in range(blocks)]
    for seq in range(seqs):
        total = start[seq].astype(F32)
        small = jnp.zeros(down.shape[1:], F32)
        for step in range(blocks):
            rows = contexts[seq * blocks + step][...]
            small += nt(rows, low[step, seq])
            total += nn(rows, tables[step])
        small = (small * ADAPTER_SCALE).astype(BF)
        down[seq] = small
        total += nn(small, up[seq])
        middle[seq] = total
        normed[seq] = (norm_parts(total)[0] * gain[...]).astype(BF)


def merge(spot, contexts, start, near, far, low, up, gain):
    seqs, own, model = start.shape
    blocks, _, rank, wide = low.shape
    inputs = [piece for context in contexts for piece in context]
    inputs += [start, near, far, low, up, gain]
    results = [
        jax.ShapeDtypeStruct((seqs, own, model), F32),
        jax.ShapeDtypeStruct((seqs, own, model), BF),
        jax.ShapeDtypeStruct((seqs, own, rank), BF),
    ]
    return pl.pallas_call(
        lambda *refs: merge_kernel(*refs, blocks=blocks, seqs=seqs),
        grid_spec=pltpu.PrefetchScalarGridSpec(
            num_scalar_prefetch=1,
            grid=(1,),
            in_specs=[full(each.shape) for each in inputs],
            out_specs=[full(each.shape) for each in results],
        ),
        out_shape=results,
        name="merge",
    )(spot, *inputs)


def merge_back_kernel(spot, *refs, blocks):
    contexts = refs[:blocks]
    grad_normed, middle, out_grad, down, near, far, low, up, gain = refs[blocks : blocks + 9]
    grad_contexts = refs[blocks + 9 : 2 * blocks + 9]
    grad_middle, low_grad, up_grad = refs[2 * blocks + 9 :]
    normed, scale = norm_parts(middle[0])
    total = out_grad[0].astype(F32) + norm_back(grad_normed[0], normed, scale, gain[...])
    grad_middle[0] = total
    rows = total.astype(BF)
    small = (nt(rows, up[0]) * ADAPTER_SCALE).astype(BF)
    for step, out in enumerate(grad_contexts):
        ref = far if step // 2 else near
        table = lanes_of(ref.at[:, pl.ds(step % 2, 1)], spot=spot)
        out[...] = (nt(rows, table) + nn(small, low[step, 0])).astype(BF)
        low_grad[step] = tn(small, contexts[step][...])
    up_grad[...] = tn(down[0], rows)


def merge_back(spot, seq, contexts, grad_normed, middle, out_grad, down, near, far, low, up, gain):
    _, own, model = middle.shape
    blocks, _, rank, wide = low.shape
    row = pl.BlockSpec((1, own, model), lambda i, p: (seq, 0, 0))
    one = full((1, own, model))
    *grads, grad_middle, low_grad, up_grad = pl.pallas_call(
        lambda *refs: merge_back_kernel(*refs, blocks=blocks),
        grid_spec=pltpu.PrefetchScalarGridSpec(
        num_scalar_prefetch=1,
        grid=(1,),
        in_specs=[full((own, wide))] * blocks
        + [
            row,
            row,
            row,
            pl.BlockSpec((1, own, rank), lambda i, p: (seq, 0, 0)),
            full(near.shape),
            full(far.shape),
            pl.BlockSpec((blocks, 1, rank, wide), lambda i, p: (0, seq, 0, 0)),
            pl.BlockSpec((1, rank, model), lambda i, p: (seq, 0, 0)),
            full((1, model)),
        ],
        out_specs=[full((own, wide))] * blocks
        + [one, full((blocks, rank, wide)), full((rank, model))],
        ),
        out_shape=[jax.ShapeDtypeStruct((own, wide), BF)] * blocks
        + [
            jax.ShapeDtypeStruct((1, own, model), F32),
            jax.ShapeDtypeStruct((blocks, rank, wide), F32),
            jax.ShapeDtypeStruct((rank, model), F32),
        ],
        name="merge_back",
    )(spot, *contexts, grad_normed, middle, out_grad, down, near, far, low, up, gain)
    return grads, grad_middle, low_grad, up_grad


def gated_kernel(
    place, rows, out_grad, expand, shrink, expand_up, shrink_low, expand_low, shrink_up, mask,
    total, grad_rows, expand_up_grad, shrink_low_grad, expand_low_grad, shrink_up_grad,
    down, down_grad, late, late_grad, *, width, blocks
):
    step = pl.program_id(0)
    scaled = ADAPTER_SCALE * mask[...]

    @pl.when(step == 0)
    def _():
        total[...] = jnp.zeros(total.shape, F32)
        grad_rows[...] = jnp.zeros(grad_rows.shape, F32)
        down[...] = (nt(rows[...], expand_low[...]) * scaled).astype(BF)
        down_grad[...] = (nt(out_grad[...], shrink_up[...]) * scaled).astype(BF)
        late[...] = jnp.zeros(late.shape, F32)
        late_grad[...] = jnp.zeros(late_grad.shape, F32)

    values = lanes_of(expand, 0, width)
    gates = lanes_of(expand, width, width)
    outs = lanes_of(shrink)
    up_values = expand_up[0, :, :width]
    up_gates = expand_up[0, :, expand_up.shape[2] // 2 : expand_up.shape[2] // 2 + width]
    low_outs = shrink_low[0, :, :width]
    first = nt(rows[...], values) + nn(down[...], up_values)
    second = nt(rows[...], gates) + nn(down[...], up_gates)
    chance = 0.5 + 0.5 * lax.erf(first * (0.5**0.5))
    curve = first * chance
    slope = chance + first * (jnp.exp(-0.5 * first * first) * 0.3989422804014327)
    active = (curve * second).astype(BF)
    grads = nt(out_grad[...], outs) + nn(down_grad[...], low_outs)
    first_grad = (grads * second * slope).astype(BF)
    second_grad = (grads * curve).astype(BF)
    total[...] += nn(active, outs)
    late[...] += nt(active, low_outs)
    grad_rows[...] += nn(first_grad, values) + nn(second_grad, gates)
    late_grad[...] += nt(first_grad, up_values) + nt(second_grad, up_gates)
    expand_up_grad[0, 0] = tn(down[...], first_grad)
    expand_up_grad[0, 1] = tn(down[...], second_grad)
    shrink_low_grad[0] = tn(down_grad[...], active)

    @pl.when(step == blocks - 1)
    def _():
        small = (late[...] * scaled).astype(BF)
        total[...] += nn(small, shrink_up[...])
        shrink_up_grad[...] = tn(small, out_grad[...])
        small_grad = (late_grad[...] * scaled).astype(BF)
        grad_rows[...] += nn(small_grad, expand_low[...])
        expand_low_grad[...] = tn(small_grad, rows[...])


def gated(place, rows, out_grad, weights, width, expand_up, shrink_low, expand_low, shrink_up, mask):
    count, model = rows.shape
    parts, blocks, _, lane = weights.shape
    rank = expand_low.shape[0]
    pad = shrink_low.shape[2]
    return pl.pallas_call(
        lambda *refs: gated_kernel(*refs, width=width, blocks=blocks),
        grid_spec=pltpu.PrefetchScalarGridSpec(
        num_scalar_prefetch=1,
        grid=(blocks,),
        in_specs=[
            full((count, model)),
            full((count, model)),
            pl.BlockSpec((parts, 1, 2 * width, lane), lambda m, p: (0, m, 0, 0)),
            pl.BlockSpec((parts, 1, width, lane), lambda m, p: (0, m, 2, 0)),
            pl.BlockSpec((1, rank, 2 * pad), lambda m, p: (p[0] ^ m, 0, 0)),
            pl.BlockSpec((1, rank, pad), lambda m, p: (p[0] ^ m, 0, 0)),
            full((rank, model)),
            full((rank, model)),
            full((count, rank)),
        ],
        out_specs=[
            full((count, model)),
            full((count, model)),
            pl.BlockSpec((1, 2, rank, width), lambda m, p: (m, 0, 0, 0)),
            pl.BlockSpec((1, rank, width), lambda m, p: (m, 0, 0)),
            full((rank, model)),
            full((rank, model)),
        ],
        scratch_shapes=[
            pltpu.VMEM((count, rank), BF),
            pltpu.VMEM((count, rank), BF),
            pltpu.VMEM((count, rank), F32),
            pltpu.VMEM((count, rank), F32),
        ],
        ),
        out_shape=[
            jax.ShapeDtypeStruct((count, model), F32),
            jax.ShapeDtypeStruct((count, model), F32),
            jax.ShapeDtypeStruct((blocks, 2, rank, width), F32),
            jax.ShapeDtypeStruct((blocks, rank, width), F32),
            jax.ShapeDtypeStruct((rank, model), F32),
            jax.ShapeDtypeStruct((rank, model), F32),
        ],
        name="gated",
    )(place, rows, out_grad, weights, weights, expand_up, shrink_low, expand_low, shrink_up, mask)


def settle_early_kernel(place, got, low, shrink_up, merge_up, merge_low, expand_up, shrink_low, *, parts, blocks, sets, part, wide, width, pad):
    at = 3 * part
    for g in range(parts):
        for block in range(blocks):
            rows = got[g * blocks + block, :, :at].astype(F32)
            for i, out in enumerate((low, shrink_up, merge_up)):
                for two in range(2):
                    cut = rows[two * sets : (two + 1) * sets, i * part : (i + 1) * part]
                    out[:, two * parts + g, block * part : (block + 1) * part] = cut
        rows = got[g * blocks + place[0], :, at:].astype(F32)
        for two in range(2):
            cut = rows[two * sets : (two + 1) * sets]
            rank = two * parts + g
            merge_low[:, rank, :] = cut[:, :wide]
            for kind in range(2):
                first = wide + kind * pad
                expand_up[:, rank, kind, :] = cut[:, first : first + width]
            shrink_low[:, rank, :] = cut[:, wide + 2 * pad : wide + 2 * pad + width]


def settle_early(place, got, parts, sets, wide, width, pad):
    owners, rows, features = got.shape
    blocks = owners // parts
    rank = rows // sets * parts
    part = (features - wide - 3 * pad) // 3
    model = blocks * part
    shapes = [(rank, model)] * 3 + [(rank, wide), (rank, 2, width), (rank, width)]
    shapes = [(sets,) + shape for shape in shapes]
    whole = lambda shape: pl.BlockSpec(shape, lambda i, p: (0,) * len(shape))
    return pl.pallas_call(
        lambda *refs: settle_early_kernel(
            *refs, parts=parts, blocks=blocks, sets=sets, part=part, wide=wide, width=width, pad=pad
        ),
        grid_spec=pltpu.PrefetchScalarGridSpec(
            num_scalar_prefetch=1,
            grid=(1,),
            in_specs=[whole(got.shape)],
            out_specs=[whole(shape) for shape in shapes],
        ),
        out_shape=[jax.ShapeDtypeStruct(shape, F32) for shape in shapes],
        name="settle_early",
    )(place, got)


def settle_late_kernel(got, low, up, *, parts, blocks, sets, part, piece):
    wide = up.shape[3]
    for g in range(parts):
        rows = [got[g * blocks + block].astype(F32) for block in range(blocks)]
        tail = jnp.concatenate([row[:, part : part + piece] for row in rows], axis=1)
        for two in range(2):
            rank = two * parts + g
            for block, row in enumerate(rows):
                low[:, rank, block * part : (block + 1) * part] = row[two * sets : (two + 1) * sets, :part]
            for kind in range(up.shape[1]):
                up[:, kind, rank, :] = tail[two * sets : (two + 1) * sets, kind * wide : (kind + 1) * wide]


def settle_late(got, parts, sets, part, wide):
    owners, rows, features = got.shape
    blocks = owners // parts
    rank = rows // sets * parts
    piece = features - part
    shapes = [(sets, rank, blocks * part), (sets, blocks * piece // wide, rank, wide)]
    return pl.pallas_call(
        lambda *refs: settle_late_kernel(*refs, parts=parts, blocks=blocks, sets=sets, part=part, piece=piece),
        grid=(1,),
        in_specs=[full(got.shape)],
        out_specs=[full(shape) for shape in shapes],
        out_shape=[jax.ShapeDtypeStruct(shape, F32) for shape in shapes],
        name="settle_late",
    )(got)


def pair_swap(values, bit):
    size = lax.axis_size("mp")
    return lax.ppermute(values, "mp", [(i, i ^ bit) for i in range(size)])


def tie(values, after):
    return lax.optimization_barrier((values, after))[0]


def swap_all(values, axes):
    return lax.all_to_all(values, axes, 0, 0, tiled=True)


def share_all(values, axes):
    size = 1
    for axis in (axes,) if isinstance(axes, str) else axes:
        size *= lax.axis_size(axis)
    return swap_all(jnp.broadcast_to(values[None], (size,) + values.shape), axes)


def gather_parts(values):
    parts = lax.axis_size("dp")
    here = lax.axis_index("dp")
    every = jnp.arange(parts, dtype=jnp.int32)
    if parts != 8:
        return share_all(values, "dp"), every
    stack = [values]
    for shift in range(2, parts, 2):
        stack.append(lax.ppermute(values, "dp", [(i, (i + shift) % parts) for i in range(parts)]))
    stack = jnp.stack(stack)
    other = lax.ppermute(stack, "dp", [(i, i ^ 1) for i in range(parts)])
    order = (every % 2 ^ here % 2) * (parts // 2) + (here // 2 - every // 2) % (parts // 2)
    return jnp.concatenate([stack, other]), order.astype(jnp.int32)


def full_lanes(whole):
    parts, blocks, count, own = whole.shape
    if own == LANES:
        return whole
    tiles = parts * own // LANES
    whole = whole.transpose(1, 2, 0, 3).reshape(blocks, count, tiles, LANES)
    return whole.transpose(2, 0, 1, 3)


def local(
    hidden,
    cotangent,
    adapter_ids,
    attn_gain,
    mlp_gain,
    joined_weight,
    merge_weight_matrix,
    expand_weight,
    shrink_weight_matrix,
    joined_lower,
    joined_up_matrices,
    merge_lower,
    merge_up_matrices,
    expand_lower,
    expand_up_matrices,
    shrink_lower,
    shrink_up_matrices,
):
    parts, blocks = lax.axis_size("dp"), lax.axis_size("mp")
    place = lax.axis_index("mp")
    pair, core = place // 2, place % 2
    spot = place[None].astype(jnp.int32)
    seqs, own, model = hidden.shape
    length = own * blocks
    row_in = joined_weight.shape[0]
    wide = joined_weight.shape[2]
    width = expand_weight.shape[2]
    rank = joined_lower.shape[2]
    count = seqs * own

    rest = jnp.concatenate(
        [expand_weight.reshape(row_in, 2 * width).T, shrink_weight_matrix.T], axis=0
    )
    rest_whole = full_lanes(
        lax.all_gather(rest, ("dp", "mp"), axis=0, tiled=True).reshape(parts, blocks, 3 * width, row_in)
    )

    note = jnp.zeros((8, row_in), BF).at[0, :seqs].set(adapter_ids.astype(BF))
    joined_mine = jnp.concatenate(
        [joined_weight.reshape(row_in, 3 * wide).T, merge_weight_matrix.T, note], axis=0
    )
    joined_got, order = gather_parts(joined_mine)
    every_id = joined_got[:, 4 * wide, :seqs][order].astype(jnp.int32)
    if row_in != LANES:
        order = jnp.arange(model // LANES, dtype=jnp.int32)
    spot = jnp.concatenate([spot, order])
    joined_whole = full_lanes(joined_got[:, None])

    attn_scale = attn_gain.astype(F32)[None, :]
    mlp_scale = mlp_gain.astype(F32)[None, :]
    first_normed, first_scale = norm_parts(hidden.astype(F32))
    normed = (first_normed * attn_scale).astype(BF)
    def pick(table):
        return table.at[adapter_ids].get(mode="promise_in_bounds")

    def pick_low(table):
        return pick(table).transpose(0, 2, 1)

    def pick_up(table):
        return pick(table).reshape(seqs, rank, -1)

    joined_low, joined_up = pick_low(joined_lower), pick_up(joined_up_matrices)
    expand_low = pick_low(expand_lower).reshape(seqs * rank, model)
    merge_up = pick_up(merge_up_matrices)
    shrink_up = pick_up(shrink_up_matrices).reshape(seqs * rank, model)
    pad = -(-width // LANES) * LANES
    side = [(0, 0), (0, 0), (0, pad - width)]
    expand_mine = pick(expand_up_matrices)
    mine = jnp.concatenate(
        [
            pick_low(merge_lower),
            jnp.pad(expand_mine[:, :, 0], side),
            jnp.pad(expand_mine[:, :, 1], side),
            jnp.pad(pick_low(shrink_lower), side),
        ],
        axis=2,
    )
    far_sets = pair_swap(mine, 2)
    split_sets = jnp.stack([mine, pair_swap(mine, 1), far_sets, pair_swap(far_sets, 1)])
    merge_low = split_sets[:, :, :, :wide]
    expand_up = split_sets[:, :, :, wide : wide + 2 * pad].reshape(blocks, seqs * rank, 2 * pad)
    shrink_low = split_sets[:, :, :, wide + 2 * pad :].reshape(blocks, seqs * rank, pad)
    mask = (
        (jnp.arange(count) // own)[:, None] == (jnp.arange(seqs * rank) // rank)[None, :]
    ).astype(F32)

    half = HEAD_DIM // 2
    inverse = ROPE_BASE ** (-((jnp.arange(LANES) % half).astype(F32) * 2.0 / HEAD_DIM))
    angles = jnp.arange(length, dtype=F32)[:, None] * inverse[None, :]
    tables = [table.reshape(blocks, own, LANES) for table in (jnp.cos(angles), jnp.sin(angles))]

    across = pair_swap(normed, 2)
    beside = pair_swap(normed, 1)
    (
        across, joined_low, joined_up, tables, merge_low, merge_up,
        expand_low, expand_up, shrink_low, shrink_up, mask,
    ) = lax.optimization_barrier(
        (
            across, joined_low, joined_up, tables, merge_low, merge_up,
            expand_low, expand_up, shrink_low, shrink_up, mask,
        )
    )
    corner = pair_swap(across, 1)
    pieces = (normed, beside, across, corner)
    query, key, value, joined_down = project(
        spot, pieces, joined_whole, joined_low, joined_up,
        tables,
    )
    merge_own = joined_whole[:, :, 3 * wide : 4 * wide]
    merge_near = jnp.concatenate([merge_own, pair_swap(merge_own, 1)], axis=1)
    contexts, logs = [], []
    for seq in range(seqs):
        if seq:
            query = tie(query, context[0])
        context, log_total = attend(spot, query, key, value, seq)
        context = [context[0]] + [pair_swap(context[bit], bit) for bit in range(1, blocks)]
        contexts.append(context)
        logs.append(log_total)
    merge_far = pair_swap(merge_near, 2)
    middle, normed_mlp, merge_down = merge(
        spot, contexts, hidden, merge_near, merge_far, merge_low, merge_up, mlp_scale
    )
    (
        shrunk,
        grad_normed_mlp,
        expand_up_grad,
        shrink_low_grad,
        expand_low_grad,
        shrink_up_grad,
    ) = gated(
        spot, normed_mlp.reshape(count, model), cotangent.reshape(count, model), rest_whole, width,
        expand_up, shrink_low, expand_low, shrink_up, mask,
    )
    result = (middle + shrunk.reshape(middle.shape)).astype(BF)
    grad_normed_mlp = grad_normed_mlp.reshape(seqs, own, model)

    paired = rank == 2 * parts
    everyone = ("dp", "mp")
    owners = parts * blocks
    ids = jnp.broadcast_to(every_id[:, None], (parts, blocks, seqs))
    choose = (jnp.arange(ADAPTERS)[:, None] == ids.reshape(1, -1)).astype(BF)
    choose_own = (jnp.arange(ADAPTERS)[:, None] == every_id.reshape(1, -1)).astype(BF)
    part_width = model // blocks

    def by_block(grad):
        return grad.reshape(seqs * rank, blocks, -1).transpose(1, 0, 2)

    def ranks_out(grad):
        if paired:
            split = grad.reshape(grad.shape[0], seqs, 2, parts, -1).transpose(3, 0, 1, 2, 4)
            return split.reshape(split.shape[:3] + (-1,))
        return grad.reshape(grad.shape[0], seqs, parts, -1).transpose(2, 0, 1, 3)

    def ranks_in(whole, features):
        whole = whole.transpose(2, 1, 0, 3).reshape(ADAPTERS, whole.shape[1], rank, features)
        return whole.transpose(0, 2, 1, 3)

    def tall(values):
        return values.transpose(0, 2, 1).astype(F32)

    merge_low_grads, merge_up_grads, joined_low_grads, joined_up_grads = [], [], [], []
    halfway, grad_normeds = [], []
    for seq in range(seqs):
        if seq:
            grad_normed_mlp = tie(grad_normed_mlp, grad_middle)
        if seq == 2:
            grad_normed_mlp = tie(grad_normed_mlp, halfway[0][1][2:])
        pieces_back, grad_middle, low_grad, up_grad = merge_back(
            spot, seq, contexts[seq], grad_normed_mlp, middle, cotangent, merge_down,
            merge_near, merge_far, merge_low, merge_up, mlp_scale,
        )
        merge_low_grads.append(low_grad)
        merge_up_grads.append(up_grad)
        pieces_back = [pieces_back[0]] + [pair_swap(pieces_back[bit], bit) for bit in range(1, blocks)]
        halfway.append((grad_middle[0], pieces_back))

    early = jnp.concatenate(
        [
            piece.astype(BF)
            for piece in (
                by_block(expand_low_grad),
                by_block(shrink_up_grad),
                by_block(jnp.concatenate(merge_up_grads)),
                jnp.take(jnp.concatenate(merge_low_grads, axis=1), place ^ jnp.arange(blocks), axis=0),
                jnp.pad(expand_up_grad[:, 0], side),
                jnp.pad(expand_up_grad[:, 1], side),
                jnp.pad(shrink_low_grad, side),
            )
        ],
        axis=2,
    )
    early_width = early.shape[2]

    early = tie(early, halfway[0][1][2])
    early = swap_all(ranks_out(early).reshape(owners, seqs, -1), everyone)
    chip, far = None, None
    for seq in range(seqs):
        grad_middle, pieces_back = halfway[seq]
        if seq:
            pieces_back[0] = tie(pieces_back[0], here)
        grads = list(attend_back(spot, query, key, value, seq, pieces_back, logs[seq], tables))
        if seq == 0:
            grads[0], halfway[1], halfway[2] = lax.optimization_barrier((grads[0], halfway[1], halfway[2]))
        if seq == 1:
            grads[0], far, early = lax.optimization_barrier((grads[0], far, early))
            early = jnp.dot(choose, early.reshape(owners * seqs, -1), preferred_element_type=F32)
            if paired:
                early = jnp.concatenate([early[:, :early_width], early[:, early_width:]], axis=0)
            shared = lax.all_gather(early.astype(BF), everyone, axis=0)
        if seq == 2:
            grads[0], far = lax.optimization_barrier((grads[0], far))
        if seq:
            grad_normeds.append(chip + far.astype(F32))
        small_grad, up_grad, low_grad = joined_grads(spot, seq, grads, pieces, joined_up, joined_down)
        here, there = project_back(spot, seq, grads, small_grad, joined_whole, joined_low)
        joined_up_grads.append(up_grad)
        joined_low_grads.append(low_grad)
        there = pair_swap(there, 1).astype(F32)
        chip, give = here[0] + there[0], (here[1] + there[1]).astype(BF)
        far = pair_swap(give, 2)

    piece = 3 * wide // blocks
    late_low = ranks_out(by_block(jnp.concatenate(joined_low_grads)).astype(BF))
    late_up = jnp.stack(joined_up_grads).astype(BF).reshape(seqs * rank, blocks, piece)
    late_up = ranks_out(late_up.transpose(1, 0, 2))
    some = 2 if paired else 1
    late_low, late_up = (each.reshape(owners, seqs * some, -1) for each in (late_low, late_up))
    low_size = late_low.shape[2]
    late = jnp.concatenate([late_low, late_up], axis=2)
    late = tie(late, give)
    late, far = lax.optimization_barrier((swap_all(late, everyone), far))
    late = late.reshape(parts, blocks, seqs, some, -1)
    grad_normeds.append(chip + far.astype(F32))
    grad_middle = jnp.stack([each[0] for each in halfway])
    grad_hidden = grad_middle + norm_back(jnp.stack(grad_normeds), first_normed, first_scale, attn_scale)
    late_low = late[..., :low_size].reshape(owners * seqs, -1)
    late_up = late[..., low_size:].transpose(1, 0, 2, 3, 4).reshape(blocks, parts * seqs, -1)
    late_low = jnp.dot(choose, late_low, preferred_element_type=F32).astype(BF)
    late_up = jnp.einsum("as,bsf->baf", choose_own, late_up, preferred_element_type=F32).astype(BF)
    if paired:
        half_low, half_up = late_low.shape[1] // 2, late_up.shape[2] // 2
        late_low = jnp.concatenate([late_low[:, :half_low], late_low[:, half_low:]], axis=0)
        late_up = jnp.concatenate([late_up[:, :, :half_up], late_up[:, :, half_up:]], axis=1)
    late = jnp.concatenate(
        [jnp.broadcast_to(late_low[None], (blocks,) + late_low.shape), late_up], axis=2
    )
    late = jnp.broadcast_to(late[None], (parts,) + late.shape).reshape((owners,) + late.shape[1:])
    late = swap_all(late, everyone)
    if paired:
        (
            expand_low_out, shrink_up_out, merge_up_out, merge_low_out, expand_up_out, shrink_low_out,
        ) = settle_early(spot, shared, parts, ADAPTERS, wide, width, pad)
        late, shrink_up_out = lax.optimization_barrier((late, shrink_up_out))
        joined_low_out, joined_up_out = settle_late(late, parts, ADAPTERS, part_width, wide)
        joined_up_out = joined_up_out.transpose(0, 2, 1, 3)
        joined_low_out, expand_low_out, merge_low_out, shrink_low_out = (
            tall(each) for each in (joined_low_out, expand_low_out, merge_low_out, shrink_low_out)
        )
    else:
        late = late.reshape(parts, blocks, ADAPTERS, -1)
        joined_low_out = tall(ranks_in(late[..., :low_size], part_width).reshape(ADAPTERS, rank, model))
        joined_up_out = ranks_in(late[..., low_size:], piece).reshape(ADAPTERS, rank, 3, wide).astype(F32)
        shared = ranks_in(shared.reshape(parts, blocks, ADAPTERS, -1), early_width).astype(F32)
        expand_low_out, shrink_up_out, merge_up_out = (
            shared[..., i * part_width : (i + 1) * part_width].reshape(ADAPTERS, rank, model)
            for i in range(3)
        )
        expand_low_out = tall(expand_low_out)
        divided = lax.dynamic_index_in_dim(shared[..., 3 * part_width :], place, 2, keepdims=False)
        merge_low_out = tall(divided[:, :, :wide])
        expand_up_out = jnp.stack(
            [divided[:, :, wide + i * pad : wide + i * pad + width] for i in range(2)], axis=2
        )
        shrink_low_out = tall(divided[:, :, wide + 2 * pad : wide + 2 * pad + width])
    return (
        result,
        grad_hidden.astype(BF),
        joined_low_out,
        joined_up_out,
        merge_low_out,
        merge_up_out,
        expand_low_out,
        expand_up_out,
        shrink_low_out,
        shrink_up_out,
    )


def solution(mesh):
    in_specs = (
        P("dp", "mp", None),
        P("dp", "mp", None),
        P("dp"),
        P(),
        P(),
        P("dp", None, "mp"),
        P("dp", "mp"),
        P("dp", None, "mp"),
        P("dp", "mp"),
        P(),
        P(None, None, None, "mp"),
        P(None, "mp", None),
        P(),
        P(),
        P(None, None, None, "mp"),
        P(None, "mp", None),
        P(),
    )
    out_specs = (
        P("dp", "mp", None),
        P("dp", "mp", None),
        P(),
        P(None, None, None, "mp"),
        P(None, "mp", None),
        P(),
        P(),
        P(None, None, None, "mp"),
        P(None, "mp", None),
        P(),
    )
    return jax.shard_map(local, mesh=mesh, in_specs=in_specs, out_specs=out_specs, check_vma=False)
```

time: 547 us -> 443 us (0.81)
  blocking collectives: 95.2 us -> 0 us
  waiting for transfers between devices: 148 us -> 99.1 us
  Pallas kernels: 176 us -> 212 us
  starting transfers between devices: 18.8 us -> 40.2 us
  local copies, waits for them, and re-layouts: 47.8 us -> 34.5 us
    all_gather x3 -> x2, waiting for transfers between devices: 97.7 us -> 0.01 us  [the longest x1 0.01 us: local(): lax.all_gather(rest, ('dp', 'mp'), axis=0, tiled=True)]
    all_gather x4 -> x0, blocking collectives: 76.6 us -> none  [the longest x2 63.2 us: share(): whole = lax.all_gather(summed, 'dp', axis=0)]
    pallas_call x8 -> x19, Pallas kernels: 126 us -> 162 us  [the longest x3 50 us: attend_back(): pl.pallas_call(attend_back_kernel, grid_spec=pltpu.PrefetchScalarGridSpec...]
    ppermute x15 -> x32, waiting for transfers between devices: 44.1 us -> 72.3 us  [pair_swap(): return lax.ppermute(values, 'mp', [(i, i ^ bit) for i in range(size)])]
    unnamed x1 -> x0, blocking collectives: 18.6 us -> none
    all_to_all x2 -> x3, waiting for transfers between devices: 5.18 us -> 16.4 us  [swap_all(): return lax.all_to_all(values, axes, 0, 0, tiled=True)]
    ppermute x0 -> x4, waiting for transfers between devices: none -> 10.4 us  [the longest x3 10.4 us: gather_parts(): lax.ppermute(values, 'dp', [(i, (i + shift) % parts) for i in range(parts)])]
    another operation x5 -> x19, other arithmetic: 2.08 us -> 10.8 us  [the longest x3 5.33 us: local(): jnp.stack(grad_normeds)]
  transfers between devices with their start and end apart: 20 -> 41, of which waited for: 6 -> 18; matrix products, arithmetic and copies ran while one was open for 13% -> 12% of each run, Pallas kernels for 15% -> 30%
where the time goes in v2:
time: 443 us; the launch traced here: 439 us
  Pallas kernels  212 us (48%)
  waiting for transfers between devices  99.1 us (22%)
  starting transfers between devices  40.2 us (9%)
  other arithmetic  36.5 us (8%)
  local copies, waits for them, and re-layouts  34.5 us (8%)
  between operations  15.6 us (4%)
    ppermute x32, waiting for transfers between devices, pair_swap(): return lax.ppermute(values, 'mp', [(i, i ^ bit) for i in range(size)])  72.3 us
    pallas_call x1, Pallas kernels, gated(): pl.pallas_call(lambda *refs: gated_kernel(*refs, width=width, blocks=bloc...  50.7 us
    pallas_call x3, Pallas kernels, attend_back(): pl.pallas_call(attend_back_kernel, grid_spec=pltpu.PrefetchScalarGridSpec...  50 us
    pallas_call x3, Pallas kernels, attend(): pl.pallas_call(attend_kernel, grid_spec=pltpu.PrefetchScalarGridSpec(num_...  29.8 us
    ppermute x32, starting transfers between devices, pair_swap(): return lax.ppermute(values, 'mp', [(i, i ^ bit) for i in range(size)])  20.3 us
    pallas_call x3, Pallas kernels, project_back(): pl.pallas_call(project_back_kernel, grid_spec=pltpu.PrefetchScalarGridSpe...  19.7 us
    pallas_call x3, Pallas kernels, merge_back(): pl.pallas_call(lambda *refs: merge_back_kernel(*refs, blocks=blocks), gri...  18 us
    all_to_all x3, waiting for transfers between devices, swap_all(): return lax.all_to_all(values, axes, 0, 0, tiled=True)  16.4 us
  transfers between devices with their start and end apart: 41, of which 18 were waited for; matrix products, arithmetic and copies ran while one was open for 12% of the time, Pallas kernels for 30%

profile of v2, /device:TPU:0, one launch (start us, length us, event | category | flops | bytes accessed | tf_op | source)
XLA Modules:
  0.0 438.7 jit_solution(17135117486710553543)
XLA Ops:
  7.3 1.9 pad_maximum_fusion.3
  13.6 2.9 collective-permute-start.3
  17.7 1.6 collective-permute-start.6
  19.3 2.6 collective-permute-start.7
  21.8 1.3 collective-permute-start.8
  25.8 1.7 fusion.5.refs_1_.own
  27.5 1.5 gather_fusion.1
  32.0 2.3 gather_fusion.7
  34.3 2.1 gather_fusion.5
  36.5 3.2 multiply_sine_fusion
  40.2 9.7 %collective-permute-done.7 = bf16[1032,128]{1,0:T(8,128)(2,1)S(1)} collective-permute-done((bf16[1032,128]{1,0:T(8,128)(2,1)}, bf16[1032,128]{1,0:T(8,128)(2,1)S(1)}, u32[]{:S(2)}, u32[]{:S(2)}) %collective-permute-start.7) | collective-permute-done | bytes 264224 | tf_op jit(solution)/shard_map/ppermute | solution.py:600
  51.8 1.6 collective-permute-start.9
  56.9 33.4 %collective-permute-done.1.refs_3_.across = bf16[3,256,1024]{2,1,0:T(8,128)(2,1)} collective-permute-done((bf16[3,256,1024]{2,1,0:T(8,128)(2,1)}, bf16[3,256,1024]{2,1,0:T(8,128)(2,1)}, u32[]{:S(2)}, u32[]{:S(2)}) %collective-permute-start.1) | collective-permute-done | bytes 1572896 | tf_op jit(solution)/shard_map/ppermute | solution.py:574
  91.1 3.4 collective-permute-done.19
  95.8 13.8 %project.1 = (bf16[3,4,256,256]{3,2,1,0:T(8,128)(2,1)}, bf16[3,4,256,256]{3,2,1,0:T(8,128)(2,1)}, bf16[3,4,256,256]{3,2,1,0:T(8,128)(2,1)}, bf16[3,4,256,16]{3,2,1,0:T(8,128)(2,1)}) custom-call(s32[9]{0:T(128)} %pad_add_fusion.refs_0_.place, bf16[3,256,1024]{2,1,0:T(8,128)(2,1)} %fusion.5.refs_1_.own, ...), custom_call_target="tpu_custom_call" | custom-call | tf_op jit(solution)/shard_map/project/pallas_call | solution.py:99
  109.7 9.8 %attend.3 = (bf16[256,256]{1,0:T(8,128)(2,1)}, bf16[256,256]{1,0:T(8,128)(2,1)}, bf16[256,256]{1,0:T(8,128)(2,1)}, bf16[256,256]{1,0:T(8,128)(2,1)}, f32[2,4,2,256]{3,2,1,0:T(2,128)}) custom-call(s32[9]{0:T(128)} %pad_add_fusion.refs_0_.place, bf16[3,4,256,256]{3,2,1,0:T(8,128)(2,1)} %get-tuple-element.161.query, ...), custom_call_target="tpu_custom_call" | custom-call | tf_op jit(solution)/shard_map/attend/pallas_call | solution.py:233
  119.5 9.8 %attend.4 = (bf16[256,256]{1,0:T(8,128)(2,1)}, bf16[256,256]{1,0:T(8,128)(2,1)}, bf16[256,256]{1,0:T(8,128)(2,1)}, bf16[256,256]{1,0:T(8,128)(2,1)}, f32[2,4,2,256]{3,2,1,0:T(2,128)}) custom-call(s32[9]{0:T(128)} %pad_add_fusion.refs_0_.place, bf16[3,4,256,256]{3,2,1,0:T(8,128)(2,1)} %get-tuple-element.161.query, ...), custom_call_target="tpu_custom_call" | custom-call | tf_op jit(solution)/shard_map/attend/pallas_call | solution.py:233
  129.3 10.2 %attend.5 = (bf16[256,256]{1,0:T(8,128)(2,1)}, bf16[256,256]{1,0:T(8,128)(2,1)}, bf16[256,256]{1,0:T(8,128)(2,1)}, bf16[256,256]{1,0:T(8,128)(2,1)}, f32[2,4,2,256]{3,2,1,0:T(2,128)}) custom-call(s32[9]{0:T(128)} %pad_add_fusion.refs_0_.place, bf16[3,4,256,256]{3,2,1,0:T(8,128)(2,1)} %get-tuple-element.161.query, ...), custom_call_target="tpu_custom_call" | custom-call | tf_op jit(solution)/shard_map/attend/pallas_call | solution.py:233
  139.5 1.6 collective-permute-start.17
  141.8 1.6 collective-permute-start.14
  143.4 5.5 %collective-permute-done.17.refs_11_.refs_3_ = bf16[256,256]{1,0:T(8,128)(2,1)S(1)} collective-permute-done((bf16[256,256]{1,0:T(8,128)(2,1)}, bf16[256,256]{1,0:T(8,128)(2,1)S(1)}, u32[]{:S(2)}, u32[]{:S(2)}) %collective-permute-start.17) | collective-permute-done | bytes 131104 | tf_op jit(solution)/shard_map/ppermute | solution.py:574
  148.9 4.9 %collective-permute-done.18.refs_12_.refs_4_ = bf16[256,256]{1,0:T(8,128)(2,1)S(1)} collective-permute-done((bf16[256,256]{1,0:T(8,128)(2,1)}, bf16[256,256]{1,0:T(8,128)(2,1)S(1)}, u32[]{:S(2)}, u32[]{:S(2)}) %collective-permute-start.18) | collective-permute-done | bytes 131104 | tf_op jit(solution)/shard_map/ppermute | solution.py:574
  154.6 1.4 collective-permute-start.12
  157.2 2.5 collective-permute-done.15.refs_8_.refs_4_
  159.7 3.1 collective-permute-done.11.refs_3_
  162.9 2.5 collective-permute-done.12.refs_4_
  166.0 8.6 %merge.1 = (f32[3,256,1024]{2,1,0:T(8,128)}, bf16[3,256,1024]{2,1,0:T(8,128)(2,1)}, bf16[3,256,16]{2,1,0:T(8,128)(2,1)}) custom-call(s32[9]{0:T(128)} %pad_add_fusion.refs_0_.place, bf16[256,256]{1,0:T(8,128)(2,1)} %get-tuple-element.152.refs_1_, bf16[256,256]{1,0:T(8,128)(2,1)} %copy-done.34, bf16[256,256]{1,0:T(8,128)(2,1)} %copy-done.35, ...), custom_call_target="tpu_custom_call" | custom-call | tf_op jit(solution)/shard_map/merge/pallas_call | solution.py:334
  174.5 50.7 %gated.1 = (f32[768,1024]{1,0:T(8,128)}, f32[768,1024]{1,0:T(8,128)}, f32[4,2,48,656]{3,2,1,0:T(8,128)}, f32[4,48,656]{2,1,0:T(8,128)}, f32[48,1024]{1,0:T(8,128)}, /*index=5*/f32[48,1024]{1,0:T(8,128)}) custom-call(s32[9]{0:T(128)} %pad_add_fusion.refs_0_.place, bf16[768,1024]{1,0:T(8,128)(2,1)} %bitcast.205, bf16[768,1024]{1,0:T(8,128)(2,1)} %bitcast.177, ...), custom_call_target="tpu_custom_call" | custom-call | tf_op jit(solution)/shard_map/gated/pallas_call | solution.py:456
  225.2 5.9 %merge_back.3 = (bf16[256,256]{1,0:T(8,128)(2,1)}, bf16[256,256]{1,0:T(8,128)(2,1)}, bf16[256,256]{1,0:T(8,128)(2,1)}, bf16[256,256]{1,0:T(8,128)(2,1)}, f32[1,2...) custom-call(s32[9]{0:T(128)} %pad_add_fusion.refs_0_.place, ...), custom_call_target="tpu_custom_call" | custom-call | tf_op jit(solution)/shard_map/merge_back/pallas_call | solution.py:370
  231.2 6.1 %merge_back.4 = (bf16[256,256]{1,0:T(8,128)(2,1)}, bf16[256,256]{1,0:T(8,128)(2,1)}, bf16[256,256]{1,0:T(8,128)(2,1)}, bf16[256,256]{1,0:T(8,128)(2,1)}, f32[1,2...) custom-call(s32[9]{0:T(128)} %pad_add_fusion.refs_0_.place, ...), custom_call_target="tpu_custom_call" | custom-call | tf_op jit(solution)/shard_map/merge_back/pallas_call | solution.py:370
  241.4 2.5 collective-permute-done.22.refs_2_
  243.9 1.7 collective-permute-done.23.refs_3_
  245.6 5.9 %merge_back.5 = (bf16[256,256]{1,0:T(8,128)(2,1)}, bf16[256,256]{1,0:T(8,128)(2,1)}, bf16[256,256]{1,0:T(8,128)(2,1)}, bf16[256,256]{1,0:T(8,128)(2,1)}, f32[1,2...) custom-call(s32[9]{0:T(128)} %pad_add_fusion.refs_0_.place, ...), custom_call_target="tpu_custom_call" | custom-call | tf_op jit(solution)/shard_map/merge_back/pallas_call | solution.py:370
  255.9 2.3 copy.79
  258.3 2.8 all-to-all-start
  261.7 1.6 collective-permute-start.25
  263.9 1.7 collective-permute-start.28
  266.3 16.6 %attend_back.3 = (bf16[4,256,256]{2,1,0:T(8,128)(2,1)}, bf16[4,256,256]{2,1,0:T(8,128)(2,1)}, bf16[4,256,256]{2,1,0:T(8,128)(2,1)}) custom-call(s32[9]{0:T(128)} %pad_add_fusion.refs_0_.place, bf16[3,4,256,256]{3,2,1,0:T(8,128)(2,1)} %get-tuple-element.161.query, bf16[3,4,256,256]{3,2,1,0:T(8,128)(2,1)} %get-tuple-element.150.key, ...), custom_call_target="tpu_custom_call" | custom-call | tf_op jit(solution)/shard_map/attend_back/pallas_call | solution.py:291
  282.9 5.8 %collective-permute-done.28.refs_2_ = bf16[256,256]{1,0:T(8,128)(2,1)S(1)} collective-permute-done((bf16[256,256]{1,0:T(8,128)(2,1)S(1)}, bf16[256,256]{1,0:T(8,128)(2,1)S(1)}, u32[]{:S(2)}, u32[]{:S(2)}) %collective-permute-start.28) | collective-permute-done | bytes 131104 | tf_op jit(solution)/shard_map/ppermute | solution.py:574
  288.7 1.8 collective-permute-done.29.refs_3_
  290.6 4.8 %joined_grads.3 = (bf16[4,256,16]{2,1,0:T(8,128)(2,1)}, f32[16,768]{1,0:T(8,128)}, f32[16,1024]{1,0:T(8,128)}) custom-call(s32[9]{0:T(128)} %pad_add_fusion.refs_0_.place, bf16[4,256,256]{2,1,0:T(8,128)(2,1)} %get-tuple-element.200.grad_query, bf16[4,256,256]{2,1,0:T(8,128)(2,1)} %get-tuple-element.201.grad_key, ...), custom_call_target="tpu_custom_call" | custom-call | tf_op jit(solution)/shard_map/joined_grads/pallas_call | solution.py:145
  295.4 6.5 %project_back.3 = (f32[2,256,1024]{2,1,0:T(8,128)}, bf16[2,256,1024]{2,1,0:T(8,128)(2,1)}) custom-call(s32[9]{0:T(128)} %pad_add_fusion.refs_0_.place, bf16[4,256,256]{2,1,0:T(8,128)(2,1)} %get-tuple-element.200.grad_query, bf16[4,256,256]{2,1,0:T(8,128)(2,1)} %get-tuple-element.201.grad_key, bf16[4,256,256]{2,1,0:T(8,128)(2,1)} %get-tuple-element.202.grad_value, ...), custom_call_target="tpu_custom_call" | custom-call | tf_op jit(solution)/shard_map/project_back/pallas_call | solution.py:180
  302.5 2.5 collective-permute-done.30
  308.8 16.8 %attend_back.4 = (bf16[4,256,256]{2,1,0:T(8,128)(2,1)}, bf16[4,256,256]{2,1,0:T(8,128)(2,1)}, bf16[4,256,256]{2,1,0:T(8,128)(2,1)}) custom-call(s32[9]{0:T(128)} %pad_add_fusion.refs_0_.place, bf16[3,4,256,256]{3,2,1,0:T(8,128)(2,1)} %get-tuple-element.161.query, bf16[3,4,256,256]{3,2,1,0:T(8,128)(2,1)} %get-tuple-element.150.key, ...), custom_call_target="tpu_custom_call" | custom-call | tf_op jit(solution)/shard_map/attend_back/pallas_call | solution.py:291
  327.9 4.8 %joined_grads.4 = (bf16[4,256,16]{2,1,0:T(8,128)(2,1)}, f32[16,768]{1,0:T(8,128)}, f32[16,1024]{1,0:T(8,128)}) custom-call(s32[9]{0:T(128)} %pad_add_fusion.refs_0_.place, bf16[4,256,256]{2,1,0:T(8,128)(2,1)} %get-tuple-element.226.grad_query, bf16[4,256,256]{2,1,0:T(8,128)(2,1)} %get-tuple-element.227.grad_key, ...), custom_call_target="tpu_custom_call" | custom-call | tf_op jit(solution)/shard_map/joined_grads/pallas_call | solution.py:145
  332.7 6.5 %project_back.4 = (f32[2,256,1024]{2,1,0:T(8,128)}, bf16[2,256,1024]{2,1,0:T(8,128)(2,1)}) custom-call(s32[9]{0:T(128)} %pad_add_fusion.refs_0_.place, bf16[4,256,256]{2,1,0:T(8,128)(2,1)} %get-tuple-element.226.grad_query, bf16[4,256,256]{2,1,0:T(8,128)(2,1)} %get-tuple-element.227.grad_key, bf16[4,256,256]{2,1,0:T(8,128)(2,1)} %get-tuple-element.228.grad_value, ...), custom_call_target="tpu_custom_call" | custom-call | tf_op jit(solution)/shard_map/project_back/pallas_call | solution.py:180
  339.9 2.1 collective-permute-done.32
  343.8 1.7 collective-permute-start.33
  345.6 16.6 %attend_back.5 = (bf16[4,256,256]{2,1,0:T(8,128)(2,1)}, bf16[4,256,256]{2,1,0:T(8,128)(2,1)}, bf16[4,256,256]{2,1,0:T(8,128)(2,1)}) custom-call(s32[9]{0:T(128)} %pad_add_fusion.refs_0_.place, bf16[3,4,256,256]{3,2,1,0:T(8,128)(2,1)} %get-tuple-element.161.query, bf16[3,4,256,256]{3,2,1,0:T(8,128)(2,1)} %get-tuple-element.150.key, ...), custom_call_target="tpu_custom_call" | custom-call | tf_op jit(solution)/shard_map/attend_back/pallas_call | solution.py:291
  362.9 4.8 %joined_grads.5 = (bf16[4,256,16]{2,1,0:T(8,128)(2,1)}, f32[16,768]{1,0:T(8,128)}, f32[16,1024]{1,0:T(8,128)}) custom-call(s32[9]{0:T(128)} %pad_add_fusion.refs_0_.place, bf16[4,256,256]{2,1,0:T(8,128)(2,1)} %get-tuple-element.240.grad_query, bf16[4,256,256]{2,1,0:T(8,128)(2,1)} %get-tuple-element.241.grad_key, ...), custom_call_target="tpu_custom_call" | custom-call | tf_op jit(solution)/shard_map/joined_grads/pallas_call | solution.py:145
  367.8 6.7 %project_back.5 = (f32[2,256,1024]{2,1,0:T(8,128)}, bf16[2,256,1024]{2,1,0:T(8,128)(2,1)}) custom-call(s32[9]{0:T(128)} %pad_add_fusion.refs_0_.place, bf16[4,256,256]{2,1,0:T(8,128)(2,1)} %get-tuple-element.240.grad_query, bf16[4,256,256]{2,1,0:T(8,128)(2,1)} %get-tuple-element.241.grad_key, bf16[4,256,256]{2,1,0:T(8,128)(2,1)} %get-tuple-element.242.grad_value, ...), custom_call_target="tpu_custom_call" | custom-call | tf_op jit(solution)/shard_map/project_back/pallas_call | solution.py:180
  374.5 3.6 add_convert_fusion
  379.4 1.5 convert_element_type.177
  382.2 2.2 fusion.29
  385.6 6.0 %all-to-all-start.1 = ((bf16[32,6,448]{2,1,0:T(8,128)(2,1)}), bf16[32,6,448]{2,1,0:T(8,128)(2,1)S(1)}, u32[]{:S(2)}, u32[]{:S(2)}) async-start(bf16[32,6,448]{2,1,0:T(8,128)(2,1)} %copy.80), calls=%async_computation.1 | async-start | bytes 524288 | tf_op jit(solution)/shard_map/all_to_all | solution.py:582
  391.6 1.8 fusion.24
  393.7 1.5 fusion.20
  395.2 12.0 %all-to-all-done.1 = bf16[32,6,448]{2,1,0:T(8,128)(2,1)S(1)} async-done(((bf16[32,6,448]{2,1,0:T(8,128)(2,1)}), bf16[32,6,448]{2,1,0:T(8,128)(2,1)S(1)}, u32[]{:S(2)}, u32[]{:S(2)}) %all-to-all-start.1) | async-done | bytes 172064 | tf_op jit(solution)/shard_map/all_to_all | solution.py:582
  409.1 3.9 all-to-all-start.2
  413.0 2.0 fusion.16
  417.1 2.1 fusion.10
  419.2 5.0 %settle_early.1 = (f32[8,16,1024]{2,1,0:T(8,128)}, f32[8,16,1024]{2,1,0:T(8,128)}, f32[8,16,1024]{2,1,0:T(8,128)}, f32[8,16,256]{2,1,0:T(8,128)}, f32[8,16,2,656]{3,2,1,0:T(2,128)}, /*index=5*/f32[8,16,656]{2,1,0:T(8,128)}) custom-call(s32[9]{0:T(128)} %pad_add_fusion.refs_0_.place, bf16[32,16,3328]{2,1,0:T(8,128)(2,1)} %all-gather.5.cloned.1.call-done.refs_1_), custom_call_target="tpu_custom_call" | custom-call | tf_op jit(solution)/shard_map/settle_early/pallas_call | solution.py:528
  424.2 4.4 all-to-all-done.2.refs_0_
  429.3 2.3 settle_late.1
  (331 shorter events, 51.1 us)
Async XLA Ops:
  7.2 167.3 %all-gather.3.cloned.1.call-start = ((), (), s32[]{:S(2)}) async-start(), calls=%async_computation.3 | async-start | bytes 16625664 | tf_op jit(solution)/shard_map/all_gather | solution.py:651
  10.8 12.4 %copy-start.67 = (bf16[1024]{0:T(1024)(128)(2,1)S(1)}, bf16[1024]{0:T(1024)(128)(2,1)}, u32[]{:S(2)}) copy-start(bf16[1024]{0:T(1024)(128)(2,1)} %param.22) | copy-start | bytes 6148
  10.9 12.4 %copy-start.2 = (bf16[3,256,1024]{2,1,0:T(8,128)(2,1)S(1)}, bf16[3,256,1024]{2,1,0:T(8,128)(2,1)}, u32[]{:S(2)}) copy-start(bf16[3,256,1024]{2,1,0:T(8,128)(2,1)} %refs_13_.1) | copy-start | bytes 4718596
  13.6 26.0 %collective-permute-start.3 = (bf16[3,16,2560]{2,1,0:T(8,128)(2,1)}, bf16[3,16,2560]{2,1,0:T(8,128)(2,1)S(1)}, u32[]{:S(2)}, u32[]{:S(2)}) collective-permute-start(bf16[3,16,2560]{2,1,0:T(8,128)(2,1)} %fusion.37), channel_id=1, source_target_pairs={{0,2},{1,3},{2,0},{3,1},{4,6},{5,7},{6,4},{7,5},{8,10},{9,11},{10,... | collective-permute-start | bytes 737288 | tf_op jit(solution)/shard_map/ppermute | solution.py:574
  16.6 38.0 %collective-permute-start.2 = (bf16[3,16,2560]{2,1,0:T(8,128)(2,1)}, bf16[3,16,2560]{2,1,0:T(8,128)(2,1)S(1)}, u32[]{:S(2)}, u32[]{:S(2)}) collective-permute-start(bf16[3,16,2560]{2,1,0:T(8,128)(2,1)} %fusion.37), channel_id=1, source_target_pairs={{0,1},{1,0},{2,3},{3,2},{4,5},{5,4},{6,7},{7,6},{8,9},{9,8},{10,11... | collective-permute-start | bytes 737288 | tf_op jit(solution)/shard_map/ppermute | solution.py:574
  17.7 22.5 %collective-permute-start.6 = (bf16[1032,128]{1,0:T(8,128)(2,1)}, bf16[1032,128]{1,0:T(8,128)(2,1)S(1)}, u32[]{:S(2)}, u32[]{:S(2)}) collective-permute-start(bf16[1032,128]{1,0:T(8,128)(2,1)} %get-tuple-element.271), channel_id=1, source_target_pairs={{0,8},{4,12},{8,16},{12,20},{16,24},{20,28},{24,0},{28,4},{1,9},{5... | collective-permute-start | bytes 792584 | tf_op jit(solution)/shard_map/ppermute | solution.py:600
  19.3 30.6 %collective-permute-start.7 = (bf16[1032,128]{1,0:T(8,128)(2,1)}, bf16[1032,128]{1,0:T(8,128)(2,1)S(1)}, u32[]{:S(2)}, u32[]{:S(2)}) collective-permute-start(bf16[1032,128]{1,0:T(8,128)(2,1)} %get-tuple-element.271), channel_id=1, source_target_pairs={{0,16},{4,20},{8,24},{12,28},{16,0},{20,4},{24,8},{28,12},{1,17},{... | collective-permute-start | bytes 792584 | tf_op jit(solution)/shard_map/ppermute | solution.py:600
  21.8 28.8 %collective-permute-start.8 = (bf16[1032,128]{1,0:T(8,128)(2,1)}, bf16[1032,128]{1,0:T(8,128)(2,1)}, u32[]{:S(2)}, u32[]{:S(2)}) collective-permute-start(bf16[1032,128]{1,0:T(8,128)(2,1)} %get-tuple-element.271), channel_id=1, source_target_pairs={{0,24},{4,28},{8,0},{12,4},{16,8},{20,12},{24,16},{28,20},{1,25},{... | collective-permute-start | bytes 792584 | tf_op jit(solution)/shard_map/ppermute | solution.py:600
  32.0 21.4 %copy-start.5 = (bf16[8,1032,128]{2,1,0:T(8,128)(2,1)S(1)}, bf16[8,1032,128]{2,1,0:T(8,128)(2,1)}, u32[]{:S(2)}) copy-start(bf16[8,1032,128]{2,1,0:T(8,128)(2,1)} %constant_dynamic-update-slice_fusion.4) | copy-start | bytes 6340612
  39.6 50.7 %collective-permute-start.1 = (bf16[3,256,1024]{2,1,0:T(8,128)(2,1)}, bf16[3,256,1024]{2,1,0:T(8,128)(2,1)}, u32[]{:S(2)}, u32[]{:S(2)}) collective-permute-start(bf16[3,256,1024]{2,1,0:T(8,128)(2,1)} %fusion.5.refs_1_.own), channel_id=1, source_target_pairs={{0,2},{1,3},{2,0},{3,1},{4,6},{5,7},{6,4},{7,5},{8,10},{9,11},{10,... | collective-permute-start | bytes 4718600 | tf_op jit(solution)/shard_map/ppermute | solution.py:574
  40.2 55.6 %collective-permute-start = (bf16[3,256,1024]{2,1,0:T(8,128)(2,1)}, bf16[3,256,1024]{2,1,0:T(8,128)(2,1)}, u32[]{:S(2)}, u32[]{:S(2)}) collective-permute-start(bf16[3,256,1024]{2,1,0:T(8,128)(2,1)} %fusion.5.refs_1_.own), channel_id=1, source_target_pairs={{0,1},{1,0},{2,3},{3,2},{4,5},{5,4},{6,7},{7,6},{8,9},{9,8},{10,11... | collective-permute-start | bytes 4718600 | tf_op jit(solution)/shard_map/ppermute | solution.py:574
  49.8 4.7 %collective-permute-start.4 = (bf16[3,16,2560]{2,1,0:T(8,128)(2,1)S(1)}, bf16[3,16,2560]{2,1,0:T(8,128)(2,1)S(1)}, u32[]{:S(2)}, u32[]{:S(2)}) collective-permute-start(bf16[3,16,2560]{2,1,0:T(8,128)(2,1)S(1)} %collective-permute-done.3), channel_id=1, source_target_pairs={{0,1},{1,0},{2,3},{3,2},{4,5},{5,4},{6,7},{7,6},{8,9},{9,8},{10,11... | collective-permute-start | bytes 737288 | tf_op jit(solution)/shard_map/ppermute | solution.py:574
  51.8 38.5 %collective-permute-start.9 = (bf16[4,1032,128]{2,1,0:T(8,128)(2,1)S(1)}, bf16[4,1032,128]{2,1,0:T(8,128)(2,1)S(1)}, u32[]{:S(2)}, u32[]{:S(2)}) collective-permute-start(bf16[4,1032,128]{2,1,0:T(8,128)(2,1)S(1)} %pad_maximum_fusion), channel_id=1, source_target_pairs={{0,4},{4,0},{8,12},{12,8},{16,20},{20,16},{24,28},{28,24},{1,5},{5... | collective-permute-start | bytes 3170312 | tf_op jit(solution)/shard_map/ppermute | solution.py:602
  90.3 5.5 %collective-permute-start.5 = (bf16[3,256,1024]{2,1,0:T(8,128)(2,1)}, bf16[3,256,1024]{2,1,0:T(8,128)(2,1)}, u32[]{:S(2)}, u32[]{:S(2)}) collective-permute-start(bf16[3,256,1024]{2,1,0:T(8,128)(2,1)} %collective-permute-done.1.refs_3_.across), channel_id=1, source_target_pairs={{0,1},{1,0},{2,3},{3,2},{4,5},{5,4},{6,7},{7,6},{8,9},{9,8},{10,11... | collective-permute-start | bytes 4718600 | tf_op jit(solution)/shard_map/ppermute | solution.py:574
  90.5 4.0 collective-permute-start.19
  94.6 15.1 %copy-start.7 = (bf16[8,2,256,128]{3,2,1,0:T(8,128)(2,1)}, bf16[8,2,256,128]{3,2,1,0:T(8,128)(2,1)S(1)}, u32[]{:S(2)}) copy-start(bf16[8,2,256,128]{3,2,1,0:T(8,128)(2,1)S(1)} %pad_maximum_fusion.1.refs_14_.refs_9_) | copy-start | bytes 3145732
  94.6 47.1 %collective-permute-start.20 = (bf16[8,2,256,128]{3,2,1,0:T(8,128)(2,1)S(1)}, bf16[8,2,256,128]{3,2,1,0:T(8,128)(2,1)}, u32[]{:S(2)}, u32[]{:S(2)}) collective-permute-start(bf16[8,2,256,128]{3,2,1,0:T(8,128)(2,1)S(1)} %pad_maximum_fusion.1.refs_14_.refs_9_), channel_id=1, source_target_pairs={{0,2},{1,3},{2,0},{3,1},{4,6},{5,7},{6,4},{7,5},{8,10},{9,11},{10,... | collective-permute-start | bytes 3145736 | tf_op jit(solution)/shard_map/ppermute | solution.py:574
  129.3 12.1 %copy-start.81 = (bf16[256,256]{1,0:T(8,128)(2,1)S(1)}, bf16[256,256]{1,0:T(8,128)(2,1)}, u32[]{:S(2)}) copy-start(bf16[256,256]{1,0:T(8,128)(2,1)} %get-tuple-element.158) | copy-start | bytes 393220
  129.3 12.5 %copy-start.80 = (bf16[256,256]{1,0:T(8,128)(2,1)S(1)}, bf16[256,256]{1,0:T(8,128)(2,1)}, u32[]{:S(2)}) copy-start(bf16[256,256]{1,0:T(8,128)(2,1)} %get-tuple-element.159) | copy-start | bytes 393220
  129.3 14.1 %copy-start.79 = (bf16[256,256]{1,0:T(8,128)(2,1)S(1)}, bf16[256,256]{1,0:T(8,128)(2,1)}, u32[]{:S(2)}) copy-start(bf16[256,256]{1,0:T(8,128)(2,1)} %get-tuple-element.160) | copy-start | bytes 393220
  129.3 19.6 %copy-start.78 = (bf16[256,256]{1,0:T(8,128)(2,1)S(1)}, bf16[256,256]{1,0:T(8,128)(2,1)}, u32[]{:S(2)}) copy-start(bf16[256,256]{1,0:T(8,128)(2,1)} %get-tuple-element.153) | copy-start | bytes 393220
  129.3 24.5 %copy-start.77 = (bf16[256,256]{1,0:T(8,128)(2,1)S(1)}, bf16[256,256]{1,0:T(8,128)(2,1)}, u32[]{:S(2)}) copy-start(bf16[256,256]{1,0:T(8,128)(2,1)} %get-tuple-element.154) | copy-start | bytes 393220
  129.3 25.3 %copy-start.76 = (bf16[256,256]{1,0:T(8,128)(2,1)S(1)}, bf16[256,256]{1,0:T(8,128)(2,1)}, u32[]{:S(2)}) copy-start(bf16[256,256]{1,0:T(8,128)(2,1)} %get-tuple-element.155) | copy-start | bytes 393220
  129.3 26.8 %copy-start.68 = (bf16[1024]{0:T(1024)(128)(2,1)S(1)}, bf16[1024]{0:T(1024)(128)(2,1)}, u32[]{:S(2)}) copy-start(bf16[1024]{0:T(1024)(128)(2,1)} %param.23) | copy-start | bytes 6148
  139.5 3.8 collective-permute-start.16
  139.5 9.4 %collective-permute-start.17 = (bf16[256,256]{1,0:T(8,128)(2,1)}, bf16[256,256]{1,0:T(8,128)(2,1)S(1)}, u32[]{:S(2)}, u32[]{:S(2)}) collective-permute-start(bf16[256,256]{1,0:T(8,128)(2,1)} %get-tuple-element.164), channel_id=1, source_target_pairs={{0,2},{1,3},{2,0},{3,1},{4,6},{5,7},{6,4},{7,5},{8,10},{9,11},{10,... | collective-permute-start | bytes 393224 | tf_op jit(solution)/shard_map/ppermute | solution.py:574
  141.1 12.8 %collective-permute-start.18 = (bf16[256,256]{1,0:T(8,128)(2,1)}, bf16[256,256]{1,0:T(8,128)(2,1)S(1)}, u32[]{:S(2)}, u32[]{:S(2)}) collective-permute-start(bf16[256,256]{1,0:T(8,128)(2,1)} %get-tuple-element.165), channel_id=1, source_target_pairs={{0,3},{1,2},{2,1},{3,0},{4,7},{5,6},{6,5},{7,4},{8,11},{9,10},{10,... | collective-permute-start | bytes 393224 | tf_op jit(solution)/shard_map/ppermute | solution.py:574
  141.4 13.3 %collective-permute-start.13 = (bf16[256,256]{1,0:T(8,128)(2,1)S(1)}, bf16[256,256]{1,0:T(8,128)(2,1)S(1)}, u32[]{:S(2)}, u32[]{:S(2)}) collective-permute-start(bf16[256,256]{1,0:T(8,128)(2,1)S(1)} %copy-done.81), channel_id=1, source_target_pairs={{0,1},{1,0},{2,3},{3,2},{4,5},{5,4},{6,7},{7,6},{8,9},{9,8},{10,11... | collective-permute-start | bytes 393224 | tf_op jit(solution)/shard_map/ppermute | solution.py:574
  141.8 15.5 %collective-permute-start.14 = (bf16[256,256]{1,0:T(8,128)(2,1)S(1)}, bf16[256,256]{1,0:T(8,128)(2,1)S(1)}, u32[]{:S(2)}, u32[]{:S(2)}) collective-permute-start(bf16[256,256]{1,0:T(8,128)(2,1)S(1)} %copy-done.80), channel_id=1, source_target_pairs={{0,2},{1,3},{2,0},{3,1},{4,6},{5,7},{6,4},{7,5},{8,10},{9,11},{10,... | collective-permute-start | bytes 393224 | tf_op jit(solution)/shard_map/ppermute | solution.py:574
  143.3 22.0 %copy-start.28 = (bf16[256,256]{1,0:T(8,128)(2,1)}, bf16[256,256]{1,0:T(8,128)(2,1)S(1)}, u32[]{:S(2)}) copy-start(bf16[256,256]{1,0:T(8,128)(2,1)S(1)} %collective-permute-done.16.refs_10_.refs_2_) | copy-start | bytes 393220
  143.3 16.4 %collective-permute-start.15 = (bf16[256,256]{1,0:T(8,128)(2,1)S(1)}, bf16[256,256]{1,0:T(8,128)(2,1)S(1)}, u32[]{:S(2)}, u32[]{:S(2)}) collective-permute-start(bf16[256,256]{1,0:T(8,128)(2,1)S(1)} %copy-done.79), channel_id=1, source_target_pairs={{0,3},{1,2},{2,1},{3,0},{4,7},{5,6},{6,5},{7,4},{8,11},{9,10},{10,... | collective-permute-start | bytes 393224 | tf_op jit(solution)/shard_map/ppermute | solution.py:574
  148.9 16.4 %copy-start.29 = (bf16[256,256]{1,0:T(8,128)(2,1)}, bf16[256,256]{1,0:T(8,128)(2,1)S(1)}, u32[]{:S(2)}) copy-start(bf16[256,256]{1,0:T(8,128)(2,1)S(1)} %collective-permute-done.17.refs_11_.refs_3_) | copy-start | bytes 393220
  148.9 10.8 %collective-permute-start.10 = (bf16[256,256]{1,0:T(8,128)(2,1)S(1)}, bf16[256,256]{1,0:T(8,128)(2,1)S(1)}, u32[]{:S(2)}, u32[]{:S(2)}) collective-permute-start(bf16[256,256]{1,0:T(8,128)(2,1)S(1)} %copy-done.78), channel_id=1, source_target_pairs={{0,1},{1,0},{2,3},{3,2},{4,5},{5,4},{6,7},{7,6},{8,9},{9,8},{10,11... | collective-permute-start | bytes 393224 | tf_op jit(solution)/shard_map/ppermute | solution.py:574
  153.8 11.5 %copy-start.30 = (bf16[256,256]{1,0:T(8,128)(2,1)}, bf16[256,256]{1,0:T(8,128)(2,1)S(1)}, u32[]{:S(2)}) copy-start(bf16[256,256]{1,0:T(8,128)(2,1)S(1)} %collective-permute-done.18.refs_12_.refs_4_) | copy-start | bytes 393220
  153.8 9.0 %collective-permute-start.11 = (bf16[256,256]{1,0:T(8,128)(2,1)S(1)}, bf16[256,256]{1,0:T(8,128)(2,1)S(1)}, u32[]{:S(2)}, u32[]{:S(2)}) collective-permute-start(bf16[256,256]{1,0:T(8,128)(2,1)S(1)} %copy-done.77), channel_id=1, source_target_pairs={{0,2},{1,3},{2,0},{3,1},{4,6},{5,7},{6,4},{7,5},{8,10},{9,11},{10,... | collective-permute-start | bytes 393224 | tf_op jit(solution)/shard_map/ppermute | solution.py:574
  154.6 10.7 %copy-start.31 = (bf16[256,256]{1,0:T(8,128)(2,1)}, bf16[256,256]{1,0:T(8,128)(2,1)S(1)}, u32[]{:S(2)}) copy-start(bf16[256,256]{1,0:T(8,128)(2,1)S(1)} %collective-permute-done.13.refs_6_.refs_2_) | copy-start | bytes 393220
  154.6 10.7 %collective-permute-start.12 = (bf16[256,256]{1,0:T(8,128)(2,1)S(1)}, bf16[256,256]{1,0:T(8,128)(2,1)S(1)}, u32[]{:S(2)}, u32[]{:S(2)}) collective-permute-start(bf16[256,256]{1,0:T(8,128)(2,1)S(1)} %copy-done.76), channel_id=1, source_target_pairs={{0,3},{1,2},{2,1},{3,0},{4,7},{5,6},{6,5},{7,4},{8,11},{9,10},{10,... | collective-permute-start | bytes 393224 | tf_op jit(solution)/shard_map/ppermute | solution.py:574
  237.3 6.6 %collective-permute-start.22 = (bf16[256,256]{1,0:T(8,128)(2,1)}, bf16[256,256]{1,0:T(8,128)(2,1)S(1)}, u32[]{:S(2)}, u32[]{:S(2)}) collective-permute-start(bf16[256,256]{1,0:T(8,128)(2,1)} %get-tuple-element.181), channel_id=1, source_target_pairs={{0,2},{1,3},{2,0},{3,1},{4,6},{5,7},{6,4},{7,5},{8,10},{9,11},{10,... | collective-permute-start | bytes 393224 | tf_op jit(solution)/shard_map/ppermute | solution.py:574
  237.9 7.7 %collective-permute-start.23 = (bf16[256,256]{1,0:T(8,128)(2,1)S(1)}, bf16[256,256]{1,0:T(8,128)(2,1)S(1)}, u32[]{:S(2)}, u32[]{:S(2)}) collective-permute-start(bf16[256,256]{1,0:T(8,128)(2,1)S(1)} %copy-done.82), channel_id=1, source_target_pairs={{0,3},{1,2},{2,1},{3,0},{4,7},{5,6},{6,5},{7,4},{8,11},{9,10},{10,... | collective-permute-start | bytes 393224 | tf_op jit(solution)/shard_map/ppermute | solution.py:574
  241.4 11.0 %copy-start.59 = (f32[4,16,256]{2,1,0:T(8,128)S(1)}, f32[4,16,256]{2,1,0:T(8,128)}, u32[]{:S(2)}) copy-start(f32[4,16,256]{2,1,0:T(8,128)} %get-tuple-element.219) | copy-start | bytes 196612
  241.4 11.0 %copy-start.60 = (f32[4,16,256]{2,1,0:T(8,128)S(1)}, f32[4,16,256]{2,1,0:T(8,128)}, u32[]{:S(2)}) copy-start(f32[4,16,256]{2,1,0:T(8,128)} %get-tuple-element.220) | copy-start | bytes 196612
  258.3 67.4 %all-to-all-start = ((bf16[32,3,6656]{2,1,0:T(4,128)(2,1)}), bf16[32,3,6656]{2,1,0:T(4,128)(2,1)S(1)}, u32[]{:S(2)}, u32[]{:S(2)}) async-start(bf16[32,3,6656]{2,1,0:T(4,128)(2,1)} %copy.79), calls=%async_computation | async-start | bytes 3407872 | tf_op jit(solution)/shard_map/all_to_all | solution.py:582
  261.1 158.1 %all-gather.5.cloned.1.call-start = ((), (), s32[]{:S(2)}) async-start(), calls=%async_computation.4 | async-start | bytes 3514368 | tf_op jit(solution)/shard_map/all_gather | solution.py:825
  261.2 2.7 collective-permute-start.24
  261.4 4.2 collective-permute-start.21
  261.7 21.1 %collective-permute-start.25 = (bf16[256,256]{1,0:T(8,128)(2,1)S(1)}, bf16[256,256]{1,0:T(8,128)(2,1)S(1)}, u32[]{:S(2)}, u32[]{:S(2)}) collective-permute-start(bf16[256,256]{1,0:T(8,128)(2,1)S(1)} %copy-done.70), channel_id=1, source_target_pairs={{0,2},{1,3},{2,0},{3,1},{4,6},{5,7},{6,4},{7,5},{8,10},{9,11},{10,... | collective-permute-start | bytes 393224 | tf_op jit(solution)/shard_map/ppermute | solution.py:574
  263.4 19.5 %collective-permute-start.26 = (bf16[256,256]{1,0:T(8,128)(2,1)S(1)}, bf16[256,256]{1,0:T(8,128)(2,1)S(1)}, u32[]{:S(2)}, u32[]{:S(2)}) collective-permute-start(bf16[256,256]{1,0:T(8,128)(2,1)S(1)} %copy-done.69), channel_id=1, source_target_pairs={{0,3},{1,2},{2,1},{3,0},{4,7},{5,6},{6,5},{7,4},{8,11},{9,10},{10,... | collective-permute-start | bytes 393224 | tf_op jit(solution)/shard_map/ppermute | solution.py:574
  263.4 19.5 %collective-permute-start.27 = (bf16[256,256]{1,0:T(8,128)(2,1)S(1)}, bf16[256,256]{1,0:T(8,128)(2,1)S(1)}, u32[]{:S(2)}, u32[]{:S(2)}) collective-permute-start(bf16[256,256]{1,0:T(8,128)(2,1)S(1)} %copy-done.75), channel_id=1, source_target_pairs={{0,1},{1,0},{2,3},{3,2},{4,5},{5,4},{6,7},{7,6},{8,9},{9,8},{10,11... | collective-permute-start | bytes 393224 | tf_op jit(solution)/shard_map/ppermute | solution.py:574
  263.9 19.0 %copy-start.48 = (bf16[256,256]{1,0:T(8,128)(2,1)}, bf16[256,256]{1,0:T(8,128)(2,1)S(1)}, u32[]{:S(2)}) copy-start(bf16[256,256]{1,0:T(8,128)(2,1)S(1)} %collective-permute-done.24.refs_1_) | copy-start | bytes 393220
  263.9 24.8 %collective-permute-start.28 = (bf16[256,256]{1,0:T(8,128)(2,1)S(1)}, bf16[256,256]{1,0:T(8,128)(2,1)S(1)}, u32[]{:S(2)}, u32[]{:S(2)}) collective-permute-start(bf16[256,256]{1,0:T(8,128)(2,1)S(1)} %copy-done.74), channel_id=1, source_target_pairs={{0,2},{1,3},{2,0},{3,1},{4,6},{5,7},{6,4},{7,5},{8,10},{9,11},{10,... | collective-permute-start | bytes 393224 | tf_op jit(solution)/shard_map/ppermute | solution.py:574
  265.6 25.0 %collective-permute-start.29 = (bf16[256,256]{1,0:T(8,128)(2,1)S(1)}, bf16[256,256]{1,0:T(8,128)(2,1)S(1)}, u32[]{:S(2)}, u32[]{:S(2)}) collective-permute-start(bf16[256,256]{1,0:T(8,128)(2,1)S(1)} %copy-done.73), channel_id=1, source_target_pairs={{0,3},{1,2},{2,1},{3,0},{4,7},{5,6},{6,5},{7,4},{8,11},{9,10},{10,... | collective-permute-start | bytes 393224 | tf_op jit(solution)/shard_map/ppermute | solution.py:574
  282.9 12.5 %copy-start.49 = (bf16[256,256]{1,0:T(8,128)(2,1)}, bf16[256,256]{1,0:T(8,128)(2,1)S(1)}, u32[]{:S(2)}) copy-start(bf16[256,256]{1,0:T(8,128)(2,1)S(1)} %collective-permute-done.25.refs_2_) | copy-start | bytes 393220
  282.9 12.5 %copy-start.50 = (bf16[256,256]{1,0:T(8,128)(2,1)}, bf16[256,256]{1,0:T(8,128)(2,1)S(1)}, u32[]{:S(2)}) copy-start(bf16[256,256]{1,0:T(8,128)(2,1)S(1)} %collective-permute-done.26.refs_3_) | copy-start | bytes 393220
  282.9 12.5 %copy-start.43 = (bf16[256,256]{1,0:T(8,128)(2,1)}, bf16[256,256]{1,0:T(8,128)(2,1)S(1)}, u32[]{:S(2)}) copy-start(bf16[256,256]{1,0:T(8,128)(2,1)S(1)} %collective-permute-done.27.refs_1_) | copy-start | bytes 393220
  301.9 3.1 collective-permute-start.30
  306.8 18.9 %collective-permute-start.31 = (bf16[256,1024]{1,0:T(8,128)(2,1)S(1)}, bf16[256,1024]{1,0:T(8,128)(2,1)S(1)}, u32[]{:S(2)}, u32[]{:S(2)}) collective-permute-start(bf16[256,1024]{1,0:T(8,128)(2,1)S(1)} %fusion.27), channel_id=1, source_target_pairs={{0,2},{1,3},{2,0},{3,1},{4,6},{5,7},{6,4},{7,5},{8,10},{9,11},{10,... | collective-permute-start | bytes 1572872 | tf_op jit(solution)/shard_map/ppermute | solution.py:574
  339.2 2.9 collective-permute-start.32
  343.8 18.3 %collective-permute-start.33 = (bf16[256,1024]{1,0:T(8,128)(2,1)S(1)}, bf16[256,1024]{1,0:T(8,128)(2,1)S(1)}, u32[]{:S(2)}, u32[]{:S(2)}) collective-permute-start(bf16[256,1024]{1,0:T(8,128)(2,1)S(1)} %fusion.28), channel_id=1, source_target_pairs={{0,2},{1,3},{2,0},{3,1},{4,6},{5,7},{6,4},{7,5},{8,10},{9,11},{10,... | collective-permute-start | bytes 1572872 | tf_op jit(solution)/shard_map/ppermute | solution.py:574
  374.4 4.9 %collective-permute-start.34 = (bf16[2,256,1024]{2,1,0:T(8,128)(2,1)}, bf16[2,256,1024]{2,1,0:T(8,128)(2,1)}, u32[]{:S(2)}, u32[]{:S(2)}) collective-permute-start(bf16[2,256,1024]{2,1,0:T(8,128)(2,1)} %get-tuple-element.245), channel_id=1, source_target_pairs={{0,1},{1,0},{2,3},{3,2},{4,5},{5,4},{6,7},{7,6},{8,9},{9,8},{10,11... | collective-permute-start | bytes 3145736 | tf_op jit(solution)/shard_map/ppermute | solution.py:574
  380.9 10.7 %copy-start.9 = (f32[2,256,1024]{2,1,0:T(8,128)S(1)}, f32[2,256,1024]{2,1,0:T(8,128)}, u32[]{:S(2)}) copy-start(f32[2,256,1024]{2,1,0:T(8,128)} %copy-done.8) | copy-start | bytes 6291460
  384.4 22.8 %collective-permute-start.35 = (bf16[256,1024]{1,0:T(8,128)(2,1)}, bf16[256,1024]{1,0:T(8,128)(2,1)}, u32[]{:S(2)}, u32[]{:S(2)}) collective-permute-start(bf16[256,1024]{1,0:T(8,128)(2,1)} %fusion.29), channel_id=1, source_target_pairs={{0,2},{1,3},{2,0},{3,1},{4,6},{5,7},{6,4},{7,5},{8,10},{9,11},{10,... | collective-permute-start | bytes 1572872 | tf_op jit(solution)/shard_map/ppermute | solution.py:574
  385.6 21.6 %all-to-all-start.1 = ((bf16[32,6,448]{2,1,0:T(8,128)(2,1)}), bf16[32,6,448]{2,1,0:T(8,128)(2,1)S(1)}, u32[]{:S(2)}, u32[]{:S(2)}) async-start(bf16[32,6,448]{2,1,0:T(8,128)(2,1)} %copy.80), calls=%async_computation.1 | async-start | bytes 524288 | tf_op jit(solution)/shard_map/all_to_all | solution.py:582
  409.1 19.4 %all-to-all-start.2 = ((bf16[32,16,448]{2,1,0:T(8,128)(2,1)}), bf16[32,16,448]{2,1,0:T(8,128)(2,1)S(1)}, u32[]{:S(2)}, u32[]{:S(2)}) async-start(bf16[32,16,448]{2,1,0:T(8,128)(2,1)} %bitcast.68), calls=%async_computation.2 | async-start | bytes 1048576 | tf_op jit(solution)/shard_map/all_to_all | solution.py:582
  417.1 14.5 %copy-start.1 = (bf16[8,16,2,656]{3,2,1,0:T(2,128)(2,1)S(1)}, bf16[8,16,2,656]{3,2,1,0:T(2,128)(2,1)}, u32[]{:S(2)}) copy-start(bf16[8,16,2,656]{3,2,1,0:T(2,128)(2,1)} %param.33) | copy-start | bytes 1007620
  (60 other events, 236.2 us)
Sparse Core Ops, SparseCore 0:
  11.5 161.8 all-gather.2
  340.0 66.6 all-gather.4

commit v3 on v2

--- a/solution.py
+++ b/solution.py
@@ -35,6 +35,10 @@
 
 def full(shape):
     return pl.BlockSpec(shape, lambda *_: (0,) * len(shape))
+
+
+def full_once(shape):
+    return pl.BlockSpec(shape, lambda *_: (0,) * len(shape), pipeline_mode=pl.Buffered(1))
 
 
 def norm_parts(values):
@@ -118,93 +122,13 @@
     )(place, *pieces, weight, low, up, *tables)
 
 
-def joined_grads_kernel(
-    place, grad_query, grad_key, grad_value, own, beside, across, corner, up, down,
-    small_grad, up_grad, low_grad
-):
-    up_total = jnp.zeros(up_grad.shape, F32)
-    low_total = jnp.zeros(low_grad.shape, F32)
-    for step, piece in enumerate((own, beside, across, corner)):
-        spot = place[0] ^ step
-        grads = jnp.concatenate([grad_query[spot], grad_key[spot], grad_value[spot]], axis=1)
-        small = (nt(grads, up[0]) * ADAPTER_SCALE).astype(BF)
-        small_grad[step] = small
-        up_total += tn(down[0, step], grads)
-        low_total += tn(small, piece[0])
-    up_grad[...] = up_total
-    low_grad[...] = low_total
-
-
-def joined_grads(place, seq, grads, pieces, up, down):
-    _, own, model = pieces[0].shape
-    _, rank, tall = up.shape
-    wide = tall // 3
-    blocks = len(pieces)
-    whole = lambda shape: pl.BlockSpec(shape, lambda i, p: (0,) * len(shape))
-    of_seq = lambda shape: pl.BlockSpec((1,) + shape, lambda i, p: (seq,) + (0,) * len(shape))
-    return pl.pallas_call(
-        joined_grads_kernel,
-        grid_spec=pltpu.PrefetchScalarGridSpec(
-            num_scalar_prefetch=1,
-            grid=(1,),
-            in_specs=[whole((blocks, own, wide))] * 3
-            + [of_seq((own, model))] * blocks
-            + [of_seq((rank, tall)), of_seq((blocks, own, rank))],
-            out_specs=[whole((blocks, own, rank)), whole((rank, tall)), whole((rank, model))],
-        ),
-        out_shape=[
-            jax.ShapeDtypeStruct((blocks, own, rank), BF),
-            jax.ShapeDtypeStruct((rank, tall), F32),
-            jax.ShapeDtypeStruct((rank, model), F32),
-        ],
-        name="joined_grads",
-    )(place, *grads, *pieces, up, down)
-
-
-def project_back_kernel(place, grad_query, grad_key, grad_value, small_grad, weight, low, here, there):
-    table = lanes_of(weight, 0, 3 * grad_query.shape[2], place)
-    for step in range(grad_query.shape[0]):
-        spot = place[0] ^ step
-        grads = jnp.concatenate([grad_query[spot], grad_key[spot], grad_value[spot]], axis=1)
-        out = nn(grads, table) + nn(small_grad[step], low[0])
-        if step % 2:
-            there[step // 2] = out.astype(BF)
-        else:
-            here[step // 2] = out
-
-
-def project_back(place, seq, grads, small_grad, weight, low):
-    blocks, own, wide = grads[0].shape
-    _, rank, model = low.shape
-    whole = lambda shape: pl.BlockSpec(shape, lambda i, p: (0,) * len(shape))
-    return pl.pallas_call(
-        project_back_kernel,
-        grid_spec=pltpu.PrefetchScalarGridSpec(
-            num_scalar_prefetch=1,
-            grid=(1,),
-            in_specs=[whole((blocks, own, wide))] * 3
-            + [
-                whole((blocks, own, rank)),
-                whole(weight.shape),
-                pl.BlockSpec((1, rank, model), lambda i, p: (seq, 0, 0)),
-            ],
-            out_specs=[whole((blocks // 2, own, model))] * 2,
-        ),
-        out_shape=[
-            jax.ShapeDtypeStruct((blocks // 2, own, model), F32),
-            jax.ShapeDtypeStruct((blocks // 2, own, model), BF),
-        ],
-        name="project_back",
-    )(place, *grads, small_grad, weight, low)
-
-
 def one_head(values, head):
     lane = lax.broadcasted_iota(jnp.int32, values.shape, 1)
     return jnp.where((lane // HEAD_DIM) == head, values, jnp.zeros_like(values))
 
 
 def attend_kernel(place, query, key, value, *outs):
-    *contexts, log_total = outs
+    *contexts, probs, shrinks = outs
     blocks, own = query.shape[1:3]
     keys = key[0].reshape(blocks * own, LANES)
     turned = value[0].reshape(blocks * own, LANES).T
@@ -215,12 +139,11 @@
             scores = nt(keys, one_head(rows, head))
             top = jnp.max(scores, axis=0, keepdims=True)
             raised = jnp.exp(scores - top)
-            total = jnp.sum(raised, axis=0, keepdims=True)
-            part = nn(turned[head * HEAD_DIM : (head + 1) * HEAD_DIM], raised.astype(BF))
-            parts.append(part * (1.0 / total))
-            logs = top + jnp.log(total)
-            for i in range(2):
-                log_total[0, step + i, head : head + 1] = logs[:, i * own : (i + 1) * own]
+            shrink = 1.0 / jnp.sum(raised, axis=0, keepdims=True)
+            raised = raised.astype(BF)
+            probs[0, step // 2, head] = raised
+            shrinks[0, step // 2, head : head + 1] = shrink
+            parts.append(nn(turned[head * HEAD_DIM : (head + 1) * HEAD_DIM], raised) * shrink)
         merged = jnp.concatenate(parts, axis=0).T.astype(BF)
         for i in range(2):
             contexts[step + i][...] = merged[i * own : (i + 1) * own]
@@ -230,77 +153,159 @@
     _, blocks, own, wide = query.shape
     pairs = wide // LANES
     whole = pl.BlockSpec((1, blocks, own, LANES), lambda h, p: (seq, 0, 0, h))
-    *contexts, logs = pl.pallas_call(
+    *contexts, probs, shrinks = pl.pallas_call(
         attend_kernel,
         grid_spec=pltpu.PrefetchScalarGridSpec(
             num_scalar_prefetch=1,
             grid=(pairs,),
             in_specs=[whole] * 3,
             out_specs=[pl.BlockSpec((own, LANES), lambda h, p: (0, h))] * blocks
-            + [pl.BlockSpec((1, blocks, 2, own), lambda h, p: (h, 0, 0, 0))],
+            + [
+                pl.BlockSpec((1, blocks // 2, 2, blocks * own, 2 * own), lambda h, p: (h, 0, 0, 0, 0)),
+                pl.BlockSpec((1, blocks // 2, 2, 2 * own), lambda h, p: (h, 0, 0, 0)),
+            ],
         ),
         out_shape=[jax.ShapeDtypeStruct((own, wide), BF)] * blocks
-        + [jax.ShapeDtypeStruct((pairs, blocks, 2, own), F32)],
+        + [
+            jax.ShapeDtypeStruct((pairs, blocks // 2, 2, blocks * own, 2 * own), BF),
+            jax.ShapeDtypeStruct((pairs, blocks // 2, 2, 2 * own), F32),
+        ],
         name="attend",
     )(place, query, key, value)
-    return contexts, logs
-
-
-def attend_back_kernel(place, query, key, value, *refs):
+    return contexts, (probs, shrinks, list(contexts))
+
+
+def attend_back_kernel(place, query, key, value, probs, shrinks, *refs):
     blocks, own = query.shape[1:3]
-    pieces = refs[:blocks]
-    log_total, cosine, sine, grad_query, grad_key, grad_value = refs[blocks:]
+    contexts = refs[:blocks]
+    pieces = refs[blocks : 2 * blocks]
+    rows_in = refs[2 * blocks : 3 * blocks]
+    cosine, sine, weight, low, up, down, here, there, up_grad, low_grad, total, small, turn_keys = refs[3 * blocks :]
+    pair = pl.program_id(0)
+    last = pl.num_programs(0) - 1
+    wide = LANES * pl.num_programs(0)
     keys = key[0].reshape(blocks * own, LANES)
     values = value[0].reshape(blocks * own, LANES)
     turned = keys.T
-    grad_keys = jnp.zeros(keys.shape, F32)
-    grad_values = jnp.zeros(keys.shape, F32)
+    backs, mines, mine_grads = [], [], []
+    grad_queries = []
     for step in range(0, blocks, 2):
         spots = [place[0] ^ (step + i) for i in range(2)]
         rows = jnp.concatenate([query[0, spot] for spot in spots], axis=0)
-        outer = jnp.concatenate([pieces[step + i][...] for i in range(2)], axis=0)
+        outer = jnp.concatenate([pieces[step + i][0] for i in range(2)], axis=0).astype(F32)
+        inner = jnp.concatenate([contexts[step + i][...] for i in range(2)], axis=0).astype(F32)
+        product = (outer * inner).T
+        factors = [shrinks[0, step // 2, head : head + 1] for head in range(2)]
+        spread = jnp.concatenate([jnp.broadcast_to(f, (HEAD_DIM, 2 * own)) for f in factors], axis=0).T
+        outer = (outer * spread).astype(BF)
         parts = []
         for head in range(2):
-            mine = one_head(rows, head)
             mine_grad = one_head(outer, head)
-            scores = nt(keys, mine)
-            logs = jnp.concatenate([log_total[0, step + i, head : head + 1] for i in range(2)], axis=1)
-            probs = jnp.exp(scores - logs)
-            wide = nt(values, mine_grad)
-            mean = jnp.sum(probs * wide, axis=0, keepdims=True)
-            back = (probs * (wide - mean)).astype(BF)
+            chances = probs[0, step // 2, head]
+            half = product[head * HEAD_DIM : (head + 1) * HEAD_DIM]
+            mean = jnp.sum(half, axis=0, keepdims=True) * factors[head]
+            back = (chances.astype(F32) * (nt(values, mine_grad) - mean)).astype(BF)
             parts.append(nn(turned[head * HEAD_DIM : (head + 1) * HEAD_DIM], back))
-            grad_keys += nn(back, mine)
-            grad_values += nn(probs.astype(BF), mine_grad)
+            backs.append(back)
+            mines.append(one_head(rows, head))
+            mine_grads.append(mine_grad)
         queries = jnp.concatenate(parts, axis=0).T * HEAD_DIM**-0.5
         for i, spot in enumerate(spots):
             part = queries[i * own : (i + 1) * own]
-            grad_query[spot] = turn(part, cosine[spot], -sine[spot]).astype(BF)
+            grad_queries.append(turn(part, cosine[spot], -sine[spot]).astype(BF))
+    grad_keys = nn(jnp.concatenate(backs, axis=1), jnp.concatenate(mines, axis=0))
+    chances = [probs[0, i // 2, i % 2] for i in range(blocks)]
+    grad_values = nn(jnp.concatenate(chances, axis=1), jnp.concatenate(mine_grads, axis=0))
     for step in range(blocks):
         part = slice(step * own, (step + 1) * own)
-        grad_key[step] = turn(grad_keys[part], cosine[step], -sine[step]).astype(BF)
-        grad_value[step] = grad_values[part].astype(BF)
-
-
-def attend_back(place, query, key, value, seq, pieces, log_total, tables):
+        turn_keys[0, step] = turn(grad_keys[part], cosine[step], -sine[step]).astype(BF)
+        turn_keys[1, step] = grad_values[part].astype(BF)
+    grads = [
+        jnp.concatenate(grad_queries, axis=0),
+        jnp.concatenate([turn_keys[0, place[0] ^ step] for step in range(blocks)], axis=0),
+        jnp.concatenate([turn_keys[1, place[0] ^ step] for step in range(blocks)], axis=0),
+    ]
+    grads = jnp.concatenate(grads, axis=1)
+    firsts = [pl.multiple_of(kind * wide + pair * LANES, LANES) for kind in range(3)]
+    table = jnp.concatenate([lanes_of(weight, first, LANES, place) for first in firsts], axis=0)
+    ups = jnp.concatenate([up[0, :, pl.ds(first, LANES)] for first in firsts], axis=1)
+    downs = jnp.concatenate([down[0, step] for step in range(blocks)], axis=0)
+    more = nn(grads, table)
+    more_small = nt(grads, ups)
+    up_part = tn(downs, grads)
+    for kind in range(3):
+        up_grad[kind] = up_part[:, kind * LANES : (kind + 1) * LANES]
+
+    @pl.when(pair == 0)
+    def _():
+        total[...] = more
+        small[...] = more_small
+
+    @pl.when(pair > 0)
+    def _():
+        total[...] += more
+        small[...] += more_small
+
+    @pl.when(pair == last)
+    def _():
+        narrow = (small[...] * ADAPTER_SCALE).astype(BF)
+        low_grad[...] = tn(narrow, jnp.concatenate([piece[0] for piece in rows_in], axis=0))
+        done = total[...] + nn(narrow, low[0])
+        for step in range(blocks):
+            part = done[step * own : (step + 1) * own]
+            if step % 2:
+                there[step // 2] = part.astype(BF)
+            else:
+                here[step // 2] = part
+
+
+def attend_back(place, seq, query, key, value, kept, grads, pieces, tables, weight, low, up, down):
     _, blocks, own, wide = query.shape
+    _, rank, model = low.shape
+    tall = up.shape[2]
     pairs = wide // LANES
-    whole = pl.BlockSpec((1, blocks, own, LANES), lambda h, p: (seq, 0, 0, h))
-    column = pl.BlockSpec((blocks, own, LANES), lambda h, p: (0, 0, h))
-    table = pl.BlockSpec((blocks, own, LANES), lambda h, p: (0, 0, 0))
+    whole = lambda shape: pl.BlockSpec(shape, lambda h, p: (0,) * len(shape))
+    of_seq = lambda shape: pl.BlockSpec((1,) + shape, lambda h, p: (seq,) + (0,) * len(shape))
+    heads = pl.BlockSpec((1, blocks, own, LANES), lambda h, p: (seq, 0, 0, h))
+    probs, shrinks, contexts = kept
     return pl.pallas_call(
         attend_back_kernel,
         grid_spec=pltpu.PrefetchScalarGridSpec(
             num_scalar_prefetch=1,
             grid=(pairs,),
-            in_specs=[whole] * 3
+            in_specs=[heads] * 3
+            + [pl.BlockSpec((1,) + probs.shape[1:], lambda h, p: (h, 0, 0, 0, 0))]
+            + [pl.BlockSpec((1,) + shrinks.shape[1:], lambda h, p: (h, 0, 0, 0))]
             + [pl.BlockSpec((own, LANES), lambda h, p: (0, h))] * blocks
-            + [pl.BlockSpec((1, blocks, 2, own), lambda h, p: (h, 0, 0, 0)), table, table],
-            out_specs=[column] * 3,
+            + [pl.BlockSpec((1, own, LANES), lambda h, p: (max(seq - 1, 0), 0, h))] * blocks
+            + [of_seq((own, model))] * blocks
+            + [whole((blocks, own, LANES))] * 2
+            + [
+                whole(weight.shape),
+                of_seq((rank, model)),
+                of_seq((rank, tall)),
+                of_seq((blocks, own, rank)),
+            ],
+            out_specs=[
+                whole((blocks // 2, own, model)),
+                whole((blocks // 2, own, model)),
+                pl.BlockSpec((3, rank, LANES), lambda h, p: (0, 0, h)),
+                whole((rank, model)),
+            ],
+            scratch_shapes=[
+                pltpu.VMEM((blocks * own, model), F32),
+                pltpu.VMEM((blocks * own, rank), F32),
+                pltpu.VMEM((2, blocks, own, LANES), BF),
+            ],
         ),
-        out_shape=[jax.ShapeDtypeStruct((blocks, own, wide), BF)] * 3,
+        out_shape=[
+            jax.ShapeDtypeStruct((blocks // 2, own, model), F32),
+            jax.ShapeDtypeStruct((blocks // 2, own, model), BF),
+            jax.ShapeDtypeStruct((3, rank, wide), F32),
+            jax.ShapeDtypeStruct((rank, model), F32),
+        ],
         name="attend_back",
-    )(place, query, key, value, *pieces, log_total, *tables)
+    )(place, query, key, value, probs, shrinks, *contexts, *grads, *pieces, *tables, weight, low, up, down)
 
 
 def merge_kernel(spot, *refs, blocks, seqs):
@@ -344,71 +349,24 @@
     )(spot, *inputs)
 
 
-def merge_back_kernel(spot, *refs, blocks):
-    contexts = refs[:blocks]
-    grad_normed, middle, out_grad, down, near, far, low, up, gain = refs[blocks : blocks + 9]
-    grad_contexts = refs[blocks + 9 : 2 * blocks + 9]
-    grad_middle, low_grad, up_grad = refs[2 * blocks + 9 :]
-    normed, scale = norm_parts(middle[0])
-    total = out_grad[0].astype(F32) + norm_back(grad_normed[0], normed, scale, gain[...])
-    grad_middle[0] = total
-    rows = total.astype(BF)
-    small = (nt(rows, up[0]) * ADAPTER_SCALE).astype(BF)
-    for step, out in enumerate(grad_contexts):
-        ref = far if step // 2 else near
-        table = lanes_of(ref.at[:, pl.ds(step % 2, 1)], spot=spot)
-        out[...] = (nt(rows, table) + nn(small, low[step, 0])).astype(BF)
-        low_grad[step] = tn(small, contexts[step][...])
-    up_grad[...] = tn(down[0], rows)
-
-
-def merge_back(spot, seq, contexts, grad_normed, middle, out_grad, down, near, far, low, up, gain):
-    _, own, model = middle.shape
-    blocks, _, rank, wide = low.shape
-    row = pl.BlockSpec((1, own, model), lambda i, p: (seq, 0, 0))
-    one = full((1, own, model))
-    *grads, grad_middle, low_grad, up_grad = pl.pallas_call(
-        lambda *refs: merge_back_kernel(*refs, blocks=blocks),
-        grid_spec=pltpu.PrefetchScalarGridSpec(
-        num_scalar_prefetch=1,
-        grid=(1,),
-        in_specs=[full((own, wide))] * blocks
-        + [
-            row,
-            row,
-            row,
-            pl.BlockSpec((1, own, rank), lambda i, p: (seq, 0, 0)),
-            full(near.shape),
-            full(far.shape),
-            pl.BlockSpec((blocks, 1, rank, wide), lambda i, p: (0, seq, 0, 0)),
-            pl.BlockSpec((1, rank, model), lambda i, p: (seq, 0, 0)),
-            full((1, model)),
-        ],
-        out_specs=[full((own, wide))] * blocks
-        + [one, full((blocks, rank, wide)), full((rank, model))],
-        ),
-        out_shape=[jax.ShapeDtypeStruct((own, wide), BF)] * blocks
-        + [
-            jax.ShapeDtypeStruct((1, own, model), F32),
-            jax.ShapeDtypeStruct((blocks, rank, wide), F32),
-            jax.ShapeDtypeStruct((rank, model), F32),
-        ],
-        name="merge_back",
-    )(spot, *contexts, grad_normed, middle, out_grad, down, near, far, low, up, gain)
-    return grads, grad_middle, low_grad, up_grad
-
-
 def gated_kernel(
-    place, rows, out_grad, expand, shrink, expand_up, shrink_low, expand_low, shrink_up, mask,
-    total, grad_rows, expand_up_grad, shrink_low_grad, expand_low_grad, shrink_up_grad,
-    down, down_grad, late, late_grad, *, width, blocks
+    place, rows, out_grad, middle, expand, shrink, expand_up, shrink_low, expand_low, shrink_up, mask,
+    near, far, merge_low, merge_up, gain, merge_down, *refs, width, blocks, seqs
 ):
+    contexts = refs[: seqs * blocks]
+    (
+        result, expand_up_grad, shrink_low_grad, expand_low_grad, shrink_up_grad,
+        grad_middle, merge_low_grad, merge_up_grad,
+    ) = refs[seqs * blocks : seqs * blocks + 8]
+    firsts = refs[seqs * blocks + 8 : seqs * blocks + 8 + blocks]
+    others = refs[seqs * blocks + 8 + blocks : seqs * blocks + 8 + 2 * blocks]
+    total, grad_rows, down, down_grad, late, late_grad = refs[seqs * blocks + 8 + 2 * blocks :]
     step = pl.program_id(0)
     scaled = ADAPTER_SCALE * mask[...]
 
     @pl.when(step == 0)
     def _():
-        total[...] = jnp.zeros(total.shape, F32)
+        total[...] = middle[...]
         grad_rows[...] = jnp.zeros(grad_rows.shape, F32)
         down[...] = (nt(rows[...], expand_low[...]) * scaled).astype(BF)
         down_grad[...] = (nt(out_grad[...], shrink_up[...]) * scaled).astype(BF)
@@ -441,59 +399,97 @@
     @pl.when(step == blocks - 1)
     def _():
         small = (late[...] * scaled).astype(BF)
-        total[...] += nn(small, shrink_up[...])
+        result[...] = (total[...] + nn(small, shrink_up[...])).astype(BF)
         shrink_up_grad[...] = tn(small, out_grad[...])
         small_grad = (late_grad[...] * scaled).astype(BF)
-        grad_rows[...] += nn(small_grad, expand_low[...])
         expand_low_grad[...] = tn(small_grad, rows[...])
-
-
-def gated(place, rows, out_grad, weights, width, expand_up, shrink_low, expand_low, shrink_up, mask):
+        own = rows.shape[0] // seqs
+        for seq in range(seqs):
+            part = slice(seq * own, (seq + 1) * own)
+            normed, scale = norm_parts(middle[part])
+            grad_normed = grad_rows[part] + nn(small_grad[part], expand_low[...])
+            whole = out_grad[part].astype(F32) + norm_back(grad_normed, normed, scale, gain[...])
+            grad_middle[seq] = whole
+            low_rows = whole.astype(BF)
+            small = (nt(low_rows, merge_up[seq]) * ADAPTER_SCALE).astype(BF)
+            for move in range(blocks):
+                ref = far if move // 2 else near
+                table = lanes_of(ref.at[:, pl.ds(move % 2, 1)], spot=place)
+                out = (nt(low_rows, table) + nn(small, merge_low[move, seq])).astype(BF)
+                if seq:
+                    others[move][seq - 1] = out
+                else:
+                    firsts[move][0] = out
+                merge_low_grad[seq, move] = tn(small, contexts[seq * blocks + move][...])
+            merge_up_grad[seq] = tn(merge_down[seq], low_rows)
+
+
+def gated(
+    place, rows, out_grad, middle, weights, width, expand_up, shrink_low, expand_low, shrink_up, mask,
+    near, far, merge_low, merge_up, gain, merge_down, contexts
+):
     count, model = rows.shape
     parts, blocks, _, lane = weights.shape
+    seqs = len(contexts)
+    own, wide = contexts[0][0].shape
+    some = merge_up.shape[1]
     rank = expand_low.shape[0]
     pad = shrink_low.shape[2]
+    pieces = [piece for context in contexts for piece in context]
+    shapes = [
+        ((count, model), BF),
+        ((blocks, 2, rank, width), F32),
+        ((blocks, rank, width), F32),
+        ((rank, model), F32),
+        ((rank, model), F32),
+        ((seqs, own, model), F32),
+        ((seqs, blocks, some, wide), F32),
+        ((seqs, some, model), F32),
+    ]
+    shapes += [((1, own, wide), BF)] * blocks + [((seqs - 1, own, wide), BF)] * blocks
+    out_specs = [full_once(shape) for shape, _ in shapes]
+    out_specs[1] = pl.BlockSpec((1, 2, rank, width), lambda m, p: (m, 0, 0, 0))
+    out_specs[2] = pl.BlockSpec((1, rank, width), lambda m, p: (m, 0, 0))
     return pl.pallas_call(
-        lambda *refs: gated_kernel(*refs, width=width, blocks=blocks),
+        lambda *refs: gated_kernel(*refs, width=width, blocks=blocks, seqs=seqs),
         grid_spec=pltpu.PrefetchScalarGridSpec(
-        num_scalar_prefetch=1,
-        grid=(blocks,),
-        in_specs=[
-            full((count, model)),
-            full((count, model)),
-            pl.BlockSpec((parts, 1, 2 * width, lane), lambda m, p: (0, m, 0, 0)),
-            pl.BlockSpec((parts, 1, width, lane), lambda m, p: (0, m, 2, 0)),
-            pl.BlockSpec((1, rank, 2 * pad), lambda m, p: (p[0] ^ m, 0, 0)),
-            pl.BlockSpec((1, rank, pad), lambda m, p: (p[0] ^ m, 0, 0)),
-            full((rank, model)),
-            full((rank, model)),
-            full((count, rank)),
-        ],
-        out_specs=[
-            full((count, model)),
-            full((count, model)),
-            pl.BlockSpec((1, 2, rank, width), lambda m, p: (m, 0, 0, 0)),
-            pl.BlockSpec((1, rank, width), lambda m, p: (m, 0, 0)),
-            full((rank, model)),
-            full((rank, model)),
-        ],
-        scratch_shapes=[
-            pltpu.VMEM((count, rank), BF),
-            pltpu.VMEM((count, rank), BF),
-            pltpu.VMEM((count, rank), F32),
-            pltpu.VMEM((count, rank), F32),
-        ],
+            num_scalar_prefetch=1,
+            grid=(blocks,),
+            in_specs=[
+                full_once((count, model)),
+                full_once((count, model)),
+                full_once((count, model)),
+                pl.BlockSpec((parts, 1, 2 * width, lane), lambda m, p: (0, m, 0, 0)),
+                pl.BlockSpec((parts, 1, width, lane), lambda m, p: (0, m, 2, 0)),
+                pl.BlockSpec((1, rank, 2 * pad), lambda m, p: (p[0] ^ m, 0, 0)),
+                pl.BlockSpec((1, rank, pad), lambda m, p: (p[0] ^ m, 0, 0)),
+                full_once((rank, model)),
+                full_once((rank, model)),
+                full_once((count, rank)),
+                full_once(near.shape),
+                full_once(far.shape),
+                full_once(merge_low.shape),
+                full_once(merge_up.shape),
+                full_once(gain.shape),
+                full_once(merge_down.shape),
+            ]
+            + [full_once((own, wide))] * len(pieces),
+            out_specs=out_specs,
+            scratch_shapes=[
+                pltpu.VMEM((count, model), F32),
+                pltpu.VMEM((count, model), F32),
+                pltpu.VMEM((count, rank), BF),
+                pltpu.VMEM((count, rank), BF),
+                pltpu.VMEM((count, rank), F32),
+                pltpu.VMEM((count, rank), F32),
+            ],
         ),
-        out_shape=[
-            jax.ShapeDtypeStruct((count, model), F32),
-            jax.ShapeDtypeStruct((count, model), F32),
-            jax.ShapeDtypeStruct((blocks, 2, rank, width), F32),
-            jax.ShapeDtypeStruct((blocks, rank, width), F32),
-            jax.ShapeDtypeStruct((rank, model), F32),
-            jax.ShapeDtypeStruct((rank, model), F32),
-        ],
+        out_shape=[jax.ShapeDtypeStruct(shape, kind) for shape, kind in shapes],
         name="gated",
-    )(place, rows, out_grad, weights, weights, expand_up, shrink_low, expand_low, shrink_up, mask)
+    )(
+        place, rows, out_grad, middle, weights, weights, expand_up, shrink_low, expand_low, shrink_up, mask,
+        near, far, merge_low, merge_up, gain, merge_down, *pieces,
+    )
 
 
 def settle_early_kernel(place, got, low, shrink_up, merge_up, merge_low, expand_up, shrink_low, *, parts, blocks, sets, part, wide, width, pad):
@@ -728,27 +724,27 @@
     for seq in range(seqs):
         if seq:
             query = tie(query, context[0])
-        context, log_total = attend(spot, query, key, value, seq)
+        context, probs = attend(spot, query, key, value, seq)
         context = [context[0]] + [pair_swap(context[bit], bit) for bit in range(1, blocks)]
         contexts.append(context)
-        logs.append(log_total)
+        logs.append(probs)
     merge_far = pair_swap(merge_near, 2)
     middle, normed_mlp, merge_down = merge(
         spot, contexts, hidden, merge_near, merge_far, merge_low, merge_up, mlp_scale
     )
     (
-        shrunk,
-        grad_normed_mlp,
-        expand_up_grad,
-        shrink_low_grad,
-        expand_low_grad,
-        shrink_up_grad,
+        result, expand_up_grad, shrink_low_grad, expand_low_grad, shrink_up_grad,
+        grad_middle, merge_low_grads, merge_up_grads, *grad_contexts,
     ) = gated(
-        spot, normed_mlp.reshape(count, model), cotangent.reshape(count, model), rest_whole, width,
+        spot, normed_mlp.reshape(count, model), cotangent.reshape(count, model),
+        middle.reshape(count, model), rest_whole, width,
         expand_up, shrink_low, expand_low, shrink_up, mask,
-    )
-    result = (middle + shrunk.reshape(middle.shape)).astype(BF)
-    grad_normed_mlp = grad_normed_mlp.reshape(seqs, own, model)
+        merge_near, merge_far, merge_low, merge_up, mlp_scale, merge_down, contexts,
+    )
+    result = result.reshape(middle.shape)
+    halfway = []
+    for some in (grad_contexts[:blocks], grad_contexts[blocks:]):
+        halfway.append([some[0]] + [pair_swap(some[bit], bit) for bit in range(1, blocks)])
 
     paired = rank == 2 * parts
     everyone = ("dp", "mp")
@@ -774,30 +770,19 @@
     def tall(values):
         return values.transpose(0, 2, 1).astype(F32)
 
-    merge_low_grads, merge_up_grads, joined_low_grads, joined_up_grads = [], [], [], []
-    halfway, grad_normeds = [], []
-    for seq in range(seqs):
-        if seq:
-            grad_normed_mlp = tie(grad_normed_mlp, grad_middle)
-        if seq == 2:
-            grad_normed_mlp = tie(grad_normed_mlp, halfway[0][1][2:])
-        pieces_back, grad_middle, low_grad, up_grad = merge_back(
-            spot, seq, contexts[seq], grad_normed_mlp, middle, cotangent, merge_down,
-            merge_near, merge_far, merge_low, merge_up, mlp_scale,
-        )
-        merge_low_grads.append(low_grad)
-        merge_up_grads.append(up_grad)
-        pieces_back = [pieces_back[0]] + [pair_swap(pieces_back[bit], bit) for bit in range(1, blocks)]
-        halfway.append((grad_middle[0], pieces_back))
-
+    joined_low_grads, joined_up_grads = [], []
+    grad_normeds = []
     early = jnp.concatenate(
         [
             piece.astype(BF)
             for piece in (
                 by_block(expand_low_grad),
                 by_block(shrink_up_grad),
-                by_block(jnp.concatenate(merge_up_grads)),
-                jnp.take(jnp.concatenate(merge_low_grads, axis=1), place ^ jnp.arange(blocks), axis=0),
+                by_block(merge_up_grads.reshape(seqs * rank, model)),
+                jnp.take(
+                    merge_low_grads.transpose(1, 0, 2, 3).reshape(blocks, seqs * rank, wide),
+                    place ^ jnp.arange(blocks), axis=0,
+                ),
                 jnp.pad(expand_up_grad[:, 0], side),
                 jnp.pad(expand_up_grad[:, 1], side),
                 jnp.pad(shrink_low_grad, side),
@@ -807,29 +792,30 @@
     )
     early_width = early.shape[2]
 
-    early = tie(early, halfway[0][1][2])
+    early, halfway[0] = lax.optimization_barrier((early, halfway[0]))
     early = swap_all(ranks_out(early).reshape(owners, seqs, -1), everyone)
     chip, far = None, None
     for seq in range(seqs):
-        grad_middle, pieces_back = halfway[seq]
+        pieces_back = list(halfway[min(seq, 1)])
         if seq:
             pieces_back[0] = tie(pieces_back[0], here)
-        grads = list(attend_back(spot, query, key, value, seq, pieces_back, logs[seq], tables))
+        here, there, up_grad, low_grad = attend_back(
+            spot, seq, query, key, value, logs[seq], pieces_back, pieces, tables,
+            joined_whole, joined_low, joined_up, joined_down,
+        )
         if seq == 0:
-            grads[0], halfway[1], halfway[2] = lax.optimization_barrier((grads[0], halfway[1], halfway[2]))
+            there, halfway[1] = lax.optimization_barrier((there, halfway[1]))
         if seq == 1:
-            grads[0], far, early = lax.optimization_barrier((grads[0], far, early))
+            there, far, early = lax.optimization_barrier((there, far, early))
             early = jnp.dot(choose, early.reshape(owners * seqs, -1), preferred_element_type=F32)
             if paired:
                 early = jnp.concatenate([early[:, :early_width], early[:, early_width:]], axis=0)
             shared = lax.all_gather(early.astype(BF), everyone, axis=0)
         if seq == 2:
-            grads[0], far = lax.optimization_barrier((grads[0], far))
+            there, far = lax.optimization_barrier((there, far))
         if seq:
             grad_normeds.append(chip + far.astype(F32))
-        small_grad, up_grad, low_grad = joined_grads(spot, seq, grads, pieces, joined_up, joined_down)
-        here, there = project_back(spot, seq, grads, small_grad, joined_whole, joined_low)
-        joined_up_grads.append(up_grad)
+        joined_up_grads.append(up_grad.transpose(1, 0, 2).reshape(rank, 3 * wide))
         joined_low_grads.append(low_grad)
         there = pair_swap(there, 1).astype(F32)
         chip, give = here[0] + there[0], (here[1] + there[1]).astype(BF)
@@ -847,7 +833,6 @@
     late, far = lax.optimization_barrier((swap_all(late, everyone), far))
     late = late.reshape(parts, blocks, seqs, some, -1)
     grad_normeds.append(chip + far.astype(F32))
-    grad_middle = jnp.stack([each[0] for each in halfway])
     grad_hidden = grad_middle + norm_back(jnp.stack(grad_normeds), first_normed, first_scale, attn_scale)
     late_low = late[..., :low_size].reshape(owners * seqs, -1)
     late_up = late[..., low_size:].transpose(1, 0, 2, 3, 4).reshape(blocks, parts * seqs, -1)

time: 443 us -> 409 us (0.923)
  Pallas kernels: 212 us -> 186 us
  waiting for transfers between devices: 99.1 us -> 91 us
    pallas_call x9 -> x0, Pallas kernels: 52.1 us -> none  [the longest x3 19.7 us: project_back(): pl.pallas_call(project_back_kernel, grid_spec=pltpu.PrefetchScalarGridSpe...]
    pallas_call x3, Pallas kernels: 50 us -> 62 us  [attend_back(): pl.pallas_call(attend_back_kernel, grid_spec=pltpu.PrefetchScalarGridSpec...]
    pallas_call x1, Pallas kernels: 50.7 us -> 57.9 us  [gated(): pl.pallas_call(lambda *refs: gated_kernel(*refs, width=width, blocks=bloc...]
    pallas_call x3, Pallas kernels: 29.8 us -> 36.6 us  [attend(): pl.pallas_call(attend_kernel, grid_spec=pltpu.PrefetchScalarGridSpec(num_...]
    ppermute x32 -> x29, waiting for transfers between devices: 72.3 us -> 66.3 us  [pair_swap(): return lax.ppermute(values, 'mp', [(i, i ^ bit) for i in range(size)])]
    unnamed x178 -> x142, local copies, waits for them, and re-layouts: 11 us -> 8.37 us
    ppermute x32 -> x29, starting transfers between devices: 20.3 us -> 18.3 us  [pair_swap(): return lax.ppermute(values, 'mp', [(i, i ^ bit) for i in range(size)])]
  transfers between devices with their start and end apart: 41 -> 38, of which waited for: 18 -> 18; matrix products, arithmetic and copies ran while one was open for 12% -> 12% of each run, Pallas kernels for 30% -> 31%
where the time goes in v3:
time: 409 us; the launch traced here: 405 us
  Pallas kernels  186 us (45%)
  waiting for transfers between devices  91 us (22%)
  starting transfers between devices  40.9 us (10%)
  local copies, waits for them, and re-layouts  36.2 us (9%)
  other arithmetic  33.5 us (8%)
  between operations  15.4 us (4%)
    ppermute x29, waiting for transfers between devices, pair_swap(): return lax.ppermute(values, 'mp', [(i, i ^ bit) for i in range(size)])  66.3 us
    pallas_call x3, Pallas kernels, attend_back(): pl.pallas_call(attend_back_kernel, grid_spec=pltpu.PrefetchScalarGridSpec...  62 us
    pallas_call x1, Pallas kernels, gated(): pl.pallas_call(lambda *refs: gated_kernel(*refs, width=width, blocks=bloc...  57.9 us
    pallas_call x3, Pallas kernels, attend(): pl.pallas_call(attend_kernel, grid_spec=pltpu.PrefetchScalarGridSpec(num_...  36.6 us
    ppermute x29, starting transfers between devices, pair_swap(): return lax.ppermute(values, 'mp', [(i, i ^ bit) for i in range(size)])  18.3 us
    all_to_all x3, starting transfers between devices, swap_all(): return lax.all_to_all(values, axes, 0, 0, tiled=True)  15.3 us
    all_to_all x3, waiting for transfers between devices, swap_all(): return lax.all_to_all(values, axes, 0, 0, tiled=True)  14.5 us
    pallas_call x1, Pallas kernels, project(): pl.pallas_call(lambda *refs: project_kernel(*refs, wide=wide), grid_spec=...  13.9 us
  transfers between devices with their start and end apart: 38, of which 18 were waited for; matrix products, arithmetic and copies ran while one was open for 12% of the time, Pallas kernels for 31%

profile of v3, /device:TPU:0, one launch (start us, length us, event | category | flops | bytes accessed | tf_op | source)
XLA Modules:
  0.0 404.6 jit_solution(9530199234278462144)
XLA Ops:
  7.3 1.9 pad_maximum_fusion.3
  13.6 2.9 collective-permute-start.3
  17.7 1.6 collective-permute-start.6
  19.3 2.6 collective-permute-start.7
  21.8 1.3 collective-permute-start.8
  25.8 1.7 fusion.5.refs_1_.refs_8_
  27.6 1.5 gather_fusion.1
  29.7 1.2 gather_fusion
  30.9 1.2 gather_fusion.6
  32.1 2.3 gather_fusion.7
  34.3 2.1 gather_fusion.5
  36.5 3.3 multiply_sine_fusion
  40.3 9.5 %collective-permute-done.7 = bf16[1032,128]{1,0:T(8,128)(2,1)S(1)} collective-permute-done((bf16[1032,128]{1,0:T(8,128)(2,1)}, bf16[1032,128]{1,0:T(8,128)(2,1)S(1)}, u32[]{:S(2)}, u32[]{:S(2)}) %collective-permute-start.7) | collective-permute-done | bytes 264224 | tf_op jit(solution)/shard_map/ppermute | solution.py:596
  50.6 1.2 pad_maximum_fusion
  51.8 1.6 collective-permute-start.9
  53.5 1.0 constant_dynamic-update-slice_fusion.1
  56.9 33.6 %collective-permute-done.1.refs_3_.refs_10_ = bf16[3,256,1024]{2,1,0:T(8,128)(2,1)} collective-permute-done((bf16[3,256,1024]{2,1,0:T(8,128)(2,1)}, bf16[3,256,1024]{2,1,0:T(8,128)(2,1)}, u32[]{:S(2)}, u32[]{:S(2)}) %collective-permute-start.1) | collective-permute-done | bytes 1572896 | tf_op jit(solution)/shard_map/ppermute | solution.py:570
  91.2 3.4 collective-permute-done.19
  96.0 13.9 %project.1 = (bf16[3,4,256,256]{3,2,1,0:T(8,128)(2,1)}, bf16[3,4,256,256]{3,2,1,0:T(8,128)(2,1)}, bf16[3,4,256,256]{3,2,1,0:T(8,128)(2,1)}, bf16[3,4,256,16]{3,2,1,0:T(8,128)(2,1)}) custom-call(s32[9]{0:T(128)} %pad_add_fusion.refs_0_.place, bf16[3,256,1024]{2,1,0:T(8,128)(2,1)} %fusion.5.refs_1_.refs_8_, ...), custom_call_target="tpu_custom_call" | custom-call | tf_op jit(solution)/shard_map/project/pallas_call | solution.py:103
  109.9 12.0 %attend.3 = (bf16[256,256]{1,0:T(8,128)(2,1)}, bf16[256,256]{1,0:T(8,128)(2,1)}, bf16[256,256]{1,0:T(8,128)(2,1)}, bf16[256,256]{1,0:T(8,128)(2,1)}, bf16[2,2,2,...) custom-call(s32[9]{0:T(128)} %pad_add_fusion.refs_0_.place, bf16[3,4,256,256]{3,2,1,0:T(8,128)(2,1)} %get-tuple-element.136.query, ...), custom_call_target="tpu_custom_call" | custom-call | tf_op jit(solution)/shard_map/attend/pallas_call | solution.py:156
  121.9 11.9 %attend.4 = (bf16[256,256]{1,0:T(8,128)(2,1)}, bf16[256,256]{1,0:T(8,128)(2,1)}, bf16[256,256]{1,0:T(8,128)(2,1)}, bf16[256,256]{1,0:T(8,128)(2,1)}, bf16[2,2,2,...) custom-call(s32[9]{0:T(128)} %pad_add_fusion.refs_0_.place, bf16[3,4,256,256]{3,2,1,0:T(8,128)(2,1)} %get-tuple-element.136.query, ...), custom_call_target="tpu_custom_call" | custom-call | tf_op jit(solution)/shard_map/attend/pallas_call | solution.py:156
  133.8 12.7 %attend.5 = (bf16[256,256]{1,0:T(8,128)(2,1)}, bf16[256,256]{1,0:T(8,128)(2,1)}, bf16[256,256]{1,0:T(8,128)(2,1)}, bf16[256,256]{1,0:T(8,128)(2,1)}, bf16[2,2,2,...) custom-call(s32[9]{0:T(128)} %pad_add_fusion.refs_0_.place, bf16[3,4,256,256]{3,2,1,0:T(8,128)(2,1)} %get-tuple-element.136.query, ...), custom_call_target="tpu_custom_call" | custom-call | tf_op jit(solution)/shard_map/attend/pallas_call | solution.py:156
  146.5 1.5 collective-permute-start.17
  148.8 1.5 collective-permute-start.14
  150.4 2.7 collective-permute-done.17.refs_11_.refs_27_
  153.1 1.9 collective-permute-done.18.refs_12_.refs_28_
  155.0 1.4 collective-permute-start.11
  156.5 1.1 collective-permute-start.12
  158.7 1.9 collective-permute-done.15.refs_8_.refs_24_
  160.6 3.7 collective-permute-done.11.refs_3_.refs_19_
  164.3 1.9 collective-permute-done.12.refs_4_.refs_20_
  166.9 8.3 %merge.1 = (f32[3,256,1024]{2,1,0:T(8,128)}, bf16[3,256,1024]{2,1,0:T(8,128)(2,1)}, bf16[3,256,16]{2,1,0:T(8,128)(2,1)}) custom-call(s32[9]{0:T(128)} %pad_add_fusion.refs_0_.place, bf16[256,256]{1,0:T(8,128)(2,1)} %get-tuple-element.127.refs_1_.refs_17_.refs_0_, bf16[256,256]{1,0:T(8,128)(2,1)} %copy-done.32, bf16[256,256]{1,0:T(8,128)(2,1)} %copy-done.33, ...), custom_call_target="tpu_custom_call" | custom-call | tf_op jit(solution)/shard_map/merge/pallas_call | solution.py:339
  175.1 57.9 %gated.1 = (bf16[768,1024]{1,0:T(8,128)(2,1)}, f32[4,2,48,656]{3,2,1,0:T(8,128)}, f32[4,48,656]{2,1,0:T(8,128)}, f32[48,1024]{1,0:T(8,128)}, f32[48,1024]{1,0:T(...) custom-call(s32[9]{0:T(128)} %pad_add_fusion.refs_0_.place, ...), custom_call_target="tpu_custom_call" | custom-call | tf_op jit(solution)/shard_map/gated/pallas_call | solution.py:453
  234.0 1.0 convert_element_type.161
  237.0 1.3 slice_bitcast_fusion
  238.6 1.5 collective-permute-start.22
  241.1 3.9 collective-permute-done.22.refs_6_
  245.0 1.4 collective-permute-done.23.refs_7_
  248.3 2.3 copy.88
  250.6 3.6 all-to-all-start
  254.5 1.5 collective-permute-start.25
  256.1 20.5 %attend_back.3 = (f32[2,256,1024]{2,1,0:T(8,128)}, bf16[2,256,1024]{2,1,0:T(8,128)(2,1)}, f32[3,16,256]{2,1,0:T(8,128)}, f32[16,1024]{1,0:T(8,128)}) custom-call(s32[9]{0:T(128)} %pad_add_fusion.refs_0_.place, bf16[3,4,256,256]{3,2,1,0:T(8,128)(2,1)} %get-tuple-element.136.query, bf16[3,4,256,256]{3,2,1,0:T(8,128)(2,1)} %get-tuple-element.125.key, ...), custom_call_target="tpu_custom_call" | custom-call | tf_op jit(solution)/shard_map/attend_back/pallas_call | solution.py:271
  276.7 1.0 collective-permute-done.25.refs_6_
  277.7 5.8 %collective-permute-done.26.refs_7_ = bf16[2,256,256]{2,1,0:T(8,128)(2,1)S(1)} collective-permute-done((bf16[2,256,256]{2,1,0:T(8,128)(2,1)S(1)}, bf16[2,256,256]{2,1,0:T(8,128)(2,1)S(1)}, u32[]{:S(2)}, u32[]{:S(2)}) %collective-permute-start.26) | collective-permute-done | bytes 262176 | tf_op jit(solution)/shard_map/ppermute | solution.py:570
  284.2 2.5 collective-permute-done.27
  290.0 20.6 %attend_back.4 = (f32[2,256,1024]{2,1,0:T(8,128)}, bf16[2,256,1024]{2,1,0:T(8,128)(2,1)}, f32[3,16,256]{2,1,0:T(8,128)}, f32[16,1024]{1,0:T(8,128)}) custom-call(s32[9]{0:T(128)} %pad_add_fusion.refs_0_.place, bf16[3,4,256,256]{3,2,1,0:T(8,128)(2,1)} %get-tuple-element.136.query, bf16[3,4,256,256]{3,2,1,0:T(8,128)(2,1)} %get-tuple-element.125.key, ...), custom_call_target="tpu_custom_call" | custom-call | tf_op jit(solution)/shard_map/attend_back/pallas_call | solution.py:271
  310.6 4.2 %reshape.407 = bf16[96,6656]{1,0:T(8,128)(2,1)} reshape(bf16[32,3,6656]{2,1,0:T(4,128)(2,1)} %all-to-all-done) | data formatting | bytes 2555904 | tf_op jit(solution)/shard_map/reshape | solution.py:810
  314.8 1.6 convolution_convert_fusion
  317.3 2.1 collective-permute-done.29
  319.6 1.3 copy-done.7
  321.1 1.7 collective-permute-start.30
  322.8 20.9 %attend_back.5 = (f32[2,256,1024]{2,1,0:T(8,128)}, bf16[2,256,1024]{2,1,0:T(8,128)(2,1)}, f32[3,16,256]{2,1,0:T(8,128)}, f32[16,1024]{1,0:T(8,128)}) custom-call(s32[9]{0:T(128)} %pad_add_fusion.refs_0_.place, bf16[3,4,256,256]{3,2,1,0:T(8,128)(2,1)} %get-tuple-element.136.query, bf16[3,4,256,256]{3,2,1,0:T(8,128)(2,1)} %get-tuple-element.125.key, ...), custom_call_target="tpu_custom_call" | custom-call | tf_op jit(solution)/shard_map/attend_back/pallas_call | solution.py:271
  348.0 1.4 copy-done.9
  352.1 5.9 %all-to-all-start.1 = ((bf16[32,6,448]{2,1,0:T(8,128)(2,1)}), bf16[32,6,448]{2,1,0:T(8,128)(2,1)S(1)}, u32[]{:S(2)}, u32[]{:S(2)}) async-start(bf16[32,6,448]{2,1,0:T(8,128)(2,1)} %copy.92), calls=%async_computation.1 | async-start | bytes 524288 | tf_op jit(solution)/shard_map/all_to_all | solution.py:578
  358.0 1.8 fusion.24
  360.2 1.5 fusion.20
  361.7 10.3 %all-to-all-done.1 = bf16[32,6,448]{2,1,0:T(8,128)(2,1)S(1)} async-done(((bf16[32,6,448]{2,1,0:T(8,128)(2,1)}), bf16[32,6,448]{2,1,0:T(8,128)(2,1)S(1)}, u32[]{:S(2)}, u32[]{:S(2)}) %all-to-all-start.1) | async-done | bytes 172064 | tf_op jit(solution)/shard_map/all_to_all | solution.py:578
  373.9 5.9 %all-to-all-start.2 = ((bf16[32,16,448]{2,1,0:T(8,128)(2,1)}), bf16[32,16,448]{2,1,0:T(8,128)(2,1)}, u32[]{:S(2)}, u32[]{:S(2)}) async-start(bf16[32,16,448]{2,1,0:T(8,128)(2,1)} %bitcast.66), calls=%async_computation.2 | async-start | bytes 1048576 | tf_op jit(solution)/shard_map/all_to_all | solution.py:578
  379.8 2.1 fusion.16
  382.0 1.1 fusion.25
  383.9 2.1 fusion.10
  386.0 5.0 %settle_early.1 = (f32[8,16,1024]{2,1,0:T(8,128)}, f32[8,16,1024]{2,1,0:T(8,128)}, f32[8,16,1024]{2,1,0:T(8,128)}, f32[8,16,256]{2,1,0:T(8,128)}, f32[8,16,2,656]{3,2,1,0:T(2,128)}, /*index=5*/f32[8,16,656]{2,1,0:T(8,128)}) custom-call(s32[9]{0:T(128)} %pad_add_fusion.refs_0_.place, bf16[32,16,3328]{2,1,0:T(8,128)(2,1)} %all-gather.5.cloned.1.call-done.refs_1_), custom_call_target="tpu_custom_call" | custom-call | tf_op jit(solution)/shard_map/settle_early/pallas_call | solution.py:524
  391.0 4.2 %all-to-all-done.2.refs_0_ = bf16[32,16,448]{2,1,0:T(8,128)(2,1)} async-done(((bf16[32,16,448]{2,1,0:T(8,128)(2,1)}), bf16[32,16,448]{2,1,0:T(8,128)(2,1)}, u32[]{:S(2)}, u32[]{:S(2)}) %all-to-all-start.2) | async-done | bytes 458784 | tf_op jit(solution)/shard_map/all_to_all | solution.py:578
  395.3 2.3 settle_late.1
  (283 shorter events, 38.9 us)
Async XLA Ops:
  7.2 167.9 %all-gather.3.cloned.1.call-start = ((), (), s32[]{:S(2)}) async-start(), calls=%async_computation.3 | async-start | bytes 16625664 | tf_op jit(solution)/shard_map/all_gather | solution.py:647
  9.2 7.4 %copy-start.38 = (bf16[128,3,256]{2,0,1:T(8,128)(2,1)S(1)}, bf16[128,3,256]{2,0,1:T(8,128)(2,1)}, u32[]{:S(2)}) copy-start(bf16[128,3,256]{2,0,1:T(8,128)(2,1)} %param.24) | copy-start | bytes 589828
  9.2 7.5 %copy-start.52 = (bf16[128,256]{1,0:T(8,128)(2,1)S(1)}, bf16[128,256]{1,0:T(8,128)(2,1)}, u32[]{:S(2)}) copy-start(bf16[128,256]{1,0:T(8,128)(2,1)} %param.25) | copy-start | bytes 196612
  10.8 12.4 %copy-start.58 = (bf16[1024]{0:T(1024)(128)(2,1)S(1)}, bf16[1024]{0:T(1024)(128)(2,1)}, u32[]{:S(2)}) copy-start(bf16[1024]{0:T(1024)(128)(2,1)} %param.22) | copy-start | bytes 6148
  10.9 12.4 %copy-start.2 = (bf16[3,256,1024]{2,1,0:T(8,128)(2,1)S(1)}, bf16[3,256,1024]{2,1,0:T(8,128)(2,1)}, u32[]{:S(2)}) copy-start(bf16[3,256,1024]{2,1,0:T(8,128)(2,1)} %refs_13_.1) | copy-start | bytes 4718596
  13.6 26.2 %collective-permute-start.3 = (bf16[3,16,2560]{2,1,0:T(8,128)(2,1)}, bf16[3,16,2560]{2,1,0:T(8,128)(2,1)S(1)}, u32[]{:S(2)}, u32[]{:S(2)}) collective-permute-start(bf16[3,16,2560]{2,1,0:T(8,128)(2,1)} %fusion.37), channel_id=1, source_target_pairs={{0,2},{1,3},{2,0},{3,1},{4,6},{5,7},{6,4},{7,5},{8,10},{9,11},{10,... | collective-permute-start | bytes 737288 | tf_op jit(solution)/shard_map/ppermute | solution.py:570
  16.6 38.0 %collective-permute-start.2 = (bf16[3,16,2560]{2,1,0:T(8,128)(2,1)}, bf16[3,16,2560]{2,1,0:T(8,128)(2,1)S(1)}, u32[]{:S(2)}, u32[]{:S(2)}) collective-permute-start(bf16[3,16,2560]{2,1,0:T(8,128)(2,1)} %fusion.37), channel_id=1, source_target_pairs={{0,1},{1,0},{2,3},{3,2},{4,5},{5,4},{6,7},{7,6},{8,9},{9,8},{10,11... | collective-permute-start | bytes 737288 | tf_op jit(solution)/shard_map/ppermute | solution.py:570
  17.7 22.6 %collective-permute-start.6 = (bf16[1032,128]{1,0:T(8,128)(2,1)}, bf16[1032,128]{1,0:T(8,128)(2,1)S(1)}, u32[]{:S(2)}, u32[]{:S(2)}) collective-permute-start(bf16[1032,128]{1,0:T(8,128)(2,1)} %get-tuple-element.221), channel_id=1, source_target_pairs={{0,8},{4,12},{8,16},{12,20},{16,24},{20,28},{24,0},{28,4},{1,9},{5... | collective-permute-start | bytes 792584 | tf_op jit(solution)/shard_map/ppermute | solution.py:596
  19.3 30.6 %collective-permute-start.7 = (bf16[1032,128]{1,0:T(8,128)(2,1)}, bf16[1032,128]{1,0:T(8,128)(2,1)S(1)}, u32[]{:S(2)}, u32[]{:S(2)}) collective-permute-start(bf16[1032,128]{1,0:T(8,128)(2,1)} %get-tuple-element.221), channel_id=1, source_target_pairs={{0,16},{4,20},{8,24},{12,28},{16,0},{20,4},{24,8},{28,12},{1,17},{... | collective-permute-start | bytes 792584 | tf_op jit(solution)/shard_map/ppermute | solution.py:596
  21.8 28.8 %collective-permute-start.8 = (bf16[1032,128]{1,0:T(8,128)(2,1)}, bf16[1032,128]{1,0:T(8,128)(2,1)}, u32[]{:S(2)}, u32[]{:S(2)}) collective-permute-start(bf16[1032,128]{1,0:T(8,128)(2,1)} %get-tuple-element.221), channel_id=1, source_target_pairs={{0,24},{4,28},{8,0},{12,4},{16,8},{20,12},{24,16},{28,20},{1,25},{... | collective-permute-start | bytes 792584 | tf_op jit(solution)/shard_map/ppermute | solution.py:596
  32.0 21.4 %copy-start.4 = (bf16[8,1032,128]{2,1,0:T(8,128)(2,1)S(1)}, bf16[8,1032,128]{2,1,0:T(8,128)(2,1)}, u32[]{:S(2)}) copy-start(bf16[8,1032,128]{2,1,0:T(8,128)(2,1)} %constant_dynamic-update-slice_fusion.4) | copy-start | bytes 6340612
  39.8 50.7 %collective-permute-start.1 = (bf16[3,256,1024]{2,1,0:T(8,128)(2,1)}, bf16[3,256,1024]{2,1,0:T(8,128)(2,1)}, u32[]{:S(2)}, u32[]{:S(2)}) collective-permute-start(bf16[3,256,1024]{2,1,0:T(8,128)(2,1)} %fusion.5.refs_1_.refs_8_), channel_id=1, source_target_pairs={{0,2},{1,3},{2,0},{3,1},{4,6},{5,7},{6,4},{7,5},{8,10},{9,11},{10,... | collective-permute-start | bytes 4718600 | tf_op jit(solution)/shard_map/ppermute | solution.py:570
  40.3 55.7 %collective-permute-start = (bf16[3,256,1024]{2,1,0:T(8,128)(2,1)}, bf16[3,256,1024]{2,1,0:T(8,128)(2,1)}, u32[]{:S(2)}, u32[]{:S(2)}) collective-permute-start(bf16[3,256,1024]{2,1,0:T(8,128)(2,1)} %fusion.5.refs_1_.refs_8_), channel_id=1, source_target_pairs={{0,1},{1,0},{2,3},{3,2},{4,5},{5,4},{6,7},{7,6},{8,9},{9,8},{10,11... | collective-permute-start | bytes 4718600 | tf_op jit(solution)/shard_map/ppermute | solution.py:570
  49.8 4.7 %collective-permute-start.4 = (bf16[3,16,2560]{2,1,0:T(8,128)(2,1)S(1)}, bf16[3,16,2560]{2,1,0:T(8,128)(2,1)S(1)}, u32[]{:S(2)}, u32[]{:S(2)}) collective-permute-start(bf16[3,16,2560]{2,1,0:T(8,128)(2,1)S(1)} %collective-permute-done.3), channel_id=1, source_target_pairs={{0,1},{1,0},{2,3},{3,2},{4,5},{5,4},{6,7},{7,6},{8,9},{9,8},{10,11... | collective-permute-start | bytes 737288 | tf_op jit(solution)/shard_map/ppermute | solution.py:570
  51.8 38.7 %collective-permute-start.9 = (bf16[4,1032,128]{2,1,0:T(8,128)(2,1)S(1)}, bf16[4,1032,128]{2,1,0:T(8,128)(2,1)S(1)}, u32[]{:S(2)}, u32[]{:S(2)}) collective-permute-start(bf16[4,1032,128]{2,1,0:T(8,128)(2,1)S(1)} %pad_maximum_fusion), channel_id=1, source_target_pairs={{0,4},{4,0},{8,12},{12,8},{16,20},{20,16},{24,28},{28,24},{1,5},{5... | collective-permute-start | bytes 3170312 | tf_op jit(solution)/shard_map/ppermute | solution.py:598
  90.5 5.5 %collective-permute-start.5 = (bf16[3,256,1024]{2,1,0:T(8,128)(2,1)}, bf16[3,256,1024]{2,1,0:T(8,128)(2,1)}, u32[]{:S(2)}, u32[]{:S(2)}) collective-permute-start(bf16[3,256,1024]{2,1,0:T(8,128)(2,1)} %collective-permute-done.1.refs_3_.refs_10_), channel_id=1, source_target_pairs={{0,1},{1,0},{2,3},{3,2},{4,5},{5,4},{6,7},{7,6},{8,9},{9,8},{10,11... | collective-permute-start | bytes 4718600 | tf_op jit(solution)/shard_map/ppermute | solution.py:570
  90.7 4.0 collective-permute-start.19
  94.7 15.1 %copy-start.6 = (bf16[8,2,256,128]{3,2,1,0:T(8,128)(2,1)}, bf16[8,2,256,128]{3,2,1,0:T(8,128)(2,1)S(1)}, u32[]{:S(2)}) copy-start(bf16[8,2,256,128]{3,2,1,0:T(8,128)(2,1)S(1)} %pad_maximum_fusion.1.refs_14_.refs_11_) | copy-start | bytes 3145732
  94.7 54.0 %collective-permute-start.20 = (bf16[8,2,256,128]{3,2,1,0:T(8,128)(2,1)S(1)}, bf16[8,2,256,128]{3,2,1,0:T(8,128)(2,1)}, u32[]{:S(2)}, u32[]{:S(2)}) collective-permute-start(bf16[8,2,256,128]{3,2,1,0:T(8,128)(2,1)S(1)} %pad_maximum_fusion.1.refs_14_.refs_11_), channel_id=1, source_target_pairs={{0,2},{1,3},{2,0},{3,1},{4,6},{5,7},{6,4},{7,5},{8,10},{9,11},{10,... | collective-permute-start | bytes 3145736 | tf_op jit(solution)/shard_map/ppermute | solution.py:570
  133.8 14.6 %copy-start.39 = (bf16[256,256]{1,0:T(8,128)(2,1)S(1)}, bf16[256,256]{1,0:T(8,128)(2,1)}, u32[]{:S(2)}) copy-start(bf16[256,256]{1,0:T(8,128)(2,1)} %get-tuple-element.133.refs_1_) | copy-start | bytes 393220
  133.8 15.0 %copy-start.40 = (bf16[256,256]{1,0:T(8,128)(2,1)S(1)}, bf16[256,256]{1,0:T(8,128)(2,1)}, u32[]{:S(2)}) copy-start(bf16[256,256]{1,0:T(8,128)(2,1)} %get-tuple-element.134.refs_2_) | copy-start | bytes 393220
  133.8 16.5 %copy-start.41 = (bf16[256,256]{1,0:T(8,128)(2,1)S(1)}, bf16[256,256]{1,0:T(8,128)(2,1)}, u32[]{:S(2)}) copy-start(bf16[256,256]{1,0:T(8,128)(2,1)} %get-tuple-element.135.refs_3_) | copy-start | bytes 393220
  133.8 19.3 %copy-start.42 = (bf16[256,256]{1,0:T(8,128)(2,1)S(1)}, bf16[256,256]{1,0:T(8,128)(2,1)}, u32[]{:S(2)}) copy-start(bf16[256,256]{1,0:T(8,128)(2,1)} %get-tuple-element.128.refs_1_) | copy-start | bytes 393220
  133.8 21.2 %copy-start.43 = (bf16[256,256]{1,0:T(8,128)(2,1)S(1)}, bf16[256,256]{1,0:T(8,128)(2,1)}, u32[]{:S(2)}) copy-start(bf16[256,256]{1,0:T(8,128)(2,1)} %get-tuple-element.129.refs_2_) | copy-start | bytes 393220
  133.8 22.6 %copy-start.44 = (bf16[256,256]{1,0:T(8,128)(2,1)S(1)}, bf16[256,256]{1,0:T(8,128)(2,1)}, u32[]{:S(2)}) copy-start(bf16[256,256]{1,0:T(8,128)(2,1)} %get-tuple-element.130.refs_3_) | copy-start | bytes 393220
  133.8 23.7 %copy-start.59 = (bf16[1024]{0:T(1024)(128)(2,1)S(1)}, bf16[1024]{0:T(1024)(128)(2,1)}, u32[]{:S(2)}) copy-start(bf16[1024]{0:T(1024)(128)(2,1)} %param.23) | copy-start | bytes 6148
  146.5 3.8 collective-permute-start.16
  146.5 6.6 %collective-permute-start.17 = (bf16[256,256]{1,0:T(8,128)(2,1)}, bf16[256,256]{1,0:T(8,128)(2,1)S(1)}, u32[]{:S(2)}, u32[]{:S(2)}) collective-permute-start(bf16[256,256]{1,0:T(8,128)(2,1)} %get-tuple-element.139.refs_2_), channel_id=1, source_target_pairs={{0,2},{1,3},{2,0},{3,1},{4,6},{5,7},{6,4},{7,5},{8,10},{9,11},{10,... | collective-permute-start | bytes 393224 | tf_op jit(solution)/shard_map/ppermute | solution.py:570
  148.1 6.9 %collective-permute-start.18 = (bf16[256,256]{1,0:T(8,128)(2,1)}, bf16[256,256]{1,0:T(8,128)(2,1)S(1)}, u32[]{:S(2)}, u32[]{:S(2)}) collective-permute-start(bf16[256,256]{1,0:T(8,128)(2,1)} %get-tuple-element.140.refs_3_), channel_id=1, source_target_pairs={{0,3},{1,2},{2,1},{3,0},{4,7},{5,6},{6,5},{7,4},{8,11},{9,10},{10,... | collective-permute-start | bytes 393224 | tf_op jit(solution)/shard_map/ppermute | solution.py:570
  148.4 8.1 %collective-permute-start.13 = (bf16[256,256]{1,0:T(8,128)(2,1)S(1)}, bf16[256,256]{1,0:T(8,128)(2,1)S(1)}, u32[]{:S(2)}, u32[]{:S(2)}) collective-permute-start(bf16[256,256]{1,0:T(8,128)(2,1)S(1)} %copy-done.39), channel_id=1, source_target_pairs={{0,1},{1,0},{2,3},{3,2},{4,5},{5,4},{6,7},{7,6},{8,9},{9,8},{10,11... | collective-permute-start | bytes 393224 | tf_op jit(solution)/shard_map/ppermute | solution.py:570
  148.8 9.9 %collective-permute-start.14 = (bf16[256,256]{1,0:T(8,128)(2,1)S(1)}, bf16[256,256]{1,0:T(8,128)(2,1)S(1)}, u32[]{:S(2)}, u32[]{:S(2)}) collective-permute-start(bf16[256,256]{1,0:T(8,128)(2,1)S(1)} %copy-done.40), channel_id=1, source_target_pairs={{0,2},{1,3},{2,0},{3,1},{4,6},{5,7},{6,4},{7,5},{8,10},{9,11},{10,... | collective-permute-start | bytes 393224 | tf_op jit(solution)/shard_map/ppermute | solution.py:570
  150.3 15.9 %copy-start.26 = (bf16[256,256]{1,0:T(8,128)(2,1)}, bf16[256,256]{1,0:T(8,128)(2,1)S(1)}, u32[]{:S(2)}) copy-start(bf16[256,256]{1,0:T(8,128)(2,1)S(1)} %collective-permute-done.16.refs_10_.refs_26_) | copy-start | bytes 393220
  150.3 10.3 %collective-permute-start.15 = (bf16[256,256]{1,0:T(8,128)(2,1)S(1)}, bf16[256,256]{1,0:T(8,128)(2,1)S(1)}, u32[]{:S(2)}, u32[]{:S(2)}) collective-permute-start(bf16[256,256]{1,0:T(8,128)(2,1)S(1)} %copy-done.41), channel_id=1, source_target_pairs={{0,3},{1,2},{2,1},{3,0},{4,7},{5,6},{6,5},{7,4},{8,11},{9,10},{10,... | collective-permute-start | bytes 393224 | tf_op jit(solution)/shard_map/ppermute | solution.py:570
  153.1 13.1 %copy-start.27 = (bf16[256,256]{1,0:T(8,128)(2,1)}, bf16[256,256]{1,0:T(8,128)(2,1)S(1)}, u32[]{:S(2)}) copy-start(bf16[256,256]{1,0:T(8,128)(2,1)S(1)} %collective-permute-done.17.refs_11_.refs_27_) | copy-start | bytes 393220
  153.1 7.5 %collective-permute-start.10 = (bf16[256,256]{1,0:T(8,128)(2,1)S(1)}, bf16[256,256]{1,0:T(8,128)(2,1)S(1)}, u32[]{:S(2)}, u32[]{:S(2)}) collective-permute-start(bf16[256,256]{1,0:T(8,128)(2,1)S(1)} %copy-done.42), channel_id=1, source_target_pairs={{0,1},{1,0},{2,3},{3,2},{4,5},{5,4},{6,7},{7,6},{8,9},{9,8},{10,11... | collective-permute-start | bytes 393224 | tf_op jit(solution)/shard_map/ppermute | solution.py:570
  155.0 11.2 %copy-start.28 = (bf16[256,256]{1,0:T(8,128)(2,1)}, bf16[256,256]{1,0:T(8,128)(2,1)S(1)}, u32[]{:S(2)}) copy-start(bf16[256,256]{1,0:T(8,128)(2,1)S(1)} %collective-permute-done.18.refs_12_.refs_28_) | copy-start | bytes 393220
  155.0 9.3 %collective-permute-start.11 = (bf16[256,256]{1,0:T(8,128)(2,1)S(1)}, bf16[256,256]{1,0:T(8,128)(2,1)S(1)}, u32[]{:S(2)}, u32[]{:S(2)}) collective-permute-start(bf16[256,256]{1,0:T(8,128)(2,1)S(1)} %copy-done.43), channel_id=1, source_target_pairs={{0,2},{1,3},{2,0},{3,1},{4,6},{5,7},{6,4},{7,5},{8,10},{9,11},{10,... | collective-permute-start | bytes 393224 | tf_op jit(solution)/shard_map/ppermute | solution.py:570
  156.5 9.8 %copy-start.29 = (bf16[256,256]{1,0:T(8,128)(2,1)}, bf16[256,256]{1,0:T(8,128)(2,1)S(1)}, u32[]{:S(2)}) copy-start(bf16[256,256]{1,0:T(8,128)(2,1)S(1)} %collective-permute-done.13.refs_6_.refs_22_) | copy-start | bytes 393220
  156.5 9.7 %collective-permute-start.12 = (bf16[256,256]{1,0:T(8,128)(2,1)S(1)}, bf16[256,256]{1,0:T(8,128)(2,1)S(1)}, u32[]{:S(2)}, u32[]{:S(2)}) collective-permute-start(bf16[256,256]{1,0:T(8,128)(2,1)S(1)} %copy-done.44), channel_id=1, source_target_pairs={{0,3},{1,2},{2,1},{3,0},{4,7},{5,6},{6,5},{7,4},{8,11},{9,10},{10,... | collective-permute-start | bytes 393224 | tf_op jit(solution)/shard_map/ppermute | solution.py:570
  158.7 7.5 %copy-start.30 = (bf16[256,256]{1,0:T(8,128)(2,1)}, bf16[256,256]{1,0:T(8,128)(2,1)S(1)}, u32[]{:S(2)}) copy-start(bf16[256,256]{1,0:T(8,128)(2,1)S(1)} %collective-permute-done.14.refs_7_.refs_23_) | copy-start | bytes 393220
  238.3 2.8 collective-permute-start.21
  238.6 6.3 %collective-permute-start.22 = (bf16[1,256,256]{2,1,0:T(8,128)(2,1)S(1)}, bf16[1,256,256]{2,1,0:T(8,128)(2,1)S(1)}, u32[]{:S(2)}, u32[]{:S(2)}) collective-permute-start(bf16[1,256,256]{2,1,0:T(8,128)(2,1)S(1)} %copy-done.64), channel_id=1, source_target_pairs={{0,2},{1,3},{2,0},{3,1},{4,6},{5,7},{6,4},{7,5},{8,10},{9,11},{10,... | collective-permute-start | bytes 393224 | tf_op jit(solution)/shard_map/ppermute | solution.py:570
  240.1 6.3 %collective-permute-start.23 = (bf16[1,256,256]{2,1,0:T(8,128)(2,1)S(1)}, bf16[1,256,256]{2,1,0:T(8,128)(2,1)S(1)}, u32[]{:S(2)}, u32[]{:S(2)}) collective-permute-start(bf16[1,256,256]{2,1,0:T(8,128)(2,1)S(1)} %copy-done.63), channel_id=1, source_target_pairs={{0,3},{1,2},{2,1},{3,0},{4,7},{5,6},{6,5},{7,4},{8,11},{9,10},{10,... | collective-permute-start | bytes 393224 | tf_op jit(solution)/shard_map/ppermute | solution.py:570
  241.1 7.2 %copy-start.45 = (bf16[1,256,256]{2,1,0:T(8,128)(2,1)}, bf16[1,256,256]{2,1,0:T(8,128)(2,1)S(1)}, u32[]{:S(2)}) copy-start(bf16[1,256,256]{2,1,0:T(8,128)(2,1)S(1)} %collective-permute-done.21.refs_5_) | copy-start | bytes 393220
  250.6 60.0 %all-to-all-start = ((bf16[32,3,6656]{2,1,0:T(4,128)(2,1)}), bf16[32,3,6656]{2,1,0:T(4,128)(2,1)}, u32[]{:S(2)}, u32[]{:S(2)}) async-start(bf16[32,3,6656]{2,1,0:T(4,128)(2,1)} %copy.88), calls=%async_computation | async-start | bytes 3407872 | tf_op jit(solution)/shard_map/all_to_all | solution.py:578
  254.1 131.9 %all-gather.5.cloned.1.call-start = ((), (), s32[]{:S(2)}) async-start(), calls=%async_computation.4 | async-start | bytes 3514368 | tf_op jit(solution)/shard_map/all_gather | solution.py:813
  254.2 22.5 %collective-permute-start.24 = (bf16[2,256,256]{2,1,0:T(8,128)(2,1)S(1)}, bf16[2,256,256]{2,1,0:T(8,128)(2,1)S(1)}, u32[]{:S(2)}, u32[]{:S(2)}) collective-permute-start(bf16[2,256,256]{2,1,0:T(8,128)(2,1)S(1)} %copy-done.62), channel_id=1, source_target_pairs={{0,1},{1,0},{2,3},{3,2},{4,5},{5,4},{6,7},{7,6},{8,9},{9,8},{10,11... | collective-permute-start | bytes 786440 | tf_op jit(solution)/shard_map/ppermute | solution.py:570
  254.5 23.2 %collective-permute-start.25 = (bf16[2,256,256]{2,1,0:T(8,128)(2,1)S(1)}, bf16[2,256,256]{2,1,0:T(8,128)(2,1)S(1)}, u32[]{:S(2)}, u32[]{:S(2)}) collective-permute-start(bf16[2,256,256]{2,1,0:T(8,128)(2,1)S(1)} %copy-done.61), channel_id=1, source_target_pairs={{0,2},{1,3},{2,0},{3,1},{4,6},{5,7},{6,4},{7,5},{8,10},{9,11},{10,... | collective-permute-start | bytes 786440 | tf_op jit(solution)/shard_map/ppermute | solution.py:570
  256.0 27.4 %collective-permute-start.26 = (bf16[2,256,256]{2,1,0:T(8,128)(2,1)S(1)}, bf16[2,256,256]{2,1,0:T(8,128)(2,1)S(1)}, u32[]{:S(2)}, u32[]{:S(2)}) collective-permute-start(bf16[2,256,256]{2,1,0:T(8,128)(2,1)S(1)} %copy-done.60), channel_id=1, source_target_pairs={{0,3},{1,2},{2,1},{3,0},{4,7},{5,6},{6,5},{7,4},{8,11},{9,10},{10,... | collective-permute-start | bytes 786440 | tf_op jit(solution)/shard_map/ppermute | solution.py:570
  276.6 10.3 %copy-start.13 = (f32[2,256,1024]{2,1,0:T(8,128)S(1)}, f32[2,256,1024]{2,1,0:T(8,128)}, u32[]{:S(2)}) copy-start(f32[2,256,1024]{2,1,0:T(8,128)} %get-tuple-element.170) | copy-start | bytes 6291460
  276.7 11.2 %copy-start.17 = (bf16[2,256,256]{2,1,0:T(8,128)(2,1)}, bf16[2,256,256]{2,1,0:T(8,128)(2,1)S(1)}, u32[]{:S(2)}) copy-start(bf16[2,256,256]{2,1,0:T(8,128)(2,1)S(1)} %collective-permute-done.24.refs_5_) | copy-start | bytes 786436
  277.7 10.2 %copy-start.18 = (bf16[2,256,256]{2,1,0:T(8,128)(2,1)}, bf16[2,256,256]{2,1,0:T(8,128)(2,1)S(1)}, u32[]{:S(2)}) copy-start(bf16[2,256,256]{2,1,0:T(8,128)(2,1)S(1)} %collective-permute-done.25.refs_6_) | copy-start | bytes 786436
  283.5 3.2 collective-permute-start.27
  287.9 22.7 %collective-permute-start.28 = (bf16[256,1024]{1,0:T(8,128)(2,1)}, bf16[256,1024]{1,0:T(8,128)(2,1)S(1)}, u32[]{:S(2)}, u32[]{:S(2)}) collective-permute-start(bf16[256,1024]{1,0:T(8,128)(2,1)} %fusion.27), channel_id=1, source_target_pairs={{0,2},{1,3},{2,0},{3,1},{4,6},{5,7},{6,4},{7,5},{8,10},{9,11},{10,... | collective-permute-start | bytes 1572872 | tf_op jit(solution)/shard_map/ppermute | solution.py:570
  316.4 2.9 collective-permute-start.29
  321.1 22.6 %collective-permute-start.30 = (bf16[256,1024]{1,0:T(8,128)(2,1)S(1)}, bf16[256,1024]{1,0:T(8,128)(2,1)S(1)}, u32[]{:S(2)}, u32[]{:S(2)}) collective-permute-start(bf16[256,1024]{1,0:T(8,128)(2,1)S(1)} %fusion.28), channel_id=1, source_target_pairs={{0,2},{1,3},{2,0},{3,1},{4,6},{5,7},{6,4},{7,5},{8,10},{9,11},{10,... | collective-permute-start | bytes 1572872 | tf_op jit(solution)/shard_map/ppermute | solution.py:570
  322.8 21.8 %copy-start.50 = (f32[16,1024]{1,0:T(8,128)S(1)}, f32[16,1024]{1,0:T(8,128)}, u32[]{:S(2)}) copy-start(f32[16,1024]{1,0:T(8,128)} %get-tuple-element.196) | copy-start | bytes 196612
  322.8 21.8 %copy-start.57 = (f32[3,16,256]{2,1,0:T(8,128)S(1)}, f32[3,16,256]{2,1,0:T(8,128)}, u32[]{:S(2)}) copy-start(f32[3,16,256]{2,1,0:T(8,128)} %get-tuple-element.199) | copy-start | bytes 147460
  322.8 22.8 %copy-start.51 = (f32[16,1024]{1,0:T(8,128)S(1)}, f32[16,1024]{1,0:T(8,128)}, u32[]{:S(2)}) copy-start(f32[16,1024]{1,0:T(8,128)} %get-tuple-element.197) | copy-start | bytes 196612
  344.5 3.2 collective-permute-start.31
  351.0 21.0 %collective-permute-start.32 = (bf16[256,1024]{1,0:T(8,128)(2,1)}, bf16[256,1024]{1,0:T(8,128)(2,1)}, u32[]{:S(2)}, u32[]{:S(2)}) collective-permute-start(bf16[256,1024]{1,0:T(8,128)(2,1)} %fusion.29), channel_id=1, source_target_pairs={{0,2},{1,3},{2,0},{3,1},{4,6},{5,7},{6,4},{7,5},{8,10},{9,11},{10,... | collective-permute-start | bytes 1572872 | tf_op jit(solution)/shard_map/ppermute | solution.py:570
  352.1 19.9 %all-to-all-start.1 = ((bf16[32,6,448]{2,1,0:T(8,128)(2,1)}), bf16[32,6,448]{2,1,0:T(8,128)(2,1)S(1)}, u32[]{:S(2)}, u32[]{:S(2)}) async-start(bf16[32,6,448]{2,1,0:T(8,128)(2,1)} %copy.92), calls=%async_computation.1 | async-start | bytes 524288 | tf_op jit(solution)/shard_map/all_to_all | solution.py:578
  373.9 21.4 %all-to-all-start.2 = ((bf16[32,16,448]{2,1,0:T(8,128)(2,1)}), bf16[32,16,448]{2,1,0:T(8,128)(2,1)}, u32[]{:S(2)}, u32[]{:S(2)}) async-start(bf16[32,16,448]{2,1,0:T(8,128)(2,1)} %bitcast.66), calls=%async_computation.2 | async-start | bytes 1048576 | tf_op jit(solution)/shard_map/all_to_all | solution.py:578
  383.9 13.6 %copy-start.1 = (bf16[8,16,2,656]{3,2,1,0:T(2,128)(2,1)S(1)}, bf16[8,16,2,656]{3,2,1,0:T(2,128)(2,1)}, u32[]{:S(2)}) copy-start(bf16[8,16,2,656]{3,2,1,0:T(2,128)(2,1)} %param.33) | copy-start | bytes 1007620
  (39 other events, 131.4 us)
Sparse Core Ops, SparseCore 0:
  11.5 156.2 all-gather.2
  317.4 65.8 all-gather.4

commit v4 on v3

--- a/solution.py
+++ b/solution.py
@@ -11,6 +11,7 @@
 NORM_EPS = 1e-05
 ROPE_BASE = 160000.0
 LANES = 128
+CH = 256
 BF = jnp.bfloat16
 F32 = jnp.float32
 
@@ -128,42 +129,52 @@
 
 
 def attend_kernel(place, query, key, value, *outs):
-    *contexts, probs, shrinks = outs
+    *contexts, probs, shrinks, held = outs
     blocks, own = query.shape[1:3]
+    tile = pl.program_id(1)
     keys = key[0].reshape(blocks * own, LANES)
     turned = value[0].reshape(blocks * own, LANES).T
-    for step in range(0, blocks, 2):
-        rows = jnp.concatenate([query[0, place[0] ^ (step + i)] for i in range(2)], axis=0)
-        parts = []
-        for head in range(2):
-            scores = nt(keys, one_head(rows, head))
-            top = jnp.max(scores, axis=0, keepdims=True)
-            raised = jnp.exp(scores - top)
-            shrink = 1.0 / jnp.sum(raised, axis=0, keepdims=True)
-            raised = raised.astype(BF)
-            probs[0, step // 2, head] = raised
-            shrinks[0, step // 2, head : head + 1] = shrink
-            parts.append(nn(turned[head * HEAD_DIM : (head + 1) * HEAD_DIM], raised) * shrink)
-        merged = jnp.concatenate(parts, axis=0).T.astype(BF)
-        for i in range(2):
-            contexts[step + i][...] = merged[i * own : (i + 1) * own]
+    rows = jnp.concatenate([query[0, place[0] ^ (2 * tile + i)] for i in range(2)], axis=0)
+    parts = []
+    for head in range(2):
+        mine = one_head(rows, head)
+        held[...] = nt(keys, mine)
+        top = jnp.max(held[...], axis=0, keepdims=True)
+
+        def some(i, sums):
+            at = pl.ds(pl.multiple_of(i * CH, CH), CH)
+            raised = jnp.exp(held[at, :] - top)
+            probs[0, 0, head, at, :] = raised.astype(BF)
+            return sums + jnp.sum(raised.reshape(CH // 8, 8, raised.shape[1]), axis=0)
+
+        sums = lax.fori_loop(0, blocks * own // CH, some, jnp.zeros((8, 2 * own), F32))
+        shrink = 1.0 / jnp.sum(sums, axis=0, keepdims=True)
+        shrinks[0, 0, head : head + 1] = shrink
+        parts.append(nn(turned[head * HEAD_DIM : (head + 1) * HEAD_DIM], probs[0, 0, head]) * shrink)
+    merged = jnp.concatenate(parts, axis=0).T.astype(BF)
+    for half in range(blocks // 2):
+        @pl.when(tile == half)
+        def _():
+            for i in range(2):
+                contexts[2 * half + i][...] = merged[i * own : (i + 1) * own]
 
 
 def attend(place, query, key, value, seq):
     _, blocks, own, wide = query.shape
     pairs = wide // LANES
-    whole = pl.BlockSpec((1, blocks, own, LANES), lambda h, p: (seq, 0, 0, h))
+    whole = pl.BlockSpec((1, blocks, own, LANES), lambda h, t, p: (seq, 0, 0, h))
     *contexts, probs, shrinks = pl.pallas_call(
         attend_kernel,
         grid_spec=pltpu.PrefetchScalarGridSpec(
             num_scalar_prefetch=1,
-            grid=(pairs,),
+            grid=(pairs, blocks // 2),
             in_specs=[whole] * 3,
-            out_specs=[pl.BlockSpec((own, LANES), lambda h, p: (0, h))] * blocks
+            out_specs=[pl.BlockSpec((own, LANES), lambda h, t, p: (0, h))] * blocks
             + [
-                pl.BlockSpec((1, blocks // 2, 2, blocks * own, 2 * own), lambda h, p: (h, 0, 0, 0, 0)),
-                pl.BlockSpec((1, blocks // 2, 2, 2 * own), lambda h, p: (h, 0, 0, 0)),
+                pl.BlockSpec((1, 1, 2, blocks * own, 2 * own), lambda h, t, p: (h, t, 0, 0, 0)),
+                pl.BlockSpec((1, 1, 2, 2 * own), lambda h, t, p: (h, t, 0, 0)),
             ],
+            scratch_shapes=[pltpu.VMEM((blocks * own, 2 * own), F32)],
         ),
         out_shape=[jax.ShapeDtypeStruct((own, wide), BF)] * blocks
         + [
@@ -234,7 +245,7 @@
     more_small = nt(grads, ups)
     up_part = tn(downs, grads)
     for kind in range(3):
-        up_grad[kind] = up_part[:, kind * LANES : (kind + 1) * LANES]
+        up_grad[kind] = up_part[:, kind * LANES : (kind + 1) * LANES].astype(BF)
 
     @pl.when(pair == 0)
     def _():
@@ -249,14 +260,11 @@
     @pl.when(pair == last)
     def _():
         narrow = (small[...] * ADAPTER_SCALE).astype(BF)
-        low_grad[...] = tn(narrow, jnp.concatenate([piece[0] for piece in rows_in], axis=0))
+        low_grad[...] = tn(narrow, jnp.concatenate([piece[0] for piece in rows_in], axis=0)).astype(BF)
         done = total[...] + nn(narrow, low[0])
         for step in range(blocks):
-            part = done[step * own : (step + 1) * own]
-            if step % 2:
-                there[step // 2] = part.astype(BF)
-            else:
-                here[step // 2] = part
+            part = done[step * own : (step + 1) * own].astype(BF)
+            (there if step % 2 else here)[step // 2] = part
 
 
 def attend_back(place, seq, query, key, value, kept, grads, pieces, tables, weight, low, up, down):
@@ -299,10 +307,10 @@
             ],
         ),
         out_shape=[
-            jax.ShapeDtypeStruct((blocks // 2, own, model), F32),
             jax.ShapeDtypeStruct((blocks // 2, own, model), BF),
-            jax.ShapeDtypeStruct((3, rank, wide), F32),
-            jax.ShapeDtypeStruct((rank, model), F32),
+            jax.ShapeDtypeStruct((blocks // 2, own, model), BF),
+            jax.ShapeDtypeStruct((3, rank, wide), BF),
+            jax.ShapeDtypeStruct((rank, model), BF),
         ],
         name="attend_back",
     )(place, query, key, value, probs, shrinks, *contexts, *grads, *pieces, *tables, weight, low, up, down)
@@ -392,17 +400,17 @@
     late[...] += nt(active, low_outs)
     grad_rows[...] += nn(first_grad, values) + nn(second_grad, gates)
     late_grad[...] += nt(first_grad, up_values) + nt(second_grad, up_gates)
-    expand_up_grad[0, 0] = tn(down[...], first_grad)
-    expand_up_grad[0, 1] = tn(down[...], second_grad)
-    shrink_low_grad[0] = tn(down_grad[...], active)
+    expand_up_grad[0, 0] = tn(down[...], first_grad).astype(BF)
+    expand_up_grad[0, 1] = tn(down[...], second_grad).astype(BF)
+    shrink_low_grad[0] = tn(down_grad[...], active).astype(BF)
 
     @pl.when(step == blocks - 1)
     def _():
         small = (late[...] * scaled).astype(BF)
         result[...] = (total[...] + nn(small, shrink_up[...])).astype(BF)
-        shrink_up_grad[...] = tn(small, out_grad[...])
+        shrink_up_grad[...] = tn(small, out_grad[...]).astype(BF)
         small_grad = (late_grad[...] * scaled).astype(BF)
-        expand_low_grad[...] = tn(small_grad, rows[...])
+        expand_low_grad[...] = tn(small_grad, rows[...]).astype(BF)
         own = rows.shape[0] // seqs
         for seq in range(seqs):
             part = slice(seq * own, (seq + 1) * own)
@@ -420,8 +428,8 @@
                     others[move][seq - 1] = out
                 else:
                     firsts[move][0] = out
-                merge_low_grad[seq, move] = tn(small, contexts[seq * blocks + move][...])
-            merge_up_grad[seq] = tn(merge_down[seq], low_rows)
+                merge_low_grad[seq, move] = tn(small, contexts[seq * blocks + move][...]).astype(BF)
+            merge_up_grad[seq] = tn(merge_down[seq], low_rows).astype(BF)
 
 
 def gated(
@@ -438,13 +446,13 @@
     pieces = [piece for context in contexts for piece in context]
     shapes = [
         ((count, model), BF),
-        ((blocks, 2, rank, width), F32),
-        ((blocks, rank, width), F32),
-        ((rank, model), F32),
-        ((rank, model), F32),
+        ((blocks, 2, rank, width), BF),
+        ((blocks, rank, width), BF),
+        ((rank, model), BF),
+        ((rank, model), BF),
         ((seqs, own, model), F32),
-        ((seqs, blocks, some, wide), F32),
-        ((seqs, some, model), F32),
+        ((seqs, blocks, some, wide), BF),
+        ((seqs, some, model), BF),
     ]
     shapes += [((1, own, wide), BF)] * blocks + [((seqs - 1, own, wide), BF)] * blocks
     out_specs = [full_once(shape) for shape, _ in shapes]
@@ -807,7 +815,10 @@
             there, halfway[1] = lax.optimization_barrier((there, halfway[1]))
         if seq == 1:
             there, far, early = lax.optimization_barrier((there, far, early))
-            early = jnp.dot(choose, early.reshape(owners * seqs, -1), preferred_element_type=F32)
+            by_seq = choose.reshape(ADAPTERS, owners, seqs)
+            early = sum(
+                jnp.dot(by_seq[:, :, i], early[:, i], preferred_element_type=F32) for i in range(seqs)
+            )
             if paired:
                 early = jnp.concatenate([early[:, :early_width], early[:, early_width:]], axis=0)
             shared = lax.all_gather(early.astype(BF), everyone, axis=0)
@@ -818,7 +829,7 @@
         joined_up_grads.append(up_grad.transpose(1, 0, 2).reshape(rank, 3 * wide))
         joined_low_grads.append(low_grad)
         there = pair_swap(there, 1).astype(F32)
-        chip, give = here[0] + there[0], (here[1] + there[1]).astype(BF)
+        chip, give = here[0].astype(F32) + there[0], (here[1].astype(F32) + there[1]).astype(BF)
         far = pair_swap(give, 2)
 
     piece = 3 * wide // blocks
@@ -829,7 +840,7 @@
     late_low, late_up = (each.reshape(owners, seqs * some, -1) for each in (late_low, late_up))
     low_size = late_low.shape[2]
     late = jnp.concatenate([late_low, late_up], axis=2)
-    late = tie(late, give)
+    late = tie(late, there)
     late, far = lax.optimization_barrier((swap_all(late, everyone), far))
     late = late.reshape(parts, blocks, seqs, some, -1)
     grad_normeds.append(chip + far.astype(F32))

time: 409 us -> 405 us (level)
    unnamed x142 -> x140, local copies, waits for them, and re-layouts: 8.37 us -> 10.2 us
where the time goes in v4:
time: 405 us; the launch traced here: 400 us
  Pallas kernels  184 us (45%)
  waiting for transfers between devices  91.2 us (23%)
  starting transfers between devices  40.7 us (10%)
  local copies, waits for them, and re-layouts  38.1 us (9%)
  other arithmetic  30.1 us (7%)
  between operations  15.4 us (4%)
    ppermute x29, waiting for transfers between devices, pair_swap(): return lax.ppermute(values, 'mp', [(i, i ^ bit) for i in range(size)])  66.6 us
    pallas_call x3, Pallas kernels, attend_back(): pl.pallas_call(attend_back_kernel, grid_spec=pltpu.PrefetchScalarGridSpec...  61.1 us
    pallas_call x1, Pallas kernels, gated(): pl.pallas_call(lambda *refs: gated_kernel(*refs, width=width, blocks=bloc...  57.6 us
    pallas_call x3, Pallas kernels, attend(): pl.pallas_call(attend_kernel, grid_spec=pltpu.PrefetchScalarGridSpec(num_...  36 us
    ppermute x29, starting transfers between devices, pair_swap(): return lax.ppermute(values, 'mp', [(i, i ^ bit) for i in range(size)])  18.3 us
    all_to_all x3, starting transfers between devices, swap_all(): return lax.all_to_all(values, axes, 0, 0, tiled=True)  15.1 us
    all_to_all x3, waiting for transfers between devices, swap_all(): return lax.all_to_all(values, axes, 0, 0, tiled=True)  14.3 us
    pallas_call x1, Pallas kernels, project(): pl.pallas_call(lambda *refs: project_kernel(*refs, wide=wide), grid_spec=...  13.8 us
  transfers between devices with their start and end apart: 38, of which 18 were waited for; matrix products, arithmetic and copies ran while one was open for 12% of the time, Pallas kernels for 31%

profile of v4, /device:TPU:0, one launch (start us, length us, event | category | flops | bytes accessed | tf_op | source)
XLA Modules:
  0.0 400.3 jit_solution(471982026974667257)
XLA Ops:
  7.3 1.9 pad_maximum_fusion.3
  13.6 2.9 collective-permute-start.3
  17.7 1.6 collective-permute-start.6
  19.3 2.6 collective-permute-start.7
  21.8 1.3 collective-permute-start.8
  25.8 1.7 fusion.6.refs_1_.refs_8_
  27.5 1.5 gather_fusion.1
  29.7 1.2 gather_fusion
  30.9 1.2 gather_fusion.6
  32.1 2.3 gather_fusion.7
  34.3 2.2 gather_fusion.5
  36.5 3.2 multiply_sine_fusion
  40.2 9.6 %collective-permute-done.7 = bf16[1032,128]{1,0:T(8,128)(2,1)S(1)} collective-permute-done((bf16[1032,128]{1,0:T(8,128)(2,1)}, bf16[1032,128]{1,0:T(8,128)(2,1)S(1)}, u32[]{:S(2)}, u32[]{:S(2)}) %collective-permute-start.7) | collective-permute-done | bytes 264224 | tf_op jit(solution)/shard_map/ppermute | solution.py:604
  50.6 1.2 pad_maximum_fusion
  51.8 1.6 collective-permute-start.9
  53.5 1.0 constant_dynamic-update-slice_fusion.1
  56.9 33.4 %collective-permute-done.1.refs_3_.refs_10_ = bf16[3,256,1024]{2,1,0:T(8,128)(2,1)} collective-permute-done((bf16[3,256,1024]{2,1,0:T(8,128)(2,1)}, bf16[3,256,1024]{2,1,0:T(8,128)(2,1)}, u32[]{:S(2)}, u32[]{:S(2)}) %collective-permute-start.1) | collective-permute-done | bytes 1572896 | tf_op jit(solution)/shard_map/ppermute | solution.py:578
  91.1 3.4 collective-permute-done.19
  95.9 13.8 %project.1 = (bf16[3,4,256,256]{3,2,1,0:T(8,128)(2,1)}, bf16[3,4,256,256]{3,2,1,0:T(8,128)(2,1)}, bf16[3,4,256,256]{3,2,1,0:T(8,128)(2,1)}, bf16[3,4,256,16]{3,2,1,0:T(8,128)(2,1)}) custom-call(s32[9]{0:T(128)} %pad_add_fusion.refs_0_.place, bf16[3,256,1024]{2,1,0:T(8,128)(2,1)} %fusion.6.refs_1_.refs_8_, ...), custom_call_target="tpu_custom_call" | custom-call | tf_op jit(solution)/shard_map/project/pallas_call | solution.py:104
  109.8 11.9 %attend.3 = (bf16[256,256]{1,0:T(8,128)(2,1)}, bf16[256,256]{1,0:T(8,128)(2,1)}, bf16[256,256]{1,0:T(8,128)(2,1)}, bf16[256,256]{1,0:T(8,128)(2,1)}, bf16[2,2,2,...) custom-call(s32[9]{0:T(128)} %pad_add_fusion.refs_0_.place, bf16[3,4,256,256]{3,2,1,0:T(8,128)(2,1)} %get-tuple-element.136.query, ...), custom_call_target="tpu_custom_call" | custom-call | tf_op jit(solution)/shard_map/attend/pallas_call | solution.py:166
  121.7 11.9 %attend.4 = (bf16[256,256]{1,0:T(8,128)(2,1)}, bf16[256,256]{1,0:T(8,128)(2,1)}, bf16[256,256]{1,0:T(8,128)(2,1)}, bf16[256,256]{1,0:T(8,128)(2,1)}, bf16[2,2,2,...) custom-call(s32[9]{0:T(128)} %pad_add_fusion.refs_0_.place, bf16[3,4,256,256]{3,2,1,0:T(8,128)(2,1)} %get-tuple-element.136.query, ...), custom_call_target="tpu_custom_call" | custom-call | tf_op jit(solution)/shard_map/attend/pallas_call | solution.py:166
  133.7 12.1 %attend.5 = (bf16[256,256]{1,0:T(8,128)(2,1)}, bf16[256,256]{1,0:T(8,128)(2,1)}, bf16[256,256]{1,0:T(8,128)(2,1)}, bf16[256,256]{1,0:T(8,128)(2,1)}, bf16[2,2,2,...) custom-call(s32[9]{0:T(128)} %pad_add_fusion.refs_0_.place, bf16[3,4,256,256]{3,2,1,0:T(8,128)(2,1)} %get-tuple-element.136.query, ...), custom_call_target="tpu_custom_call" | custom-call | tf_op jit(solution)/shard_map/attend/pallas_call | solution.py:166
  145.9 1.6 collective-permute-start.17
  148.1 1.6 collective-permute-start.14
  149.8 2.7 collective-permute-done.17.refs_11_.refs_27_
  152.4 1.9 collective-permute-done.18.refs_12_.refs_28_
  154.4 1.4 collective-permute-start.11
  155.8 1.1 collective-permute-start.12
  158.1 1.9 collective-permute-done.15.refs_8_.refs_24_
  159.9 3.7 collective-permute-done.11.refs_3_.refs_19_
  163.7 1.9 collective-permute-done.12.refs_4_.refs_20_
  166.2 8.2 %merge.1 = (f32[3,256,1024]{2,1,0:T(8,128)}, bf16[3,256,1024]{2,1,0:T(8,128)(2,1)}, bf16[3,256,16]{2,1,0:T(8,128)(2,1)}) custom-call(s32[9]{0:T(128)} %pad_add_fusion.refs_0_.place, bf16[256,256]{1,0:T(8,128)(2,1)} %get-tuple-element.127.refs_1_.refs_17_.refs_0_, bf16[256,256]{1,0:T(8,128)(2,1)} %copy-done.33, bf16[256,256]{1,0:T(8,128)(2,1)} %copy-done.34, ...), custom_call_target="tpu_custom_call" | custom-call | tf_op jit(solution)/shard_map/merge/pallas_call | solution.py:347
  174.4 57.6 %gated.1 = (bf16[768,1024]{1,0:T(8,128)(2,1)}, bf16[4,2,48,656]{3,2,1,0:T(8,128)(2,1)}, bf16[4,48,656]{2,1,0:T(8,128)(2,1)}, bf16[48,1024]{1,0:T(8,128)(2,1)}, b...) custom-call(s32[9]{0:T(128)} %pad_add_fusion.refs_0_.place, ...), custom_call_target="tpu_custom_call" | custom-call | tf_op jit(solution)/shard_map/gated/pallas_call | solution.py:461
  232.1 0.9 fusion.42
  234.9 1.1 slice_bitcast_fusion.6
  236.3 1.5 collective-permute-start.22
  239.6 3.3 collective-permute-done.22.refs_6_
  242.9 1.4 collective-permute-done.23.refs_7_
  244.3 1.0 copy.135
  246.2 2.3 copy.101
  248.4 3.6 all-to-all-start
  252.4 1.5 collective-permute-start.25
  254.0 20.2 %attend_back.3 = (bf16[2,256,1024]{2,1,0:T(8,128)(2,1)}, bf16[2,256,1024]{2,1,0:T(8,128)(2,1)}, bf16[3,16,256]{2,1,0:T(8,128)(2,1)}, bf16[16,1024]{1,0:T(8,128)(2,1)}) custom-call(s32[9]{0:T(128)} %pad_add_fusion.refs_0_.place, bf16[3,4,256,256]{3,2,1,0:T(8,128)(2,1)} %get-tuple-element.136.query, bf16[3,4,256,256]{3,2,1,0:T(8,128)(2,1)} %get-tuple-element.125.key, ...), custom_call_target="tpu_custom_call" | custom-call | tf_op jit(solution)/shard_map/attend_back/pallas_call | solution.py:279
  274.2 1.4 collective-permute-done.25.refs_6_
  275.6 5.8 %collective-permute-done.26.refs_7_ = bf16[2,256,256]{2,1,0:T(8,128)(2,1)S(1)} collective-permute-done((bf16[2,256,256]{2,1,0:T(8,128)(2,1)S(1)}, bf16[2,256,256]{2,1,0:T(8,128)(2,1)S(1)}, u32[]{:S(2)}, u32[]{:S(2)}) %collective-permute-start.26) | collective-permute-done | bytes 262176 | tf_op jit(solution)/shard_map/ppermute | solution.py:578
  282.1 2.5 collective-permute-done.27
  288.0 20.2 %attend_back.4 = (bf16[2,256,1024]{2,1,0:T(8,128)(2,1)}, bf16[2,256,1024]{2,1,0:T(8,128)(2,1)}, bf16[3,16,256]{2,1,0:T(8,128)(2,1)}, bf16[16,1024]{1,0:T(8,128)(2,1)}) custom-call(s32[9]{0:T(128)} %pad_add_fusion.refs_0_.place, bf16[3,4,256,256]{3,2,1,0:T(8,128)(2,1)} %get-tuple-element.136.query, bf16[3,4,256,256]{3,2,1,0:T(8,128)(2,1)} %get-tuple-element.125.key, ...), custom_call_target="tpu_custom_call" | custom-call | tf_op jit(solution)/shard_map/attend_back/pallas_call | solution.py:279
  308.3 1.9 copy.113
  311.6 2.8 collective-permute-done.29
  314.6 1.4 copy-done.8
  316.9 1.6 collective-permute-start.30
  318.5 20.7 %attend_back.5 = (bf16[2,256,1024]{2,1,0:T(8,128)(2,1)}, bf16[2,256,1024]{2,1,0:T(8,128)(2,1)}, bf16[3,16,256]{2,1,0:T(8,128)(2,1)}, bf16[16,1024]{1,0:T(8,128)(2,1)}) custom-call(s32[9]{0:T(128)} %pad_add_fusion.refs_0_.place, bf16[3,4,256,256]{3,2,1,0:T(8,128)(2,1)} %get-tuple-element.136.query, bf16[3,4,256,256]{3,2,1,0:T(8,128)(2,1)} %get-tuple-element.125.key, ...), custom_call_target="tpu_custom_call" | custom-call | tf_op jit(solution)/shard_map/attend_back/pallas_call | solution.py:279
  343.3 1.4 copy-done.10
  346.8 5.8 %all-to-all-start.1 = ((bf16[32,6,448]{2,1,0:T(8,128)(2,1)}), bf16[32,6,448]{2,1,0:T(8,128)(2,1)S(1)}, u32[]{:S(2)}, u32[]{:S(2)}) async-start(bf16[32,6,448]{2,1,0:T(8,128)(2,1)} %copy.105), calls=%async_computation.1 | async-start | bytes 524288 | tf_op jit(solution)/shard_map/all_to_all | solution.py:586
  352.7 1.6 fusion.25
  354.6 2.7 fusion.21
  357.3 9.7 %all-to-all-done.1 = bf16[32,6,448]{2,1,0:T(8,128)(2,1)S(1)} async-done(((bf16[32,6,448]{2,1,0:T(8,128)(2,1)}), bf16[32,6,448]{2,1,0:T(8,128)(2,1)S(1)}, u32[]{:S(2)}, u32[]{:S(2)}) %all-to-all-start.1) | async-done | bytes 172064 | tf_op jit(solution)/shard_map/all_to_all | solution.py:586
  368.8 5.8 %all-to-all-start.2 = ((bf16[32,16,448]{2,1,0:T(8,128)(2,1)}), bf16[32,16,448]{2,1,0:T(8,128)(2,1)S(1)}, u32[]{:S(2)}, u32[]{:S(2)}) async-start(bf16[32,16,448]{2,1,0:T(8,128)(2,1)} %bitcast.202), calls=%async_computation.2 | async-start | bytes 1048576 | tf_op jit(solution)/shard_map/all_to_all | solution.py:586
  374.6 1.9 fusion.17
  376.6 1.1 fusion.26
  378.5 2.1 fusion.11
  380.6 5.0 %settle_early.1 = (f32[8,16,1024]{2,1,0:T(8,128)}, f32[8,16,1024]{2,1,0:T(8,128)}, f32[8,16,1024]{2,1,0:T(8,128)}, f32[8,16,256]{2,1,0:T(8,128)}, f32[8,16,2,656]{3,2,1,0:T(2,128)}, /*index=5*/f32[8,16,656]{2,1,0:T(8,128)}) custom-call(s32[9]{0:T(128)} %pad_add_fusion.refs_0_.place, bf16[32,16,3328]{2,1,0:T(8,128)(2,1)} %all-gather.5.cloned.1.call-done.refs_1_), custom_call_target="tpu_custom_call" | custom-call | tf_op jit(solution)/shard_map/settle_early/pallas_call | solution.py:532
  385.6 4.6 %all-to-all-done.2.refs_0_ = bf16[32,16,448]{2,1,0:T(8,128)(2,1)S(1)} async-done(((bf16[32,16,448]{2,1,0:T(8,128)(2,1)}), bf16[32,16,448]{2,1,0:T(8,128)(2,1)S(1)}, u32[]{:S(2)}, u32[]{:S(2)}) %all-to-all-start.2) | async-done | bytes 458784 | tf_op jit(solution)/shard_map/all_to_all | solution.py:586
  391.0 2.3 settle_late.1
  (277 shorter events, 39.1 us)
Async XLA Ops:
  7.2 167.2 %all-gather.3.cloned.1.call-start = ((), (), s32[]{:S(2)}) async-start(), calls=%async_computation.3 | async-start | bytes 16625664 | tf_op jit(solution)/shard_map/all_gather | solution.py:655
  10.8 12.4 %copy-start.59 = (bf16[1024]{0:T(1024)(128)(2,1)S(1)}, bf16[1024]{0:T(1024)(128)(2,1)}, u32[]{:S(2)}) copy-start(bf16[1024]{0:T(1024)(128)(2,1)} %param.22) | copy-start | bytes 6148
  10.9 12.4 %copy-start.2 = (bf16[3,256,1024]{2,1,0:T(8,128)(2,1)S(1)}, bf16[3,256,1024]{2,1,0:T(8,128)(2,1)}, u32[]{:S(2)}) copy-start(bf16[3,256,1024]{2,1,0:T(8,128)(2,1)} %refs_13_.1) | copy-start | bytes 4718596
  13.6 26.1 %collective-permute-start.3 = (bf16[3,16,2560]{2,1,0:T(8,128)(2,1)}, bf16[3,16,2560]{2,1,0:T(8,128)(2,1)S(1)}, u32[]{:S(2)}, u32[]{:S(2)}) collective-permute-start(bf16[3,16,2560]{2,1,0:T(8,128)(2,1)} %fusion.39), channel_id=1, source_target_pairs={{0,2},{1,3},{2,0},{3,1},{4,6},{5,7},{6,4},{7,5},{8,10},{9,11},{10,... | collective-permute-start | bytes 737288 | tf_op jit(solution)/shard_map/ppermute | solution.py:578
  16.6 38.0 %collective-permute-start.2 = (bf16[3,16,2560]{2,1,0:T(8,128)(2,1)}, bf16[3,16,2560]{2,1,0:T(8,128)(2,1)S(1)}, u32[]{:S(2)}, u32[]{:S(2)}) collective-permute-start(bf16[3,16,2560]{2,1,0:T(8,128)(2,1)} %fusion.39), channel_id=1, source_target_pairs={{0,1},{1,0},{2,3},{3,2},{4,5},{5,4},{6,7},{7,6},{8,9},{9,8},{10,11... | collective-permute-start | bytes 737288 | tf_op jit(solution)/shard_map/ppermute | solution.py:578
  17.7 22.5 %collective-permute-start.6 = (bf16[1032,128]{1,0:T(8,128)(2,1)}, bf16[1032,128]{1,0:T(8,128)(2,1)S(1)}, u32[]{:S(2)}, u32[]{:S(2)}) collective-permute-start(bf16[1032,128]{1,0:T(8,128)(2,1)} %get-tuple-element.221), channel_id=1, source_target_pairs={{0,8},{4,12},{8,16},{12,20},{16,24},{20,28},{24,0},{28,4},{1,9},{5... | collective-permute-start | bytes 792584 | tf_op jit(solution)/shard_map/ppermute | solution.py:604
  19.3 30.6 %collective-permute-start.7 = (bf16[1032,128]{1,0:T(8,128)(2,1)}, bf16[1032,128]{1,0:T(8,128)(2,1)S(1)}, u32[]{:S(2)}, u32[]{:S(2)}) collective-permute-start(bf16[1032,128]{1,0:T(8,128)(2,1)} %get-tuple-element.221), channel_id=1, source_target_pairs={{0,16},{4,20},{8,24},{12,28},{16,0},{20,4},{24,8},{28,12},{1,17},{... | collective-permute-start | bytes 792584 | tf_op jit(solution)/shard_map/ppermute | solution.py:604
  21.8 28.8 %collective-permute-start.8 = (bf16[1032,128]{1,0:T(8,128)(2,1)}, bf16[1032,128]{1,0:T(8,128)(2,1)}, u32[]{:S(2)}, u32[]{:S(2)}) collective-permute-start(bf16[1032,128]{1,0:T(8,128)(2,1)} %get-tuple-element.221), channel_id=1, source_target_pairs={{0,24},{4,28},{8,0},{12,4},{16,8},{20,12},{24,16},{28,20},{1,25},{... | collective-permute-start | bytes 792584 | tf_op jit(solution)/shard_map/ppermute | solution.py:604
  32.1 21.4 %copy-start.4 = (bf16[8,1032,128]{2,1,0:T(8,128)(2,1)S(1)}, bf16[8,1032,128]{2,1,0:T(8,128)(2,1)}, u32[]{:S(2)}) copy-start(bf16[8,1032,128]{2,1,0:T(8,128)(2,1)} %constant_dynamic-update-slice_fusion.4) | copy-start | bytes 6340612
  39.7 50.7 %collective-permute-start.1 = (bf16[3,256,1024]{2,1,0:T(8,128)(2,1)}, bf16[3,256,1024]{2,1,0:T(8,128)(2,1)}, u32[]{:S(2)}, u32[]{:S(2)}) collective-permute-start(bf16[3,256,1024]{2,1,0:T(8,128)(2,1)} %fusion.6.refs_1_.refs_8_), channel_id=1, source_target_pairs={{0,2},{1,3},{2,0},{3,1},{4,6},{5,7},{6,4},{7,5},{8,10},{9,11},{10,... | collective-permute-start | bytes 4718600 | tf_op jit(solution)/shard_map/ppermute | solution.py:578
  40.2 55.7 %collective-permute-start = (bf16[3,256,1024]{2,1,0:T(8,128)(2,1)}, bf16[3,256,1024]{2,1,0:T(8,128)(2,1)}, u32[]{:S(2)}, u32[]{:S(2)}) collective-permute-start(bf16[3,256,1024]{2,1,0:T(8,128)(2,1)} %fusion.6.refs_1_.refs_8_), channel_id=1, source_target_pairs={{0,1},{1,0},{2,3},{3,2},{4,5},{5,4},{6,7},{7,6},{8,9},{9,8},{10,11... | collective-permute-start | bytes 4718600 | tf_op jit(solution)/shard_map/ppermute | solution.py:578
  49.8 4.7 %collective-permute-start.4 = (bf16[3,16,2560]{2,1,0:T(8,128)(2,1)S(1)}, bf16[3,16,2560]{2,1,0:T(8,128)(2,1)S(1)}, u32[]{:S(2)}, u32[]{:S(2)}) collective-permute-start(bf16[3,16,2560]{2,1,0:T(8,128)(2,1)S(1)} %collective-permute-done.3), channel_id=1, source_target_pairs={{0,1},{1,0},{2,3},{3,2},{4,5},{5,4},{6,7},{7,6},{8,9},{9,8},{10,11... | collective-permute-start | bytes 737288 | tf_op jit(solution)/shard_map/ppermute | solution.py:578
  51.8 38.6 %collective-permute-start.9 = (bf16[4,1032,128]{2,1,0:T(8,128)(2,1)S(1)}, bf16[4,1032,128]{2,1,0:T(8,128)(2,1)S(1)}, u32[]{:S(2)}, u32[]{:S(2)}) collective-permute-start(bf16[4,1032,128]{2,1,0:T(8,128)(2,1)S(1)} %pad_maximum_fusion), channel_id=1, source_target_pairs={{0,4},{4,0},{8,12},{12,8},{16,20},{20,16},{24,28},{28,24},{1,5},{5... | collective-permute-start | bytes 3170312 | tf_op jit(solution)/shard_map/ppermute | solution.py:606
  90.4 5.5 %collective-permute-start.5 = (bf16[3,256,1024]{2,1,0:T(8,128)(2,1)}, bf16[3,256,1024]{2,1,0:T(8,128)(2,1)}, u32[]{:S(2)}, u32[]{:S(2)}) collective-permute-start(bf16[3,256,1024]{2,1,0:T(8,128)(2,1)} %collective-permute-done.1.refs_3_.refs_10_), channel_id=1, source_target_pairs={{0,1},{1,0},{2,3},{3,2},{4,5},{5,4},{6,7},{7,6},{8,9},{9,8},{10,11... | collective-permute-start | bytes 4718600 | tf_op jit(solution)/shard_map/ppermute | solution.py:578
  90.6 4.0 collective-permute-start.19
  94.6 15.1 %copy-start.6 = (bf16[8,2,256,128]{3,2,1,0:T(8,128)(2,1)}, bf16[8,2,256,128]{3,2,1,0:T(8,128)(2,1)S(1)}, u32[]{:S(2)}) copy-start(bf16[8,2,256,128]{3,2,1,0:T(8,128)(2,1)S(1)} %pad_maximum_fusion.1.refs_14_.refs_11_) | copy-start | bytes 3145732
  94.6 53.5 %collective-permute-start.20 = (bf16[8,2,256,128]{3,2,1,0:T(8,128)(2,1)S(1)}, bf16[8,2,256,128]{3,2,1,0:T(8,128)(2,1)}, u32[]{:S(2)}, u32[]{:S(2)}) collective-permute-start(bf16[8,2,256,128]{3,2,1,0:T(8,128)(2,1)S(1)} %pad_maximum_fusion.1.refs_14_.refs_11_), channel_id=1, source_target_pairs={{0,2},{1,3},{2,0},{3,1},{4,6},{5,7},{6,4},{7,5},{8,10},{9,11},{10,... | collective-permute-start | bytes 3145736 | tf_op jit(solution)/shard_map/ppermute | solution.py:578
  133.6 14.1 %copy-start.40 = (bf16[256,256]{1,0:T(8,128)(2,1)S(1)}, bf16[256,256]{1,0:T(8,128)(2,1)}, u32[]{:S(2)}) copy-start(bf16[256,256]{1,0:T(8,128)(2,1)} %get-tuple-element.133.refs_1_) | copy-start | bytes 393220
  133.7 14.5 %copy-start.41 = (bf16[256,256]{1,0:T(8,128)(2,1)S(1)}, bf16[256,256]{1,0:T(8,128)(2,1)}, u32[]{:S(2)}) copy-start(bf16[256,256]{1,0:T(8,128)(2,1)} %get-tuple-element.134.refs_2_) | copy-start | bytes 393220
  133.7 16.0 %copy-start.42 = (bf16[256,256]{1,0:T(8,128)(2,1)S(1)}, bf16[256,256]{1,0:T(8,128)(2,1)}, u32[]{:S(2)}) copy-start(bf16[256,256]{1,0:T(8,128)(2,1)} %get-tuple-element.135.refs_3_) | copy-start | bytes 393220
  133.7 18.8 %copy-start.43 = (bf16[256,256]{1,0:T(8,128)(2,1)S(1)}, bf16[256,256]{1,0:T(8,128)(2,1)}, u32[]{:S(2)}) copy-start(bf16[256,256]{1,0:T(8,128)(2,1)} %get-tuple-element.128.refs_1_) | copy-start | bytes 393220
  133.7 20.7 %copy-start.44 = (bf16[256,256]{1,0:T(8,128)(2,1)S(1)}, bf16[256,256]{1,0:T(8,128)(2,1)}, u32[]{:S(2)}) copy-start(bf16[256,256]{1,0:T(8,128)(2,1)} %get-tuple-element.129.refs_2_) | copy-start | bytes 393220
  133.7 22.1 %copy-start.45 = (bf16[256,256]{1,0:T(8,128)(2,1)S(1)}, bf16[256,256]{1,0:T(8,128)(2,1)}, u32[]{:S(2)}) copy-start(bf16[256,256]{1,0:T(8,128)(2,1)} %get-tuple-element.130.refs_3_) | copy-start | bytes 393220
  133.7 23.2 %copy-start.60 = (bf16[1024]{0:T(1024)(128)(2,1)S(1)}, bf16[1024]{0:T(1024)(128)(2,1)}, u32[]{:S(2)}) copy-start(bf16[1024]{0:T(1024)(128)(2,1)} %param.23) | copy-start | bytes 6148
  145.9 3.8 collective-permute-start.16
  145.9 6.6 %collective-permute-start.17 = (bf16[256,256]{1,0:T(8,128)(2,1)}, bf16[256,256]{1,0:T(8,128)(2,1)S(1)}, u32[]{:S(2)}, u32[]{:S(2)}) collective-permute-start(bf16[256,256]{1,0:T(8,128)(2,1)} %get-tuple-element.139.refs_2_), channel_id=1, source_target_pairs={{0,2},{1,3},{2,0},{3,1},{4,6},{5,7},{6,4},{7,5},{8,10},{9,11},{10,... | collective-permute-start | bytes 393224 | tf_op jit(solution)/shard_map/ppermute | solution.py:578
  147.4 6.9 %collective-permute-start.18 = (bf16[256,256]{1,0:T(8,128)(2,1)}, bf16[256,256]{1,0:T(8,128)(2,1)S(1)}, u32[]{:S(2)}, u32[]{:S(2)}) collective-permute-start(bf16[256,256]{1,0:T(8,128)(2,1)} %get-tuple-element.140.refs_3_), channel_id=1, source_target_pairs={{0,3},{1,2},{2,1},{3,0},{4,7},{5,6},{6,5},{7,4},{8,11},{9,10},{10,... | collective-permute-start | bytes 393224 | tf_op jit(solution)/shard_map/ppermute | solution.py:578
  147.7 8.1 %collective-permute-start.13 = (bf16[256,256]{1,0:T(8,128)(2,1)S(1)}, bf16[256,256]{1,0:T(8,128)(2,1)S(1)}, u32[]{:S(2)}, u32[]{:S(2)}) collective-permute-start(bf16[256,256]{1,0:T(8,128)(2,1)S(1)} %copy-done.40), channel_id=1, source_target_pairs={{0,1},{1,0},{2,3},{3,2},{4,5},{5,4},{6,7},{7,6},{8,9},{9,8},{10,11... | collective-permute-start | bytes 393224 | tf_op jit(solution)/shard_map/ppermute | solution.py:578
  148.1 9.9 %collective-permute-start.14 = (bf16[256,256]{1,0:T(8,128)(2,1)S(1)}, bf16[256,256]{1,0:T(8,128)(2,1)S(1)}, u32[]{:S(2)}, u32[]{:S(2)}) collective-permute-start(bf16[256,256]{1,0:T(8,128)(2,1)S(1)} %copy-done.41), channel_id=1, source_target_pairs={{0,2},{1,3},{2,0},{3,1},{4,6},{5,7},{6,4},{7,5},{8,10},{9,11},{10,... | collective-permute-start | bytes 393224 | tf_op jit(solution)/shard_map/ppermute | solution.py:578
  149.7 15.9 %copy-start.27 = (bf16[256,256]{1,0:T(8,128)(2,1)}, bf16[256,256]{1,0:T(8,128)(2,1)S(1)}, u32[]{:S(2)}) copy-start(bf16[256,256]{1,0:T(8,128)(2,1)S(1)} %collective-permute-done.16.refs_10_.refs_26_) | copy-start | bytes 393220
  149.7 10.3 %collective-permute-start.15 = (bf16[256,256]{1,0:T(8,128)(2,1)S(1)}, bf16[256,256]{1,0:T(8,128)(2,1)S(1)}, u32[]{:S(2)}, u32[]{:S(2)}) collective-permute-start(bf16[256,256]{1,0:T(8,128)(2,1)S(1)} %copy-done.42), channel_id=1, source_target_pairs={{0,3},{1,2},{2,1},{3,0},{4,7},{5,6},{6,5},{7,4},{8,11},{9,10},{10,... | collective-permute-start | bytes 393224 | tf_op jit(solution)/shard_map/ppermute | solution.py:578
  152.4 13.1 %copy-start.28 = (bf16[256,256]{1,0:T(8,128)(2,1)}, bf16[256,256]{1,0:T(8,128)(2,1)S(1)}, u32[]{:S(2)}) copy-start(bf16[256,256]{1,0:T(8,128)(2,1)S(1)} %collective-permute-done.17.refs_11_.refs_27_) | copy-start | bytes 393220
  152.4 7.5 %collective-permute-start.10 = (bf16[256,256]{1,0:T(8,128)(2,1)S(1)}, bf16[256,256]{1,0:T(8,128)(2,1)S(1)}, u32[]{:S(2)}, u32[]{:S(2)}) collective-permute-start(bf16[256,256]{1,0:T(8,128)(2,1)S(1)} %copy-done.43), channel_id=1, source_target_pairs={{0,1},{1,0},{2,3},{3,2},{4,5},{5,4},{6,7},{7,6},{8,9},{9,8},{10,11... | collective-permute-start | bytes 393224 | tf_op jit(solution)/shard_map/ppermute | solution.py:578
  154.4 11.2 %copy-start.29 = (bf16[256,256]{1,0:T(8,128)(2,1)}, bf16[256,256]{1,0:T(8,128)(2,1)S(1)}, u32[]{:S(2)}) copy-start(bf16[256,256]{1,0:T(8,128)(2,1)S(1)} %collective-permute-done.18.refs_12_.refs_28_) | copy-start | bytes 393220
  154.4 9.3 %collective-permute-start.11 = (bf16[256,256]{1,0:T(8,128)(2,1)S(1)}, bf16[256,256]{1,0:T(8,128)(2,1)S(1)}, u32[]{:S(2)}, u32[]{:S(2)}) collective-permute-start(bf16[256,256]{1,0:T(8,128)(2,1)S(1)} %copy-done.44), channel_id=1, source_target_pairs={{0,2},{1,3},{2,0},{3,1},{4,6},{5,7},{6,4},{7,5},{8,10},{9,11},{10,... | collective-permute-start | bytes 393224 | tf_op jit(solution)/shard_map/ppermute | solution.py:578
  155.8 9.8 %copy-start.30 = (bf16[256,256]{1,0:T(8,128)(2,1)}, bf16[256,256]{1,0:T(8,128)(2,1)S(1)}, u32[]{:S(2)}) copy-start(bf16[256,256]{1,0:T(8,128)(2,1)S(1)} %collective-permute-done.13.refs_6_.refs_22_) | copy-start | bytes 393220
  155.8 9.7 %collective-permute-start.12 = (bf16[256,256]{1,0:T(8,128)(2,1)S(1)}, bf16[256,256]{1,0:T(8,128)(2,1)S(1)}, u32[]{:S(2)}, u32[]{:S(2)}) collective-permute-start(bf16[256,256]{1,0:T(8,128)(2,1)S(1)} %copy-done.45), channel_id=1, source_target_pairs={{0,3},{1,2},{2,1},{3,0},{4,7},{5,6},{6,5},{7,4},{8,11},{9,10},{10,... | collective-permute-start | bytes 393224 | tf_op jit(solution)/shard_map/ppermute | solution.py:578
  236.0 3.6 collective-permute-start.21
  236.3 6.5 %collective-permute-start.22 = (bf16[1,256,256]{2,1,0:T(8,128)(2,1)}, bf16[1,256,256]{2,1,0:T(8,128)(2,1)S(1)}, u32[]{:S(2)}, u32[]{:S(2)}) collective-permute-start(bf16[1,256,256]{2,1,0:T(8,128)(2,1)} %get-tuple-element.163), channel_id=1, source_target_pairs={{0,2},{1,3},{2,0},{3,1},{4,6},{5,7},{6,4},{7,5},{8,10},{9,11},{10,... | collective-permute-start | bytes 393224 | tf_op jit(solution)/shard_map/ppermute | solution.py:578
  237.8 6.5 %collective-permute-start.23 = (bf16[1,256,256]{2,1,0:T(8,128)(2,1)}, bf16[1,256,256]{2,1,0:T(8,128)(2,1)S(1)}, u32[]{:S(2)}, u32[]{:S(2)}) collective-permute-start(bf16[1,256,256]{2,1,0:T(8,128)(2,1)} %get-tuple-element.164), channel_id=1, source_target_pairs={{0,3},{1,2},{2,1},{3,0},{4,7},{5,6},{6,5},{7,4},{8,11},{9,10},{10,... | collective-permute-start | bytes 393224 | tf_op jit(solution)/shard_map/ppermute | solution.py:578
  248.4 59.8 %all-to-all-start = ((bf16[32,3,6656]{2,1,0:T(4,128)(2,1)}), bf16[32,3,6656]{2,1,0:T(4,128)(2,1)}, u32[]{:S(2)}, u32[]{:S(2)}) async-start(bf16[32,3,6656]{2,1,0:T(4,128)(2,1)} %copy.101), calls=%async_computation | async-start | bytes 3407872 | tf_op jit(solution)/shard_map/all_to_all | solution.py:586
  252.0 128.6 %all-gather.5.cloned.1.call-start = ((), (), s32[]{:S(2)}) async-start(), calls=%async_computation.4 | async-start | bytes 3514368 | tf_op jit(solution)/shard_map/all_gather | solution.py:824
  252.1 22.1 %collective-permute-start.24 = (bf16[2,256,256]{2,1,0:T(8,128)(2,1)S(1)}, bf16[2,256,256]{2,1,0:T(8,128)(2,1)S(1)}, u32[]{:S(2)}, u32[]{:S(2)}) collective-permute-start(bf16[2,256,256]{2,1,0:T(8,128)(2,1)S(1)} %copy-done.63), channel_id=1, source_target_pairs={{0,1},{1,0},{2,3},{3,2},{4,5},{5,4},{6,7},{7,6},{8,9},{9,8},{10,11... | collective-permute-start | bytes 786440 | tf_op jit(solution)/shard_map/ppermute | solution.py:578
  252.4 23.1 %collective-permute-start.25 = (bf16[2,256,256]{2,1,0:T(8,128)(2,1)S(1)}, bf16[2,256,256]{2,1,0:T(8,128)(2,1)S(1)}, u32[]{:S(2)}, u32[]{:S(2)}) collective-permute-start(bf16[2,256,256]{2,1,0:T(8,128)(2,1)S(1)} %copy-done.62), channel_id=1, source_target_pairs={{0,2},{1,3},{2,0},{3,1},{4,6},{5,7},{6,4},{7,5},{8,10},{9,11},{10,... | collective-permute-start | bytes 786440 | tf_op jit(solution)/shard_map/ppermute | solution.py:578
  253.9 27.4 %collective-permute-start.26 = (bf16[2,256,256]{2,1,0:T(8,128)(2,1)S(1)}, bf16[2,256,256]{2,1,0:T(8,128)(2,1)S(1)}, u32[]{:S(2)}, u32[]{:S(2)}) collective-permute-start(bf16[2,256,256]{2,1,0:T(8,128)(2,1)S(1)} %copy-done.61), channel_id=1, source_target_pairs={{0,3},{1,2},{2,1},{3,0},{4,7},{5,6},{6,5},{7,4},{8,11},{9,10},{10,... | collective-permute-start | bytes 786440 | tf_op jit(solution)/shard_map/ppermute | solution.py:578
  274.2 10.6 %copy-start.19 = (bf16[2,256,1024]{2,1,0:T(8,128)(2,1)S(1)}, bf16[2,256,1024]{2,1,0:T(8,128)(2,1)}, u32[]{:S(2)}) copy-start(bf16[2,256,1024]{2,1,0:T(8,128)(2,1)} %get-tuple-element.170) | copy-start | bytes 3145732
  274.2 11.6 %copy-start.16 = (bf16[2,256,256]{2,1,0:T(8,128)(2,1)}, bf16[2,256,256]{2,1,0:T(8,128)(2,1)S(1)}, u32[]{:S(2)}) copy-start(bf16[2,256,256]{2,1,0:T(8,128)(2,1)S(1)} %collective-permute-done.24.refs_5_) | copy-start | bytes 786436
  275.6 10.2 %copy-start.17 = (bf16[2,256,256]{2,1,0:T(8,128)(2,1)}, bf16[2,256,256]{2,1,0:T(8,128)(2,1)S(1)}, u32[]{:S(2)}) copy-start(bf16[2,256,256]{2,1,0:T(8,128)(2,1)S(1)} %collective-permute-done.25.refs_6_) | copy-start | bytes 786436
  281.4 3.2 collective-permute-start.27
  285.8 22.5 %collective-permute-start.28 = (bf16[256,1024]{1,0:T(8,128)(2,1)}, bf16[256,1024]{1,0:T(8,128)(2,1)S(1)}, u32[]{:S(2)}, u32[]{:S(2)}) collective-permute-start(bf16[256,1024]{1,0:T(8,128)(2,1)} %fusion.28), channel_id=1, source_target_pairs={{0,2},{1,3},{2,0},{3,1},{4,6},{5,7},{6,4},{7,5},{8,10},{9,11},{10,... | collective-permute-start | bytes 1572872 | tf_op jit(solution)/shard_map/ppermute | solution.py:578
  311.4 2.9 collective-permute-start.29
  316.9 22.3 %collective-permute-start.30 = (bf16[256,1024]{1,0:T(8,128)(2,1)}, bf16[256,1024]{1,0:T(8,128)(2,1)S(1)}, u32[]{:S(2)}, u32[]{:S(2)}) collective-permute-start(bf16[256,1024]{1,0:T(8,128)(2,1)} %fusion.29), channel_id=1, source_target_pairs={{0,2},{1,3},{2,0},{3,1},{4,6},{5,7},{6,4},{7,5},{8,10},{9,11},{10,... | collective-permute-start | bytes 1572872 | tf_op jit(solution)/shard_map/ppermute | solution.py:578
  318.5 21.7 %copy-start.58 = (bf16[3,16,256]{2,1,0:T(8,128)(2,1)S(1)}, bf16[3,16,256]{2,1,0:T(8,128)(2,1)}, u32[]{:S(2)}) copy-start(bf16[3,16,256]{2,1,0:T(8,128)(2,1)} %get-tuple-element.199) | copy-start | bytes 73732
  318.5 21.8 %copy-start.56 = (bf16[16,1024]{1,0:T(8,128)(2,1)S(1)}, bf16[16,1024]{1,0:T(8,128)(2,1)}, u32[]{:S(2)}) copy-start(bf16[16,1024]{1,0:T(8,128)(2,1)} %get-tuple-element.196) | copy-start | bytes 98308
  318.5 21.8 %copy-start.57 = (bf16[16,1024]{1,0:T(8,128)(2,1)S(1)}, bf16[16,1024]{1,0:T(8,128)(2,1)}, u32[]{:S(2)}) copy-start(bf16[16,1024]{1,0:T(8,128)(2,1)} %get-tuple-element.197) | copy-start | bytes 98308
  340.0 3.0 collective-permute-start.31
  345.6 21.4 %collective-permute-start.32 = (bf16[256,1024]{1,0:T(8,128)(2,1)}, bf16[256,1024]{1,0:T(8,128)(2,1)}, u32[]{:S(2)}, u32[]{:S(2)}) collective-permute-start(bf16[256,1024]{1,0:T(8,128)(2,1)} %fusion.30), channel_id=1, source_target_pairs={{0,2},{1,3},{2,0},{3,1},{4,6},{5,7},{6,4},{7,5},{8,10},{9,11},{10,... | collective-permute-start | bytes 1572872 | tf_op jit(solution)/shard_map/ppermute | solution.py:578
  346.8 20.1 %all-to-all-start.1 = ((bf16[32,6,448]{2,1,0:T(8,128)(2,1)}), bf16[32,6,448]{2,1,0:T(8,128)(2,1)S(1)}, u32[]{:S(2)}, u32[]{:S(2)}) async-start(bf16[32,6,448]{2,1,0:T(8,128)(2,1)} %copy.105), calls=%async_computation.1 | async-start | bytes 524288 | tf_op jit(solution)/shard_map/all_to_all | solution.py:586
  368.8 7.7 %copy-start.3 = (bf16[3,256,1024]{2,1,0:T(8,128)(2,1)S(1)}, bf16[3,256,1024]{2,1,0:T(8,128)(2,1)}, u32[]{:S(2)}) copy-start(bf16[3,256,1024]{2,1,0:T(8,128)(2,1)} %refs_13_.1) | copy-start | bytes 4718596
  368.8 7.7 %copy-start.50 = (f32[3,256]{1,0:T(4,128)S(1)}, f32[3,256]{1,0:T(4,128)}, u32[]{:S(2)}) copy-start(f32[3,256]{1,0:T(4,128)} %copy-done.49) | copy-start | bytes 9220
  368.8 7.7 %copy-start.53 = (f32[1024]{0:T(1024)S(1)}, f32[1024]{0:T(1024)}, u32[]{:S(2)}) copy-start(f32[1024]{0:T(1024)} %copy-done.52) | copy-start | bytes 12292
  368.8 7.7 %copy-start.55 = (f32[3,256]{1,0:T(4,128)S(1)}, f32[3,256]{1,0:T(4,128)}, u32[]{:S(2)}) copy-start(f32[3,256]{1,0:T(4,128)} %copy-done.54) | copy-start | bytes 9220
  368.8 21.3 %all-to-all-start.2 = ((bf16[32,16,448]{2,1,0:T(8,128)(2,1)}), bf16[32,16,448]{2,1,0:T(8,128)(2,1)S(1)}, u32[]{:S(2)}, u32[]{:S(2)}) async-start(bf16[32,16,448]{2,1,0:T(8,128)(2,1)} %bitcast.202), calls=%async_computation.2 | async-start | bytes 1048576 | tf_op jit(solution)/shard_map/all_to_all | solution.py:586
  378.5 14.7 %copy-start.1 = (bf16[8,16,2,656]{3,2,1,0:T(2,128)(2,1)S(1)}, bf16[8,16,2,656]{3,2,1,0:T(2,128)(2,1)}, u32[]{:S(2)}) copy-start(bf16[8,16,2,656]{3,2,1,0:T(2,128)(2,1)} %param.33) | copy-start | bytes 1007620
  (38 other events, 136.9 us)
Sparse Core Ops, SparseCore 0:
  11.5 155.9 all-gather.2
  311.5 66.3 all-gather.4

commit v5 on v4

--- a/solution.py
+++ b/solution.py
@@ -825,11 +825,12 @@
         if seq == 2:
             there, far = lax.optimization_barrier((there, far))
         if seq:
-            grad_normeds.append(chip + far.astype(F32))
+            grad_normeds.append(chip + (far,))
         joined_up_grads.append(up_grad.transpose(1, 0, 2).reshape(rank, 3 * wide))
         joined_low_grads.append(low_grad)
-        there = pair_swap(there, 1).astype(F32)
-        chip, give = here[0].astype(F32) + there[0], (here[1].astype(F32) + there[1]).astype(BF)
+        there = pair_swap(there, 1)
+        give = (here[1].astype(F32) + there[1].astype(F32)).astype(BF)
+        chip = (here[0], there[0])
         far = pair_swap(give, 2)
 
     piece = 3 * wide // blocks
@@ -843,7 +844,8 @@
     late = tie(late, there)
     late, far = lax.optimization_barrier((swap_all(late, everyone), far))
     late = late.reshape(parts, blocks, seqs, some, -1)
-    grad_normeds.append(chip + far.astype(F32))
+    grad_normeds.append(chip + (far,))
+    grad_normeds = [sum(part.astype(F32) for part in parts_of) for parts_of in grad_normeds]
     grad_hidden = grad_middle + norm_back(jnp.stack(grad_normeds), first_normed, first_scale, attn_scale)
     late_low = late[..., :low_size].reshape(owners * seqs, -1)
     late_up = late[..., low_size:].transpose(1, 0, 2, 3, 4).reshape(blocks, parts * seqs, -1)

time: 405 us -> 400 us (0.988)
  no operation moved by 1% of the time
where the time goes in v5:
time: 400 us; the launch traced here: 396 us
  Pallas kernels  184 us (46%)
  waiting for transfers between devices  90 us (22%)
  starting transfers between devices  40.1 us (10%)
  local copies, waits for them, and re-layouts  35 us (9%)
  other arithmetic  30.5 us (8%)
  between operations  15.4 us (4%)
    ppermute x29, waiting for transfers between devices, pair_swap(): return lax.ppermute(values, 'mp', [(i, i ^ bit) for i in range(size)])  66.5 us
    pallas_call x3, Pallas kernels, attend_back(): pl.pallas_call(attend_back_kernel, grid_spec=pltpu.PrefetchScalarGridSpec...  61 us
    pallas_call x1, Pallas kernels, gated(): pl.pallas_call(lambda *refs: gated_kernel(*refs, width=width, blocks=bloc...  57.6 us
    pallas_call x3, Pallas kernels, attend(): pl.pallas_call(attend_kernel, grid_spec=pltpu.PrefetchScalarGridSpec(num_...  36 us
    ppermute x29, starting transfers between devices, pair_swap(): return lax.ppermute(values, 'mp', [(i, i ^ bit) for i in range(size)])  18.2 us
    all_to_all x3, starting transfers between devices, swap_all(): return lax.all_to_all(values, axes, 0, 0, tiled=True)  14.6 us
    pallas_call x1, Pallas kernels, project(): pl.pallas_call(lambda *refs: project_kernel(*refs, wide=wide), grid_spec=...  13.8 us
    all_to_all x3, waiting for transfers between devices, swap_all(): return lax.all_to_all(values, axes, 0, 0, tiled=True)  13.1 us
  transfers between devices with their start and end apart: 38, of which 18 were waited for; matrix products, arithmetic and copies ran while one was open for 12% of the time, Pallas kernels for 31%

profile of v5, /device:TPU:0, one launch (start us, length us, event | category | flops | bytes accessed | tf_op | source)
XLA Modules:
  0.0 395.8 jit_solution(8354580606313810539)
XLA Ops:
  7.3 1.9 pad_maximum_fusion.3
  13.6 2.9 collective-permute-start.3
  17.7 1.6 collective-permute-start.6
  19.3 2.6 collective-permute-start.7
  21.8 1.3 collective-permute-start.8
  25.8 1.7 fusion.6.refs_1_.refs_8_
  27.5 1.5 gather_fusion.1
  29.7 1.2 gather_fusion
  30.9 1.2 gather_fusion.6
  32.1 2.3 gather_fusion.7
  34.3 2.2 gather_fusion.5
  36.5 3.2 multiply_sine_fusion
  40.2 9.6 %collective-permute-done.7 = bf16[1032,128]{1,0:T(8,128)(2,1)S(1)} collective-permute-done((bf16[1032,128]{1,0:T(8,128)(2,1)}, bf16[1032,128]{1,0:T(8,128)(2,1)S(1)}, u32[]{:S(2)}, u32[]{:S(2)}) %collective-permute-start.7) | collective-permute-done | bytes 264224 | tf_op jit(solution)/shard_map/ppermute | solution.py:604
  50.6 1.2 pad_maximum_fusion
  51.8 1.6 collective-permute-start.9
  53.5 1.0 constant_dynamic-update-slice_fusion.1
  56.9 33.4 %collective-permute-done.1.refs_3_.refs_10_ = bf16[3,256,1024]{2,1,0:T(8,128)(2,1)} collective-permute-done((bf16[3,256,1024]{2,1,0:T(8,128)(2,1)}, bf16[3,256,1024]{2,1,0:T(8,128)(2,1)}, u32[]{:S(2)}, u32[]{:S(2)}) %collective-permute-start.1) | collective-permute-done | bytes 1572896 | tf_op jit(solution)/shard_map/ppermute | solution.py:578
  91.1 3.4 collective-permute-done.19
  95.9 13.8 %project.1 = (bf16[3,4,256,256]{3,2,1,0:T(8,128)(2,1)}, bf16[3,4,256,256]{3,2,1,0:T(8,128)(2,1)}, bf16[3,4,256,256]{3,2,1,0:T(8,128)(2,1)}, bf16[3,4,256,16]{3,2,1,0:T(8,128)(2,1)}) custom-call(s32[9]{0:T(128)} %pad_add_fusion.refs_0_.place, bf16[3,256,1024]{2,1,0:T(8,128)(2,1)} %fusion.6.refs_1_.refs_8_, ...), custom_call_target="tpu_custom_call" | custom-call | tf_op jit(solution)/shard_map/project/pallas_call | solution.py:104
  109.8 11.9 %attend.3 = (bf16[256,256]{1,0:T(8,128)(2,1)}, bf16[256,256]{1,0:T(8,128)(2,1)}, bf16[256,256]{1,0:T(8,128)(2,1)}, bf16[256,256]{1,0:T(8,128)(2,1)}, bf16[2,2,2,...) custom-call(s32[9]{0:T(128)} %pad_add_fusion.refs_0_.place, bf16[3,4,256,256]{3,2,1,0:T(8,128)(2,1)} %get-tuple-element.136.query, ...), custom_call_target="tpu_custom_call" | custom-call | tf_op jit(solution)/shard_map/attend/pallas_call | solution.py:166
  121.7 11.9 %attend.4 = (bf16[256,256]{1,0:T(8,128)(2,1)}, bf16[256,256]{1,0:T(8,128)(2,1)}, bf16[256,256]{1,0:T(8,128)(2,1)}, bf16[256,256]{1,0:T(8,128)(2,1)}, bf16[2,2,2,...) custom-call(s32[9]{0:T(128)} %pad_add_fusion.refs_0_.place, bf16[3,4,256,256]{3,2,1,0:T(8,128)(2,1)} %get-tuple-element.136.query, ...), custom_call_target="tpu_custom_call" | custom-call | tf_op jit(solution)/shard_map/attend/pallas_call | solution.py:166
  133.7 12.1 %attend.5 = (bf16[256,256]{1,0:T(8,128)(2,1)}, bf16[256,256]{1,0:T(8,128)(2,1)}, bf16[256,256]{1,0:T(8,128)(2,1)}, bf16[256,256]{1,0:T(8,128)(2,1)}, bf16[2,2,2,...) custom-call(s32[9]{0:T(128)} %pad_add_fusion.refs_0_.place, bf16[3,4,256,256]{3,2,1,0:T(8,128)(2,1)} %get-tuple-element.136.query, ...), custom_call_target="tpu_custom_call" | custom-call | tf_op jit(solution)/shard_map/attend/pallas_call | solution.py:166
  145.9 1.6 collective-permute-start.17
  148.1 1.6 collective-permute-start.14
  149.8 2.7 collective-permute-done.17.refs_11_.refs_27_
  152.4 1.9 collective-permute-done.18.refs_12_.refs_28_
  154.4 1.4 collective-permute-start.11
  155.8 1.1 collective-permute-start.12
  158.1 1.9 collective-permute-done.15.refs_8_.refs_24_
  159.9 3.7 collective-permute-done.11.refs_3_.refs_19_
  163.7 1.9 collective-permute-done.12.refs_4_.refs_20_
  166.2 8.2 %merge.1 = (f32[3,256,1024]{2,1,0:T(8,128)}, bf16[3,256,1024]{2,1,0:T(8,128)(2,1)}, bf16[3,256,16]{2,1,0:T(8,128)(2,1)}) custom-call(s32[9]{0:T(128)} %pad_add_fusion.refs_0_.place, bf16[256,256]{1,0:T(8,128)(2,1)} %get-tuple-element.127.refs_1_.refs_17_.refs_0_, bf16[256,256]{1,0:T(8,128)(2,1)} %copy-done.33, bf16[256,256]{1,0:T(8,128)(2,1)} %copy-done.34, ...), custom_call_target="tpu_custom_call" | custom-call | tf_op jit(solution)/shard_map/merge/pallas_call | solution.py:347
  174.4 57.6 %gated.1 = (bf16[768,1024]{1,0:T(8,128)(2,1)}, bf16[4,2,48,656]{3,2,1,0:T(8,128)(2,1)}, bf16[4,48,656]{2,1,0:T(8,128)(2,1)}, bf16[48,1024]{1,0:T(8,128)(2,1)}, b...) custom-call(s32[9]{0:T(128)} %pad_add_fusion.refs_0_.place, ...), custom_call_target="tpu_custom_call" | custom-call | tf_op jit(solution)/shard_map/gated/pallas_call | solution.py:461
  232.1 0.9 fusion.33
  234.9 1.1 slice_bitcast_fusion.6
  236.3 1.5 collective-permute-start.22
  239.6 3.3 collective-permute-done.22.refs_6_
  242.9 1.4 collective-permute-done.23.refs_7_
  244.3 1.0 copy.135
  246.2 2.3 copy.101
  248.5 3.1 all-to-all-start
  251.9 1.7 collective-permute-start.25
  253.6 20.2 %attend_back.3 = (bf16[2,256,1024]{2,1,0:T(8,128)(2,1)}, bf16[2,256,1024]{2,1,0:T(8,128)(2,1)}, bf16[3,16,256]{2,1,0:T(8,128)(2,1)}, bf16[16,1024]{1,0:T(8,128)(2,1)}) custom-call(s32[9]{0:T(128)} %pad_add_fusion.refs_0_.place, bf16[3,4,256,256]{3,2,1,0:T(8,128)(2,1)} %get-tuple-element.136.query, bf16[3,4,256,256]{3,2,1,0:T(8,128)(2,1)} %get-tuple-element.125.key, ...), custom_call_target="tpu_custom_call" | custom-call | tf_op jit(solution)/shard_map/attend_back/pallas_call | solution.py:279
  273.8 1.5 collective-permute-done.25.refs_6_
  275.3 5.8 %collective-permute-done.26.refs_7_ = bf16[2,256,256]{2,1,0:T(8,128)(2,1)S(1)} collective-permute-done((bf16[2,256,256]{2,1,0:T(8,128)(2,1)S(1)}, bf16[2,256,256]{2,1,0:T(8,128)(2,1)S(1)}, u32[]{:S(2)}, u32[]{:S(2)}) %collective-permute-start.26) | collective-permute-done | bytes 262176 | tf_op jit(solution)/shard_map/ppermute | solution.py:578
  281.7 2.5 collective-permute-done.27
  284.2 1.0 copy-done.17
  285.2 2.0 fusion.19
  289.4 20.2 %attend_back.4 = (bf16[2,256,1024]{2,1,0:T(8,128)(2,1)}, bf16[2,256,1024]{2,1,0:T(8,128)(2,1)}, bf16[3,16,256]{2,1,0:T(8,128)(2,1)}, bf16[16,1024]{1,0:T(8,128)(2,1)}) custom-call(s32[9]{0:T(128)} %pad_add_fusion.refs_0_.place, bf16[3,4,256,256]{3,2,1,0:T(8,128)(2,1)} %get-tuple-element.136.query, bf16[3,4,256,256]{3,2,1,0:T(8,128)(2,1)} %get-tuple-element.125.key, ...), custom_call_target="tpu_custom_call" | custom-call | tf_op jit(solution)/shard_map/attend_back/pallas_call | solution.py:279
  311.5 2.6 collective-permute-done.29
  315.1 1.7 collective-permute-start.30
  316.7 20.7 %attend_back.5 = (bf16[2,256,1024]{2,1,0:T(8,128)(2,1)}, bf16[2,256,1024]{2,1,0:T(8,128)(2,1)}, bf16[3,16,256]{2,1,0:T(8,128)(2,1)}, bf16[16,1024]{1,0:T(8,128)(2,1)}) custom-call(s32[9]{0:T(128)} %pad_add_fusion.refs_0_.place, bf16[3,4,256,256]{3,2,1,0:T(8,128)(2,1)} %get-tuple-element.136.query, bf16[3,4,256,256]{3,2,1,0:T(8,128)(2,1)} %get-tuple-element.125.key, ...), custom_call_target="tpu_custom_call" | custom-call | tf_op jit(solution)/shard_map/attend_back/pallas_call | solution.py:279
  341.1 2.0 fusion.21
  344.3 5.9 %all-to-all-start.1 = ((bf16[32,6,448]{2,1,0:T(8,128)(2,1)}), bf16[32,6,448]{2,1,0:T(8,128)(2,1)S(1)}, u32[]{:S(2)}, u32[]{:S(2)}) async-start(bf16[32,6,448]{2,1,0:T(8,128)(2,1)} %copy.105), calls=%async_computation.1 | async-start | bytes 524288 | tf_op jit(solution)/shard_map/all_to_all | solution.py:586
  350.2 1.3 fusion.16
  351.5 2.6 fusion.15
  354.1 8.4 %all-to-all-done.1 = bf16[32,6,448]{2,1,0:T(8,128)(2,1)S(1)} async-done(((bf16[32,6,448]{2,1,0:T(8,128)(2,1)}), bf16[32,6,448]{2,1,0:T(8,128)(2,1)S(1)}, u32[]{:S(2)}, u32[]{:S(2)}) %all-to-all-start.1) | async-done | bytes 172064 | tf_op jit(solution)/shard_map/all_to_all | solution.py:586
  364.4 5.6 %all-to-all-start.2 = ((bf16[32,16,448]{2,1,0:T(8,128)(2,1)}), bf16[32,16,448]{2,1,0:T(8,128)(2,1)S(1)}, u32[]{:S(2)}, u32[]{:S(2)}) async-start(bf16[32,16,448]{2,1,0:T(8,128)(2,1)} %bitcast.196), calls=%async_computation.2 | async-start | bytes 1048576 | tf_op jit(solution)/shard_map/all_to_all | solution.py:586
  370.1 1.7 fusion.14
  371.9 1.1 fusion.17
  373.8 2.1 fusion.11
  375.9 5.0 %settle_early.1 = (f32[8,16,1024]{2,1,0:T(8,128)}, f32[8,16,1024]{2,1,0:T(8,128)}, f32[8,16,1024]{2,1,0:T(8,128)}, f32[8,16,256]{2,1,0:T(8,128)}, f32[8,16,2,656]{3,2,1,0:T(2,128)}, /*index=5*/f32[8,16,656]{2,1,0:T(8,128)}) custom-call(s32[9]{0:T(128)} %pad_add_fusion.refs_0_.place, bf16[32,16,3328]{2,1,0:T(8,128)(2,1)} %all-gather.5.cloned.1.call-done.refs_1_), custom_call_target="tpu_custom_call" | custom-call | tf_op jit(solution)/shard_map/settle_early/pallas_call | solution.py:532
  380.9 4.7 %all-to-all-done.2.refs_0_ = bf16[32,16,448]{2,1,0:T(8,128)(2,1)S(1)} async-done(((bf16[32,16,448]{2,1,0:T(8,128)(2,1)}), bf16[32,16,448]{2,1,0:T(8,128)(2,1)S(1)}, u32[]{:S(2)}, u32[]{:S(2)}) %all-to-all-start.2) | async-done | bytes 458784 | tf_op jit(solution)/shard_map/all_to_all | solution.py:586
  386.4 2.3 settle_late.1
  (274 shorter events, 36.1 us)
Async XLA Ops:
  7.2 167.2 %all-gather.3.cloned.1.call-start = ((), (), s32[]{:S(2)}) async-start(), calls=%async_computation.3 | async-start | bytes 16625664 | tf_op jit(solution)/shard_map/all_gather | solution.py:655
  10.8 12.4 %copy-start.59 = (bf16[1024]{0:T(1024)(128)(2,1)S(1)}, bf16[1024]{0:T(1024)(128)(2,1)}, u32[]{:S(2)}) copy-start(bf16[1024]{0:T(1024)(128)(2,1)} %param.22) | copy-start | bytes 6148
  10.9 12.4 %copy-start.2 = (bf16[3,256,1024]{2,1,0:T(8,128)(2,1)S(1)}, bf16[3,256,1024]{2,1,0:T(8,128)(2,1)}, u32[]{:S(2)}) copy-start(bf16[3,256,1024]{2,1,0:T(8,128)(2,1)} %refs_13_.1) | copy-start | bytes 4718596
  13.6 26.1 %collective-permute-start.3 = (bf16[3,16,2560]{2,1,0:T(8,128)(2,1)}, bf16[3,16,2560]{2,1,0:T(8,128)(2,1)S(1)}, u32[]{:S(2)}, u32[]{:S(2)}) collective-permute-start(bf16[3,16,2560]{2,1,0:T(8,128)(2,1)} %fusion.30), channel_id=1, source_target_pairs={{0,2},{1,3},{2,0},{3,1},{4,6},{5,7},{6,4},{7,5},{8,10},{9,11},{10,... | collective-permute-start | bytes 737288 | tf_op jit(solution)/shard_map/ppermute | solution.py:578
  16.6 38.0 %collective-permute-start.2 = (bf16[3,16,2560]{2,1,0:T(8,128)(2,1)}, bf16[3,16,2560]{2,1,0:T(8,128)(2,1)S(1)}, u32[]{:S(2)}, u32[]{:S(2)}) collective-permute-start(bf16[3,16,2560]{2,1,0:T(8,128)(2,1)} %fusion.30), channel_id=1, source_target_pairs={{0,1},{1,0},{2,3},{3,2},{4,5},{5,4},{6,7},{7,6},{8,9},{9,8},{10,11... | collective-permute-start | bytes 737288 | tf_op jit(solution)/shard_map/ppermute | solution.py:578
  17.7 22.5 %collective-permute-start.6 = (bf16[1032,128]{1,0:T(8,128)(2,1)}, bf16[1032,128]{1,0:T(8,128)(2,1)S(1)}, u32[]{:S(2)}, u32[]{:S(2)}) collective-permute-start(bf16[1032,128]{1,0:T(8,128)(2,1)} %get-tuple-element.221), channel_id=1, source_target_pairs={{0,8},{4,12},{8,16},{12,20},{16,24},{20,28},{24,0},{28,4},{1,9},{5... | collective-permute-start | bytes 792584 | tf_op jit(solution)/shard_map/ppermute | solution.py:604
  19.3 30.6 %collective-permute-start.7 = (bf16[1032,128]{1,0:T(8,128)(2,1)}, bf16[1032,128]{1,0:T(8,128)(2,1)S(1)}, u32[]{:S(2)}, u32[]{:S(2)}) collective-permute-start(bf16[1032,128]{1,0:T(8,128)(2,1)} %get-tuple-element.221), channel_id=1, source_target_pairs={{0,16},{4,20},{8,24},{12,28},{16,0},{20,4},{24,8},{28,12},{1,17},{... | collective-permute-start | bytes 792584 | tf_op jit(solution)/shard_map/ppermute | solution.py:604
  21.8 28.8 %collective-permute-start.8 = (bf16[1032,128]{1,0:T(8,128)(2,1)}, bf16[1032,128]{1,0:T(8,128)(2,1)}, u32[]{:S(2)}, u32[]{:S(2)}) collective-permute-start(bf16[1032,128]{1,0:T(8,128)(2,1)} %get-tuple-element.221), channel_id=1, source_target_pairs={{0,24},{4,28},{8,0},{12,4},{16,8},{20,12},{24,16},{28,20},{1,25},{... | collective-permute-start | bytes 792584 | tf_op jit(solution)/shard_map/ppermute | solution.py:604
  32.1 21.4 %copy-start.4 = (bf16[8,1032,128]{2,1,0:T(8,128)(2,1)S(1)}, bf16[8,1032,128]{2,1,0:T(8,128)(2,1)}, u32[]{:S(2)}) copy-start(bf16[8,1032,128]{2,1,0:T(8,128)(2,1)} %constant_dynamic-update-slice_fusion.4) | copy-start | bytes 6340612
  39.7 50.7 %collective-permute-start.1 = (bf16[3,256,1024]{2,1,0:T(8,128)(2,1)}, bf16[3,256,1024]{2,1,0:T(8,128)(2,1)}, u32[]{:S(2)}, u32[]{:S(2)}) collective-permute-start(bf16[3,256,1024]{2,1,0:T(8,128)(2,1)} %fusion.6.refs_1_.refs_8_), channel_id=1, source_target_pairs={{0,2},{1,3},{2,0},{3,1},{4,6},{5,7},{6,4},{7,5},{8,10},{9,11},{10,... | collective-permute-start | bytes 4718600 | tf_op jit(solution)/shard_map/ppermute | solution.py:578
  40.2 55.7 %collective-permute-start = (bf16[3,256,1024]{2,1,0:T(8,128)(2,1)}, bf16[3,256,1024]{2,1,0:T(8,128)(2,1)}, u32[]{:S(2)}, u32[]{:S(2)}) collective-permute-start(bf16[3,256,1024]{2,1,0:T(8,128)(2,1)} %fusion.6.refs_1_.refs_8_), channel_id=1, source_target_pairs={{0,1},{1,0},{2,3},{3,2},{4,5},{5,4},{6,7},{7,6},{8,9},{9,8},{10,11... | collective-permute-start | bytes 4718600 | tf_op jit(solution)/shard_map/ppermute | solution.py:578
  49.8 4.7 %collective-permute-start.4 = (bf16[3,16,2560]{2,1,0:T(8,128)(2,1)S(1)}, bf16[3,16,2560]{2,1,0:T(8,128)(2,1)S(1)}, u32[]{:S(2)}, u32[]{:S(2)}) collective-permute-start(bf16[3,16,2560]{2,1,0:T(8,128)(2,1)S(1)} %collective-permute-done.3), channel_id=1, source_target_pairs={{0,1},{1,0},{2,3},{3,2},{4,5},{5,4},{6,7},{7,6},{8,9},{9,8},{10,11... | collective-permute-start | bytes 737288 | tf_op jit(solution)/shard_map/ppermute | solution.py:578
  51.8 38.6 %collective-permute-start.9 = (bf16[4,1032,128]{2,1,0:T(8,128)(2,1)S(1)}, bf16[4,1032,128]{2,1,0:T(8,128)(2,1)S(1)}, u32[]{:S(2)}, u32[]{:S(2)}) collective-permute-start(bf16[4,1032,128]{2,1,0:T(8,128)(2,1)S(1)} %pad_maximum_fusion), channel_id=1, source_target_pairs={{0,4},{4,0},{8,12},{12,8},{16,20},{20,16},{24,28},{28,24},{1,5},{5... | collective-permute-start | bytes 3170312 | tf_op jit(solution)/shard_map/ppermute | solution.py:606
  90.4 5.5 %collective-permute-start.5 = (bf16[3,256,1024]{2,1,0:T(8,128)(2,1)}, bf16[3,256,1024]{2,1,0:T(8,128)(2,1)}, u32[]{:S(2)}, u32[]{:S(2)}) collective-permute-start(bf16[3,256,1024]{2,1,0:T(8,128)(2,1)} %collective-permute-done.1.refs_3_.refs_10_), channel_id=1, source_target_pairs={{0,1},{1,0},{2,3},{3,2},{4,5},{5,4},{6,7},{7,6},{8,9},{9,8},{10,11... | collective-permute-start | bytes 4718600 | tf_op jit(solution)/shard_map/ppermute | solution.py:578
  90.6 4.0 collective-permute-start.19
  94.6 15.1 %copy-start.6 = (bf16[8,2,256,128]{3,2,1,0:T(8,128)(2,1)}, bf16[8,2,256,128]{3,2,1,0:T(8,128)(2,1)S(1)}, u32[]{:S(2)}) copy-start(bf16[8,2,256,128]{3,2,1,0:T(8,128)(2,1)S(1)} %pad_maximum_fusion.1.refs_14_.refs_11_) | copy-start | bytes 3145732
  94.6 53.5 %collective-permute-start.20 = (bf16[8,2,256,128]{3,2,1,0:T(8,128)(2,1)S(1)}, bf16[8,2,256,128]{3,2,1,0:T(8,128)(2,1)}, u32[]{:S(2)}, u32[]{:S(2)}) collective-permute-start(bf16[8,2,256,128]{3,2,1,0:T(8,128)(2,1)S(1)} %pad_maximum_fusion.1.refs_14_.refs_11_), channel_id=1, source_target_pairs={{0,2},{1,3},{2,0},{3,1},{4,6},{5,7},{6,4},{7,5},{8,10},{9,11},{10,... | collective-permute-start | bytes 3145736 | tf_op jit(solution)/shard_map/ppermute | solution.py:578
  133.6 14.1 %copy-start.40 = (bf16[256,256]{1,0:T(8,128)(2,1)S(1)}, bf16[256,256]{1,0:T(8,128)(2,1)}, u32[]{:S(2)}) copy-start(bf16[256,256]{1,0:T(8,128)(2,1)} %get-tuple-element.133.refs_1_) | copy-start | bytes 393220
  133.7 14.5 %copy-start.41 = (bf16[256,256]{1,0:T(8,128)(2,1)S(1)}, bf16[256,256]{1,0:T(8,128)(2,1)}, u32[]{:S(2)}) copy-start(bf16[256,256]{1,0:T(8,128)(2,1)} %get-tuple-element.134.refs_2_) | copy-start | bytes 393220
  133.7 16.0 %copy-start.42 = (bf16[256,256]{1,0:T(8,128)(2,1)S(1)}, bf16[256,256]{1,0:T(8,128)(2,1)}, u32[]{:S(2)}) copy-start(bf16[256,256]{1,0:T(8,128)(2,1)} %get-tuple-element.135.refs_3_) | copy-start | bytes 393220
  133.7 18.8 %copy-start.43 = (bf16[256,256]{1,0:T(8,128)(2,1)S(1)}, bf16[256,256]{1,0:T(8,128)(2,1)}, u32[]{:S(2)}) copy-start(bf16[256,256]{1,0:T(8,128)(2,1)} %get-tuple-element.128.refs_1_) | copy-start | bytes 393220
  133.7 20.7 %copy-start.44 = (bf16[256,256]{1,0:T(8,128)(2,1)S(1)}, bf16[256,256]{1,0:T(8,128)(2,1)}, u32[]{:S(2)}) copy-start(bf16[256,256]{1,0:T(8,128)(2,1)} %get-tuple-element.129.refs_2_) | copy-start | bytes 393220
  133.7 22.1 %copy-start.45 = (bf16[256,256]{1,0:T(8,128)(2,1)S(1)}, bf16[256,256]{1,0:T(8,128)(2,1)}, u32[]{:S(2)}) copy-start(bf16[256,256]{1,0:T(8,128)(2,1)} %get-tuple-element.130.refs_3_) | copy-start | bytes 393220
  133.7 23.2 %copy-start.60 = (bf16[1024]{0:T(1024)(128)(2,1)S(1)}, bf16[1024]{0:T(1024)(128)(2,1)}, u32[]{:S(2)}) copy-start(bf16[1024]{0:T(1024)(128)(2,1)} %param.23) | copy-start | bytes 6148
  145.9 3.8 collective-permute-start.16
  145.9 6.6 %collective-permute-start.17 = (bf16[256,256]{1,0:T(8,128)(2,1)}, bf16[256,256]{1,0:T(8,128)(2,1)S(1)}, u32[]{:S(2)}, u32[]{:S(2)}) collective-permute-start(bf16[256,256]{1,0:T(8,128)(2,1)} %get-tuple-element.139.refs_2_), channel_id=1, source_target_pairs={{0,2},{1,3},{2,0},{3,1},{4,6},{5,7},{6,4},{7,5},{8,10},{9,11},{10,... | collective-permute-start | bytes 393224 | tf_op jit(solution)/shard_map/ppermute | solution.py:578
  147.4 6.9 %collective-permute-start.18 = (bf16[256,256]{1,0:T(8,128)(2,1)}, bf16[256,256]{1,0:T(8,128)(2,1)S(1)}, u32[]{:S(2)}, u32[]{:S(2)}) collective-permute-start(bf16[256,256]{1,0:T(8,128)(2,1)} %get-tuple-element.140.refs_3_), channel_id=1, source_target_pairs={{0,3},{1,2},{2,1},{3,0},{4,7},{5,6},{6,5},{7,4},{8,11},{9,10},{10,... | collective-permute-start | bytes 393224 | tf_op jit(solution)/shard_map/ppermute | solution.py:578
  147.7 8.1 %collective-permute-start.13 = (bf16[256,256]{1,0:T(8,128)(2,1)S(1)}, bf16[256,256]{1,0:T(8,128)(2,1)S(1)}, u32[]{:S(2)}, u32[]{:S(2)}) collective-permute-start(bf16[256,256]{1,0:T(8,128)(2,1)S(1)} %copy-done.40), channel_id=1, source_target_pairs={{0,1},{1,0},{2,3},{3,2},{4,5},{5,4},{6,7},{7,6},{8,9},{9,8},{10,11... | collective-permute-start | bytes 393224 | tf_op jit(solution)/shard_map/ppermute | solution.py:578
  148.1 9.9 %collective-permute-start.14 = (bf16[256,256]{1,0:T(8,128)(2,1)S(1)}, bf16[256,256]{1,0:T(8,128)(2,1)S(1)}, u32[]{:S(2)}, u32[]{:S(2)}) collective-permute-start(bf16[256,256]{1,0:T(8,128)(2,1)S(1)} %copy-done.41), channel_id=1, source_target_pairs={{0,2},{1,3},{2,0},{3,1},{4,6},{5,7},{6,4},{7,5},{8,10},{9,11},{10,... | collective-permute-start | bytes 393224 | tf_op jit(solution)/shard_map/ppermute | solution.py:578
  149.7 15.9 %copy-start.27 = (bf16[256,256]{1,0:T(8,128)(2,1)}, bf16[256,256]{1,0:T(8,128)(2,1)S(1)}, u32[]{:S(2)}) copy-start(bf16[256,256]{1,0:T(8,128)(2,1)S(1)} %collective-permute-done.16.refs_10_.refs_26_) | copy-start | bytes 393220
  149.7 10.3 %collective-permute-start.15 = (bf16[256,256]{1,0:T(8,128)(2,1)S(1)}, bf16[256,256]{1,0:T(8,128)(2,1)S(1)}, u32[]{:S(2)}, u32[]{:S(2)}) collective-permute-start(bf16[256,256]{1,0:T(8,128)(2,1)S(1)} %copy-done.42), channel_id=1, source_target_pairs={{0,3},{1,2},{2,1},{3,0},{4,7},{5,6},{6,5},{7,4},{8,11},{9,10},{10,... | collective-permute-start | bytes 393224 | tf_op jit(solution)/shard_map/ppermute | solution.py:578
  152.4 13.1 %copy-start.28 = (bf16[256,256]{1,0:T(8,128)(2,1)}, bf16[256,256]{1,0:T(8,128)(2,1)S(1)}, u32[]{:S(2)}) copy-start(bf16[256,256]{1,0:T(8,128)(2,1)S(1)} %collective-permute-done.17.refs_11_.refs_27_) | copy-start | bytes 393220
  152.4 7.5 %collective-permute-start.10 = (bf16[256,256]{1,0:T(8,128)(2,1)S(1)}, bf16[256,256]{1,0:T(8,128)(2,1)S(1)}, u32[]{:S(2)}, u32[]{:S(2)}) collective-permute-start(bf16[256,256]{1,0:T(8,128)(2,1)S(1)} %copy-done.43), channel_id=1, source_target_pairs={{0,1},{1,0},{2,3},{3,2},{4,5},{5,4},{6,7},{7,6},{8,9},{9,8},{10,11... | collective-permute-start | bytes 393224 | tf_op jit(solution)/shard_map/ppermute | solution.py:578
  154.4 11.2 %copy-start.29 = (bf16[256,256]{1,0:T(8,128)(2,1)}, bf16[256,256]{1,0:T(8,128)(2,1)S(1)}, u32[]{:S(2)}) copy-start(bf16[256,256]{1,0:T(8,128)(2,1)S(1)} %collective-permute-done.18.refs_12_.refs_28_) | copy-start | bytes 393220
  154.4 9.3 %collective-permute-start.11 = (bf16[256,256]{1,0:T(8,128)(2,1)S(1)}, bf16[256,256]{1,0:T(8,128)(2,1)S(1)}, u32[]{:S(2)}, u32[]{:S(2)}) collective-permute-start(bf16[256,256]{1,0:T(8,128)(2,1)S(1)} %copy-done.44), channel_id=1, source_target_pairs={{0,2},{1,3},{2,0},{3,1},{4,6},{5,7},{6,4},{7,5},{8,10},{9,11},{10,... | collective-permute-start | bytes 393224 | tf_op jit(solution)/shard_map/ppermute | solution.py:578
  155.8 9.8 %copy-start.30 = (bf16[256,256]{1,0:T(8,128)(2,1)}, bf16[256,256]{1,0:T(8,128)(2,1)S(1)}, u32[]{:S(2)}) copy-start(bf16[256,256]{1,0:T(8,128)(2,1)S(1)} %collective-permute-done.13.refs_6_.refs_22_) | copy-start | bytes 393220
  155.8 9.7 %collective-permute-start.12 = (bf16[256,256]{1,0:T(8,128)(2,1)S(1)}, bf16[256,256]{1,0:T(8,128)(2,1)S(1)}, u32[]{:S(2)}, u32[]{:S(2)}) collective-permute-start(bf16[256,256]{1,0:T(8,128)(2,1)S(1)} %copy-done.45), channel_id=1, source_target_pairs={{0,3},{1,2},{2,1},{3,0},{4,7},{5,6},{6,5},{7,4},{8,11},{9,10},{10,... | collective-permute-start | bytes 393224 | tf_op jit(solution)/shard_map/ppermute | solution.py:578
  236.0 3.6 collective-permute-start.21
  236.3 6.5 %collective-permute-start.22 = (bf16[1,256,256]{2,1,0:T(8,128)(2,1)}, bf16[1,256,256]{2,1,0:T(8,128)(2,1)S(1)}, u32[]{:S(2)}, u32[]{:S(2)}) collective-permute-start(bf16[1,256,256]{2,1,0:T(8,128)(2,1)} %get-tuple-element.163), channel_id=1, source_target_pairs={{0,2},{1,3},{2,0},{3,1},{4,6},{5,7},{6,4},{7,5},{8,10},{9,11},{10,... | collective-permute-start | bytes 393224 | tf_op jit(solution)/shard_map/ppermute | solution.py:578
  237.8 6.5 %collective-permute-start.23 = (bf16[1,256,256]{2,1,0:T(8,128)(2,1)}, bf16[1,256,256]{2,1,0:T(8,128)(2,1)S(1)}, u32[]{:S(2)}, u32[]{:S(2)}) collective-permute-start(bf16[1,256,256]{2,1,0:T(8,128)(2,1)} %get-tuple-element.164), channel_id=1, source_target_pairs={{0,3},{1,2},{2,1},{3,0},{4,7},{5,6},{6,5},{7,4},{8,11},{9,10},{10,... | collective-permute-start | bytes 393224 | tf_op jit(solution)/shard_map/ppermute | solution.py:578
  248.5 61.2 %all-to-all-start = ((bf16[32,3,6656]{2,1,0:T(4,128)(2,1)}), bf16[32,3,6656]{2,1,0:T(4,128)(2,1)S(1)}, u32[]{:S(2)}, u32[]{:S(2)}) async-start(bf16[32,3,6656]{2,1,0:T(4,128)(2,1)} %copy.101), calls=%async_computation | async-start | bytes 3407872 | tf_op jit(solution)/shard_map/all_to_all | solution.py:586
  251.5 124.4 %all-gather.5.cloned.1.call-start = ((), (), s32[]{:S(2)}) async-start(), calls=%async_computation.4 | async-start | bytes 3514368 | tf_op jit(solution)/shard_map/all_gather | solution.py:824
  251.6 22.2 %collective-permute-start.24 = (bf16[2,256,256]{2,1,0:T(8,128)(2,1)}, bf16[2,256,256]{2,1,0:T(8,128)(2,1)S(1)}, u32[]{:S(2)}, u32[]{:S(2)}) collective-permute-start(bf16[2,256,256]{2,1,0:T(8,128)(2,1)} %get-tuple-element.173), channel_id=1, source_target_pairs={{0,1},{1,0},{2,3},{3,2},{4,5},{5,4},{6,7},{7,6},{8,9},{9,8},{10,11... | collective-permute-start | bytes 786440 | tf_op jit(solution)/shard_map/ppermute | solution.py:578
  251.9 23.4 %collective-permute-start.25 = (bf16[2,256,256]{2,1,0:T(8,128)(2,1)S(1)}, bf16[2,256,256]{2,1,0:T(8,128)(2,1)S(1)}, u32[]{:S(2)}, u32[]{:S(2)}) collective-permute-start(bf16[2,256,256]{2,1,0:T(8,128)(2,1)S(1)} %copy-done.63), channel_id=1, source_target_pairs={{0,2},{1,3},{2,0},{3,1},{4,6},{5,7},{6,4},{7,5},{8,10},{9,11},{10,... | collective-permute-start | bytes 786440 | tf_op jit(solution)/shard_map/ppermute | solution.py:578
  253.6 27.5 %collective-permute-start.26 = (bf16[2,256,256]{2,1,0:T(8,128)(2,1)S(1)}, bf16[2,256,256]{2,1,0:T(8,128)(2,1)S(1)}, u32[]{:S(2)}, u32[]{:S(2)}) collective-permute-start(bf16[2,256,256]{2,1,0:T(8,128)(2,1)S(1)} %copy-done.62), channel_id=1, source_target_pairs={{0,3},{1,2},{2,1},{3,0},{4,7},{5,6},{6,5},{7,4},{8,11},{9,10},{10,... | collective-permute-start | bytes 786440 | tf_op jit(solution)/shard_map/ppermute | solution.py:578
  273.8 15.6 %copy-start.13 = (bf16[2,256,256]{2,1,0:T(8,128)(2,1)}, bf16[2,256,256]{2,1,0:T(8,128)(2,1)S(1)}, u32[]{:S(2)}) copy-start(bf16[2,256,256]{2,1,0:T(8,128)(2,1)S(1)} %collective-permute-done.24.refs_5_) | copy-start | bytes 786436
  275.3 14.0 %copy-start.14 = (bf16[2,256,256]{2,1,0:T(8,128)(2,1)}, bf16[2,256,256]{2,1,0:T(8,128)(2,1)S(1)}, u32[]{:S(2)}) copy-start(bf16[2,256,256]{2,1,0:T(8,128)(2,1)S(1)} %collective-permute-done.25.refs_6_) | copy-start | bytes 786436
  281.1 3.1 collective-permute-start.27
  287.2 22.4 %collective-permute-start.28 = (bf16[256,1024]{1,0:T(8,128)(2,1)}, bf16[256,1024]{1,0:T(8,128)(2,1)S(1)}, u32[]{:S(2)}, u32[]{:S(2)}) collective-permute-start(bf16[256,1024]{1,0:T(8,128)(2,1)} %fusion.19), channel_id=1, source_target_pairs={{0,2},{1,3},{2,0},{3,1},{4,6},{5,7},{6,4},{7,5},{8,10},{9,11},{10,... | collective-permute-start | bytes 1572872 | tf_op jit(solution)/shard_map/ppermute | solution.py:578
  311.3 2.7 collective-permute-start.29
  315.1 22.3 %collective-permute-start.30 = (bf16[256,1024]{1,0:T(8,128)(2,1)S(1)}, bf16[256,1024]{1,0:T(8,128)(2,1)S(1)}, u32[]{:S(2)}, u32[]{:S(2)}) collective-permute-start(bf16[256,1024]{1,0:T(8,128)(2,1)S(1)} %fusion.20), channel_id=1, source_target_pairs={{0,2},{1,3},{2,0},{3,1},{4,6},{5,7},{6,4},{7,5},{8,10},{9,11},{10,... | collective-permute-start | bytes 1572872 | tf_op jit(solution)/shard_map/ppermute | solution.py:578
  316.7 21.0 %copy-start.58 = (bf16[3,16,256]{2,1,0:T(8,128)(2,1)S(1)}, bf16[3,16,256]{2,1,0:T(8,128)(2,1)}, u32[]{:S(2)}) copy-start(bf16[3,16,256]{2,1,0:T(8,128)(2,1)} %get-tuple-element.199) | copy-start | bytes 73732
  316.7 21.5 %copy-start.56 = (bf16[16,1024]{1,0:T(8,128)(2,1)S(1)}, bf16[16,1024]{1,0:T(8,128)(2,1)}, u32[]{:S(2)}) copy-start(bf16[16,1024]{1,0:T(8,128)(2,1)} %get-tuple-element.196) | copy-start | bytes 98308
  316.7 21.5 %copy-start.57 = (bf16[16,1024]{1,0:T(8,128)(2,1)S(1)}, bf16[16,1024]{1,0:T(8,128)(2,1)}, u32[]{:S(2)}) copy-start(bf16[16,1024]{1,0:T(8,128)(2,1)} %get-tuple-element.197) | copy-start | bytes 98308
  337.4 3.7 collective-permute-start.31
  338.2 12.0 %copy-start.16 = (bf16[2,256,1024]{2,1,0:T(8,128)(2,1)S(1)}, bf16[2,256,1024]{2,1,0:T(8,128)(2,1)}, u32[]{:S(2)}) copy-start(bf16[2,256,1024]{2,1,0:T(8,128)(2,1)} %get-tuple-element.170) | copy-start | bytes 3145732
  338.2 12.0 %copy-start.18 = (bf16[2,256,1024]{2,1,0:T(8,128)(2,1)S(1)}, bf16[2,256,1024]{2,1,0:T(8,128)(2,1)}, u32[]{:S(2)}) copy-start(bf16[2,256,1024]{2,1,0:T(8,128)(2,1)} %copy-done.17) | copy-start | bytes 3145732
  343.1 19.4 %collective-permute-start.32 = (bf16[256,1024]{1,0:T(8,128)(2,1)}, bf16[256,1024]{1,0:T(8,128)(2,1)}, u32[]{:S(2)}, u32[]{:S(2)}) collective-permute-start(bf16[256,1024]{1,0:T(8,128)(2,1)} %fusion.21), channel_id=1, source_target_pairs={{0,2},{1,3},{2,0},{3,1},{4,6},{5,7},{6,4},{7,5},{8,10},{9,11},{10,... | collective-permute-start | bytes 1572872 | tf_op jit(solution)/shard_map/ppermute | solution.py:578
  344.3 18.3 %all-to-all-start.1 = ((bf16[32,6,448]{2,1,0:T(8,128)(2,1)}), bf16[32,6,448]{2,1,0:T(8,128)(2,1)S(1)}, u32[]{:S(2)}, u32[]{:S(2)}) async-start(bf16[32,6,448]{2,1,0:T(8,128)(2,1)} %copy.105), calls=%async_computation.1 | async-start | bytes 524288 | tf_op jit(solution)/shard_map/all_to_all | solution.py:586
  363.5 8.3 %copy-start.3 = (bf16[3,256,1024]{2,1,0:T(8,128)(2,1)S(1)}, bf16[3,256,1024]{2,1,0:T(8,128)(2,1)}, u32[]{:S(2)}) copy-start(bf16[3,256,1024]{2,1,0:T(8,128)(2,1)} %refs_13_.1) | copy-start | bytes 4718596
  363.5 8.3 %copy-start.50 = (f32[3,256]{1,0:T(4,128)S(1)}, f32[3,256]{1,0:T(4,128)}, u32[]{:S(2)}) copy-start(f32[3,256]{1,0:T(4,128)} %copy-done.49) | copy-start | bytes 9220
  363.5 8.3 %copy-start.53 = (f32[1024]{0:T(1024)S(1)}, f32[1024]{0:T(1024)}, u32[]{:S(2)}) copy-start(f32[1024]{0:T(1024)} %copy-done.52) | copy-start | bytes 12292
  364.4 21.2 %all-to-all-start.2 = ((bf16[32,16,448]{2,1,0:T(8,128)(2,1)}), bf16[32,16,448]{2,1,0:T(8,128)(2,1)S(1)}, u32[]{:S(2)}, u32[]{:S(2)}) async-start(bf16[32,16,448]{2,1,0:T(8,128)(2,1)} %bitcast.196), calls=%async_computation.2 | async-start | bytes 1048576 | tf_op jit(solution)/shard_map/all_to_all | solution.py:586
  373.8 14.9 %copy-start.1 = (bf16[8,16,2,656]{3,2,1,0:T(2,128)(2,1)S(1)}, bf16[8,16,2,656]{3,2,1,0:T(2,128)(2,1)}, u32[]{:S(2)}) copy-start(bf16[8,16,2,656]{3,2,1,0:T(2,128)(2,1)} %param.33) | copy-start | bytes 1007620
  (38 other events, 142.5 us)
Sparse Core Ops, SparseCore 0:
  11.5 155.9 all-gather.2
  311.4 63.6 all-gather.4

commit v6 on v5

--- a/solution.py
+++ b/solution.py
@@ -285,7 +285,7 @@
             + [pl.BlockSpec((1,) + probs.shape[1:], lambda h, p: (h, 0, 0, 0, 0))]
             + [pl.BlockSpec((1,) + shrinks.shape[1:], lambda h, p: (h, 0, 0, 0))]
             + [pl.BlockSpec((own, LANES), lambda h, p: (0, h))] * blocks
-            + [pl.BlockSpec((1, own, LANES), lambda h, p: (max(seq - 1, 0), 0, h))] * blocks
+            + [pl.BlockSpec((1, own, LANES), lambda h, p: (seq, 0, h))] * blocks
             + [of_seq((own, model))] * blocks
             + [whole((blocks, own, LANES))] * 2
             + [
@@ -366,9 +366,8 @@
         result, expand_up_grad, shrink_low_grad, expand_low_grad, shrink_up_grad,
         grad_middle, merge_low_grad, merge_up_grad,
     ) = refs[seqs * blocks : seqs * blocks + 8]
-    firsts = refs[seqs * blocks + 8 : seqs * blocks + 8 + blocks]
-    others = refs[seqs * blocks + 8 + blocks : seqs * blocks + 8 + 2 * blocks]
-    total, grad_rows, down, down_grad, late, late_grad = refs[seqs * blocks + 8 + 2 * blocks :]
+    grad_contexts = refs[seqs * blocks + 8 : seqs * blocks + 8 + blocks]
+    total, grad_rows, down, down_grad, late, late_grad = refs[seqs * blocks + 8 + blocks :]
     step = pl.program_id(0)
     scaled = ADAPTER_SCALE * mask[...]
 
@@ -424,10 +423,7 @@
                 ref = far if move // 2 else near
                 table = lanes_of(ref.at[:, pl.ds(move % 2, 1)], spot=place)
                 out = (nt(low_rows, table) + nn(small, merge_low[move, seq])).astype(BF)
-                if seq:
-                    others[move][seq - 1] = out
-                else:
-                    firsts[move][0] = out
+                grad_contexts[move][seq] = out
                 merge_low_grad[seq, move] = tn(small, contexts[seq * blocks + move][...]).astype(BF)
             merge_up_grad[seq] = tn(merge_down[seq], low_rows).astype(BF)
 
@@ -454,7 +450,7 @@
         ((seqs, blocks, some, wide), BF),
         ((seqs, some, model), BF),
     ]
-    shapes += [((1, own, wide), BF)] * blocks + [((seqs - 1, own, wide), BF)] * blocks
+    shapes += [((seqs, own, wide), BF)] * blocks
     out_specs = [full_once(shape) for shape, _ in shapes]
     out_specs[1] = pl.BlockSpec((1, 2, rank, width), lambda m, p: (m, 0, 0, 0))
     out_specs[2] = pl.BlockSpec((1, rank, width), lambda m, p: (m, 0, 0))
@@ -750,9 +746,7 @@
         merge_near, merge_far, merge_low, merge_up, mlp_scale, merge_down, contexts,
     )
     result = result.reshape(middle.shape)
-    halfway = []
-    for some in (grad_contexts[:blocks], grad_contexts[blocks:]):
-        halfway.append([some[0]] + [pair_swap(some[bit], bit) for bit in range(1, blocks)])
+    halfway = [grad_contexts[0]] + [pair_swap(grad_contexts[bit], bit) for bit in range(1, blocks)]
 
     paired = rank == 2 * parts
     everyone = ("dp", "mp")
@@ -800,19 +794,18 @@
     )
     early_width = early.shape[2]
 
-    early, halfway[0] = lax.optimization_barrier((early, halfway[0]))
-    early = swap_all(ranks_out(early).reshape(owners, seqs, -1), everyone)
+    early = ranks_out(early).reshape(owners, seqs, -1)
+    early, halfway = lax.optimization_barrier((early, halfway))
+    early = swap_all(early, everyone)
     chip, far = None, None
     for seq in range(seqs):
-        pieces_back = list(halfway[min(seq, 1)])
+        pieces_back = list(halfway)
         if seq:
             pieces_back[0] = tie(pieces_back[0], here)
         here, there, up_grad, low_grad = attend_back(
             spot, seq, query, key, value, logs[seq], pieces_back, pieces, tables,
             joined_whole, joined_low, joined_up, joined_down,
         )
-        if seq == 0:
-            there, halfway[1] = lax.optimization_barrier((there, halfway[1]))
         if seq == 1:
             there, far, early = lax.optimization_barrier((there, far, early))
             by_seq = choose.reshape(ADAPTERS, owners, seqs)

time: 400 us -> 399 us (level)
  waiting for transfers between devices: 90 us -> 94.3 us
    ppermute x29 -> x26, waiting for transfers between devices: 66.5 us -> 69.9 us  [pair_swap(): return lax.ppermute(values, 'mp', [(i, i ^ bit) for i in range(size)])]
    unnamed x140 -> x120, local copies, waits for them, and re-layouts: 8.79 us -> 5.74 us
    ppermute x29 -> x26, starting transfers between devices: 18.2 us -> 17.2 us  [pair_swap(): return lax.ppermute(values, 'mp', [(i, i ^ bit) for i in range(size)])]
  transfers between devices with their start and end apart: 38 -> 35, of which waited for: 18 -> 17; matrix products, arithmetic and copies ran while one was open for 12% -> 13% of each run, Pallas kernels for 31% -> 31%
where the time goes in v6:
time: 399 us; the launch traced here: 395 us
  Pallas kernels  184 us (46%)
  waiting for transfers between devices  94.3 us (24%)
  starting transfers between devices  37.9 us (9%)
  local copies, waits for them, and re-layouts  31.3 us (8%)
  other arithmetic  31.3 us (8%)
  between operations  15.3 us (4%)
    ppermute x26, waiting for transfers between devices, pair_swap(): return lax.ppermute(values, 'mp', [(i, i ^ bit) for i in range(size)])  69.9 us
    pallas_call x3, Pallas kernels, attend_back(): pl.pallas_call(attend_back_kernel, grid_spec=pltpu.PrefetchScalarGridSpec...  61.1 us
    pallas_call x1, Pallas kernels, gated(): pl.pallas_call(lambda *refs: gated_kernel(*refs, width=width, blocks=bloc...  57.6 us
    pallas_call x3, Pallas kernels, attend(): pl.pallas_call(attend_kernel, grid_spec=pltpu.PrefetchScalarGridSpec(num_...  36 us
    ppermute x26, starting transfers between devices, pair_swap(): return lax.ppermute(values, 'mp', [(i, i ^ bit) for i in range(size)])  17.2 us
    all_to_all x3, waiting for transfers between devices, swap_all(): return lax.all_to_all(values, axes, 0, 0, tiled=True)  14.3 us
    pallas_call x1, Pallas kernels, project(): pl.pallas_call(lambda *refs: project_kernel(*refs, wide=wide), grid_spec=...  13.8 us
    all_to_all x3, starting transfers between devices, swap_all(): return lax.all_to_all(values, axes, 0, 0, tiled=True)  13.4 us
  transfers between devices with their start and end apart: 35, of which 17 were waited for; matrix products, arithmetic and copies ran while one was open for 13% of the time, Pallas kernels for 31%

profile of v6, /device:TPU:0, one launch (start us, length us, event | category | flops | bytes accessed | tf_op | source)
XLA Modules:
  0.0 394.9 jit_solution(6133069140618068472)
XLA Ops:
  7.3 1.9 pad_maximum_fusion.3
  13.0 2.9 collective-permute-start.3
  17.1 1.6 collective-permute-start.6
  18.6 2.6 collective-permute-start.7
  21.2 1.3 collective-permute-start.8
  23.5 0.9 compare_convert_fusion.refs_10_
  25.2 1.7 fusion.6.refs_1_.refs_8_
  26.9 1.5 gather_fusion.1
  29.0 1.2 gather_fusion
  30.2 1.2 gather_fusion.6
  31.4 2.3 gather_fusion.7
  33.7 2.1 gather_fusion.5
  35.9 3.2 multiply_sine_fusion
  39.6 9.6 %collective-permute-done.7 = bf16[1032,128]{1,0:T(8,128)(2,1)S(1)} collective-permute-done((bf16[1032,128]{1,0:T(8,128)(2,1)}, bf16[1032,128]{1,0:T(8,128)(2,1)S(1)}, u32[]{:S(2)}, u32[]{:S(2)}) %collective-permute-start.7) | collective-permute-done | bytes 264224 | tf_op jit(solution)/shard_map/ppermute | solution.py:600
  49.7 1.2 pad_maximum_fusion
  50.8 1.6 collective-permute-start.9
  52.5 1.0 constant_dynamic-update-slice_fusion.1
  56.0 33.8 %collective-permute-done.1.refs_3_.refs_10_ = bf16[3,256,1024]{2,1,0:T(8,128)(2,1)} collective-permute-done((bf16[3,256,1024]{2,1,0:T(8,128)(2,1)}, bf16[3,256,1024]{2,1,0:T(8,128)(2,1)}, u32[]{:S(2)}, u32[]{:S(2)}) %collective-permute-start.1) | collective-permute-done | bytes 1572896 | tf_op jit(solution)/shard_map/ppermute | solution.py:574
  90.5 3.4 collective-permute-done.19
  95.2 13.8 %project.1 = (bf16[3,4,256,256]{3,2,1,0:T(8,128)(2,1)}, bf16[3,4,256,256]{3,2,1,0:T(8,128)(2,1)}, bf16[3,4,256,256]{3,2,1,0:T(8,128)(2,1)}, bf16[3,4,256,16]{3,2,1,0:T(8,128)(2,1)}) custom-call(s32[9]{0:T(128)} %pad_add_fusion.refs_0_.place, bf16[3,256,1024]{2,1,0:T(8,128)(2,1)} %fusion.6.refs_1_.refs_8_, ...), custom_call_target="tpu_custom_call" | custom-call | tf_op jit(solution)/shard_map/project/pallas_call | solution.py:104
  109.1 12.0 %attend.3 = (bf16[256,256]{1,0:T(8,128)(2,1)}, bf16[256,256]{1,0:T(8,128)(2,1)}, bf16[256,256]{1,0:T(8,128)(2,1)}, bf16[256,256]{1,0:T(8,128)(2,1)}, bf16[2,2,2,...) custom-call(s32[9]{0:T(128)} %pad_add_fusion.refs_0_.place, bf16[3,4,256,256]{3,2,1,0:T(8,128)(2,1)} %get-tuple-element.127.query, ...), custom_call_target="tpu_custom_call" | custom-call | tf_op jit(solution)/shard_map/attend/pallas_call | solution.py:166
  121.0 11.9 %attend.4 = (bf16[256,256]{1,0:T(8,128)(2,1)}, bf16[256,256]{1,0:T(8,128)(2,1)}, bf16[256,256]{1,0:T(8,128)(2,1)}, bf16[256,256]{1,0:T(8,128)(2,1)}, bf16[2,2,2,...) custom-call(s32[9]{0:T(128)} %pad_add_fusion.refs_0_.place, bf16[3,4,256,256]{3,2,1,0:T(8,128)(2,1)} %get-tuple-element.127.query, ...), custom_call_target="tpu_custom_call" | custom-call | tf_op jit(solution)/shard_map/attend/pallas_call | solution.py:166
  133.0 12.1 %attend.5 = (bf16[256,256]{1,0:T(8,128)(2,1)}, bf16[256,256]{1,0:T(8,128)(2,1)}, bf16[256,256]{1,0:T(8,128)(2,1)}, bf16[256,256]{1,0:T(8,128)(2,1)}, bf16[2,2,2,...) custom-call(s32[9]{0:T(128)} %pad_add_fusion.refs_0_.place, bf16[3,4,256,256]{3,2,1,0:T(8,128)(2,1)} %get-tuple-element.127.query, ...), custom_call_target="tpu_custom_call" | custom-call | tf_op jit(solution)/shard_map/attend/pallas_call | solution.py:166
  145.2 1.5 collective-permute-start.17
  147.4 1.5 collective-permute-start.14
  149.1 2.7 collective-permute-done.17.refs_11_.refs_27_
  151.7 1.9 collective-permute-done.18.refs_12_.refs_28_
  153.6 1.4 collective-permute-start.11
  155.1 1.1 collective-permute-start.12
  157.4 1.9 collective-permute-done.15.refs_8_.refs_24_
  159.2 3.7 collective-permute-done.11.refs_3_.refs_19_
  163.0 1.9 collective-permute-done.12.refs_4_.refs_20_
  165.5 8.2 %merge.1 = (f32[3,256,1024]{2,1,0:T(8,128)}, bf16[3,256,1024]{2,1,0:T(8,128)(2,1)}, bf16[3,256,16]{2,1,0:T(8,128)(2,1)}) custom-call(s32[9]{0:T(128)} %pad_add_fusion.refs_0_.place, bf16[256,256]{1,0:T(8,128)(2,1)} %get-tuple-element.118.refs_1_.refs_17_.refs_0_, bf16[256,256]{1,0:T(8,128)(2,1)} %copy-done.30, bf16[256,256]{1,0:T(8,128)(2,1)} %copy-done.31, ...), custom_call_target="tpu_custom_call" | custom-call | tf_op jit(solution)/shard_map/merge/pallas_call | solution.py:347
  173.7 57.6 %gated.1 = (bf16[768,1024]{1,0:T(8,128)(2,1)}, bf16[4,2,48,656]{3,2,1,0:T(8,128)(2,1)}, bf16[4,48,656]{2,1,0:T(8,128)(2,1)}, bf16[48,1024]{1,0:T(8,128)(2,1)}, b...) custom-call(s32[9]{0:T(128)} %pad_add_fusion.refs_0_.place, ...), custom_call_target="tpu_custom_call" | custom-call | tf_op jit(solution)/shard_map/gated/pallas_call | solution.py:457
  231.3 0.9 fusion.33
  232.2 0.9 reshape_reshape.12
  234.1 1.1 slice_bitcast_fusion.6
  235.6 1.5 collective-permute-start.22
  238.8 1.0 copy.135
  240.7 7.1 %collective-permute-done.22.refs_6_ = bf16[3,256,256]{2,1,0:T(8,128)(2,1)S(1)} collective-permute-done((bf16[3,256,256]{2,1,0:T(8,128)(2,1)}, bf16[3,256,256]{2,1,0:T(8,128)(2,1)S(1)}, u32[]{:S(2)}, u32[]{:S(2)}) %collective-permute-start.22) | collective-permute-done | bytes 393248 | tf_op jit(solution)/shard_map/ppermute | solution.py:574
  247.8 6.9 %collective-permute-done.23.refs_7_ = bf16[3,256,256]{2,1,0:T(8,128)(2,1)} collective-permute-done((bf16[3,256,256]{2,1,0:T(8,128)(2,1)}, bf16[3,256,256]{2,1,0:T(8,128)(2,1)}, u32[]{:S(2)}, u32[]{:S(2)}) %collective-permute-start.23) | collective-permute-done | bytes 393248 | tf_op jit(solution)/shard_map/ppermute | solution.py:574
  254.7 2.3 copy.101
  257.0 3.1 all-to-all-start
  260.2 20.2 %attend_back.3 = (bf16[2,256,1024]{2,1,0:T(8,128)(2,1)}, bf16[2,256,1024]{2,1,0:T(8,128)(2,1)}, bf16[3,16,256]{2,1,0:T(8,128)(2,1)}, bf16[16,1024]{1,0:T(8,128)(2,1)}) custom-call(s32[9]{0:T(128)} %pad_add_fusion.refs_0_.place, bf16[3,4,256,256]{3,2,1,0:T(8,128)(2,1)} %get-tuple-element.127.query, bf16[3,4,256,256]{3,2,1,0:T(8,128)(2,1)} %get-tuple-element.116.key, ...), custom_call_target="tpu_custom_call" | custom-call | tf_op jit(solution)/shard_map/attend_back/pallas_call | solution.py:279
  280.7 2.6 collective-permute-done.24
  283.3 2.0 fusion.19
  285.3 1.8 collective-permute-start.25
  288.8 20.2 %attend_back.4 = (bf16[2,256,1024]{2,1,0:T(8,128)(2,1)}, bf16[2,256,1024]{2,1,0:T(8,128)(2,1)}, bf16[3,16,256]{2,1,0:T(8,128)(2,1)}, bf16[16,1024]{1,0:T(8,128)(2,1)}) custom-call(s32[9]{0:T(128)} %pad_add_fusion.refs_0_.place, bf16[3,4,256,256]{3,2,1,0:T(8,128)(2,1)} %get-tuple-element.127.query, bf16[3,4,256,256]{3,2,1,0:T(8,128)(2,1)} %get-tuple-element.116.key, ...), custom_call_target="tpu_custom_call" | custom-call | tf_op jit(solution)/shard_map/attend_back/pallas_call | solution.py:279
  310.7 2.9 collective-permute-done.26
  313.5 1.1 fusion.20
  314.9 20.7 %attend_back.5 = (bf16[2,256,1024]{2,1,0:T(8,128)(2,1)}, bf16[2,256,1024]{2,1,0:T(8,128)(2,1)}, bf16[3,16,256]{2,1,0:T(8,128)(2,1)}, bf16[16,1024]{1,0:T(8,128)(2,1)}) custom-call(s32[9]{0:T(128)} %pad_add_fusion.refs_0_.place, bf16[3,4,256,256]{3,2,1,0:T(8,128)(2,1)} %get-tuple-element.127.query, bf16[3,4,256,256]{3,2,1,0:T(8,128)(2,1)} %get-tuple-element.116.key, ...), custom_call_target="tpu_custom_call" | custom-call | tf_op jit(solution)/shard_map/attend_back/pallas_call | solution.py:279
  338.7 2.0 fusion.21
  340.8 1.8 collective-permute-start.29
  343.3 4.6 %all-to-all-start.1 = ((bf16[32,6,448]{2,1,0:T(8,128)(2,1)}), bf16[32,6,448]{2,1,0:T(8,128)(2,1)S(1)}, u32[]{:S(2)}, u32[]{:S(2)}) async-start(bf16[32,6,448]{2,1,0:T(8,128)(2,1)} %copy.105), calls=%async_computation.1 | async-start | bytes 524288 | tf_op jit(solution)/shard_map/all_to_all | solution.py:582
  348.0 1.3 fusion.16
  349.3 2.6 fusion.15
  351.9 9.7 %all-to-all-done.1 = bf16[32,6,448]{2,1,0:T(8,128)(2,1)S(1)} async-done(((bf16[32,6,448]{2,1,0:T(8,128)(2,1)}), bf16[32,6,448]{2,1,0:T(8,128)(2,1)S(1)}, u32[]{:S(2)}, u32[]{:S(2)}) %all-to-all-start.1) | async-done | bytes 172064 | tf_op jit(solution)/shard_map/all_to_all | solution.py:582
  363.5 5.7 %all-to-all-start.2 = ((bf16[32,16,448]{2,1,0:T(8,128)(2,1)}), bf16[32,16,448]{2,1,0:T(8,128)(2,1)S(1)}, u32[]{:S(2)}, u32[]{:S(2)}) async-start(bf16[32,16,448]{2,1,0:T(8,128)(2,1)} %bitcast.196), calls=%async_computation.2 | async-start | bytes 1048576 | tf_op jit(solution)/shard_map/all_to_all | solution.py:582
  369.2 1.8 fusion.14
  371.1 1.1 fusion.17
  373.1 2.1 fusion.11
  375.2 5.0 %settle_early.1 = (f32[8,16,1024]{2,1,0:T(8,128)}, f32[8,16,1024]{2,1,0:T(8,128)}, f32[8,16,1024]{2,1,0:T(8,128)}, f32[8,16,256]{2,1,0:T(8,128)}, f32[8,16,2,656]{3,2,1,0:T(2,128)}, /*index=5*/f32[8,16,656]{2,1,0:T(8,128)}) custom-call(s32[9]{0:T(128)} %pad_add_fusion.refs_0_.place, bf16[32,16,3328]{2,1,0:T(8,128)(2,1)} %all-gather.5.cloned.1.call-done.refs_1_), custom_call_target="tpu_custom_call" | custom-call | tf_op jit(solution)/shard_map/settle_early/pallas_call | solution.py:528
  380.2 4.6 %all-to-all-done.2.refs_0_ = bf16[32,16,448]{2,1,0:T(8,128)(2,1)S(1)} async-done(((bf16[32,16,448]{2,1,0:T(8,128)(2,1)}), bf16[32,16,448]{2,1,0:T(8,128)(2,1)S(1)}, u32[]{:S(2)}, u32[]{:S(2)}) %all-to-all-start.2) | async-done | bytes 458784 | tf_op jit(solution)/shard_map/all_to_all | solution.py:582
  385.6 2.3 settle_late.1
  (248 shorter events, 30.3 us)
Async XLA Ops:
  7.2 166.5 %all-gather.3.cloned.1.call-start = ((), (), s32[]{:S(2)}) async-start(), calls=%async_computation.3 | async-start | bytes 16625664 | tf_op jit(solution)/shard_map/all_gather | solution.py:651
  10.8 11.7 %copy-start.52 = (bf16[1024]{0:T(1024)(128)(2,1)S(1)}, bf16[1024]{0:T(1024)(128)(2,1)}, u32[]{:S(2)}) copy-start(bf16[1024]{0:T(1024)(128)(2,1)} %param.22) | copy-start | bytes 6148
  10.9 11.8 %copy-start.2 = (bf16[3,256,1024]{2,1,0:T(8,128)(2,1)S(1)}, bf16[3,256,1024]{2,1,0:T(8,128)(2,1)}, u32[]{:S(2)}) copy-start(bf16[3,256,1024]{2,1,0:T(8,128)(2,1)} %refs_13_.1) | copy-start | bytes 4718596
  13.0 26.1 %collective-permute-start.3 = (bf16[3,16,2560]{2,1,0:T(8,128)(2,1)}, bf16[3,16,2560]{2,1,0:T(8,128)(2,1)S(1)}, u32[]{:S(2)}, u32[]{:S(2)}) collective-permute-start(bf16[3,16,2560]{2,1,0:T(8,128)(2,1)} %fusion.30), channel_id=1, source_target_pairs={{0,2},{1,3},{2,0},{3,1},{4,6},{5,7},{6,4},{7,5},{8,10},{9,11},{10,... | collective-permute-start | bytes 737288 | tf_op jit(solution)/shard_map/ppermute | solution.py:574
  15.9 37.6 %collective-permute-start.2 = (bf16[3,16,2560]{2,1,0:T(8,128)(2,1)}, bf16[3,16,2560]{2,1,0:T(8,128)(2,1)S(1)}, u32[]{:S(2)}, u32[]{:S(2)}) collective-permute-start(bf16[3,16,2560]{2,1,0:T(8,128)(2,1)} %fusion.30), channel_id=1, source_target_pairs={{0,1},{1,0},{2,3},{3,2},{4,5},{5,4},{6,7},{7,6},{8,9},{9,8},{10,11... | collective-permute-start | bytes 737288 | tf_op jit(solution)/shard_map/ppermute | solution.py:574
  17.1 22.5 %collective-permute-start.6 = (bf16[1032,128]{1,0:T(8,128)(2,1)}, bf16[1032,128]{1,0:T(8,128)(2,1)S(1)}, u32[]{:S(2)}, u32[]{:S(2)}) collective-permute-start(bf16[1032,128]{1,0:T(8,128)(2,1)} %get-tuple-element.203), channel_id=1, source_target_pairs={{0,8},{4,12},{8,16},{12,20},{16,24},{20,28},{24,0},{28,4},{1,9},{5... | collective-permute-start | bytes 792584 | tf_op jit(solution)/shard_map/ppermute | solution.py:600
  18.6 30.6 %collective-permute-start.7 = (bf16[1032,128]{1,0:T(8,128)(2,1)}, bf16[1032,128]{1,0:T(8,128)(2,1)S(1)}, u32[]{:S(2)}, u32[]{:S(2)}) collective-permute-start(bf16[1032,128]{1,0:T(8,128)(2,1)} %get-tuple-element.203), channel_id=1, source_target_pairs={{0,16},{4,20},{8,24},{12,28},{16,0},{20,4},{24,8},{28,12},{1,17},{... | collective-permute-start | bytes 792584 | tf_op jit(solution)/shard_map/ppermute | solution.py:600
  21.2 28.4 %collective-permute-start.8 = (bf16[1032,128]{1,0:T(8,128)(2,1)}, bf16[1032,128]{1,0:T(8,128)(2,1)}, u32[]{:S(2)}, u32[]{:S(2)}) collective-permute-start(bf16[1032,128]{1,0:T(8,128)(2,1)} %get-tuple-element.203), channel_id=1, source_target_pairs={{0,24},{4,28},{8,0},{12,4},{16,8},{20,12},{24,16},{28,20},{1,25},{... | collective-permute-start | bytes 792584 | tf_op jit(solution)/shard_map/ppermute | solution.py:600
  31.4 21.0 %copy-start.4 = (bf16[8,1032,128]{2,1,0:T(8,128)(2,1)S(1)}, bf16[8,1032,128]{2,1,0:T(8,128)(2,1)}, u32[]{:S(2)}) copy-start(bf16[8,1032,128]{2,1,0:T(8,128)(2,1)} %constant_dynamic-update-slice_fusion.4) | copy-start | bytes 6340612
  39.1 50.7 %collective-permute-start.1 = (bf16[3,256,1024]{2,1,0:T(8,128)(2,1)}, bf16[3,256,1024]{2,1,0:T(8,128)(2,1)}, u32[]{:S(2)}, u32[]{:S(2)}) collective-permute-start(bf16[3,256,1024]{2,1,0:T(8,128)(2,1)} %fusion.6.refs_1_.refs_8_), channel_id=1, source_target_pairs={{0,2},{1,3},{2,0},{3,1},{4,6},{5,7},{6,4},{7,5},{8,10},{9,11},{10,... | collective-permute-start | bytes 4718600 | tf_op jit(solution)/shard_map/ppermute | solution.py:574
  39.6 55.6 %collective-permute-start = (bf16[3,256,1024]{2,1,0:T(8,128)(2,1)}, bf16[3,256,1024]{2,1,0:T(8,128)(2,1)}, u32[]{:S(2)}, u32[]{:S(2)}) collective-permute-start(bf16[3,256,1024]{2,1,0:T(8,128)(2,1)} %fusion.6.refs_1_.refs_8_), channel_id=1, source_target_pairs={{0,1},{1,0},{2,3},{3,2},{4,5},{5,4},{6,7},{7,6},{8,9},{9,8},{10,11... | collective-permute-start | bytes 4718600 | tf_op jit(solution)/shard_map/ppermute | solution.py:574
  49.2 4.3 %collective-permute-start.4 = (bf16[3,16,2560]{2,1,0:T(8,128)(2,1)S(1)}, bf16[3,16,2560]{2,1,0:T(8,128)(2,1)S(1)}, u32[]{:S(2)}, u32[]{:S(2)}) collective-permute-start(bf16[3,16,2560]{2,1,0:T(8,128)(2,1)S(1)} %collective-permute-done.3), channel_id=1, source_target_pairs={{0,1},{1,0},{2,3},{3,2},{4,5},{5,4},{6,7},{7,6},{8,9},{9,8},{10,11... | collective-permute-start | bytes 737288 | tf_op jit(solution)/shard_map/ppermute | solution.py:574
  50.8 38.9 %collective-permute-start.9 = (bf16[4,1032,128]{2,1,0:T(8,128)(2,1)S(1)}, bf16[4,1032,128]{2,1,0:T(8,128)(2,1)S(1)}, u32[]{:S(2)}, u32[]{:S(2)}) collective-permute-start(bf16[4,1032,128]{2,1,0:T(8,128)(2,1)S(1)} %pad_maximum_fusion), channel_id=1, source_target_pairs={{0,4},{4,0},{8,12},{12,8},{16,20},{20,16},{24,28},{28,24},{1,5},{5... | collective-permute-start | bytes 3170312 | tf_op jit(solution)/shard_map/ppermute | solution.py:602
  89.7 5.5 %collective-permute-start.5 = (bf16[3,256,1024]{2,1,0:T(8,128)(2,1)}, bf16[3,256,1024]{2,1,0:T(8,128)(2,1)}, u32[]{:S(2)}, u32[]{:S(2)}) collective-permute-start(bf16[3,256,1024]{2,1,0:T(8,128)(2,1)} %collective-permute-done.1.refs_3_.refs_10_), channel_id=1, source_target_pairs={{0,1},{1,0},{2,3},{3,2},{4,5},{5,4},{6,7},{7,6},{8,9},{9,8},{10,11... | collective-permute-start | bytes 4718600 | tf_op jit(solution)/shard_map/ppermute | solution.py:574
  89.9 4.0 %collective-permute-start.19 = (bf16[8,1,256,128]{3,2,1,0:T(8,128)(2,1)S(1)}, bf16[8,1,256,128]{3,2,1,0:T(8,128)(2,1)S(1)}, u32[]{:S(2)}, u32[]{:S(2)}) collective-permute-start(bf16[8,1,256,128]{3,2,1,0:T(8,128)(2,1)S(1)} %slice.181), channel_id=1, source_target_pairs={{0,1},{1,0},{2,3},{3,2},{4,5},{5,4},{6,7},{7,6},{8,9},{9,8},{10,11... | collective-permute-start | bytes 1572872 | tf_op jit(solution)/shard_map/ppermute | solution.py:574
  94.0 15.1 %copy-start.6 = (bf16[8,2,256,128]{3,2,1,0:T(8,128)(2,1)}, bf16[8,2,256,128]{3,2,1,0:T(8,128)(2,1)S(1)}, u32[]{:S(2)}) copy-start(bf16[8,2,256,128]{3,2,1,0:T(8,128)(2,1)S(1)} %pad_maximum_fusion.1.refs_14_.refs_11_) | copy-start | bytes 3145732
  94.0 53.4 %collective-permute-start.20 = (bf16[8,2,256,128]{3,2,1,0:T(8,128)(2,1)S(1)}, bf16[8,2,256,128]{3,2,1,0:T(8,128)(2,1)}, u32[]{:S(2)}, u32[]{:S(2)}) collective-permute-start(bf16[8,2,256,128]{3,2,1,0:T(8,128)(2,1)S(1)} %pad_maximum_fusion.1.refs_14_.refs_11_), channel_id=1, source_target_pairs={{0,2},{1,3},{2,0},{3,1},{4,6},{5,7},{6,4},{7,5},{8,10},{9,11},{10,... | collective-permute-start | bytes 3145736 | tf_op jit(solution)/shard_map/ppermute | solution.py:574
  133.0 14.0 %copy-start.35 = (bf16[256,256]{1,0:T(8,128)(2,1)S(1)}, bf16[256,256]{1,0:T(8,128)(2,1)}, u32[]{:S(2)}) copy-start(bf16[256,256]{1,0:T(8,128)(2,1)} %get-tuple-element.124.refs_1_) | copy-start | bytes 393220
  133.0 14.4 %copy-start.36 = (bf16[256,256]{1,0:T(8,128)(2,1)S(1)}, bf16[256,256]{1,0:T(8,128)(2,1)}, u32[]{:S(2)}) copy-start(bf16[256,256]{1,0:T(8,128)(2,1)} %get-tuple-element.125.refs_2_) | copy-start | bytes 393220
  133.0 16.0 %copy-start.37 = (bf16[256,256]{1,0:T(8,128)(2,1)S(1)}, bf16[256,256]{1,0:T(8,128)(2,1)}, u32[]{:S(2)}) copy-start(bf16[256,256]{1,0:T(8,128)(2,1)} %get-tuple-element.126.refs_3_) | copy-start | bytes 393220
  133.0 18.8 %copy-start.38 = (bf16[256,256]{1,0:T(8,128)(2,1)S(1)}, bf16[256,256]{1,0:T(8,128)(2,1)}, u32[]{:S(2)}) copy-start(bf16[256,256]{1,0:T(8,128)(2,1)} %get-tuple-element.119.refs_1_) | copy-start | bytes 393220
  133.0 20.7 %copy-start.39 = (bf16[256,256]{1,0:T(8,128)(2,1)S(1)}, bf16[256,256]{1,0:T(8,128)(2,1)}, u32[]{:S(2)}) copy-start(bf16[256,256]{1,0:T(8,128)(2,1)} %get-tuple-element.120.refs_2_) | copy-start | bytes 393220
  133.0 22.1 %copy-start.40 = (bf16[256,256]{1,0:T(8,128)(2,1)S(1)}, bf16[256,256]{1,0:T(8,128)(2,1)}, u32[]{:S(2)}) copy-start(bf16[256,256]{1,0:T(8,128)(2,1)} %get-tuple-element.121.refs_3_) | copy-start | bytes 393220
  133.0 23.2 %copy-start.53 = (bf16[1024]{0:T(1024)(128)(2,1)S(1)}, bf16[1024]{0:T(1024)(128)(2,1)}, u32[]{:S(2)}) copy-start(bf16[1024]{0:T(1024)(128)(2,1)} %param.23) | copy-start | bytes 6148
  145.1 3.8 collective-permute-start.16
  145.2 6.6 %collective-permute-start.17 = (bf16[256,256]{1,0:T(8,128)(2,1)}, bf16[256,256]{1,0:T(8,128)(2,1)S(1)}, u32[]{:S(2)}, u32[]{:S(2)}) collective-permute-start(bf16[256,256]{1,0:T(8,128)(2,1)} %get-tuple-element.130.refs_2_), channel_id=1, source_target_pairs={{0,2},{1,3},{2,0},{3,1},{4,6},{5,7},{6,4},{7,5},{8,10},{9,11},{10,... | collective-permute-start | bytes 393224 | tf_op jit(solution)/shard_map/ppermute | solution.py:574
  146.7 6.9 %collective-permute-start.18 = (bf16[256,256]{1,0:T(8,128)(2,1)}, bf16[256,256]{1,0:T(8,128)(2,1)S(1)}, u32[]{:S(2)}, u32[]{:S(2)}) collective-permute-start(bf16[256,256]{1,0:T(8,128)(2,1)} %get-tuple-element.131.refs_3_), channel_id=1, source_target_pairs={{0,3},{1,2},{2,1},{3,0},{4,7},{5,6},{6,5},{7,4},{8,11},{9,10},{10,... | collective-permute-start | bytes 393224 | tf_op jit(solution)/shard_map/ppermute | solution.py:574
  147.0 8.1 %collective-permute-start.13 = (bf16[256,256]{1,0:T(8,128)(2,1)S(1)}, bf16[256,256]{1,0:T(8,128)(2,1)S(1)}, u32[]{:S(2)}, u32[]{:S(2)}) collective-permute-start(bf16[256,256]{1,0:T(8,128)(2,1)S(1)} %copy-done.35), channel_id=1, source_target_pairs={{0,1},{1,0},{2,3},{3,2},{4,5},{5,4},{6,7},{7,6},{8,9},{9,8},{10,11... | collective-permute-start | bytes 393224 | tf_op jit(solution)/shard_map/ppermute | solution.py:574
  147.4 9.9 %collective-permute-start.14 = (bf16[256,256]{1,0:T(8,128)(2,1)S(1)}, bf16[256,256]{1,0:T(8,128)(2,1)S(1)}, u32[]{:S(2)}, u32[]{:S(2)}) collective-permute-start(bf16[256,256]{1,0:T(8,128)(2,1)S(1)} %copy-done.36), channel_id=1, source_target_pairs={{0,2},{1,3},{2,0},{3,1},{4,6},{5,7},{6,4},{7,5},{8,10},{9,11},{10,... | collective-permute-start | bytes 393224 | tf_op jit(solution)/shard_map/ppermute | solution.py:574
  149.0 15.9 %copy-start.24 = (bf16[256,256]{1,0:T(8,128)(2,1)}, bf16[256,256]{1,0:T(8,128)(2,1)S(1)}, u32[]{:S(2)}) copy-start(bf16[256,256]{1,0:T(8,128)(2,1)S(1)} %collective-permute-done.16.refs_10_.refs_26_) | copy-start | bytes 393220
  149.0 10.3 %collective-permute-start.15 = (bf16[256,256]{1,0:T(8,128)(2,1)S(1)}, bf16[256,256]{1,0:T(8,128)(2,1)S(1)}, u32[]{:S(2)}, u32[]{:S(2)}) collective-permute-start(bf16[256,256]{1,0:T(8,128)(2,1)S(1)} %copy-done.37), channel_id=1, source_target_pairs={{0,3},{1,2},{2,1},{3,0},{4,7},{5,6},{6,5},{7,4},{8,11},{9,10},{10,... | collective-permute-start | bytes 393224 | tf_op jit(solution)/shard_map/ppermute | solution.py:574
  151.7 13.1 %copy-start.25 = (bf16[256,256]{1,0:T(8,128)(2,1)}, bf16[256,256]{1,0:T(8,128)(2,1)S(1)}, u32[]{:S(2)}) copy-start(bf16[256,256]{1,0:T(8,128)(2,1)S(1)} %collective-permute-done.17.refs_11_.refs_27_) | copy-start | bytes 393220
  151.7 7.5 %collective-permute-start.10 = (bf16[256,256]{1,0:T(8,128)(2,1)S(1)}, bf16[256,256]{1,0:T(8,128)(2,1)S(1)}, u32[]{:S(2)}, u32[]{:S(2)}) collective-permute-start(bf16[256,256]{1,0:T(8,128)(2,1)S(1)} %copy-done.38), channel_id=1, source_target_pairs={{0,1},{1,0},{2,3},{3,2},{4,5},{5,4},{6,7},{7,6},{8,9},{9,8},{10,11... | collective-permute-start | bytes 393224 | tf_op jit(solution)/shard_map/ppermute | solution.py:574
  153.6 11.2 %copy-start.26 = (bf16[256,256]{1,0:T(8,128)(2,1)}, bf16[256,256]{1,0:T(8,128)(2,1)S(1)}, u32[]{:S(2)}) copy-start(bf16[256,256]{1,0:T(8,128)(2,1)S(1)} %collective-permute-done.18.refs_12_.refs_28_) | copy-start | bytes 393220
  153.6 9.3 %collective-permute-start.11 = (bf16[256,256]{1,0:T(8,128)(2,1)S(1)}, bf16[256,256]{1,0:T(8,128)(2,1)S(1)}, u32[]{:S(2)}, u32[]{:S(2)}) collective-permute-start(bf16[256,256]{1,0:T(8,128)(2,1)S(1)} %copy-done.39), channel_id=1, source_target_pairs={{0,2},{1,3},{2,0},{3,1},{4,6},{5,7},{6,4},{7,5},{8,10},{9,11},{10,... | collective-permute-start | bytes 393224 | tf_op jit(solution)/shard_map/ppermute | solution.py:574
  155.1 9.8 %copy-start.27 = (bf16[256,256]{1,0:T(8,128)(2,1)}, bf16[256,256]{1,0:T(8,128)(2,1)S(1)}, u32[]{:S(2)}) copy-start(bf16[256,256]{1,0:T(8,128)(2,1)S(1)} %collective-permute-done.13.refs_6_.refs_22_) | copy-start | bytes 393220
  155.1 9.7 %collective-permute-start.12 = (bf16[256,256]{1,0:T(8,128)(2,1)S(1)}, bf16[256,256]{1,0:T(8,128)(2,1)S(1)}, u32[]{:S(2)}, u32[]{:S(2)}) collective-permute-start(bf16[256,256]{1,0:T(8,128)(2,1)S(1)} %copy-done.40), channel_id=1, source_target_pairs={{0,3},{1,2},{2,1},{3,0},{4,7},{5,6},{6,5},{7,4},{8,11},{9,10},{10,... | collective-permute-start | bytes 393224 | tf_op jit(solution)/shard_map/ppermute | solution.py:574
  157.3 7.5 %copy-start.28 = (bf16[256,256]{1,0:T(8,128)(2,1)}, bf16[256,256]{1,0:T(8,128)(2,1)S(1)}, u32[]{:S(2)}) copy-start(bf16[256,256]{1,0:T(8,128)(2,1)S(1)} %collective-permute-done.14.refs_7_.refs_23_) | copy-start | bytes 393220
  235.2 5.5 %collective-permute-start.21 = (bf16[3,256,256]{2,1,0:T(8,128)(2,1)}, bf16[3,256,256]{2,1,0:T(8,128)(2,1)S(1)}, u32[]{:S(2)}, u32[]{:S(2)}) collective-permute-start(bf16[3,256,256]{2,1,0:T(8,128)(2,1)} %get-tuple-element.153), channel_id=1, source_target_pairs={{0,1},{1,0},{2,3},{3,2},{4,5},{5,4},{6,7},{7,6},{8,9},{9,8},{10,11... | collective-permute-start | bytes 1179656 | tf_op jit(solution)/shard_map/ppermute | solution.py:574
  235.6 12.2 %collective-permute-start.22 = (bf16[3,256,256]{2,1,0:T(8,128)(2,1)}, bf16[3,256,256]{2,1,0:T(8,128)(2,1)S(1)}, u32[]{:S(2)}, u32[]{:S(2)}) collective-permute-start(bf16[3,256,256]{2,1,0:T(8,128)(2,1)} %get-tuple-element.154), channel_id=1, source_target_pairs={{0,2},{1,3},{2,0},{3,1},{4,6},{5,7},{6,4},{7,5},{8,10},{9,11},{10,... | collective-permute-start | bytes 1179656 | tf_op jit(solution)/shard_map/ppermute | solution.py:574
  237.1 17.6 %collective-permute-start.23 = (bf16[3,256,256]{2,1,0:T(8,128)(2,1)}, bf16[3,256,256]{2,1,0:T(8,128)(2,1)}, u32[]{:S(2)}, u32[]{:S(2)}) collective-permute-start(bf16[3,256,256]{2,1,0:T(8,128)(2,1)} %get-tuple-element.155), channel_id=1, source_target_pairs={{0,3},{1,2},{2,1},{3,0},{4,7},{5,6},{6,5},{7,4},{8,11},{9,10},{10,... | collective-permute-start | bytes 1179656 | tf_op jit(solution)/shard_map/ppermute | solution.py:574
  240.7 16.3 %copy-start.8 = (bf16[3,256,256]{2,1,0:T(8,128)(2,1)}, bf16[3,256,256]{2,1,0:T(8,128)(2,1)S(1)}, u32[]{:S(2)}) copy-start(bf16[3,256,256]{2,1,0:T(8,128)(2,1)S(1)} %collective-permute-done.21.refs_5_) | copy-start | bytes 1179652
  247.8 9.2 %copy-start.9 = (bf16[3,256,256]{2,1,0:T(8,128)(2,1)}, bf16[3,256,256]{2,1,0:T(8,128)(2,1)S(1)}, u32[]{:S(2)}) copy-start(bf16[3,256,256]{2,1,0:T(8,128)(2,1)S(1)} %collective-permute-done.22.refs_6_) | copy-start | bytes 1179652
  257.0 52.0 %all-to-all-start = ((bf16[32,3,6656]{2,1,0:T(4,128)(2,1)}), bf16[32,3,6656]{2,1,0:T(4,128)(2,1)S(1)}, u32[]{:S(2)}, u32[]{:S(2)}) async-start(bf16[32,3,6656]{2,1,0:T(4,128)(2,1)} %copy.101), calls=%async_computation | async-start | bytes 3407872 | tf_op jit(solution)/shard_map/all_to_all | solution.py:582
  260.1 115.0 %all-gather.5.cloned.1.call-start = ((), (), s32[]{:S(2)}) async-start(), calls=%async_computation.4 | async-start | bytes 3514368 | tf_op jit(solution)/shard_map/all_gather | solution.py:817
  280.4 2.9 collective-permute-start.24
  285.3 23.7 %collective-permute-start.25 = (bf16[256,1024]{1,0:T(8,128)(2,1)}, bf16[256,1024]{1,0:T(8,128)(2,1)}, u32[]{:S(2)}, u32[]{:S(2)}) collective-permute-start(bf16[256,1024]{1,0:T(8,128)(2,1)} %fusion.19), channel_id=1, source_target_pairs={{0,2},{1,3},{2,0},{3,1},{4,6},{5,7},{6,4},{7,5},{8,10},{9,11},{10,... | collective-permute-start | bytes 1572872 | tf_op jit(solution)/shard_map/ppermute | solution.py:574
  310.6 2.9 collective-permute-start.26
  313.5 22.1 %copy-start.18 = (bf16[2,256,1024]{2,1,0:T(8,128)(2,1)}, bf16[2,256,1024]{2,1,0:T(8,128)(2,1)S(1)}, u32[]{:S(2)}) copy-start(bf16[2,256,1024]{2,1,0:T(8,128)(2,1)S(1)} %collective-permute-done.26) | copy-start | bytes 3145732
  314.7 21.0 %collective-permute-start.27 = (bf16[256,1024]{1,0:T(8,128)(2,1)}, bf16[256,1024]{1,0:T(8,128)(2,1)}, u32[]{:S(2)}, u32[]{:S(2)}) collective-permute-start(bf16[256,1024]{1,0:T(8,128)(2,1)} %fusion.20), channel_id=1, source_target_pairs={{0,2},{1,3},{2,0},{3,1},{4,6},{5,7},{6,4},{7,5},{8,10},{9,11},{10,... | collective-permute-start | bytes 1572872 | tf_op jit(solution)/shard_map/ppermute | solution.py:574
  314.9 21.0 %copy-start.48 = (bf16[16,1024]{1,0:T(8,128)(2,1)S(1)}, bf16[16,1024]{1,0:T(8,128)(2,1)}, u32[]{:S(2)}) copy-start(bf16[16,1024]{1,0:T(8,128)(2,1)} %get-tuple-element.178) | copy-start | bytes 98308
  314.9 21.0 %copy-start.49 = (bf16[16,1024]{1,0:T(8,128)(2,1)S(1)}, bf16[16,1024]{1,0:T(8,128)(2,1)}, u32[]{:S(2)}) copy-start(bf16[16,1024]{1,0:T(8,128)(2,1)} %get-tuple-element.179) | copy-start | bytes 98308
  314.9 22.7 %copy-start.51 = (bf16[3,16,256]{2,1,0:T(8,128)(2,1)S(1)}, bf16[3,16,256]{2,1,0:T(8,128)(2,1)}, u32[]{:S(2)}) copy-start(bf16[3,16,256]{2,1,0:T(8,128)(2,1)} %get-tuple-element.182) | copy-start | bytes 73732
  314.9 22.8 %copy-start.50 = (bf16[3,16,256]{2,1,0:T(8,128)(2,1)S(1)}, bf16[3,16,256]{2,1,0:T(8,128)(2,1)}, u32[]{:S(2)}) copy-start(bf16[3,16,256]{2,1,0:T(8,128)(2,1)} %get-tuple-element.181) | copy-start | bytes 73732
  335.7 3.1 collective-permute-start.28
  336.7 11.2 %copy-start.15 = (bf16[2,256,1024]{2,1,0:T(8,128)(2,1)S(1)}, bf16[2,256,1024]{2,1,0:T(8,128)(2,1)}, u32[]{:S(2)}) copy-start(bf16[2,256,1024]{2,1,0:T(8,128)(2,1)} %get-tuple-element.161) | copy-start | bytes 3145732
  340.8 20.8 %collective-permute-start.29 = (bf16[256,1024]{1,0:T(8,128)(2,1)}, bf16[256,1024]{1,0:T(8,128)(2,1)}, u32[]{:S(2)}, u32[]{:S(2)}) collective-permute-start(bf16[256,1024]{1,0:T(8,128)(2,1)} %fusion.21), channel_id=1, source_target_pairs={{0,2},{1,3},{2,0},{3,1},{4,6},{5,7},{6,4},{7,5},{8,10},{9,11},{10,... | collective-permute-start | bytes 1572872 | tf_op jit(solution)/shard_map/ppermute | solution.py:574
  343.3 18.2 %all-to-all-start.1 = ((bf16[32,6,448]{2,1,0:T(8,128)(2,1)}), bf16[32,6,448]{2,1,0:T(8,128)(2,1)S(1)}, u32[]{:S(2)}, u32[]{:S(2)}) async-start(bf16[32,6,448]{2,1,0:T(8,128)(2,1)} %copy.105), calls=%async_computation.1 | async-start | bytes 524288 | tf_op jit(solution)/shard_map/all_to_all | solution.py:582
  362.6 8.5 %copy-start.3 = (bf16[3,256,1024]{2,1,0:T(8,128)(2,1)S(1)}, bf16[3,256,1024]{2,1,0:T(8,128)(2,1)}, u32[]{:S(2)}) copy-start(bf16[3,256,1024]{2,1,0:T(8,128)(2,1)} %refs_13_.1) | copy-start | bytes 4718596
  362.6 8.5 %copy-start.42 = (f32[3,256]{1,0:T(4,128)S(1)}, f32[3,256]{1,0:T(4,128)}, u32[]{:S(2)}) copy-start(f32[3,256]{1,0:T(4,128)} %copy-done.41) | copy-start | bytes 9220
  362.6 8.5 %copy-start.45 = (f32[1024]{0:T(1024)S(1)}, f32[1024]{0:T(1024)}, u32[]{:S(2)}) copy-start(f32[1024]{0:T(1024)} %copy-done.44) | copy-start | bytes 12292
  362.6 8.5 %copy-start.47 = (f32[3,256]{1,0:T(4,128)S(1)}, f32[3,256]{1,0:T(4,128)}, u32[]{:S(2)}) copy-start(f32[3,256]{1,0:T(4,128)} %copy-done.46) | copy-start | bytes 9220
  363.5 21.3 %all-to-all-start.2 = ((bf16[32,16,448]{2,1,0:T(8,128)(2,1)}), bf16[32,16,448]{2,1,0:T(8,128)(2,1)S(1)}, u32[]{:S(2)}, u32[]{:S(2)}) async-start(bf16[32,16,448]{2,1,0:T(8,128)(2,1)} %bitcast.196), calls=%async_computation.2 | async-start | bytes 1048576 | tf_op jit(solution)/shard_map/all_to_all | solution.py:582
  373.0 14.8 %copy-start.1 = (bf16[8,16,2,656]{3,2,1,0:T(2,128)(2,1)S(1)}, bf16[8,16,2,656]{3,2,1,0:T(2,128)(2,1)}, u32[]{:S(2)}) copy-start(bf16[8,16,2,656]{3,2,1,0:T(2,128)(2,1)} %param.33) | copy-start | bytes 1007620
  (25 other events, 97.5 us)
Sparse Core Ops, SparseCore 0:
  11.5 154.6 all-gather.2
  310.7 62.4 all-gather.4
